TPU v7x, 32 devices: a whole 2x2x4 slice. The times are simulated.
32 devices in a mesh: seq: 8 (over z, x), batch: 4 (over y, core).
Axes of the slice: x: 2, y: 2, z: 4, core: 2. Of those that a mesh axis runs over, the one named last changes fastest.
Arguments:
- tokens: bfloat16 [4, 2048, 2048], P('batch', 'seq'), may hold values from -6 to 6
- lengths: int32 [4, 1], replicated, may hold values from 512 to 2048, as said below
- cotangent: bfloat16 [4, 2048, 2048], P('batch', 'seq'), may hold values from -6 to 6
- ln1_gain: bfloat16 [2048], P(('seq', 'batch')), may hold values from 0.5 to 1.5
- ln1_bias: bfloat16 [2048], P(('seq', 'batch')), may hold values from -1.5 to 1.5
- w_qkv: bfloat16 [2048, 3, 2048], P('seq', None, 'batch'), may hold values from -0.1875 to 0.1875
- qv_bias: bfloat16 [2, 2048], P(None, 'batch'), may hold values from -1.5 to 1.5
- w_out: bfloat16 [2048, 2048], P('batch', 'seq'), may hold values from -0.375 to 0.375
- out_bias: bfloat16 [2048], P(('seq', 'batch')), may hold values from -1.5 to 1.5
- ln2_gain: bfloat16 [2048], P(('seq', 'batch')), may hold values from 0.5 to 1.5
- ln2_bias: bfloat16 [2048], P(('seq', 'batch')), may hold values from -1.5 to 1.5
- w_fc: bfloat16 [2048, 8192], P('seq', 'batch'), may hold values from -0.125 to 0.125
- fc_bias: bfloat16 [8192], P('batch'), may hold values from -1.5 to 1.5
- w_proj: bfloat16 [8192, 2048], P('batch', 'seq'), may hold values from -0.0625 to 0.0625
- proj_bias: bfloat16 [2048], P(('seq', 'batch')), may hold values from -1.5 to 1.5
Outputs:
- block_out: bfloat16 [4, 2048, 2048], P('batch', 'seq')
- grad_tokens: bfloat16 [4, 2048, 2048], P('batch', 'seq')
- grad_ln1_gain: float32 [2048], P(('seq', 'batch'))
- grad_ln1_bias: float32 [2048], P(('seq', 'batch'))
- grad_w_qkv: float32 [2048, 3, 2048], P('seq', None, 'batch')
- grad_qv_bias: float32 [2, 2048], P(None, 'batch')
- grad_w_out: float32 [2048, 2048], P('batch', 'seq')
- grad_out_bias: float32 [2048], P(('seq', 'batch'))
- grad_ln2_gain: float32 [2048], P(('seq', 'batch'))
- grad_ln2_bias: float32 [2048], P(('seq', 'batch'))
- grad_w_fc: float32 [2048, 8192], P('seq', 'batch')
- grad_fc_bias: float32 [8192], P('batch')
- grad_w_proj: float32 [8192, 2048], P('batch', 'seq')
- grad_proj_bias: float32 [2048], P(('seq', 'batch'))
Inputs may be any that keep to these rules, and one draw needn't show every extreme that they name: `lengths`: some sequence has all 2048 slots true and some other has exactly 512.
All inputs are finite; a program needn't handle non-finite values.
Results may differ from a plain program's by a relative error of at most 0.018.
Values may be sent and summed in bfloat16 or wider, within the bound.
No kernel may reach another device: no remote copies, remote signals or barrier semaphores. Data moves between devices by JAX's collectives and lax.ppermute only.
A program may use at most 448 MiB of HBM per device.

v0:
```python
import jax
import jax.numpy as jnp
from jax import lax
from jax.sharding import PartitionSpec as P

HEAD_DIM = 128
WINDOW = 256


def shifted(value, axis, steps):
    count = lax.axis_size(axis)
    initial, last = (max(0, -steps), min(count, count - steps))
    return lax.ppermute(value, axis, [(source, source + steps) for source in range(initial, last)])


def layer_norm(values, gain, shift):
    mean = jnp.mean(values, axis=-1, keepdims=True)
    centered = values - mean
    factor = lax.rsqrt(jnp.mean(centered * centered, axis=-1, keepdims=True) + 1e-05)
    return centered * factor * gain + shift


def gelu_tanh(values):
    return jax.nn.gelu(values, approximate=True)


def allowed_keys(query_pos, key_pos, limit, seq_length):
    later = query_pos[:, None]
    earlier = key_pos[None, :]
    gap = later - earlier
    same = later // seq_length == earlier // seq_length
    live = (earlier % seq_length < limit[:, None]) | (gap == 0)
    return (earlier >= 0) & (gap >= 0) & (gap < WINDOW) & same & live


def limits_of(chain_lengths, chain_pos, seq_length):
    owner = chain_pos // seq_length
    slots = jnp.arange(chain_lengths.shape[1], dtype=jnp.int32)
    match = owner[:, None] == slots[None, :]
    return jnp.sum(jnp.where(match[None], chain_lengths[:, None, :], 0), axis=2)


def bias_total(values):
    return lax.psum(values.astype(jnp.bfloat16), "seq").astype(jnp.float32)


def rows_total(pair):
    return (
        lax.psum_scatter(
            pair[0].astype(jnp.bfloat16), "seq", scatter_dimension=0, tiled=True
        ).astype(jnp.float32),
        lax.psum_scatter(
            pair[1].astype(jnp.bfloat16), "seq", scatter_dimension=1, tiled=True
        ).astype(jnp.float32),
    )


def shards(
    tokens,
    lengths,
    cotangent,
    ln1_gain,
    ln1_bias,
    w_qkv,
    qv_bias,
    w_out,
    out_bias,
    ln2_gain,
    ln2_bias,
    w_fc,
    fc_bias,
    w_proj,
    proj_bias,
):
    floaty = jnp.float32
    brain = jnp.bfloat16
    rows = tokens.shape[1]
    width = tokens.shape[2]
    head_dim = HEAD_DIM
    scale = head_dim ** (-0.5)
    seq_length = rows * lax.axis_size("seq") // lengths.shape[1]
    norm_vectors = (
        lax.all_gather(ln1_gain, ("seq", "batch"), axis=0, tiled=True),
        lax.all_gather(ln1_bias, ("seq", "batch"), axis=0, tiled=True),
        lax.all_gather(out_bias, ("seq", "batch"), axis=0, tiled=True),
        lax.all_gather(ln2_gain, ("seq", "batch"), axis=0, tiled=True),
        lax.all_gather(ln2_bias, ("seq", "batch"), axis=0, tiled=True),
        lax.all_gather(proj_bias, ("seq", "batch"), axis=0, tiled=True),
    )
    gain_one, shift_one, mix_shift, gain_two, shift_two, down_shift = (
        v.astype(floaty) for v in norm_vectors
    )
    proj_in, proj_mix, proj_up, proj_down = (
        lax.all_gather(w_qkv, "seq", axis=0, tiled=True),
        lax.all_gather(w_out, "seq", axis=1, tiled=True),
        lax.all_gather(w_fc, "seq", axis=0, tiled=True),
        lax.all_gather(w_proj, "seq", axis=1, tiled=True),
    )
    own_lengths = lax.dynamic_slice_in_dim(lengths, lax.axis_index("batch"), 1, 0)
    proj_in, qv_shift, proj_mix, proj_up, up_shift, proj_down = (
        lax.all_gather(proj_in, "batch", axis=2, tiled=True),
        lax.all_gather(qv_bias, "batch", axis=1, tiled=True),
        lax.all_gather(proj_mix, "batch", axis=0, tiled=True),
        lax.all_gather(proj_up, "batch", axis=1, tiled=True),
        lax.all_gather(fc_bias, "batch", axis=0, tiled=True),
        lax.all_gather(proj_down, "batch", axis=0, tiled=True),
    )
    local_width = proj_in.shape[2]
    local_heads = local_width // head_dim
    chains = own_lengths.shape[0]
    flat_rows = chains * rows
    block_start = lax.axis_index("seq") * rows
    chain_pos = block_start + jnp.arange(rows, dtype=jnp.int32)
    key_pos = block_start - WINDOW + jnp.arange(rows + WINDOW, dtype=jnp.int32)
    own_limit = limits_of(own_lengths, chain_pos, seq_length)[0]
    valid = (chain_pos % seq_length < own_limit).astype(floaty)
    limits = limits_of(own_lengths, chain_pos, seq_length)
    mask = jax.vmap(lambda bound: allowed_keys(chain_pos, key_pos, bound, seq_length))(limits)
    inputs = tokens.astype(floaty)
    normed_f, norm_one_back = jax.vjp(layer_norm, inputs, gain_one, shift_one)
    normed = normed_f.astype(brain).reshape(flat_rows, width)
    packed = jnp.dot(
        normed, proj_in.reshape(width, 3 * local_width), preferred_element_type=floaty
    ).reshape(chains, rows, 3, local_width)
    qv_float = qv_shift.astype(floaty)
    query = (packed[:, :, 0] + qv_float[0]).astype(brain)
    key = packed[:, :, 1].astype(brain)
    value = (packed[:, :, 2] + qv_float[1]).astype(brain)
    halo_keys, halo_values = shifted((key, value), "seq", 1)
    keys = jnp.concatenate([halo_keys, key], axis=1).reshape(
        chains, rows + WINDOW, local_heads, head_dim
    )
    values = jnp.concatenate([halo_values, value], axis=1).reshape(
        chains, rows + WINDOW, local_heads, head_dim
    )
    query4 = query.reshape(chains, rows, local_heads, head_dim)
    scores = jnp.einsum("cqhd,ckhd->chqk", query4, keys, preferred_element_type=floaty) * scale
    scores = jnp.where(mask[:, None], scores, -1e30)
    top = jnp.max(scores, axis=-1, keepdims=True)
    expo = jnp.exp(scores - top)
    total = jnp.sum(expo, axis=-1, keepdims=True)
    logsum = top + jnp.log(total)
    probs = (expo / total).astype(brain)
    mixed = (
        jnp.einsum("chqk,ckhd->cqhd", probs, values, preferred_element_type=floaty)
        .reshape(flat_rows, local_width)
        .astype(brain)
    )
    branch = jnp.dot(mixed, proj_mix, preferred_element_type=floaty).reshape(chains, rows, width)
    resid = inputs + branch + mix_shift
    second_f, norm_two_back = jax.vjp(layer_norm, resid, gain_two, shift_two)
    second = second_f.astype(brain).reshape(flat_rows, width)
    pre = jnp.dot(second, proj_up, preferred_element_type=floaty) + up_shift.astype(floaty)
    active_f, gelu_back = jax.vjp(gelu_tanh, pre)
    active = active_f.astype(brain)
    ffn = jnp.dot(active, proj_down, preferred_element_type=floaty).reshape(chains, rows, width)
    result = resid + ffn + down_shift
    block_out = result.astype(brain)
    grad_out = cotangent.astype(floaty) * valid[None, :, None]
    grad_y_own = grad_out.astype(brain)
    grad_proj_bias = jnp.sum(grad_y_own.astype(floaty), axis=(0, 1))
    grad_y = grad_y_own.reshape(flat_rows, width)
    grad_w_proj = jnp.einsum("tf,td->fd", active, grad_y, preferred_element_type=floaty)
    grad_active = jnp.einsum("td,fd->tf", grad_y, proj_down, preferred_element_type=floaty)
    grad_pre = gelu_back(grad_active)[0].astype(brain)
    grad_fc_bias = bias_total(jnp.sum(grad_pre.astype(floaty), axis=0))
    grad_w_fc = jnp.einsum("td,tf->df", second, grad_pre, preferred_element_type=floaty)
    grad_second = jnp.einsum("tf,df->td", grad_pre, proj_up, preferred_element_type=floaty).reshape(
        chains, rows, width
    )
    grad_resid_norm, grad_ln2_gain, grad_ln2_bias = norm_two_back(grad_second)
    grad_resid = grad_out + grad_resid_norm
    fc_rows, proj_rows = rows_total((grad_w_fc, grad_w_proj))
    fc_rows, grad_fc_bias, proj_rows = (
        lax.psum_scatter(
            fc_rows.astype(jnp.bfloat16), "batch", scatter_dimension=1, tiled=True
        ).astype(jnp.float32),
        lax.psum_scatter(
            grad_fc_bias.astype(jnp.bfloat16), "batch", scatter_dimension=0, tiled=True
        ).astype(jnp.float32),
        lax.psum_scatter(
            proj_rows.astype(jnp.bfloat16), "batch", scatter_dimension=0, tiled=True
        ).astype(jnp.float32),
    )
    grad_branch_own = grad_resid.astype(brain)
    grad_out_bias = jnp.sum(grad_branch_own.astype(floaty), axis=(0, 1))
    grad_branch = grad_branch_own.reshape(flat_rows, width)
    grad_w_out = jnp.einsum("td,te->de", mixed, grad_branch, preferred_element_type=floaty)
    grad_mixed = jnp.einsum(
        "te,de->td", grad_branch, proj_mix, preferred_element_type=floaty
    ).astype(brain)
    grad_mixed4 = grad_mixed.reshape(chains, rows, local_heads, head_dim)
    again = jnp.einsum("cqhd,ckhd->chqk", query4, keys, preferred_element_type=floaty) * scale
    weights_f = jnp.where(mask[:, None], jnp.exp(again - logsum), 0.0)
    grad_probs = jnp.einsum("cqhd,ckhd->chqk", grad_mixed4, values, preferred_element_type=floaty)
    delta = jnp.sum(weights_f * grad_probs, axis=-1, keepdims=True)
    grad_scores = (weights_f * (grad_probs - delta)).astype(brain)
    grad_values = jnp.einsum(
        "chqk,cqhd->ckhd", weights_f.astype(brain), grad_mixed4, preferred_element_type=floaty
    ).reshape(chains, rows + WINDOW, local_width)
    grad_query = (
        (jnp.einsum("chqk,ckhd->cqhd", grad_scores, keys, preferred_element_type=floaty) * scale)
        .reshape(chains, rows, local_width)
        .astype(brain)
    )
    grad_keys = (
        jnp.einsum("chqk,cqhd->ckhd", grad_scores, query4, preferred_element_type=floaty) * scale
    ).reshape(chains, rows + WINDOW, local_width)
    back_keys, back_values = (
        shifted(grad_keys[:, :WINDOW].astype(jnp.bfloat16), "seq", -1).astype(jnp.float32),
        shifted(grad_values[:, :WINDOW].astype(jnp.bfloat16), "seq", -1).astype(jnp.float32),
    )
    own_keys = grad_keys[:, WINDOW:]
    own_values = grad_values[:, WINDOW:]
    own_keys = jnp.concatenate([own_keys[:, : rows - WINDOW], own_keys + back_keys], axis=1).astype(
        brain
    )
    own_values = jnp.concatenate(
        [own_values[:, : rows - WINDOW], own_values + back_values], axis=1
    ).astype(brain)
    grad_packed = jnp.stack([grad_query, own_keys, own_values], axis=2).reshape(
        flat_rows, 3 * local_width
    )
    grad_qv_bias = bias_total(
        jnp.stack(
            [
                jnp.sum(grad_query.astype(floaty), axis=(0, 1)),
                jnp.sum(own_values.astype(floaty), axis=(0, 1)),
            ],
            axis=0,
        )
    )
    grad_w_qkv = jnp.einsum(
        "td,te->de", normed, grad_packed, preferred_element_type=floaty
    ).reshape(width, 3, local_width)
    grad_normed = jnp.einsum(
        "te,de->td",
        grad_packed,
        proj_in.reshape(width, 3 * local_width),
        preferred_element_type=floaty,
    ).reshape(chains, rows, width)
    grad_input_norm, grad_ln1_gain, grad_ln1_bias = norm_one_back(grad_normed)
    grad_tokens = (grad_resid + grad_input_norm).astype(brain)
    qkv_rows, out_rows = rows_total((grad_w_qkv, grad_w_out))
    qkv_rows, grad_qv_bias, out_rows = (
        lax.psum_scatter(
            qkv_rows.astype(jnp.bfloat16), "batch", scatter_dimension=2, tiled=True
        ).astype(jnp.float32),
        lax.psum_scatter(
            grad_qv_bias.astype(jnp.bfloat16), "batch", scatter_dimension=1, tiled=True
        ).astype(jnp.float32),
        lax.psum_scatter(
            out_rows.astype(jnp.bfloat16), "batch", scatter_dimension=0, tiled=True
        ).astype(jnp.float32),
    )
    norm_sums = (
        lax.psum_scatter(grad_ln1_gain, ("seq", "batch"), scatter_dimension=0, tiled=True),
        lax.psum_scatter(grad_ln1_bias, ("seq", "batch"), scatter_dimension=0, tiled=True),
        lax.psum_scatter(grad_out_bias, ("seq", "batch"), scatter_dimension=0, tiled=True),
        lax.psum_scatter(grad_ln2_gain, ("seq", "batch"), scatter_dimension=0, tiled=True),
        lax.psum_scatter(grad_ln2_bias, ("seq", "batch"), scatter_dimension=0, tiled=True),
        lax.psum_scatter(grad_proj_bias, ("seq", "batch"), scatter_dimension=0, tiled=True),
    )
    return (
        block_out,
        grad_tokens,
        norm_sums[0],
        norm_sums[1],
        qkv_rows,
        grad_qv_bias,
        out_rows,
        norm_sums[2],
        norm_sums[3],
        norm_sums[4],
        fc_rows,
        grad_fc_bias,
        proj_rows,
        norm_sums[5],
    )


def solution(mesh):
    placed = (
        P("batch", "seq", None),
        P(),
        P("batch", "seq", None),
        P(("seq", "batch")),
        P(("seq", "batch")),
        P("seq", None, "batch"),
        P(None, "batch"),
        P("batch", "seq"),
        P(("seq", "batch")),
        P(("seq", "batch")),
        P(("seq", "batch")),
        P("seq", "batch"),
        P("batch"),
        P("batch", "seq"),
        P(("seq", "batch")),
    )
    return jax.shard_map(
        shards,
        mesh=mesh,
        in_specs=placed,
        out_specs=(
            P("batch", "seq", None),
            P("batch", "seq", None),
            P(("seq", "batch")),
            P(("seq", "batch")),
            P("seq", None, "batch"),
            P(None, "batch"),
            P("batch", "seq"),
            P(("seq", "batch")),
            P(("seq", "batch")),
            P(("seq", "batch")),
            P("seq", "batch"),
            P("batch"),
            P("batch", "seq"),
            P(("seq", "batch")),
        ),
        check_vma=False,
    )
```

profile of v0, /device:TPU:0, one launch (start us, length us, event | category | flops | bytes accessed | tf_op | source)
XLA Modules:
  0.0 2975.8 jit_solution(15007568904424727592)
XLA Ops:
  7.2 2.3 copy.54
  11.7 101.7 %all-gather.9.cloned.1.call-done = bf16[2048,3,512]{0,2,1:T(8,128)(2,1)} async-done(((bf16[256,3,512]{0,2,1:T(8,128)(2,1)}), bf16[2048,3,512]{0,2,1:T(8,128)(2,1)}) %all-gather.9.cloned.1.call-update) | async-done | bytes 6291472 | tf_op jit(solution)/shard_map/all_gather | solution.py:94
  113.4 51.3 %all-gather.13.cloned.1.call-done = bf16[512,2048]{1,0:T(8,128)(2,1)} async-done(((bf16[512,256]{1,0:T(8,128)(2,1)}), bf16[512,2048]{1,0:T(8,128)(2,1)}) %all-gather.13.cloned.1.call-update) | async-done | bytes 2097168 | tf_op jit(solution)/shard_map/all_gather | solution.py:95
  164.7 125.2 %all-gather.17.cloned.1.call-done = bf16[2048,2048]{1,0:T(8,128)(2,1)} async-done(((bf16[256,2048]{1,0:T(8,128)(2,1)}), bf16[2048,2048]{1,0:T(8,128)(2,1)}) %all-gather.17.cloned.1.call-update) | async-done | bytes 8388624 | tf_op jit(solution)/shard_map/all_gather | solution.py:96
  290.0 125.4 %all-gather.21.cloned.1.call-done = bf16[2048,2048]{1,0:T(8,128)(2,1)} async-done(((bf16[2048,256]{1,0:T(8,128)(2,1)}), bf16[2048,2048]{1,0:T(8,128)(2,1)}) %all-gather.21.cloned.1.call-update) | async-done | bytes 8388624 | tf_op jit(solution)/shard_map/all_gather | solution.py:97
  417.5 39.1 %all-reduce.14 = (bf16[2048]{0:T(1024)(128)(2,1)S(1)}, bf16[2048]{0:T(1024)(128)(2,1)S(1)}, bf16[2048]{0:T(1024)(128)(2,1)S(1)}, bf16[2048]{0:T(1024)(128)(2,1)}...) all-reduce(bf16[2048]{0:T(1024)(128)(2,1)S(1)} %dynamic-update-slic, ...), channel_id=1, replica_groups=mesh['seq'=8,'batch'=4] {'seq','batch'}, use_global_device_ids=true, to_apply=%add.1 | all-reduce | flops 12288 | bytes 49152
  456.7 6.2 all_gather.60
  463.4 5.4 all_gather.52
  470.9 99.9 %all-gather.11.cloned.1.call-done = bf16[2048,3,2048]{0,2,1:T(8,128)(2,1)} async-done(((bf16[2048,3,512]{0,2,1:T(8,128)(2,1)}), bf16[2048,3,2048]{0,2,1:T(8,128)(2,1)}) %all-gather.11.cloned.1.call-update) | async-done | bytes 25165840 | tf_op jit(solution)/shard_map/all_gather | solution.py:101
  570.8 13.9 fusion.18
  584.8 2.8 fusion.47
  587.6 4.6 collective-permute-start
  592.2 2.9 fusion.69
  595.1 3.6 collective-permute-start.1
  600.5 3.2 slice_bitcast_fusion
  603.7 1.9 copy.72
  605.7 3.7 copy.71
  609.3 2.9 add_convert_fusion.3
  612.2 2.8 collective-permute-done
  615.0 2.3 copy.70
  617.3 19.5 collective-permute-done.1
  638.5 4.1 select_reduce_fusion
  642.6 2.3 fusion.9
  645.0 2.2 copy-done.2
  647.2 4.1 fusion.50
  651.3 8.9 fusion.97
  660.6 173.1 %all-gather.19.cloned.1.call-done = bf16[2048,8192]{1,0:T(8,128)(2,1)} async-done(((bf16[2048,2048]{1,0:T(8,128)(2,1)}), bf16[2048,8192]{1,0:T(8,128)(2,1)}) %all-gather.19.cloned.1.call-update) | async-done | bytes 33554448 | tf_op jit(solution)/shard_map/all_gather | solution.py:104
  833.6 21.9 convolution_add_fusion
  855.5 181.2 %all-gather.23.cloned.1.call-done = bf16[8192,2048]{1,0:T(8,128)(2,1)} async-done(((bf16[2048,2048]{1,0:T(8,128)(2,1)}), bf16[8192,2048]{1,0:T(8,128)(2,1)}) %all-gather.23.cloned.1.call-update) | async-done | bytes 33554448 | tf_op jit(solution)/shard_map/all_gather | solution.py:106
  1036.7 21.5 fusion.99
  1058.3 17.5 fusion.45
  1075.8 2.3 fusion.95
  1081.0 5.6 convolution_convert_fusion.3
  1086.8 2.0 copy.80
  1093.2 7.3 convolution_convert_fusion.4
  1100.5 2.3 copy.76
  1102.8 5.8 fusion.11
  1111.4 6.3 multiply_reduce_fusion
  1117.7 4.3 multiply_convert_fusion
  1121.9 3.2 convolution_multiply_fusion
  1126.9 2.3 fusion.98
  1129.2 20.3 collective-permute-done.3
  1149.5 2.6 fusion.88
  1152.0 29.3 collective-permute-done.2
  1182.7 13.8 convolution_convert_fusion.2
  1196.6 18.4 convolution_convert_fusion
  1215.0 16.2 convolution_convert_fusion.1
  1231.3 2.3 fusion.87
  1234.7 44.1 %reduce-scatter.16.cloned.1.call-done = bf16[2048,256]{1,0:T(8,128)(2,1)} async-done(((bf16[2048,2048]{1,0:T(8,128)(2,1)}), bf16[2048,256]{1,0:T(8,128)(2,1)}) %reduce-scatter.16.cloned.1.call-update) | async-done | bytes 1048592 | tf_op jit(solution)/shard_map/reduce_scatter | solution.py:52
  1278.9 407.7 %reduce-scatter.12.cloned.1.call-done = bf16[256,3,2048]{2,0,1:T(8,128)(2,1)} async-done(((bf16[2048,3,2048]{2,0,1:T(8,128)(2,1)}), bf16[256,3,2048]{2,0,1:T(8,128)(2,1)}) %reduce-scatter.12.cloned.1.call-update) | async-done | bytes 3145744 | tf_op jit(solution)/shard_map/reduce_scatter | solution.py:49
  1686.7 546.5 %reduce-scatter.24.cloned.1.call-done = bf16[8192,256]{1,0:T(8,128)(2,1)} async-done(((bf16[8192,2048]{1,0:T(8,128)(2,1)}), bf16[8192,256]{1,0:T(8,128)(2,1)}) %reduce-scatter.24.cloned.1.call-update) | async-done | bytes 4194320 | tf_op jit(solution)/shard_map/reduce_scatter | solution.py:52
  2233.3 546.1 %reduce-scatter.20.cloned.1.call-done = bf16[256,8192]{1,0:T(8,128)(2,1)} async-done(((bf16[2048,8192]{1,0:T(8,128)(2,1)}), bf16[256,8192]{1,0:T(8,128)(2,1)}) %reduce-scatter.20.cloned.1.call-update) | async-done | bytes 4194320 | tf_op jit(solution)/shard_map/reduce_scatter | solution.py:49
  2782.4 11.5 all-reduce.11
  2793.9 19.7 fusion.29
  2813.6 2.3 pad_maximum_fusion
  2815.9 11.9 fusion.36
  2829.0 38.6 %all-reduce.13 = (f32[2048]{0:T(1024)S(1)}, f32[2048]{0:T(1024)S(1)}, f32[2048]{0:T(1024)S(1)}, f32[2048]{0:T(1024)S(1)}, f32[2048]{0:T(1024)S(1)}, /*index=5*/f32[2048]{0:T(1024)S(1)}) all-reduce(f32[2048]{0:T(1024)S(1)} %get-tuple-element.16, f32[2048]{0:T(1024)S(1)} %reduce_sum.190, ...), channel_id=2, replica_groups=mesh['seq'=8,'batch'=4] {'seq','batch'}, use_global_device_ids=true, to_apply=%region_12.13.clone | all-reduce | flops 12288 | bytes 98304
  2871.2 3.9 add_convert_fusion
  2876.1 21.3 all-reduce.15
  2900.4 2.5 convert_element_type.290
  2902.9 16.1 reduce-scatter.26.cloned.1.call-done
  2919.0 2.7 convert_element_type.301
  2921.7 44.4 %reduce-scatter.22.cloned.1.call-done = bf16[256,2048]{1,0:T(8,128)(2,1)} async-done(((bf16[256,8192]{1,0:T(8,128)(2,1)}), bf16[256,2048]{1,0:T(8,128)(2,1)}) %reduce-scatter.22.cloned.1.call-update) | async-done | bytes 1048592 | tf_op jit(solution)/shard_map/reduce_scatter | solution.py:175
  2966.0 2.8 convert_element_type.298
  (182 shorter events, 36.6 us)
Async XLA Ops:
  7.2 455.7 %copy-start = (s32[4,1]{0,1:T(1,128)S(1)}, s32[4,1]{0,1:T(1,128)}, u32[]{:S(2)}) copy-start(s32[4,1]{0,1:T(1,128)} %param.16) | copy-start | bytes 52
  7.2 106.1 %all-gather.9.cloned.1.call-start = ((), (), s32[]{:S(2)}) async-start(), calls=%async_computation.9 | async-start | bytes 7077888 | tf_op jit(solution)/shard_map/all_gather | solution.py:94
  9.6 155.1 %all-gather.13.cloned.1.call-start = ((), (), s32[]{:S(2)}) async-start(), calls=%async_computation.11 | async-start | bytes 2359296 | tf_op jit(solution)/shard_map/all_gather | solution.py:95
  10.3 279.6 %all-gather.17.cloned.1.call-start = ((), (), s32[]{:S(2)}) async-start(), calls=%async_computation.13 | async-start | bytes 9437184 | tf_op jit(solution)/shard_map/all_gather | solution.py:96
  11.0 404.4 %all-gather.21.cloned.1.call-start = ((), (), s32[]{:S(2)}) async-start(), calls=%async_computation.15 | async-start | bytes 9437184 | tf_op jit(solution)/shard_map/all_gather | solution.py:97
  11.6 559.2 %all-gather.11.cloned.1.call-start = ((), (), s32[]{:S(2)}) async-start(), calls=%async_computation.10 | async-start | bytes 31457280 | tf_op jit(solution)/shard_map/all_gather | solution.py:101
  113.3 538.0 %all-gather.15.cloned.1.call-start = ((), (), s32[]{:S(2)}) async-start(), calls=%async_computation.12 | async-start | bytes 10485760 | tf_op jit(solution)/shard_map/all_gather | solution.py:103
  164.7 669.0 %all-gather.19.cloned.1.call-start = ((), (), s32[]{:S(2)}) async-start(), calls=%async_computation.14 | async-start | bytes 41943040 | tf_op jit(solution)/shard_map/all_gather | solution.py:104
  290.0 746.8 %all-gather.23.cloned.1.call-start = ((), (), s32[]{:S(2)}) async-start(), calls=%async_computation.16 | async-start | bytes 41943040 | tf_op jit(solution)/shard_map/all_gather | solution.py:106
  415.4 0.7 copy-start.27
  415.4 0.8 copy-start.28
  415.4 1.1 copy-start.29
  415.4 1.3 copy-start.30
  415.4 1.6 copy-start.31
  415.5 1.8 copy-start.32
  415.5 41.2 %copy-start.24 = (bf16[2048]{0:T(1024)(128)(2,1)S(1)}, bf16[2048]{0:T(1024)(128)(2,1)}, u32[]{:S(2)}) copy-start(bf16[2048]{0:T(1024)(128)(2,1)} %param.27) | copy-start | bytes 12292
  415.5 47.9 %copy-start.26 = (bf16[2,512]{1,0:T(2,128)(2,1)S(1)}, bf16[2,512]{1,0:T(2,128)(2,1)}, u32[]{:S(2)}) copy-start(bf16[2,512]{1,0:T(2,128)(2,1)} %param.21) | copy-start | bytes 6148
  415.5 54.7 %copy-start.3 = (bf16[1,256,2048]{2,1,0:T(8,128)(2,1)S(1)}, bf16[1,256,2048]{2,1,0:T(8,128)(2,1)}, u32[]{:S(2)}) copy-start(bf16[1,256,2048]{2,1,0:T(8,128)(2,1)} %param.15) | copy-start | bytes 3145732
  415.5 863.3 %reduce-scatter.16.cloned.1.call-start = ((), (), s32[]{:S(2)}) async-start(), calls=%async_computation.19 | async-start | bytes 9437184 | tf_op jit(solution)/shard_map/reduce_scatter | solution.py:52
  470.8 113.9 %copy-start.22 = (f32[256]{0:T(256)}, f32[256]{0:T(256)S(1)}, u32[]{:S(2)}) copy-start(f32[256]{0:T(256)S(1)} %fusion.35) | copy-start | bytes 3076
  587.6 12.9 copy-start.10
  587.6 27.4 collective-permute-start
  595.1 41.7 %collective-permute-start.1 = (bf16[1,256,2048]{2,1,0:T(8,128)(2,1)}, bf16[1,256,2048]{2,1,0:T(8,128)(2,1)}, u32[]{:S(2)}, u32[]{:S(2)}) collective-permute-start(bf16[1,256,2048]{2,1,0:T(8,128)(2,1)} %get-tuple-element.39), channel_id=1, source_target_pairs={{0,4},{4,8},{8,12},{12,16},{16,20},{20,24},{24,28},{1,5},{5,9},{9,... | collective-permute-start | bytes 3145736 | tf_op jit(solution)/shard_map/ppermute | solution.py:13
  605.6 32.8 %copy-start.6 = (f32[1,256,1,2048]{1,3,2,0:T(8,128)}, f32[1,256,1,2048]{1,3,2,0:T(8,128)S(1)}, u32[]{:S(2)}) copy-start(f32[1,256,1,2048]{1,3,2,0:T(8,128)S(1)} %copy.72) | copy-start | bytes 6291460
  638.5 4.1 copy-start.15
  642.6 4.6 copy-start.2
  642.6 4.6 copy-start.19
  642.6 4.6 copy-start.20
  1075.8 3.6 copy-start.13
  1078.1 1.3 copy-start.5
  1078.1 2.9 copy-start.11
  1080.0 1.0 copy-start.17
  1086.6 600.1 %reduce-scatter.12.cloned.1.call-start = ((), (), s32[]{:S(2)}) async-start(), calls=%async_computation.17 | async-start | bytes 28311552 | tf_op jit(solution)/shard_map/reduce_scatter | solution.py:49
  1088.8 4.4 copy-start.18
  1102.7 8.6 copy-start.9
  1102.7 8.6 copy-start.12
  1102.7 14.9 slice-start
  1108.6 40.9 %copy-start.4 = (f32[16,128,512]{2,1,0:T(8,128)}, f32[16,128,512]{2,1,0:T(8,128)S(1)}, u32[]{:S(2)}) copy-start(f32[16,128,512]{2,1,0:T(8,128)S(1)} %fusion.11) | copy-start | bytes 12582916
  1109.8 7.8 slice-start.1
  1109.8 39.7 %collective-permute-start.3 = (bf16[1,256,2048]{1,2,0:T(8,128)(2,1)}, bf16[1,256,2048]{1,2,0:T(8,128)(2,1)}, u32[]{:S(2)}, u32[]{:S(2)}) collective-permute-start(bf16[1,256,2048]{1,2,0:T(8,128)(2,1)} %slice.68), channel_id=1, source_target_pairs={{4,0},{8,4},{12,8},{16,12},{20,16},{24,20},{28,24},{5,1},{9,5},{13... | collective-permute-start | bytes 3145736 | tf_op jit(solution)/shard_map/ppermute | solution.py:13
  1117.6 4.3 copy-start.7
  1121.9 4.9 copy-start.8
  1121.9 4.9 copy-start.14
  1121.9 4.9 copy-start.16
  1125.3 56.0 %collective-permute-start.2 = (bf16[1,256,2048]{1,2,0:T(8,128)(2,1)S(1)}, bf16[1,256,2048]{1,2,0:T(8,128)(2,1)S(1)}, u32[]{:S(2)}, u32[]{:S(2)}) collective-permute-start(bf16[1,256,2048]{1,2,0:T(8,128)(2,1)S(1)} %slice.69), channel_id=1, source_target_pairs={{4,0},{8,4},{12,8},{16,12},{20,16},{24,20},{28,24},{5,1},{9,5},{13... | collective-permute-start | bytes 3145736 | tf_op jit(solution)/shard_map/ppermute | solution.py:13
  1196.5 1036.7 %reduce-scatter.24.cloned.1.call-start = ((), (), s32[]{:S(2)}) async-start(), calls=%async_computation.23 | async-start | bytes 37748736 | tf_op jit(solution)/shard_map/reduce_scatter | solution.py:52
  1215.0 1564.5 %reduce-scatter.20.cloned.1.call-start = ((), (), s32[]{:S(2)}) async-start(), calls=%async_computation.21 | async-start | bytes 37748736 | tf_op jit(solution)/shard_map/reduce_scatter | solution.py:49
  1231.2 1643.9 %reduce-scatter.28.cloned.1.call-start = ((), (), s32[]{:S(2)}) async-start(), calls=%async_computation.25 | async-start | bytes 655360
  1234.7 1663.9 %reduce-scatter.18.cloned.1.call-start = ((), (), s32[]{:S(2)}) async-start(), calls=%async_computation.20 | async-start | bytes 1310720 | tf_op jit(solution)/shard_map/reduce_scatter | solution.py:252
  1278.9 1621.5 %reduce-scatter.14.cloned.1.call-start = ((), (), s32[]{:S(2)}) async-start(), calls=%async_computation.18 | async-start | bytes 3932160 | tf_op jit(solution)/shard_map/reduce_scatter | solution.py:246
  1686.7 1232.3 %reduce-scatter.26.cloned.1.call-start = ((), (), s32[]{:S(2)}) async-start(), calls=%async_computation.24 | async-start | bytes 5242880 | tf_op jit(solution)/shard_map/reduce_scatter | solution.py:181
  2233.3 546.2 %copy-start.33 = (u32[32]{0:T(128)S(1)}, u32[32]{0:T(128)}, u32[]{:S(2)}) copy-start(u32[32]{0:T(128)} %constant.159) | copy-start | bytes 388
  2233.3 546.8 %copy-start.25 = (bf16[2048]{0:T(1024)(128)(2,1)S(1)}, bf16[2048]{0:T(1024)(128)(2,1)}, u32[]{:S(2)}) copy-start(bf16[2048]{0:T(1024)(128)(2,1)} %get-tuple-element.27) | copy-start | bytes 12292
  2233.3 732.8 %reduce-scatter.22.cloned.1.call-start = ((), (), s32[]{:S(2)}) async-start(), calls=%async_computation.22 | async-start | bytes 5242880 | tf_op jit(solution)/shard_map/reduce_scatter | solution.py:175
  2793.9 19.7 copy-start.21
  2815.9 12.0 copy-start.23
  2871.2 4.9 dynamic-slice-start
  2900.4 68.5 %copy-start.1 = (s32[4,1]{0,1:T(1,128)S(1)}, s32[4,1]{0,1:T(1,128)}, u32[]{:S(2)}) copy-start(s32[4,1]{0,1:T(1,128)} %param.16) | copy-start | bytes 52
Sparse Core Ops, SparseCore 0:
  10.6 102.6 all-gather.8
  115.4 49.2 all-gather.12
  166.8 123.1 all-gather.16
  291.8 123.5 all-gather.20
  416.9 153.9 all-gather.10
  572.2 58.2 all-gather.14
  632.1 201.5 all-gather.18
  835.2 201.4 all-gather.22
  1086.7 192.1 reduce-scatter.15
  1283.1 403.4 reduce-scatter.11
  1690.9 542.2 reduce-scatter.23
  2237.3 542.0 reduce-scatter.19
  2782.7 20.7 reduce-scatter.27
  2805.9 24.8 reduce-scatter.17
  2833.3 38.6 reduce-scatter.13
  2874.4 44.4 reduce-scatter.25
  2921.5 44.5 reduce-scatter.21
where the time goes:
time: 2980 us
  waiting for transfers between devices  2540 us (85%)
  matrix products  202 us (7%)
  blocking collectives  122 us (4%)
  other arithmetic  46 us (2%)
  local copies, waits for them, and re-layouts  41 us (1%)
    reduce_scatter x2, waiting for transfers between devices, rows_total(): lax.psum_scatter(pair[0].astype(jnp.bfloat16), 'seq', scatter_dimension=0...  954 us
    reduce_scatter x2, waiting for transfers between devices, rows_total(): lax.psum_scatter(pair[1].astype(jnp.bfloat16), 'seq', scatter_dimension=1...  591 us
    all_gather x1, waiting for transfers between devices, shards(): lax.all_gather(proj_down, 'batch', axis=0, tiled=True)  181 us
    all_gather x1, waiting for transfers between devices, shards(): lax.all_gather(proj_up, 'batch', axis=1, tiled=True)  173 us
    all_gather x1, waiting for transfers between devices, shards(): lax.all_gather(w_proj, 'seq', axis=1, tiled=True)  125 us
    all_gather x1, waiting for transfers between devices, shards(): lax.all_gather(w_fc, 'seq', axis=0, tiled=True)  125 us
    all_gather x1, waiting for transfers between devices, shards(): lax.all_gather(w_qkv, 'seq', axis=0, tiled=True)  102 us
    all_gather x1, waiting for transfers between devices, shards(): lax.all_gather(proj_in, 'batch', axis=2, tiled=True)  99.9 us
  transfers between devices with their start and end apart: 21, of which 17 were waited for; matrix products, arithmetic and copies ran while one was open for 8% of the time, Pallas kernels for 0%

commit v1 on v0

v1 whole, which is shorter than its diff:
```python
import jax
import jax.numpy as jnp
from jax import lax
from jax.experimental import pallas as pl
from jax.experimental.pallas import tpu as pltpu
from jax.sharding import PartitionSpec as P

HEAD_DIM = 128
WINDOW = 256
F32 = jnp.float32
BF16 = jnp.bfloat16


def ring_order(count):
    return list(range(0, count, 2)) + list(range(count - 1, 0, -2))


def ring_place(index, count):
    return jnp.where(index % 2 == 0, index // 2, count - 1 - index // 2)


def ring_index(place, count):
    return jnp.where(place < count // 2, 2 * place, 2 * (count - 1 - place) + 1)


def hop(value, forward):
    order = ring_order(lax.axis_size("seq"))
    ahead = order[1:] + order[:1]
    pairs = zip(order, ahead) if forward else zip(ahead, order)
    return lax.ppermute(value, "seq", list(pairs))


def swap(value, axis, bit):
    return lax.ppermute(value, axis, [(i, i ^ bit) for i in range(lax.axis_size(axis))])


def bits_of(count):
    return [1 << k for k in range(count.bit_length() - 1)]


def forward_steps(count, flip):
    return count - 1 - count // 2 if flip else count // 2


def ring_gather(value, flip=False):
    count = lax.axis_size("seq")
    slots = [value] + [None] * (count - 1)
    steps = forward_steps(count, flip)
    ahead = behind = value
    for t in range(1, steps + 1):
        ahead = hop(ahead, True)
        slots[count - t] = ahead
        if t <= count - 1 - steps:
            behind = hop(behind, False)
            slots[t] = behind
    for t in range(steps + 1, count - steps):
        behind = hop(behind, False)
        slots[t] = behind
    return slots


def ring_scatter(make, flip=False, wire=BF16):
    count = lax.axis_size("seq")
    steps = forward_steps(count, flip)
    ahead = behind = None
    for j in range(steps, 0, -1):
        part = make(j) if ahead is None else make(j) + ahead.astype(F32)
        ahead = hop(part.astype(wire), True)
    for j in range(steps + 1, count):
        part = make(j) if behind is None else make(j) + behind.astype(F32)
        behind = hop(part.astype(wire), False)
    return make(0) + ahead.astype(F32) + behind.astype(F32)


def seq_total(value):
    for bit in bits_of(lax.axis_size("seq")):
        value = value + swap(value, "seq", bit)
    return value


def batch_gather(value):
    parts = {0: value}
    for bit in reversed(bits_of(lax.axis_size("batch"))):
        parts.update({r | bit: swap(v, "batch", bit) for r, v in list(parts.items())})
    return [parts[r] for r in range(len(parts))]


def batch_scatter(parts, wire=BF16):
    parts = dict(enumerate(parts))
    for bit in bits_of(len(parts)):
        for r in [r for r in parts if r & bit]:
            got = swap(parts[r].astype(wire), "batch", bit)
            parts[r ^ bit] = parts[r ^ bit].astype(F32) + got.astype(F32)
            del parts[r]
    return parts[0]


def to_slots(value, axis=-1):
    count = lax.axis_size("seq")
    width = value.shape[axis] // count
    place = ring_place(lax.axis_index("seq"), count)
    return jnp.concatenate(
        [
            lax.dynamic_slice_in_dim(
                value, ring_index((place + j) % count, count) * width, width, axis
            )
            for j in range(count)
        ],
        axis=axis,
    )


def from_slots(value, axis=-1):
    count = lax.axis_size("seq")
    width = value.shape[axis] // count
    place = ring_place(lax.axis_index("seq"), count)
    return jnp.concatenate(
        [
            lax.dynamic_slice_in_dim(
                value, (ring_place(jnp.int32(i), count) - place) % count * width, width, axis
            )
            for i in range(count)
        ],
        axis=axis,
    )


def norm_stats(values):
    mean = jnp.mean(values, axis=-1, keepdims=True)
    centered = values - mean
    factor = lax.rsqrt(jnp.mean(centered * centered, axis=-1, keepdims=True) + 1e-05)
    return centered * factor, factor


def norm_back(grad, unit, factor, gain):
    scaled = grad * gain
    inner = jnp.mean(scaled * unit, axis=-1, keepdims=True)
    return factor * (scaled - jnp.mean(scaled, axis=-1, keepdims=True) - unit * inner)


def gelu_tanh(values):
    return jax.nn.gelu(values, approximate=True)


def dot_t(left, right, left_dim, right_dim):
    return lax.dot_general(
        left, right, (((left_dim,), (right_dim,)), ((), ())), preferred_element_type=F32
    )


def masks(start, limit):
    row = lax.broadcasted_iota(jnp.int32, (WINDOW, WINDOW), 0)
    col = lax.broadcasted_iota(jnp.int32, (WINDOW, WINDOW), 1)
    own = col <= row
    spot = jnp.where(own, start + col, start - WINDOW + col)
    return own, (spot >= 0) & ((spot < limit) | (row == col))


def weights_of(query, key, early_key, own, live):
    scores = jnp.where(own, dot_t(query, key, 1, 1), dot_t(query, early_key, 1, 1))
    scores = jnp.where(live, scores * (HEAD_DIM**-0.5), -1e30)
    expo = jnp.exp(scores - jnp.max(scores, axis=-1, keepdims=True))
    return expo / jnp.sum(expo, axis=-1, keepdims=True)


def attend_kernel(limits, start, packed, early, mixed):
    width = mixed.shape[1]
    own, live = masks(start[0], limits[pl.program_id(0)])
    for at in range(0, width, HEAD_DIM):
        cols = lambda k: slice(k * width + at, k * width + at + HEAD_DIM)
        probs = weights_of(packed[:, cols(0)], packed[:, cols(1)], early[:, cols(0)], own, live)
        near = jnp.where(own, probs, 0.0).astype(BF16)
        far = jnp.where(own, 0.0, probs).astype(BF16)
        mixed[:, cols(0)] = (
            dot_t(near, packed[:, cols(2)], 1, 0) + dot_t(far, early[:, cols(1)], 1, 0)
        ).astype(BF16)


def attend_back_kernel(limits, start, packed, early, grad, g_packed, g_early):
    width = grad.shape[1]
    scale = HEAD_DIM**-0.5
    own, live = masks(start[0], limits[pl.program_id(0)])
    for at in range(0, width, HEAD_DIM):
        cols = lambda k: slice(k * width + at, k * width + at + HEAD_DIM)
        query, key, value = (packed[:, cols(k)] for k in range(3))
        early_key, early_value = (early[:, cols(k)] for k in range(2))
        out = grad[:, cols(0)]
        probs = weights_of(query, key, early_key, own, live)
        g_probs = jnp.where(own, dot_t(out, value, 1, 1), dot_t(out, early_value, 1, 1))
        delta = jnp.sum(probs * g_probs, axis=-1, keepdims=True)
        g_scores = probs * (g_probs - delta)
        near = jnp.where(own, probs, 0.0).astype(BF16)
        far = jnp.where(own, 0.0, probs).astype(BF16)
        g_near = jnp.where(own, g_scores, 0.0).astype(BF16)
        g_far = jnp.where(own, 0.0, g_scores).astype(BF16)
        g_packed[:, cols(0)] = (
            (dot_t(g_near, key, 1, 0) + dot_t(g_far, early_key, 1, 0)) * scale
        ).astype(BF16)
        g_packed[:, cols(1)] = (dot_t(g_near, query, 0, 0) * scale).astype(BF16)
        g_packed[:, cols(2)] = dot_t(near, out, 0, 0).astype(BF16)
        g_early[:, cols(0)] = (dot_t(g_far, query, 0, 0) * scale).astype(BF16)
        g_early[:, cols(1)] = dot_t(far, out, 0, 0).astype(BF16)


def per_chain(kernel, limits, start, arrays, widths, flops):
    rows = arrays[0].shape[0]
    block = lambda w: pl.BlockSpec((WINDOW, w), lambda i, *_: (i, 0))
    moved = 2 * rows * (sum(a.shape[1] for a in arrays) + sum(widths))
    return pl.pallas_call(
        kernel,
        grid_spec=pltpu.PrefetchScalarGridSpec(
            num_scalar_prefetch=2,
            grid=(rows // WINDOW,),
            in_specs=[block(a.shape[1]) for a in arrays],
            out_specs=[block(w) for w in widths],
        ),
        out_shape=[jax.ShapeDtypeStruct((rows, w), BF16) for w in widths],
        cost_estimate=pl.CostEstimate(
            flops=flops, bytes_accessed=moved, transcendentals=rows * WINDOW
        ),
    )(limits, start, *arrays)


def shards(
    tokens,
    lengths,
    cotangent,
    ln1_gain,
    ln1_bias,
    w_qkv,
    qv_bias,
    w_out,
    out_bias,
    ln2_gain,
    ln2_bias,
    w_fc,
    fc_bias,
    w_proj,
    proj_bias,
):
    groups = lax.axis_size("batch")
    chain = lax.axis_index("batch")
    place = lax.axis_index("seq")
    rows, width = tokens.shape[1:]
    slice_width = width // lax.axis_size("seq")
    heads_width = w_out.shape[0]
    assert rows == WINDOW and lengths.shape[1] == 1 and tokens.shape[0] == 1
    start = (place * rows).astype(jnp.int32)
    limits = jnp.stack([lengths[chain ^ r, 0] for r in range(groups)])
    valid = (start + jnp.arange(rows, dtype=jnp.int32) < limits[0]).astype(F32)

    tokens, cotangent = tokens[0], cotangent[0]
    count = lax.axis_size("seq")
    early_tokens = lax.ppermute(tokens, "seq", [(i, i + 1) for i in range(count - 1)])
    own_tokens = to_slots(tokens)
    all_tokens = jnp.concatenate(batch_gather(own_tokens), axis=0)
    all_early = jnp.concatenate(batch_gather(to_slots(early_tokens)), axis=0)
    grad_out = to_slots(cotangent).astype(F32) * valid[:, None]
    grad_y_own = grad_out.astype(BF16)
    grad_y = jnp.concatenate(batch_gather(grad_y_own), axis=0)

    vectors = jnp.stack([ln1_gain, ln1_bias, out_bias, ln2_gain, ln2_bias, proj_bias])
    parts = jnp.stack(batch_gather(vectors))
    parts = jnp.concatenate([parts[chain ^ r] for r in range(groups)], axis=1)
    vectors = jnp.concatenate(ring_gather(parts), axis=1).astype(F32)
    gain_one, shift_one, mix_shift, gain_two, shift_two, down_shift = (
        vectors[i] for i in range(6)
    )

    proj_in = jnp.concatenate(ring_gather(w_qkv.reshape(slice_width, 3 * heads_width)), axis=0)
    proj_mix = jnp.concatenate(ring_gather(w_out, True), axis=1)
    proj_up = jnp.concatenate(ring_gather(w_fc), axis=0)
    proj_down = jnp.concatenate(ring_gather(w_proj, True), axis=1)

    normed = (norm_stats(all_tokens.astype(F32))[0] * gain_one + shift_one).astype(BF16)
    normed_early = (norm_stats(all_early.astype(F32))[0] * gain_one + shift_one).astype(BF16)
    qv_float = qv_bias.astype(F32)
    no_shift = jnp.zeros_like(qv_float[0])
    packed_shift = jnp.concatenate([qv_float[0], no_shift, qv_float[1]])
    packed = (dot_t(normed, proj_in, 1, 0) + packed_shift).astype(BF16)
    early = (
        dot_t(normed_early, proj_in[:, heads_width:], 1, 0) + packed_shift[heads_width:]
    ).astype(BF16)
    square = 2 * packed.shape[0] * WINDOW * heads_width
    starts = start.reshape(1)
    (mixed,) = per_chain(
        attend_kernel, limits, starts, (packed, early), (heads_width,), 4 * square
    )

    def spread(left, right, right_dim):
        half = left.shape[0] // 2
        far = dot_t(left[half:], right, 1, right_dim).astype(BF16)
        near = dot_t(left[:half], right, 1, right_dim).astype(BF16)
        each = [near[i : i + rows] for i in range(0, half, rows)]
        return batch_scatter(each + [far[i : i + rows] for i in range(0, half, rows)])

    inputs = own_tokens.astype(F32)
    resid = inputs + spread(mixed, proj_mix, 0) + mix_shift

    unit_two, factor_two = norm_stats(resid)
    second = jnp.concatenate(
        batch_gather((unit_two * gain_two + shift_two).astype(BF16)), axis=0
    )
    pre = dot_t(second, proj_up, 1, 0) + fc_bias.astype(F32)
    active_f, gelu_back = jax.vjp(gelu_tanh, pre)
    active = active_f.astype(BF16)
    result = resid + spread(active, proj_down, 0) + down_shift
    block_out = from_slots(result.astype(BF16))

    def cut(value, j):
        return value[:, j * slice_width : (j + 1) * slice_width]

    grad_w_proj = ring_scatter(lambda j: dot_t(active, cut(grad_y, j), 0, 0))
    grad_pre = gelu_back(dot_t(grad_y, proj_down, 1, 1))[0].astype(BF16)
    grad_w_fc = ring_scatter(lambda j: dot_t(cut(second, j), grad_pre, 0, 0), True)
    grad_fc_bias = jnp.sum(grad_pre.astype(F32), axis=0)
    grad_second = spread(grad_pre, proj_up, 1)
    grad_resid = grad_out + norm_back(grad_second, unit_two, factor_two, gain_two)
    grad_branch_own = grad_resid.astype(BF16)

    grad_branch = jnp.concatenate(batch_gather(grad_branch_own), axis=0)
    grad_w_out = ring_scatter(lambda j: dot_t(mixed, cut(grad_branch, j), 0, 0), True)
    grad_mixed = dot_t(grad_branch, proj_mix, 1, 1).astype(BF16)
    g_packed, g_early = per_chain(
        attend_back_kernel,
        limits,
        starts,
        (packed, early, grad_mixed),
        (3 * heads_width, 2 * heads_width),
        10 * square,
    )

    def qkv_part(j):
        late = dot_t(cut(normed_early, j), g_early, 0, 0)
        return dot_t(cut(normed, j), g_packed, 0, 0) + jnp.pad(late, ((0, 0), (heads_width, 0)))

    grad_w_qkv = ring_scatter(qkv_part).reshape(slice_width, 3, heads_width)
    back = spread(g_early, proj_in[:, heads_width:], 1)
    back = lax.ppermute(
        from_slots(back.astype(BF16)), "seq", [(i + 1, i) for i in range(count - 1)]
    )
    grad_normed = spread(g_packed, proj_in, 1) + to_slots(back).astype(F32)
    unit_one, factor_one = norm_stats(inputs)
    grad_tokens = grad_resid + norm_back(grad_normed, unit_one, factor_one, gain_one)

    column = lambda value: jnp.sum(value.astype(F32), axis=0)
    flat = jnp.concatenate(
        [
            grad_fc_bias,
            column(g_packed[:, :heads_width]),
            column(g_packed[:, 2 * heads_width :]) + column(g_early[:, heads_width:]),
        ]
    )
    flat = seq_total(flat)
    ff = grad_fc_bias.shape[0]
    sums = jnp.stack(
        [
            jnp.sum(grad_normed * unit_one, axis=0),
            jnp.sum(grad_normed, axis=0),
            column(grad_branch_own),
            jnp.sum(grad_second * unit_two, axis=0),
            jnp.sum(grad_second, axis=0),
            column(grad_y_own),
        ]
    )
    sums = ring_scatter(lambda j: cut(sums, j), wire=F32)
    piece = slice_width // groups
    sums = batch_scatter(
        [lax.dynamic_slice_in_dim(sums, (chain ^ r) * piece, piece, 1) for r in range(groups)],
        wire=F32,
    )
    return (
        block_out[None],
        from_slots(grad_tokens.astype(BF16))[None],
        sums[0],
        sums[1],
        grad_w_qkv,
        flat[ff:].reshape(2, heads_width),
        grad_w_out,
        sums[2],
        sums[3],
        sums[4],
        grad_w_fc,
        flat[:ff],
        grad_w_proj,
        sums[5],
    )


def solution(mesh):
    everywhere = P(("seq", "batch"))
    rows = P("batch", "seq", None)
    return jax.shard_map(
        shards,
        mesh=mesh,
        in_specs=(
            rows,
            P(),
            rows,
            everywhere,
            everywhere,
            P("seq", None, "batch"),
            P(None, "batch"),
            P("batch", "seq"),
            everywhere,
            everywhere,
            everywhere,
            P("seq", "batch"),
            P("batch"),
            P("batch", "seq"),
            everywhere,
        ),
        out_specs=(
            rows,
            rows,
            everywhere,
            everywhere,
            P("seq", None, "batch"),
            P(None, "batch"),
            P("batch", "seq"),
            everywhere,
            everywhere,
            everywhere,
            P("seq", "batch"),
            P("batch"),
            P("batch", "seq"),
            everywhere,
        ),
        check_vma=False,
    )
```

time: 2980 us -> 909 us (0.31)
  waiting for transfers between devices: 2540 us -> 446 us
  blocking collectives: 122 us -> 0 us
  starting transfers between devices: 12.1 us -> 100 us
  local copies, waits for them, and re-layouts: 41 us -> 85.9 us
    reduce_scatter x8 -> x0, waiting for transfers between devices: 1600 us -> none  [the longest x2 954 us: rows_total(): lax.psum_scatter(pair[0].astype(jnp.bfloat16), 'seq', scatter_dimension=0...]
    all_gather x8 -> x0, waiting for transfers between devices: 858 us -> none  [the longest x1 181 us: shards(): lax.all_gather(proj_down, 'batch', axis=0, tiled=True)]
    ppermute x4 -> x111, waiting for transfers between devices: 71.9 us -> 446 us  [the longest x70 378 us: hop(): return lax.ppermute(value, 'seq', list(pairs))]
    unnamed x3 -> x0, blocking collectives: 89.2 us -> none
    ppermute x4 -> x111, starting transfers between devices: 11.2 us -> 100 us  [the longest x70 69.7 us: hop(): return lax.ppermute(value, 'seq', list(pairs))]
    unnamed x101 -> x248, local copies, waits for them, and re-layouts: 21.9 us -> 66.1 us
    dot_general x18 -> x55, matrix products: 202 us -> 190 us  [dot_t(): lax.dot_general(left, right, (((left_dim,), (right_dim,)), ((), ())), pre...]
  transfers between devices with their start and end apart: 21 -> 111, of which waited for: 17 -> 42; matrix products, arithmetic and copies ran while one was open for 8% -> 27% of each run, Pallas kernels for 0% -> 3%
where the time goes in v1:
time: 909 us; the launch traced here: 901 us
  waiting for transfers between devices  446 us (49%)
  matrix products  190 us (21%)
  starting transfers between devices  100 us (11%)
  local copies, waits for them, and re-layouts  85.9 us (9%)
  other arithmetic  50.7 us (6%)
  Pallas kernels  25.2 us (3%)
    ppermute x70, waiting for transfers between devices, hop(): return lax.ppermute(value, 'seq', list(pairs))  378 us
    dot_general x55, matrix products, dot_t(): lax.dot_general(left, right, (((left_dim,), (right_dim,)), ((), ())), pre...  190 us
    ppermute x70, starting transfers between devices, hop(): return lax.ppermute(value, 'seq', list(pairs))  69.7 us
    unnamed x248, local copies, waits for them, and re-layouts  66.1 us
    ppermute x39, waiting for transfers between devices, swap(): lax.ppermute(value, axis, [(i, i ^ bit) for i in range(lax.axis_size(axis...  48.4 us
    pallas_call x2, Pallas kernels, per_chain(): pl.pallas_call(kernel, grid_spec=pltpu.PrefetchScalarGridSpec(num_scalar_...  25.2 us
    ppermute x39, starting transfers between devices, swap(): lax.ppermute(value, axis, [(i, i ^ bit) for i in range(lax.axis_size(axis...  24.8 us
    ppermute x1, waiting for transfers between devices, shards(): lax.ppermute(from_slots(back.astype(BF16)), 'seq', [(i + 1, i) for i in r...  19.9 us
  transfers between devices with their start and end apart: 111, of which 42 were waited for; matrix products, arithmetic and copies ran while one was open for 27% of the time, Pallas kernels for 3%

profile of v1, /device:TPU:0, one launch (start us, length us, event | category | flops | bytes accessed | tf_op | source)
XLA Modules:
  0.0 901.4 jit_solution(9230009184373949564)
XLA Ops:
  1.4 3.0 collective-permute-start.4
  20.9 2.4 constant_dynamic-update-slice_fusion.47
  30.3 3.2 pad_add_fusion.limits
  42.5 4.5 collective-permute-start.20
  52.2 32.7 %collective-permute-done.26 = bf16[512,256]{1,0:T(8,128)(2,1)S(1)} collective-permute-done((bf16[512,256]{1,0:T(8,128)(2,1)}, bf16[512,256]{1,0:T(8,128)(2,1)S(1)}, u32[]{:S(2)}, u32[]{:S(2)}) %collective-permute-start.26) | collective-permute-done | bytes 262176 | tf_op jit(solution)/shard_map/ppermute | solution.py:30
  87.9 2.4 collective-permute-start.27
  98.8 7.7 collective-permute-done.16
  116.6 9.3 %collective-permute-done.14 = bf16[256,1536]{0,1:T(8,128)(2,1)S(1)} collective-permute-done((bf16[256,1536]{0,1:T(8,128)(2,1)}, bf16[256,1536]{0,1:T(8,128)(2,1)S(1)}, u32[]{:S(2)}, u32[]{:S(2)}) %collective-permute-start.14) | collective-permute-done | bytes 786464 | tf_op jit(solution)/shard_map/ppermute | solution.py:30
  131.5 5.4 collective-permute-done.22
  136.9 3.6 fusion.8
  140.5 26.3 %collective-permute-done.15 = bf16[256,1536]{0,1:T(8,128)(2,1)S(1)} collective-permute-done((bf16[256,1536]{0,1:T(8,128)(2,1)S(1)}, bf16[256,1536]{0,1:T(8,128)(2,1)S(1)}, u32[]{:S(2)}, u32[]{:S(2)}) %collective-permute-start.15) | collective-permute-done | bytes 786464 | tf_op jit(solution)/shard_map/ppermute | solution.py:30
  172.8 3.7 fusion.4
  176.5 13.1 %fusion.7 = (bf16[1024,2048]{1,0:T(8,128)(2,1)S(1)}, bf16[1024,2048]{1,0:T(8,128)(2,1)S(1)}) fusion(f32[1024]{0:T(1024)S(1)} %add_rsqrt_fusion, f32[1024]{0:T(1024)S(1)} %broadcast_multiply_fusion, f32[2048]{0:T(1024)S(1)} %bitcast.161, f32[2048]{0:T(1024)S(1)} %bitcast.146, bf16[256,2048]{1,0:T(8,128)(2,1)S(1)} %collective-permute-done.23, ...), kind=kLoop, calls=%fused_computation.13 | loop fusion | flops 54525952 | bytes 16809984 | tf_op jit(solution)/shard_map/convert_element_type | solution.py:276
  192.4 37.0 %collective-permute-done.19 = bf16[256,1536]{0,1:T(8,128)(2,1)S(1)} collective-permute-done((bf16[256,1536]{0,1:T(8,128)(2,1)S(1)}, bf16[256,1536]{0,1:T(8,128)(2,1)S(1)}, u32[]{:S(2)}, u32[]{:S(2)}) %collective-permute-start.19) | collective-permute-done | bytes 786464 | tf_op jit(solution)/shard_map/ppermute | solution.py:30
  230.5 8.1 add_convert_fusion.packed
  238.6 5.7 add_convert_fusion.1.early
  244.4 9.9 %shard_map.254 = bf16[1024,512]{1,0:T(8,128)(2,1)} custom-call(s32[4]{0:T(128)} %pad_add_fusion.limits, s32[1]{0:T(128)} %bitcast.12.start, bf16[1024,1536]{1,0:T(8,128)(2,1)} %add_convert_fusion.packed, bf16[1024,1024]{1,0:T(8,128)(2,1)} %add_convert_fusion.1.early), custom_call_target="tpu_custom_call" | custom-call | flops 1073741824 | bytes 6291456 | tf_op jit(solution)/shard_map/pallas_call | solution.py:209
  254.3 3.0 convolution_convert_fusion.6
  257.5 2.5 constant_dynamic-update-slice_fusion.38
  263.9 2.4 constant_dynamic-update-slice_fusion.46
  268.6 17.6 %collective-permute-done.41 = bf16[256,2048]{1,0:T(8,128)(2,1)S(1)} collective-permute-done((bf16[256,2048]{1,0:T(8,128)(2,1)}, bf16[256,2048]{1,0:T(8,128)(2,1)S(1)}, u32[]{:S(2)}, u32[]{:S(2)}) %collective-permute-start.41) | collective-permute-done | bytes 1048608 | tf_op jit(solution)/shard_map/ppermute | solution.py:30
  287.6 21.1 %collective-permute-done.49 = bf16[2048,256]{1,0:T(8,128)(2,1)S(1)} collective-permute-done((bf16[2048,256]{1,0:T(8,128)(2,1)}, bf16[2048,256]{1,0:T(8,128)(2,1)S(1)}, u32[]{:S(2)}, u32[]{:S(2)}) %collective-permute-start.49) | collective-permute-done | bytes 1048608 | tf_op jit(solution)/shard_map/ppermute | solution.py:30
  316.6 7.6 pad_maximum_fusion.3
  324.2 6.9 collective-permute-done.42
  337.6 3.0 collective-permute-done.39
  341.7 33.9 %collective-permute-done.43 = bf16[256,2048]{1,0:T(8,128)(2,1)S(1)} collective-permute-done((bf16[256,2048]{1,0:T(8,128)(2,1)S(1)}, bf16[256,2048]{1,0:T(8,128)(2,1)S(1)}, u32[]{:S(2)}, u32[]{:S(2)}) %collective-permute-start.43) | collective-permute-done | bytes 1048608 | tf_op jit(solution)/shard_map/ppermute | solution.py:30
  385.0 2.4 constant_dynamic-update-slice_fusion.40
  388.0 20.5 %multiply_convert_fusion = (bf16[1024,2048]{1,0:T(8,128)(2,1)}, f32[1024,2048]{1,0:T(8,128)}) fusion(f32[2048]{0:T(1024)S(1)} %convert_element_type.403, bf16[2048,2048]{1,0:T(8,128)(2,1)} %constant_dynamic-update-slice_fusion.32, bf16[256,2048]{1,0:T(8,128)(2,1)S(1)} %collective-permute-done.36, bf16[256,2048]{1,0:T(8,128)(2,1)S(1)} %collective-permute-done.35, ...), kind=kOutput, calls=%fused_computation.26 | convolution fusion | flops 8627683328 | bytes 25174016 | tf_op jit(solution)/shard_map/dot_general | solution.py:146
  408.5 21.9 %convert_reduce_fusion.2 = (f32[2048]{0:T(1024)S(1)}, bf16[1024,2048]{1,0:T(8,128)(2,1)}) fusion(f32[1024,2048]{1,0:T(8,128)} %get-tuple-element.95, f32[2048]{0:T(1024)S(1)} %convert_element_type.403, bf16[2048,2048]{1,0:T(8,128)(2,1)} %constant_dynamic-update-slice_fusion.40, bf16[256,2048]{1,0:T(8,128)(2,1)} %copy-done.48, ...), kind=kOutput, calls=%fused_computation.25 | convolution fusion | flops 8654944256 | bytes 25182208 | tf_op jit(solution)/shard_map/dot_general | solution.py:146
  430.4 8.7 convolution_convert_fusion.2
  439.1 9.2 %convolution_convert_fusion.3 = bf16[512,2048]{1,0:T(8,128)(2,1)S(1)} fusion(bf16[2048,2048]{1,0:T(8,128)(2,1)} %constant_dynamic-update-slice_fusion.32, bf16[1024,2048]{1,0:T(8,128)(2,1)S(1)} %copy-done.8), kind=kOutput, calls=%fused_computation.48 | convolution fusion | flops 4296015872 | bytes 12582912 | tf_op jit(solution)/shard_map/dot_general | solution.py:146
  448.4 8.2 convolution_convert_fusion.4
  456.6 8.2 convolution_convert_fusion.5
  478.2 41.6 %collective-permute-done.108 = bf16[2048,256]{1,0:T(8,128)(2,1)S(1)} collective-permute-done((bf16[2048,256]{1,0:T(8,128)(2,1)S(1)}, bf16[2048,256]{1,0:T(8,128)(2,1)S(1)}, u32[]{:S(2)}, u32[]{:S(2)}) %collective-permute-start.108) | collective-permute-done | bytes 1048608 | tf_op jit(solution)/shard_map/ppermute | solution.py:30
  527.4 17.0 %collective-permute-done.97 = bf16[256,2048]{1,0:T(8,128)(2,1)S(1)} collective-permute-done((bf16[256,2048]{1,0:T(8,128)(2,1)S(1)}, bf16[256,2048]{1,0:T(8,128)(2,1)S(1)}, u32[]{:S(2)}, u32[]{:S(2)}) %collective-permute-start.97) | collective-permute-done | bytes 1048608 | tf_op jit(solution)/shard_map/ppermute | solution.py:30
  552.1 17.3 %collective-permute-done.53 = bf16[256,2048]{1,0:T(8,128)(2,1)S(1)} collective-permute-done((bf16[256,2048]{1,0:T(8,128)(2,1)S(1)}, bf16[256,2048]{1,0:T(8,128)(2,1)S(1)}, u32[]{:S(2)}, u32[]{:S(2)}) %collective-permute-start.53) | collective-permute-done | bytes 1048608 | tf_op jit(solution)/shard_map/ppermute | solution.py:34
  569.4 3.1 convert_reduce_fusion.8
  578.5 14.7 %collective-permute-done.105 = bf16[2048,256]{1,0:T(8,128)(2,1)S(1)} collective-permute-done((bf16[2048,256]{1,0:T(8,128)(2,1)S(1)}, bf16[2048,256]{1,0:T(8,128)(2,1)S(1)}, u32[]{:S(2)}, u32[]{:S(2)}) %collective-permute-start.105) | collective-permute-done | bytes 1048608 | tf_op jit(solution)/shard_map/ppermute | solution.py:30
  596.6 2.4 fusion.50
  599.1 13.9 %collective-permute-done.102 = bf16[256,2048]{1,0:T(8,128)(2,1)S(1)} collective-permute-done((bf16[256,2048]{1,0:T(8,128)(2,1)S(1)}, bf16[256,2048]{1,0:T(8,128)(2,1)S(1)}, u32[]{:S(2)}, u32[]{:S(2)}) %collective-permute-start.102) | collective-permute-done | bytes 1048608 | tf_op jit(solution)/shard_map/ppermute | solution.py:30
  616.9 21.6 %collective-permute-done.106 = bf16[2048,256]{1,0:T(8,128)(2,1)S(1)} collective-permute-done((bf16[2048,256]{1,0:T(8,128)(2,1)S(1)}, bf16[2048,256]{1,0:T(8,128)(2,1)S(1)}, u32[]{:S(2)}, u32[]{:S(2)}) %collective-permute-start.106) | collective-permute-done | bytes 1048608 | tf_op jit(solution)/shard_map/ppermute | solution.py:30
  640.1 2.4 fusion.47
  644.5 6.0 convolution_convert_fusion.12.grad
  650.5 15.3 %shard_map.255 = (bf16[1024,1536]{1,0:T(8,128)(2,1)}, bf16[1024,1024]{1,0:T(8,128)(2,1)}) custom-call(s32[4]{0:T(128)} %pad_add_fusion.limits, s32[1]{0:T(128)} %bitcast.12.start, bf16[1024,1536]{1,0:T(8,128)(2,1)} %add_convert_fusion.packed, bf16[1024,1024]{1,0:T(8,128)(2,1)} %add_convert_fusion.1.early, bf16[1024,512]{1,0:T(8,128)(2,1)} %convolution_convert_fusion.12.grad), custom_call_target="tpu_custom_call" | custom-call | flops 2684354560 | bytes 11534336 | tf_op jit(solution)/shard_map/pallas_call | solution.py:209
  665.8 5.0 fusion.28
  683.7 3.1 fusion.41
  688.9 3.6 convolution_convert_fusion
  694.6 4.3 fusion.38
  700.7 4.0 convolution_convert_fusion.1
  704.7 5.1 fusion.39
  717.0 2.9 fusion.40
  720.0 15.4 %collective-permute-done.88 = f32[3072]{0:T(1024)S(1)} collective-permute-done((f32[3072]{0:T(1024)S(1)}, f32[3072]{0:T(1024)S(1)}, u32[]{:S(2)}, u32[]{:S(2)}) %collective-permute-start.88) | collective-permute-done | bytes 12320 | tf_op jit(solution)/shard_map/ppermute | solution.py:34
  741.2 2.7 collective-permute-start.90
  745.8 18.1 %collective-permute-done.90 = bf16[512,256]{1,0:T(8,128)(2,1)S(1)} collective-permute-done((bf16[512,256]{1,0:T(8,128)(2,1)}, bf16[512,256]{1,0:T(8,128)(2,1)S(1)}, u32[]{:S(2)}, u32[]{:S(2)}) %collective-permute-start.90) | collective-permute-done | bytes 262176 | tf_op jit(solution)/shard_map/ppermute | solution.py:30
  765.8 4.5 collective-permute-done.94
  772.7 4.0 collective-permute-done.91
  787.1 2.4 collective-permute-done.95
  792.7 11.4 %collective-permute-done.81 = bf16[256,1536]{1,0:T(8,128)(2,1)S(1)} collective-permute-done((bf16[256,1536]{1,0:T(8,128)(2,1)S(1)}, bf16[256,1536]{1,0:T(8,128)(2,1)S(1)}, u32[]{:S(2)}, u32[]{:S(2)}) %collective-permute-start.81) | collective-permute-done | bytes 786464 | tf_op jit(solution)/shard_map/ppermute | solution.py:30
  807.3 6.4 collective-permute-done.68
  818.6 8.8 collective-permute-done.96
  831.8 2.7 collective-permute-start.86
  836.5 19.9 %collective-permute-done.69 = bf16[256,2048]{1,0:T(8,128)(2,1)S(1)} collective-permute-done((bf16[256,2048]{1,0:T(8,128)(2,1)S(1)}, bf16[256,2048]{1,0:T(8,128)(2,1)S(1)}, u32[]{:S(2)}, u32[]{:S(2)}) %collective-permute-start.69) | collective-permute-done | bytes 1048608 | tf_op jit(solution)/shard_map/ppermute | solution.py:339
  862.5 8.6 collective-permute-done.70
  893.0 4.1 fusion.37
  (558 shorter events, 251.1 us)
Async XLA Ops:
  5.9 41.9 %collective-permute-start.28 = (bf16[512,256]{1,0:T(8,128)(2,1)}, bf16[512,256]{1,0:T(8,128)(2,1)S(1)}, u32[]{:S(2)}, u32[]{:S(2)}) collective-permute-start(bf16[512,256]{1,0:T(8,128)(2,1)} %param.22), channel_id=1, source_target_pairs={{0,8},{8,16},{16,24},{24,28},{28,20},{20,12},{12,4},{4,0},{1,9},{9... | collective-permute-start | bytes 786440 | tf_op jit(solution)/shard_map/ppermute | solution.py:30
  13.9 94.6 %collective-permute-start.1 = (bf16[256,2048]{1,0:T(8,128)(2,1)S(1)}, bf16[256,2048]{1,0:T(8,128)(2,1)S(1)}, u32[]{:S(2)}, u32[]{:S(2)}) collective-permute-start(bf16[256,2048]{1,0:T(8,128)(2,1)S(1)} %constant_dynamic-update-slice_fusion), channel_id=1, source_target_pairs={{0,2},{1,3},{2,0},{3,1},{4,6},{5,7},{6,4},{7,5},{8,10},{9,11},{10,... | collective-permute-start | bytes 3145736 | tf_op jit(solution)/shard_map/ppermute | solution.py:34
  40.8 44.8 %collective-permute-start.13 = (bf16[256,1536]{0,1:T(8,128)(2,1)S(1)}, bf16[256,1536]{0,1:T(8,128)(2,1)}, u32[]{:S(2)}, u32[]{:S(2)}) collective-permute-start(bf16[256,1536]{0,1:T(8,128)(2,1)S(1)} %bitcast.143), channel_id=1, source_target_pairs={{8,0},{16,8},{24,16},{28,24},{20,28},{12,20},{4,12},{0,4},{9,1},{1... | collective-permute-start | bytes 2359304 | tf_op jit(solution)/shard_map/ppermute | solution.py:30
  42.5 45.3 %collective-permute-start.20 = (bf16[256,2048]{1,0:T(8,128)(2,1)}, bf16[256,2048]{1,0:T(8,128)(2,1)}, u32[]{:S(2)}, u32[]{:S(2)}) collective-permute-start(bf16[256,2048]{1,0:T(8,128)(2,1)} %bitcast.145), channel_id=1, source_target_pairs={{0,4},{4,8},{8,12},{12,16},{16,20},{20,24},{24,28},{1,5},{5,9},{9,... | collective-permute-start | bytes 3145736 | tf_op jit(solution)/shard_map/ppermute | solution.py:254
  47.1 37.8 %collective-permute-start.26 = (bf16[512,256]{1,0:T(8,128)(2,1)}, bf16[512,256]{1,0:T(8,128)(2,1)S(1)}, u32[]{:S(2)}, u32[]{:S(2)}) collective-permute-start(bf16[512,256]{1,0:T(8,128)(2,1)} %collective-permute-done.25), channel_id=1, source_target_pairs={{8,0},{16,8},{24,16},{28,24},{20,28},{12,20},{4,12},{0,4},{9,1},{1... | collective-permute-start | bytes 786440 | tf_op jit(solution)/shard_map/ppermute | solution.py:30
  47.8 37.9 %collective-permute-start.29 = (bf16[512,256]{1,0:T(8,128)(2,1)S(1)}, bf16[512,256]{1,0:T(8,128)(2,1)S(1)}, u32[]{:S(2)}, u32[]{:S(2)}) collective-permute-start(bf16[512,256]{1,0:T(8,128)(2,1)S(1)} %collective-permute-done.28), channel_id=1, source_target_pairs={{0,8},{8,16},{16,24},{24,28},{28,20},{20,12},{12,4},{4,0},{1,9},{9... | collective-permute-start | bytes 786440 | tf_op jit(solution)/shard_map/ppermute | solution.py:30
  84.9 42.6 %collective-permute-start = (bf16[256,2048]{1,0:T(8,128)(2,1)S(1)}, bf16[256,2048]{1,0:T(8,128)(2,1)S(1)}, u32[]{:S(2)}, u32[]{:S(2)}) collective-permute-start(bf16[256,2048]{1,0:T(8,128)(2,1)S(1)} %constant_dynamic-update-slice_fusion), channel_id=1, source_target_pairs={{0,1},{1,0},{2,3},{3,2},{4,5},{5,4},{6,7},{7,6},{8,9},{9,8},{10,11... | collective-permute-start | bytes 3145736 | tf_op jit(solution)/shard_map/ppermute | solution.py:34
  85.7 26.4 %collective-permute-start.30 = (bf16[512,256]{1,0:T(8,128)(2,1)S(1)}, bf16[512,256]{1,0:T(8,128)(2,1)S(1)}, u32[]{:S(2)}, u32[]{:S(2)}) collective-permute-start(bf16[512,256]{1,0:T(8,128)(2,1)S(1)} %collective-permute-done.29), channel_id=1, source_target_pairs={{0,8},{8,16},{16,24},{24,28},{28,20},{20,12},{12,4},{4,0},{1,9},{9... | collective-permute-start | bytes 786440 | tf_op jit(solution)/shard_map/ppermute | solution.py:30
  112.1 24.8 %collective-permute-start.22 = (bf16[256,2048]{1,0:T(8,128)(2,1)S(1)}, bf16[256,2048]{1,0:T(8,128)(2,1)S(1)}, u32[]{:S(2)}, u32[]{:S(2)}) collective-permute-start(bf16[256,2048]{1,0:T(8,128)(2,1)S(1)} %constant_dynamic-update-slice_fusion.16), channel_id=1, source_target_pairs={{0,2},{1,3},{2,0},{3,1},{4,6},{5,7},{6,4},{7,5},{8,10},{9,11},{10,... | collective-permute-start | bytes 3145736 | tf_op jit(solution)/shard_map/ppermute | solution.py:34
  125.8 63.8 %collective-permute-start.37 = (bf16[256,2048]{1,0:T(8,128)(2,1)}, bf16[256,2048]{1,0:T(8,128)(2,1)}, u32[]{:S(2)}, u32[]{:S(2)}) collective-permute-start(bf16[256,2048]{1,0:T(8,128)(2,1)} %param.26), channel_id=1, source_target_pairs={{8,0},{16,8},{24,16},{28,24},{20,28},{12,20},{4,12},{0,4},{9,1},{1... | collective-permute-start | bytes 3145736 | tf_op jit(solution)/shard_map/ppermute | solution.py:30
  127.5 40.6 %collective-permute-start.21 = (bf16[256,2048]{1,0:T(8,128)(2,1)S(1)}, bf16[256,2048]{1,0:T(8,128)(2,1)S(1)}, u32[]{:S(2)}, u32[]{:S(2)}) collective-permute-start(bf16[256,2048]{1,0:T(8,128)(2,1)S(1)} %constant_dynamic-update-slice_fusion.16), channel_id=1, source_target_pairs={{0,1},{1,0},{2,3},{3,2},{4,5},{5,4},{6,7},{7,6},{8,9},{9,8},{10,11... | collective-permute-start | bytes 3145736 | tf_op jit(solution)/shard_map/ppermute | solution.py:34
  128.7 38.1 %collective-permute-start.15 = (bf16[256,1536]{0,1:T(8,128)(2,1)S(1)}, bf16[256,1536]{0,1:T(8,128)(2,1)S(1)}, u32[]{:S(2)}, u32[]{:S(2)}) collective-permute-start(bf16[256,1536]{0,1:T(8,128)(2,1)S(1)} %collective-permute-done.14), channel_id=1, source_target_pairs={{8,0},{16,8},{24,16},{28,24},{20,28},{12,20},{4,12},{0,4},{9,1},{1... | collective-permute-start | bytes 2359304 | tf_op jit(solution)/shard_map/ppermute | solution.py:30
  130.5 38.6 %collective-permute-start.18 = (bf16[256,1536]{0,1:T(8,128)(2,1)S(1)}, bf16[256,1536]{0,1:T(8,128)(2,1)S(1)}, u32[]{:S(2)}, u32[]{:S(2)}) collective-permute-start(bf16[256,1536]{0,1:T(8,128)(2,1)S(1)} %collective-permute-done.17), channel_id=1, source_target_pairs={{0,8},{8,16},{16,24},{24,28},{28,20},{20,12},{12,4},{4,0},{1,9},{9... | collective-permute-start | bytes 2359304 | tf_op jit(solution)/shard_map/ppermute | solution.py:30
  136.9 33.3 %collective-permute-start.23 = (bf16[256,2048]{1,0:T(8,128)(2,1)S(1)}, bf16[256,2048]{1,0:T(8,128)(2,1)S(1)}, u32[]{:S(2)}, u32[]{:S(2)}) collective-permute-start(bf16[256,2048]{1,0:T(8,128)(2,1)S(1)} %collective-permute-done.22), channel_id=1, source_target_pairs={{0,1},{1,0},{2,3},{3,2},{4,5},{5,4},{6,7},{7,6},{8,9},{9,8},{10,11... | collective-permute-start | bytes 3145736 | tf_op jit(solution)/shard_map/ppermute | solution.py:34
  166.8 90.6 %collective-permute-start.40 = (bf16[256,2048]{1,0:T(8,128)(2,1)}, bf16[256,2048]{1,0:T(8,128)(2,1)}, u32[]{:S(2)}, u32[]{:S(2)}) collective-permute-start(bf16[256,2048]{1,0:T(8,128)(2,1)} %param.26), channel_id=1, source_target_pairs={{0,8},{8,16},{16,24},{24,28},{28,20},{20,12},{12,4},{4,0},{1,9},{9... | collective-permute-start | bytes 3145736 | tf_op jit(solution)/shard_map/ppermute | solution.py:30
  169.0 91.0 %collective-permute-start.48 = (bf16[2048,256]{1,0:T(8,128)(2,1)}, bf16[2048,256]{1,0:T(8,128)(2,1)}, u32[]{:S(2)}, u32[]{:S(2)}) collective-permute-start(bf16[2048,256]{1,0:T(8,128)(2,1)} %param.28), channel_id=1, source_target_pairs={{0,8},{8,16},{16,24},{24,28},{28,20},{20,12},{12,4},{4,0},{1,9},{9... | collective-permute-start | bytes 3145736 | tf_op jit(solution)/shard_map/ppermute | solution.py:30
  170.2 59.2 %collective-permute-start.19 = (bf16[256,1536]{0,1:T(8,128)(2,1)S(1)}, bf16[256,1536]{0,1:T(8,128)(2,1)S(1)}, u32[]{:S(2)}, u32[]{:S(2)}) collective-permute-start(bf16[256,1536]{0,1:T(8,128)(2,1)S(1)} %collective-permute-done.18), channel_id=1, source_target_pairs={{0,8},{8,16},{16,24},{24,28},{28,20},{20,12},{12,4},{4,0},{1,9},{9... | collective-permute-start | bytes 2359304 | tf_op jit(solution)/shard_map/ppermute | solution.py:30
  189.6 78.0 %collective-permute-start.55 = (bf16[256,2048]{1,0:T(8,128)(2,1)S(1)}, bf16[256,2048]{1,0:T(8,128)(2,1)}, u32[]{:S(2)}, u32[]{:S(2)}) collective-permute-start(bf16[256,2048]{1,0:T(8,128)(2,1)S(1)} %get-tuple-element.57), channel_id=1, source_target_pairs={{0,2},{1,3},{2,0},{3,1},{4,6},{5,7},{6,4},{7,5},{8,10},{9,11},{10,... | collective-permute-start | bytes 3145736 | tf_op jit(solution)/shard_map/ppermute | solution.py:34
  191.5 69.9 %collective-permute-start.38 = (bf16[256,2048]{1,0:T(8,128)(2,1)}, bf16[256,2048]{1,0:T(8,128)(2,1)S(1)}, u32[]{:S(2)}, u32[]{:S(2)}) collective-permute-start(bf16[256,2048]{1,0:T(8,128)(2,1)} %collective-permute-done.37), channel_id=1, source_target_pairs={{8,0},{16,8},{24,16},{28,24},{20,28},{12,20},{4,12},{0,4},{9,1},{1... | collective-permute-start | bytes 3145736 | tf_op jit(solution)/shard_map/ppermute | solution.py:30
  229.4 33.3 %collective-permute-start.45 = (bf16[2048,256]{1,0:T(8,128)(2,1)}, bf16[2048,256]{1,0:T(8,128)(2,1)}, u32[]{:S(2)}, u32[]{:S(2)}) collective-permute-start(bf16[2048,256]{1,0:T(8,128)(2,1)} %collective-permute-done.44), channel_id=1, source_target_pairs={{8,0},{16,8},{24,16},{28,24},{20,28},{12,20},{4,12},{0,4},{9,1},{1... | collective-permute-start | bytes 3145736 | tf_op jit(solution)/shard_map/ppermute | solution.py:30
  260.0 26.2 %collective-permute-start.41 = (bf16[256,2048]{1,0:T(8,128)(2,1)}, bf16[256,2048]{1,0:T(8,128)(2,1)S(1)}, u32[]{:S(2)}, u32[]{:S(2)}) collective-permute-start(bf16[256,2048]{1,0:T(8,128)(2,1)} %collective-permute-done.40), channel_id=1, source_target_pairs={{0,8},{8,16},{16,24},{24,28},{28,20},{20,12},{12,4},{4,0},{1,9},{9... | collective-permute-start | bytes 3145736 | tf_op jit(solution)/shard_map/ppermute | solution.py:30
  261.4 47.3 %collective-permute-start.49 = (bf16[2048,256]{1,0:T(8,128)(2,1)}, bf16[2048,256]{1,0:T(8,128)(2,1)S(1)}, u32[]{:S(2)}, u32[]{:S(2)}) collective-permute-start(bf16[2048,256]{1,0:T(8,128)(2,1)} %collective-permute-done.48), channel_id=1, source_target_pairs={{0,8},{8,16},{16,24},{24,28},{28,20},{20,12},{12,4},{4,0},{1,9},{9... | collective-permute-start | bytes 3145736 | tf_op jit(solution)/shard_map/ppermute | solution.py:30
  262.7 46.0 %collective-permute-start.46 = (bf16[2048,256]{1,0:T(8,128)(2,1)}, bf16[2048,256]{1,0:T(8,128)(2,1)S(1)}, u32[]{:S(2)}, u32[]{:S(2)}) collective-permute-start(bf16[2048,256]{1,0:T(8,128)(2,1)} %collective-permute-done.45), channel_id=1, source_target_pairs={{8,0},{16,8},{24,16},{28,24},{20,28},{12,20},{4,12},{0,4},{9,1},{1... | collective-permute-start | bytes 3145736 | tf_op jit(solution)/shard_map/ppermute | solution.py:30
  267.6 46.9 %collective-permute-start.54 = (bf16[256,2048]{1,0:T(8,128)(2,1)S(1)}, bf16[256,2048]{1,0:T(8,128)(2,1)S(1)}, u32[]{:S(2)}, u32[]{:S(2)}) collective-permute-start(bf16[256,2048]{1,0:T(8,128)(2,1)S(1)} %get-tuple-element.57), channel_id=1, source_target_pairs={{0,1},{1,0},{2,3},{3,2},{4,5},{5,4},{6,7},{7,6},{8,9},{9,8},{10,11... | collective-permute-start | bytes 3145736 | tf_op jit(solution)/shard_map/ppermute | solution.py:34
  267.7 48.5 %collective-permute-start.56 = (bf16[256,2048]{1,0:T(8,128)(2,1)}, bf16[256,2048]{1,0:T(8,128)(2,1)S(1)}, u32[]{:S(2)}, u32[]{:S(2)}) collective-permute-start(bf16[256,2048]{1,0:T(8,128)(2,1)} %collective-permute-done.55), channel_id=1, source_target_pairs={{0,1},{1,0},{2,3},{3,2},{4,5},{5,4},{6,7},{7,6},{8,9},{9,8},{10,11... | collective-permute-start | bytes 3145736 | tf_op jit(solution)/shard_map/ppermute | solution.py:34
  286.2 44.9 %collective-permute-start.42 = (bf16[256,2048]{1,0:T(8,128)(2,1)S(1)}, bf16[256,2048]{1,0:T(8,128)(2,1)S(1)}, u32[]{:S(2)}, u32[]{:S(2)}) collective-permute-start(bf16[256,2048]{1,0:T(8,128)(2,1)S(1)} %collective-permute-done.41), channel_id=1, source_target_pairs={{0,8},{8,16},{16,24},{24,28},{28,20},{20,12},{12,4},{4,0},{1,9},{9... | collective-permute-start | bytes 3145736 | tf_op jit(solution)/shard_map/ppermute | solution.py:30
  308.7 25.6 %collective-permute-start.33 = (bf16[256,2048]{1,0:T(8,128)(2,1)S(1)}, bf16[256,2048]{1,0:T(8,128)(2,1)S(1)}, u32[]{:S(2)}, u32[]{:S(2)}) collective-permute-start(bf16[256,2048]{1,0:T(8,128)(2,1)S(1)} %add_convert_fusion.9), channel_id=1, source_target_pairs={{0,2},{1,3},{2,0},{3,1},{4,6},{5,7},{6,4},{7,5},{8,10},{9,11},{10,... | collective-permute-start | bytes 3145736 | tf_op jit(solution)/shard_map/ppermute | solution.py:34
  314.6 26.0 %collective-permute-start.39 = (bf16[256,2048]{1,0:T(8,128)(2,1)S(1)}, bf16[256,2048]{1,0:T(8,128)(2,1)S(1)}, u32[]{:S(2)}, u32[]{:S(2)}) collective-permute-start(bf16[256,2048]{1,0:T(8,128)(2,1)S(1)} %copy-done.42), channel_id=1, source_target_pairs={{8,0},{16,8},{24,16},{28,24},{20,28},{12,20},{4,12},{0,4},{9,1},{1... | collective-permute-start | bytes 3145736 | tf_op jit(solution)/shard_map/ppermute | solution.py:30
  316.2 66.5 %collective-permute-start.50 = (bf16[2048,256]{1,0:T(8,128)(2,1)S(1)}, bf16[2048,256]{1,0:T(8,128)(2,1)S(1)}, u32[]{:S(2)}, u32[]{:S(2)}) collective-permute-start(bf16[2048,256]{1,0:T(8,128)(2,1)S(1)} %collective-permute-done.49), channel_id=1, source_target_pairs={{0,8},{8,16},{16,24},{24,28},{28,20},{20,12},{12,4},{4,0},{1,9},{9... | collective-permute-start | bytes 3145736 | tf_op jit(solution)/shard_map/ppermute | solution.py:30
  331.2 50.4 %collective-permute-start.47 = (bf16[2048,256]{1,0:T(8,128)(2,1)S(1)}, bf16[2048,256]{1,0:T(8,128)(2,1)S(1)}, u32[]{:S(2)}, u32[]{:S(2)}) collective-permute-start(bf16[2048,256]{1,0:T(8,128)(2,1)S(1)} %collective-permute-done.46), channel_id=1, source_target_pairs={{8,0},{16,8},{24,16},{28,24},{20,28},{12,20},{4,12},{0,4},{9,1},{1... | collective-permute-start | bytes 3145736 | tf_op jit(solution)/shard_map/ppermute | solution.py:30
  332.7 42.8 %collective-permute-start.43 = (bf16[256,2048]{1,0:T(8,128)(2,1)S(1)}, bf16[256,2048]{1,0:T(8,128)(2,1)S(1)}, u32[]{:S(2)}, u32[]{:S(2)}) collective-permute-start(bf16[256,2048]{1,0:T(8,128)(2,1)S(1)} %collective-permute-done.42), channel_id=1, source_target_pairs={{0,8},{8,16},{16,24},{24,28},{28,20},{20,12},{12,4},{4,0},{1,9},{9... | collective-permute-start | bytes 3145736 | tf_op jit(solution)/shard_map/ppermute | solution.py:30
  336.2 44.8 %collective-permute-start.35 = (bf16[256,2048]{1,0:T(8,128)(2,1)S(1)}, bf16[256,2048]{1,0:T(8,128)(2,1)S(1)}, u32[]{:S(2)}, u32[]{:S(2)}) collective-permute-start(bf16[256,2048]{1,0:T(8,128)(2,1)S(1)} %add_convert_fusion.8), channel_id=1, source_target_pairs={{0,2},{1,3},{2,0},{3,1},{4,6},{5,7},{6,4},{7,5},{8,10},{9,11},{10,... | collective-permute-start | bytes 3145736 | tf_op jit(solution)/shard_map/ppermute | solution.py:34
  465.2 82.1 %collective-permute-start.57 = (bf16[256,2048]{1,0:T(8,128)(2,1)S(1)}, bf16[256,2048]{1,0:T(8,128)(2,1)S(1)}, u32[]{:S(2)}, u32[]{:S(2)}) collective-permute-start(bf16[256,2048]{1,0:T(8,128)(2,1)S(1)} %slice.429), channel_id=1, source_target_pairs={{0,1},{1,0},{2,3},{3,2},{4,5},{5,4},{6,7},{7,6},{8,9},{9,8},{10,11... | collective-permute-start | bytes 3145736 | tf_op jit(solution)/shard_map/ppermute | solution.py:34
  471.7 79.0 %collective-permute-start.51 = (bf16[256,2048]{1,0:T(8,128)(2,1)S(1)}, bf16[256,2048]{1,0:T(8,128)(2,1)S(1)}, u32[]{:S(2)}, u32[]{:S(2)}) collective-permute-start(bf16[256,2048]{1,0:T(8,128)(2,1)S(1)} %slice.422), channel_id=1, source_target_pairs={{0,1},{1,0},{2,3},{3,2},{4,5},{5,4},{6,7},{7,6},{8,9},{9,8},{10,11... | collective-permute-start | bytes 3145736 | tf_op jit(solution)/shard_map/ppermute | solution.py:34
  471.9 50.6 %collective-permute-start.100 = (bf16[256,2048]{1,0:T(8,128)(2,1)S(1)}, bf16[256,2048]{1,0:T(8,128)(2,1)S(1)}, u32[]{:S(2)}, u32[]{:S(2)}) collective-permute-start(bf16[256,2048]{1,0:T(8,128)(2,1)S(1)} %convolution_convert_fusion.10), channel_id=1, source_target_pairs={{8,0},{16,8},{24,16},{28,24},{20,28},{12,20},{4,12},{0,4},{9,1},{1... | collective-permute-start | bytes 3145736 | tf_op jit(solution)/shard_map/ppermute | solution.py:30
  474.9 44.9 %collective-permute-start.108 = (bf16[2048,256]{1,0:T(8,128)(2,1)S(1)}, bf16[2048,256]{1,0:T(8,128)(2,1)S(1)}, u32[]{:S(2)}, u32[]{:S(2)}) collective-permute-start(bf16[2048,256]{1,0:T(8,128)(2,1)S(1)} %convolution_convert_fusion.8), channel_id=1, source_target_pairs={{8,0},{16,8},{24,16},{28,24},{20,28},{12,20},{4,12},{0,4},{9,1},{1... | collective-permute-start | bytes 3145736 | tf_op jit(solution)/shard_map/ppermute | solution.py:30
  476.9 48.3 %collective-permute-start.104 = (bf16[2048,256]{1,0:T(8,128)(2,1)S(1)}, bf16[2048,256]{1,0:T(8,128)(2,1)S(1)}, u32[]{:S(2)}, u32[]{:S(2)}) collective-permute-start(bf16[2048,256]{1,0:T(8,128)(2,1)S(1)} %convolution_convert_fusion.9), channel_id=1, source_target_pairs={{0,8},{8,16},{16,24},{24,28},{28,20},{20,12},{12,4},{4,0},{1,9},{9... | collective-permute-start | bytes 3145736 | tf_op jit(solution)/shard_map/ppermute | solution.py:30
  522.6 26.2 %collective-permute-start.59 = (bf16[256,2048]{1,0:T(8,128)(2,1)S(1)}, bf16[256,2048]{1,0:T(8,128)(2,1)S(1)}, u32[]{:S(2)}, u32[]{:S(2)}) collective-permute-start(bf16[256,2048]{1,0:T(8,128)(2,1)S(1)} %add_convert_fusion.5), channel_id=1, source_target_pairs={{0,2},{1,3},{2,0},{3,1},{4,6},{5,7},{6,4},{7,5},{8,10},{9,11},{10,... | collective-permute-start | bytes 3145736 | tf_op jit(solution)/shard_map/ppermute | solution.py:34
  525.2 44.2 %collective-permute-start.53 = (bf16[256,2048]{1,0:T(8,128)(2,1)S(1)}, bf16[256,2048]{1,0:T(8,128)(2,1)S(1)}, u32[]{:S(2)}, u32[]{:S(2)}) collective-permute-start(bf16[256,2048]{1,0:T(8,128)(2,1)S(1)} %add_convert_fusion.7), channel_id=1, source_target_pairs={{0,2},{1,3},{2,0},{3,1},{4,6},{5,7},{6,4},{7,5},{8,10},{9,11},{10,... | collective-permute-start | bytes 3145736 | tf_op jit(solution)/shard_map/ppermute | solution.py:34
  544.4 29.7 %collective-permute-start.101 = (bf16[256,2048]{1,0:T(8,128)(2,1)S(1)}, bf16[256,2048]{1,0:T(8,128)(2,1)S(1)}, u32[]{:S(2)}, u32[]{:S(2)}) collective-permute-start(bf16[256,2048]{1,0:T(8,128)(2,1)S(1)} %fusion.46), channel_id=1, source_target_pairs={{8,0},{16,8},{24,16},{28,24},{20,28},{12,20},{4,12},{0,4},{9,1},{1... | collective-permute-start | bytes 3145736 | tf_op jit(solution)/shard_map/ppermute | solution.py:30
  547.3 28.2 %collective-permute-start.98 = (bf16[256,2048]{1,0:T(8,128)(2,1)S(1)}, bf16[256,2048]{1,0:T(8,128)(2,1)S(1)}, u32[]{:S(2)}, u32[]{:S(2)}) collective-permute-start(bf16[256,2048]{1,0:T(8,128)(2,1)S(1)} %fusion.43), channel_id=1, source_target_pairs={{0,8},{8,16},{16,24},{24,28},{28,20},{20,12},{12,4},{4,0},{1,9},{9... | collective-permute-start | bytes 3145736 | tf_op jit(solution)/shard_map/ppermute | solution.py:30
  548.7 46.6 %collective-permute-start.109 = (bf16[2048,256]{1,0:T(8,128)(2,1)S(1)}, bf16[2048,256]{1,0:T(8,128)(2,1)S(1)}, u32[]{:S(2)}, u32[]{:S(2)}) collective-permute-start(bf16[2048,256]{1,0:T(8,128)(2,1)S(1)} %fusion.51), channel_id=1, source_target_pairs={{8,0},{16,8},{24,16},{28,24},{20,28},{12,20},{4,12},{0,4},{9,1},{1... | collective-permute-start | bytes 3145736 | tf_op jit(solution)/shard_map/ppermute | solution.py:30
  550.7 42.5 %collective-permute-start.105 = (bf16[2048,256]{1,0:T(8,128)(2,1)S(1)}, bf16[2048,256]{1,0:T(8,128)(2,1)S(1)}, u32[]{:S(2)}, u32[]{:S(2)}) collective-permute-start(bf16[2048,256]{1,0:T(8,128)(2,1)S(1)} %fusion.49), channel_id=1, source_target_pairs={{0,8},{8,16},{16,24},{24,28},{28,20},{20,12},{12,4},{4,0},{1,9},{9... | collective-permute-start | bytes 3145736 | tf_op jit(solution)/shard_map/ppermute | solution.py:30
  572.6 26.5 %collective-permute-start.61 = (bf16[256,2048]{1,0:T(8,128)(2,1)S(1)}, bf16[256,2048]{1,0:T(8,128)(2,1)S(1)}, u32[]{:S(2)}, u32[]{:S(2)}) collective-permute-start(bf16[256,2048]{1,0:T(8,128)(2,1)S(1)} %get-tuple-element.59), channel_id=1, source_target_pairs={{0,2},{1,3},{2,0},{3,1},{4,6},{5,7},{6,4},{7,5},{8,10},{9,11},{10,... | collective-permute-start | bytes 3145736 | tf_op jit(solution)/shard_map/ppermute | solution.py:34
  574.1 68.4 %collective-permute-start.60 = (bf16[256,2048]{1,0:T(8,128)(2,1)S(1)}, bf16[256,2048]{1,0:T(8,128)(2,1)S(1)}, u32[]{:S(2)}, u32[]{:S(2)}) collective-permute-start(bf16[256,2048]{1,0:T(8,128)(2,1)S(1)} %get-tuple-element.59), channel_id=1, source_target_pairs={{0,1},{1,0},{2,3},{3,2},{4,5},{5,4},{6,7},{7,6},{8,9},{9,8},{10,11... | collective-permute-start | bytes 3145736 | tf_op jit(solution)/shard_map/ppermute | solution.py:34
  575.5 37.6 %collective-permute-start.102 = (bf16[256,2048]{1,0:T(8,128)(2,1)S(1)}, bf16[256,2048]{1,0:T(8,128)(2,1)S(1)}, u32[]{:S(2)}, u32[]{:S(2)}) collective-permute-start(bf16[256,2048]{1,0:T(8,128)(2,1)S(1)} %fusion.45), channel_id=1, source_target_pairs={{8,0},{16,8},{24,16},{28,24},{20,28},{12,20},{4,12},{0,4},{9,1},{1... | collective-permute-start | bytes 3145736 | tf_op jit(solution)/shard_map/ppermute | solution.py:30
  593.2 99.3 %collective-permute-start.99 = (bf16[256,2048]{1,0:T(8,128)(2,1)}, bf16[256,2048]{1,0:T(8,128)(2,1)}, u32[]{:S(2)}, u32[]{:S(2)}) collective-permute-start(bf16[256,2048]{1,0:T(8,128)(2,1)} %fusion.42), channel_id=1, source_target_pairs={{0,8},{8,16},{16,24},{24,28},{28,20},{20,12},{12,4},{4,0},{1,9},{9... | collective-permute-start | bytes 3145736 | tf_op jit(solution)/shard_map/ppermute | solution.py:30
  595.3 43.3 %collective-permute-start.106 = (bf16[2048,256]{1,0:T(8,128)(2,1)S(1)}, bf16[2048,256]{1,0:T(8,128)(2,1)S(1)}, u32[]{:S(2)}, u32[]{:S(2)}) collective-permute-start(bf16[2048,256]{1,0:T(8,128)(2,1)S(1)} %fusion.48), channel_id=1, source_target_pairs={{0,8},{8,16},{16,24},{24,28},{28,20},{20,12},{12,4},{4,0},{1,9},{9... | collective-permute-start | bytes 3145736 | tf_op jit(solution)/shard_map/ppermute | solution.py:30
  599.1 44.0 %collective-permute-start.62 = (bf16[256,2048]{1,0:T(8,128)(2,1)S(1)}, bf16[256,2048]{1,0:T(8,128)(2,1)S(1)}, u32[]{:S(2)}, u32[]{:S(2)}) collective-permute-start(bf16[256,2048]{1,0:T(8,128)(2,1)S(1)} %collective-permute-done.61), channel_id=1, source_target_pairs={{0,1},{1,0},{2,3},{3,2},{4,5},{5,4},{6,7},{7,6},{8,9},{9,8},{10,11... | collective-permute-start | bytes 3145736 | tf_op jit(solution)/shard_map/ppermute | solution.py:34
  613.0 91.7 %collective-permute-start.110 = (bf16[2048,256]{1,0:T(8,128)(2,1)}, bf16[2048,256]{1,0:T(8,128)(2,1)}, u32[]{:S(2)}, u32[]{:S(2)}) collective-permute-start(bf16[2048,256]{1,0:T(8,128)(2,1)} %fusion.50), channel_id=1, source_target_pairs={{8,0},{16,8},{24,16},{28,24},{20,28},{12,20},{4,12},{0,4},{9,1},{1... | collective-permute-start | bytes 3145736 | tf_op jit(solution)/shard_map/ppermute | solution.py:30
  638.6 55.7 %collective-permute-start.103 = (bf16[256,2048]{1,0:T(8,128)(2,1)}, bf16[256,2048]{1,0:T(8,128)(2,1)}, u32[]{:S(2)}, u32[]{:S(2)}) collective-permute-start(bf16[256,2048]{1,0:T(8,128)(2,1)} %fusion.44), channel_id=1, source_target_pairs={{8,0},{16,8},{24,16},{28,24},{20,28},{12,20},{4,12},{0,4},{9,1},{1... | collective-permute-start | bytes 3145736 | tf_op jit(solution)/shard_map/ppermute | solution.py:30
  642.5 62.2 %collective-permute-start.107 = (bf16[2048,256]{1,0:T(8,128)(2,1)}, bf16[2048,256]{1,0:T(8,128)(2,1)}, u32[]{:S(2)}, u32[]{:S(2)}) collective-permute-start(bf16[2048,256]{1,0:T(8,128)(2,1)} %fusion.47), channel_id=1, source_target_pairs={{0,8},{8,16},{16,24},{24,28},{28,20},{20,12},{12,4},{4,0},{1,9},{9... | collective-permute-start | bytes 3145736 | tf_op jit(solution)/shard_map/ppermute | solution.py:30
  683.3 100.3 %collective-permute-start.67 = (bf16[256,2048]{1,0:T(8,128)(2,1)}, bf16[256,2048]{1,0:T(8,128)(2,1)}, u32[]{:S(2)}, u32[]{:S(2)}) collective-permute-start(bf16[256,2048]{1,0:T(8,128)(2,1)} %slice.440), channel_id=1, source_target_pairs={{0,1},{1,0},{2,3},{3,2},{4,5},{5,4},{6,7},{7,6},{8,9},{9,8},{10,11... | collective-permute-start | bytes 3145736 | tf_op jit(solution)/shard_map/ppermute | solution.py:34
  694.2 47.0 %collective-permute-start.93 = (bf16[512,256]{1,0:T(8,128)(2,1)S(1)}, bf16[512,256]{1,0:T(8,128)(2,1)}, u32[]{:S(2)}, u32[]{:S(2)}) collective-permute-start(bf16[512,256]{1,0:T(8,128)(2,1)S(1)} %convolution_convert_fusion.13), channel_id=1, source_target_pairs={{8,0},{16,8},{24,16},{28,24},{20,28},{12,20},{4,12},{0,4},{9,1},{1... | collective-permute-start | bytes 786440 | tf_op jit(solution)/shard_map/ppermute | solution.py:30
  712.8 93.1 %collective-permute-start.66 = (bf16[256,2048]{1,0:T(8,128)(2,1)}, bf16[256,2048]{1,0:T(8,128)(2,1)}, u32[]{:S(2)}, u32[]{:S(2)}) collective-permute-start(bf16[256,2048]{1,0:T(8,128)(2,1)} %slice.438), channel_id=1, source_target_pairs={{0,1},{1,0},{2,3},{3,2},{4,5},{5,4},{6,7},{7,6},{8,9},{9,8},{10,11... | collective-permute-start | bytes 3145736 | tf_op jit(solution)/shard_map/ppermute | solution.py:34
  714.9 63.5 %collective-permute-start.84 = (bf16[256,1536]{1,0:T(8,128)(2,1)}, bf16[256,1536]{1,0:T(8,128)(2,1)}, u32[]{:S(2)}, u32[]{:S(2)}) collective-permute-start(bf16[256,1536]{1,0:T(8,128)(2,1)} %fusion.41), channel_id=1, source_target_pairs={{8,0},{16,8},{24,16},{28,24},{20,28},{12,20},{4,12},{0,4},{9,1},{1... | collective-permute-start | bytes 2359304 | tf_op jit(solution)/shard_map/ppermute | solution.py:30
  740.0 41.2 %collective-permute-start.80 = (bf16[256,1536]{1,0:T(8,128)(2,1)}, bf16[256,1536]{1,0:T(8,128)(2,1)}, u32[]{:S(2)}, u32[]{:S(2)}) collective-permute-start(bf16[256,1536]{1,0:T(8,128)(2,1)} %fusion.40), channel_id=1, source_target_pairs={{0,8},{8,16},{16,24},{24,28},{28,20},{20,12},{12,4},{4,0},{1,9},{9... | collective-permute-start | bytes 2359304 | tf_op jit(solution)/shard_map/ppermute | solution.py:30
  778.4 78.2 %collective-permute-start.63 = (bf16[256,2048]{1,0:T(8,128)(2,1)S(1)}, bf16[256,2048]{1,0:T(8,128)(2,1)S(1)}, u32[]{:S(2)}, u32[]{:S(2)}) collective-permute-start(bf16[256,2048]{1,0:T(8,128)(2,1)S(1)} %copy-done.40), channel_id=1, source_target_pairs={{0,1},{1,0},{2,3},{3,2},{4,5},{5,4},{6,7},{7,6},{8,9},{9,8},{10,11... | collective-permute-start | bytes 3145736 | tf_op jit(solution)/shard_map/ppermute | solution.py:34
  791.4 25.8 %collective-permute-start.92 = (bf16[512,256]{1,0:T(8,128)(2,1)S(1)}, bf16[512,256]{1,0:T(8,128)(2,1)S(1)}, u32[]{:S(2)}, u32[]{:S(2)}) collective-permute-start(bf16[512,256]{1,0:T(8,128)(2,1)S(1)} %fusion.80), channel_id=1, source_target_pairs={{0,8},{8,16},{16,24},{24,28},{28,20},{20,12},{12,4},{4,0},{1,9},{9... | collective-permute-start | bytes 786440 | tf_op jit(solution)/shard_map/ppermute | solution.py:30
  804.0 25.9 %collective-permute-start.85 = (bf16[256,1536]{1,0:T(8,128)(2,1)S(1)}, bf16[256,1536]{1,0:T(8,128)(2,1)S(1)}, u32[]{:S(2)}, u32[]{:S(2)}) collective-permute-start(bf16[256,1536]{1,0:T(8,128)(2,1)S(1)} %fusion.52), channel_id=1, source_target_pairs={{8,0},{16,8},{24,16},{28,24},{20,28},{12,20},{4,12},{0,4},{9,1},{1... | collective-permute-start | bytes 2359304 | tf_op jit(solution)/shard_map/ppermute | solution.py:30
  817.2 39.5 %collective-permute-start.65 = (bf16[256,2048]{1,0:T(8,128)(2,1)S(1)}, bf16[256,2048]{1,0:T(8,128)(2,1)S(1)}, u32[]{:S(2)}, u32[]{:S(2)}) collective-permute-start(bf16[256,2048]{1,0:T(8,128)(2,1)S(1)} %add_convert_fusion.4), channel_id=1, source_target_pairs={{0,2},{1,3},{2,0},{3,1},{4,6},{5,7},{6,4},{7,5},{8,10},{9,11},{10,... | collective-permute-start | bytes 3145736 | tf_op jit(solution)/shard_map/ppermute | solution.py:34
  827.3 29.0 %collective-permute-start.69 = (bf16[256,2048]{1,0:T(8,128)(2,1)S(1)}, bf16[256,2048]{1,0:T(8,128)(2,1)S(1)}, u32[]{:S(2)}, u32[]{:S(2)}) collective-permute-start(bf16[256,2048]{1,0:T(8,128)(2,1)S(1)} %constant_dynamic-update-slice_fusion.64), channel_id=1, source_target_pairs={{4,0},{8,4},{12,8},{16,12},{20,16},{24,20},{28,24},{5,1},{9,5},{13... | collective-permute-start | bytes 3145736 | tf_op jit(solution)/shard_map/ppermute | solution.py:339
  831.8 61.2 %collective-permute-start.86 = (bf16[256,1536]{1,0:T(8,128)(2,1)}, bf16[256,1536]{1,0:T(8,128)(2,1)}, u32[]{:S(2)}, u32[]{:S(2)}) collective-permute-start(bf16[256,1536]{1,0:T(8,128)(2,1)} %fusion.53), channel_id=1, source_target_pairs={{8,0},{16,8},{24,16},{28,24},{20,28},{12,20},{4,12},{0,4},{9,1},{1... | collective-permute-start | bytes 2359304 | tf_op jit(solution)/shard_map/ppermute | solution.py:30
  836.4 56.6 %collective-permute-start.83 = (bf16[256,1536]{1,0:T(8,128)(2,1)}, bf16[256,1536]{1,0:T(8,128)(2,1)}, u32[]{:S(2)}, u32[]{:S(2)}) collective-permute-start(bf16[256,1536]{1,0:T(8,128)(2,1)} %fusion.56), channel_id=1, source_target_pairs={{0,8},{8,16},{16,24},{24,28},{28,20},{20,12},{12,4},{4,0},{1,9},{9... | collective-permute-start | bytes 2359304 | tf_op jit(solution)/shard_map/ppermute | solution.py:30
  (132 other events, 2904.8 us)

commit v2 on v1

v2 whole, which is shorter than its diff:
```python
import jax
import jax.numpy as jnp
from jax import lax
from jax.experimental import pallas as pl
from jax.experimental.pallas import tpu as pltpu
from jax.sharding import PartitionSpec as P

HEAD_DIM = 128
WINDOW = 256
F32 = jnp.float32
BF16 = jnp.bfloat16


def ring_order(count):
    return list(range(0, count, 2)) + list(range(count - 1, 0, -2))


def ring_place(index, count):
    return jnp.where(index % 2 == 0, index // 2, count - 1 - index // 2)


def ring_index(place, count):
    return jnp.where(place < count // 2, 2 * place, 2 * (count - 1 - place) + 1)


def slot_owners():
    count = lax.axis_size("seq")
    place = ring_place(lax.axis_index("seq"), count)
    return ring_index((place + jnp.arange(count, dtype=jnp.int32)) % count, count)


def owner_slots():
    count = lax.axis_size("seq")
    place = ring_place(lax.axis_index("seq"), count)
    return (ring_place(jnp.arange(count, dtype=jnp.int32), count) - place) % count


def tie(value, *after):
    after = [v for v in after if v is not None]
    return lax.optimization_barrier((value, *after))[0] if after else value


class Ring:
    def __init__(self):
        self.count = lax.axis_size("seq")
        self.queue = {True: [], False: []}
        self.last = {True: None, False: None}
        self.before = []
        self.flip = False

    def hop(self, value, forward):
        order = ring_order(self.count)
        ahead = order[1:] + order[:1]
        pairs = zip(order, ahead) if forward else zip(ahead, order)
        got = lax.ppermute(tie(value, self.last[forward]), "seq", list(pairs))
        self.last[forward] = got
        return got

    def advance(self):
        self.before = [v for v in self.last.values() if v is not None]
        for forward, queue in self.queue.items():
            if queue:
                queue.pop(0)()
        for queue in self.queue.values():
            if queue and hasattr(queue[0], "ready"):
                queue[0].ready()

    def now(self, value):
        return tie(value, *self.before)

    def legs(self):
        steps = self.count - 1 - self.count // 2 if self.flip else self.count // 2
        self.flip = not self.flip
        return ((True, steps), (False, self.count - 1 - steps))

    def gather(self, value):
        slots = [value] + [None] * (self.count - 1)
        for forward, steps in self.legs():
            for t in range(1, steps + 1):
                at = self.count - t if forward else t

                def step(source=(at + (1 if forward else -1)) % self.count, at=at, way=forward):
                    slots[at] = self.hop(slots[source], way)

                self.queue[forward].append(step)
        return slots

    def scatter(self, make):
        return Scatter(self, make)


class Scatter:
    def __init__(self, ring, make):
        self.ring, self.make = ring, make
        self.got = {True: None, False: None}
        for forward, steps in ring.legs():
            for t in range(steps):
                j = steps - t if forward else ring.count - steps + t
                ring.queue[forward].append(Leg(self, forward, j))

    def total(self):
        return self.make(0) + self.got[True].astype(F32) + self.got[False].astype(F32)


class Leg:
    def __init__(self, scatter, forward, j):
        self.scatter, self.forward, self.j = scatter, forward, j
        self.part = None

    def ready(self):
        if self.part is None:
            self.part = self.scatter.make(self.j)

    def __call__(self):
        self.ready()
        part, got = self.part, self.scatter.got[self.forward]
        if got is not None:
            part = part + got.astype(F32)
        self.scatter.got[self.forward] = self.scatter.ring.hop(part.astype(BF16), self.forward)


def swap(value, axis, bit):
    return lax.ppermute(value, axis, [(i, i ^ bit) for i in range(lax.axis_size(axis))])


def bits_of(count):
    return [1 << k for k in range(count.bit_length() - 1)]


def small_gather(value):
    count, groups = lax.axis_size("seq"), lax.axis_size("batch")
    parts = value[None]
    for axis in ("seq", "batch"):
        for bit in bits_of(lax.axis_size(axis)):
            parts = jnp.concatenate([parts, swap(parts, axis, bit)], axis=0)
    own_s, own_b = lax.axis_index("seq"), lax.axis_index("batch")
    order = (slot_owners() ^ own_s)[:, None] + count * (
        jnp.arange(groups, dtype=jnp.int32) ^ own_b
    )
    parts = jnp.take(parts, order.reshape(-1), axis=0)
    return jnp.moveaxis(parts, 0, -2).reshape(*value.shape[:-1], -1)


def small_totals(value, flat):
    count, groups = lax.axis_size("seq"), lax.axis_size("batch")
    own_s, own_b = lax.axis_index("seq"), lax.axis_index("batch")
    parts = jnp.moveaxis(value.reshape(*value.shape[:-1], count * groups, -1), -2, 0)
    order = owner_slots()[jnp.arange(count, dtype=jnp.int32) ^ own_s] * groups + (
        jnp.arange(groups, dtype=jnp.int32) ^ own_b
    )[:, None]
    parts = jnp.take(parts, order.reshape(-1), axis=0)
    for bit in reversed(bits_of(groups)):
        half = parts.shape[0] // 2
        parts = parts[:half] + swap(parts[half:], "batch", bit)
    piece = parts.shape[1:]
    parts = parts.reshape(count, -1)
    for bit in reversed(bits_of(count)):
        half = parts.shape[0] // 2
        sent = jnp.concatenate([parts[half:].reshape(-1), flat])
        got = swap(sent, "seq", bit)
        at = half * parts.shape[1]
        parts = parts[:half] + got[:at].reshape(half, -1)
        flat = flat + got[at:]
    return parts.reshape(piece), flat


def batch_gather(value):
    parts = {0: value}
    for bit in reversed(bits_of(lax.axis_size("batch"))):
        parts.update({r | bit: swap(v, "batch", bit) for r, v in list(parts.items())})
    return [parts[r] for r in range(len(parts))]


def batch_scatter(parts, wire=BF16):
    parts = dict(enumerate(parts))
    for bit in bits_of(len(parts)):
        for r in [r for r in parts if r & bit]:
            got = swap(parts[r].astype(wire), "batch", bit)
            parts[r ^ bit] = parts[r ^ bit].astype(F32) + got.astype(F32)
            del parts[r]
    return parts[0]


def move_kernel(order, value, moved):
    width = value.shape[1] // order.shape[0]
    for i in range(order.shape[0]):
        source = pl.multiple_of(order[i] * width, width)
        moved[:, i * width : (i + 1) * width] = value[:, pl.ds(source, width)]


def reorder(value, order):
    rows, columns = value.shape
    width = columns // order.shape[0]
    if width % 128:
        return jnp.take(value.reshape(rows, -1, width), order, axis=1).reshape(value.shape)
    block = pl.BlockSpec((rows // 4, columns), lambda i, *_: (i, 0))
    return pl.pallas_call(
        move_kernel,
        grid_spec=pltpu.PrefetchScalarGridSpec(
            num_scalar_prefetch=1, grid=(4,), in_specs=[block], out_specs=block
        ),
        out_shape=jax.ShapeDtypeStruct(value.shape, value.dtype),
        cost_estimate=pl.CostEstimate(
            flops=0, bytes_accessed=2 * value.size * value.dtype.itemsize, transcendentals=0
        ),
    )(order, value)


def norm_stats(values):
    mean = jnp.mean(values, axis=-1, keepdims=True)
    centered = values - mean
    factor = lax.rsqrt(jnp.mean(centered * centered, axis=-1, keepdims=True) + 1e-05)
    return centered * factor, factor


def norm_back(grad, unit, factor, gain):
    scaled = grad * gain
    inner = jnp.mean(scaled * unit, axis=-1, keepdims=True)
    return factor * (scaled - jnp.mean(scaled, axis=-1, keepdims=True) - unit * inner)


def gelu_and_slope(values):
    root, cubic = (2 / jnp.pi) ** 0.5, 0.044715
    square = values * values
    bend = jnp.tanh(values * (root + root * cubic * square))
    half = 0.5 + 0.5 * bend
    slope = half + values * (0.5 - 0.5 * bend * bend) * (root + 3 * root * cubic * square)
    return values * half, slope


def dot_t(left, right, left_dim, right_dim):
    return lax.dot_general(
        left, right, (((left_dim,), (right_dim,)), ((), ())), preferred_element_type=F32
    )


def masks(start, limit):
    row = lax.broadcasted_iota(jnp.int32, (WINDOW, WINDOW), 0)
    col = lax.broadcasted_iota(jnp.int32, (WINDOW, WINDOW), 1)
    own = col <= row
    spot = jnp.where(own, start + col, start - WINDOW + col)
    return own, (spot >= 0) & ((spot < limit) | (row == col))


def weights_of(query, key, early_key, own, live):
    scores = jnp.where(own, dot_t(query, key, 1, 1), dot_t(query, early_key, 1, 1))
    scores = jnp.where(live, scores * (HEAD_DIM**-0.5), -1e30)
    expo = jnp.exp(scores - jnp.max(scores, axis=-1, keepdims=True))
    return expo / jnp.sum(expo, axis=-1, keepdims=True)


def attend_kernel(limits, start, packed, early, mixed):
    width = mixed.shape[1]
    own, live = masks(start[0], limits[pl.program_id(0)])
    for at in range(0, width, HEAD_DIM):
        cols = lambda k: slice(k * width + at, k * width + at + HEAD_DIM)
        probs = weights_of(packed[:, cols(0)], packed[:, cols(1)], early[:, cols(0)], own, live)
        near = jnp.where(own, probs, 0.0).astype(BF16)
        far = jnp.where(own, 0.0, probs).astype(BF16)
        mixed[:, cols(0)] = (
            dot_t(near, packed[:, cols(2)], 1, 0) + dot_t(far, early[:, cols(1)], 1, 0)
        ).astype(BF16)


def attend_back_kernel(limits, start, packed, early, grad, g_packed, g_early):
    width = grad.shape[1]
    scale = HEAD_DIM**-0.5
    own, live = masks(start[0], limits[pl.program_id(0)])
    for at in range(0, width, HEAD_DIM):
        cols = lambda k: slice(k * width + at, k * width + at + HEAD_DIM)
        query, key, value = (packed[:, cols(k)] for k in range(3))
        early_key, early_value = (early[:, cols(k)] for k in range(2))
        out = grad[:, cols(0)]
        probs = weights_of(query, key, early_key, own, live)
        g_probs = jnp.where(own, dot_t(out, value, 1, 1), dot_t(out, early_value, 1, 1))
        delta = jnp.sum(probs * g_probs, axis=-1, keepdims=True)
        g_scores = probs * (g_probs - delta)
        near = jnp.where(own, probs, 0.0).astype(BF16)
        far = jnp.where(own, 0.0, probs).astype(BF16)
        g_near = jnp.where(own, g_scores, 0.0).astype(BF16)
        g_far = jnp.where(own, 0.0, g_scores).astype(BF16)
        g_packed[:, cols(0)] = (
            (dot_t(g_near, key, 1, 0) + dot_t(g_far, early_key, 1, 0)) * scale
        ).astype(BF16)
        g_packed[:, cols(1)] = (dot_t(g_near, query, 0, 0) * scale).astype(BF16)
        g_packed[:, cols(2)] = dot_t(near, out, 0, 0).astype(BF16)
        g_early[:, cols(0)] = (dot_t(g_far, query, 0, 0) * scale).astype(BF16)
        g_early[:, cols(1)] = dot_t(far, out, 0, 0).astype(BF16)


def per_chain(kernel, limits, start, arrays, widths, flops):
    rows = arrays[0].shape[0]
    block = lambda w: pl.BlockSpec((WINDOW, w), lambda i, *_: (i, 0))
    moved = 2 * rows * (sum(a.shape[1] for a in arrays) + sum(widths))
    return pl.pallas_call(
        kernel,
        grid_spec=pltpu.PrefetchScalarGridSpec(
            num_scalar_prefetch=2,
            grid=(rows // WINDOW,),
            in_specs=[block(a.shape[1]) for a in arrays],
            out_specs=[block(w) for w in widths],
        ),
        out_shape=[jax.ShapeDtypeStruct((rows, w), BF16) for w in widths],
        cost_estimate=pl.CostEstimate(
            flops=flops, bytes_accessed=moved, transcendentals=rows * WINDOW
        ),
    )(limits, start, *arrays)


def shards(
    tokens,
    lengths,
    cotangent,
    ln1_gain,
    ln1_bias,
    w_qkv,
    qv_bias,
    w_out,
    out_bias,
    ln2_gain,
    ln2_bias,
    w_fc,
    fc_bias,
    w_proj,
    proj_bias,
):
    groups = lax.axis_size("batch")
    chain = lax.axis_index("batch")
    place = lax.axis_index("seq")
    rows, width = tokens.shape[1:]
    count = lax.axis_size("seq")
    slice_width = width // count
    heads_width = w_out.shape[0]
    assert rows == WINDOW and lengths.shape[1] == 1 and tokens.shape[0] == 1
    start = (place * rows).astype(jnp.int32)
    limits = lengths[:, 0][chain ^ jnp.arange(groups, dtype=jnp.int32)]
    valid = (start + jnp.arange(rows, dtype=jnp.int32) < limits[0]).astype(F32)
    to_slots, from_slots = slot_owners(), owner_slots()

    tokens, cotangent = tokens[0], cotangent[0]
    vectors = small_gather(
        jnp.stack([ln1_gain, ln1_bias, out_bias, ln2_gain, ln2_bias, proj_bias])
    ).astype(F32)
    gain_one, shift_one, mix_shift, gain_two, shift_two, down_shift = (
        vectors[i] for i in range(6)
    )
    def cut(value, j):
        return value[:, j * slice_width : (j + 1) * slice_width]

    def rows_of(parts):
        return jnp.concatenate(parts, axis=0)

    def spread(left, right, right_dim):
        half = left.shape[0] // 2
        far = dot_t(left[half:], right, 1, right_dim).astype(BF16)
        near = dot_t(left[:half], right, 1, right_dim).astype(BF16)
        each = [near[i : i + rows] for i in range(0, half, rows)]
        return batch_scatter(each + [far[i : i + rows] for i in range(0, half, rows)])

    ring = Ring()
    qkv_width = 3 * heads_width
    mix_slots = ring.gather(
        jnp.concatenate([w_qkv.reshape(slice_width, qkv_width), w_out.T], axis=1)
    )
    up_slots = ring.gather(w_fc)
    down_slots = ring.gather(w_proj)
    late = {}
    g_down = ring.scatter(lambda j: dot_t(late["active"], cut(late["dy"], j), 0, 0))
    g_up = ring.scatter(lambda j: dot_t(cut(late["second"], j), late["df"], 0, 0))

    def mix_part(j):
        early = dot_t(cut(late["normed_early"], j), late["g_early"], 0, 0)
        part = dot_t(cut(late["normed"], j), late["g_packed"], 0, 0)
        part = part + jnp.pad(early, ((0, 0), (heads_width, 0)))
        return jnp.concatenate([part, dot_t(cut(late["da"], j), late["mixed"], 0, 0)], axis=1)

    g_mix = ring.scatter(mix_part)
    turns = count // 2
    more = max(0, turns - 4)

    def advance(times=1):
        for _ in range(times):
            ring.advance()

    early_tokens = lax.ppermute(tokens, "seq", [(i, i + 1) for i in range(count - 1)])
    advance()
    own_tokens = reorder(tokens, to_slots)
    grad_out = reorder(cotangent, to_slots).astype(F32) * valid[:, None]
    grad_y_own = grad_out.astype(BF16)
    pairs = batch_gather(tie(rows_of([own_tokens, grad_y_own]), vectors))
    all_tokens = rows_of([p[:rows] for p in pairs])
    grad_y = rows_of([p[rows:] for p in pairs])
    own_early = reorder(early_tokens, to_slots)
    all_early = rows_of(batch_gather(own_early))
    advance(2 + more)
    normed = (norm_stats(all_tokens.astype(F32))[0] * gain_one + shift_one).astype(BF16)
    normed_early = (norm_stats(all_early.astype(F32))[0] * gain_one + shift_one).astype(BF16)
    advance()

    advance()
    mix_in = rows_of(mix_slots)
    proj_in, proj_mix = mix_in[:, :qkv_width], mix_in[:, qkv_width:]
    qv_float = qv_bias.astype(F32)
    packed_shift = jnp.concatenate([qv_float[0], jnp.zeros_like(qv_float[0]), qv_float[1]])
    packed = (dot_t(ring.now(normed), proj_in, 1, 0) + packed_shift).astype(BF16)
    early = (
        dot_t(ring.now(normed_early), proj_in[:, heads_width:], 1, 0) + packed_shift[heads_width:]
    ).astype(BF16)
    square = 2 * packed.shape[0] * WINDOW * heads_width
    starts = start.reshape(1)
    advance()
    (mixed,) = per_chain(
        attend_kernel, limits, starts, (ring.now(packed), early), (heads_width,), 4 * square
    )
    branch = spread(mixed, proj_mix, 1)
    advance()
    inputs = own_tokens.astype(F32)
    resid = inputs + ring.now(branch) + mix_shift
    unit_two, factor_two = norm_stats(resid)
    second_own = (unit_two * gain_two + shift_two).astype(BF16)
    second = rows_of(batch_gather(second_own))
    advance()

    advance(1 + more)
    proj_up = rows_of(up_slots)
    pre = dot_t(ring.now(second), proj_up, 1, 0) + fc_bias.astype(F32)
    active, slope = (v.astype(BF16) for v in gelu_and_slope(pre))
    late.update(active=active, dy=grad_y)
    advance(2 + more)
    proj_down = jnp.concatenate(down_slots, axis=1)
    advance()
    grad_active = dot_t(ring.now(grad_y), proj_down, 1, 1)
    grad_pre = (grad_active * slope.astype(F32)).astype(BF16)
    grad_fc_bias = jnp.sum(grad_pre.astype(F32), axis=0)
    late.update(second=second, df=grad_pre)
    advance()
    grad_second = spread(ring.now(grad_pre), proj_up, 1)
    advance()
    result = resid + spread(ring.now(active), proj_down, 0) + down_shift
    block_out = reorder(result.astype(BF16), from_slots)
    advance(1 + more)
    grad_resid = grad_out + norm_back(grad_second, unit_two, factor_two, gain_two)
    grad_branch_own = grad_resid.astype(BF16)
    grad_branch = rows_of(batch_gather(grad_branch_own))
    advance()

    grad_mixed = dot_t(ring.now(grad_branch), proj_mix, 1, 0).astype(BF16)
    g_packed, g_early = per_chain(
        attend_back_kernel,
        limits,
        starts,
        (packed, early, grad_mixed),
        (qkv_width, 2 * heads_width),
        10 * square,
    )
    late.update(
        normed=normed, normed_early=normed_early, g_packed=g_packed, g_early=g_early,
        da=grad_branch, mixed=mixed,
    )
    advance()
    back = spread(ring.now(g_early), proj_in[:, heads_width:], 1)
    moved = lax.ppermute(
        reorder(back.astype(BF16), from_slots), "seq", [(i + 1, i) for i in range(count - 1)]
    )
    advance()
    grad_own = spread(ring.now(g_packed), proj_in, 1)
    while ring.queue[True] or ring.queue[False]:
        advance()
    unit_one, factor_one = norm_stats(inputs)
    unit_early, _ = norm_stats(own_early.astype(F32))
    grad_normed = grad_own + reorder(moved, to_slots).astype(F32)
    grad_tokens = grad_resid + norm_back(grad_normed, unit_one, factor_one, gain_one)

    column = lambda value: jnp.sum(value.astype(F32), axis=0)
    flat = jnp.concatenate(
        [
            grad_fc_bias,
            column(g_packed[:, :heads_width]),
            column(g_packed[:, 2 * heads_width :]) + column(g_early[:, heads_width:]),
        ]
    )
    ff = grad_fc_bias.shape[0]
    sums = jnp.stack(
        [
            jnp.sum(grad_own * unit_one + back * unit_early, axis=0),
            jnp.sum(grad_own + back, axis=0),
            column(grad_branch_own),
            jnp.sum(grad_second * unit_two, axis=0),
            jnp.sum(grad_second, axis=0),
            column(grad_y_own),
        ]
    )
    sums, flat = small_totals(sums, flat)
    grad_mix_in = g_mix.total()
    return (
        block_out[None],
        reorder(grad_tokens.astype(BF16), from_slots)[None],
        sums[0],
        sums[1],
        grad_mix_in[:, :qkv_width].reshape(slice_width, 3, heads_width),
        flat[ff:].reshape(2, heads_width),
        grad_mix_in[:, qkv_width:].T,
        sums[2],
        sums[3],
        sums[4],
        g_up.total(),
        flat[:ff],
        g_down.total(),
        sums[5],
    )


def solution(mesh):
    everywhere = P(("seq", "batch"))
    rows = P("batch", "seq", None)
    return jax.shard_map(
        shards,
        mesh=mesh,
        in_specs=(
            rows,
            P(),
            rows,
            everywhere,
            everywhere,
            P("seq", None, "batch"),
            P(None, "batch"),
            P("batch", "seq"),
            everywhere,
            everywhere,
            everywhere,
            P("seq", "batch"),
            P("batch"),
            P("batch", "seq"),
            everywhere,
        ),
        out_specs=(
            rows,
            rows,
            everywhere,
            everywhere,
            P("seq", None, "batch"),
            P(None, "batch"),
            P("batch", "seq"),
            everywhere,
            everywhere,
            everywhere,
            P("seq", "batch"),
            P("batch"),
            P("batch", "seq"),
            everywhere,
        ),
        check_vma=False,
    )
```

time: 909 us -> 712 us (0.78)
  waiting for transfers between devices: 446 us -> 230 us
  Pallas kernels: 25.2 us -> 53.4 us
  other arithmetic: 50.7 us -> 76.1 us
  local copies, waits for them, and re-layouts: 85.9 us -> 64.5 us
  starting transfers between devices: 100 us -> 85.2 us
    ppermute x71 -> x43, waiting for transfers between devices: 398 us -> 126 us  [the longest x42 114 us: hop(): got = lax.ppermute(tie(value, self.last[forward]), 'seq', list(pairs))]
    ppermute x39 -> x37, waiting for transfers between devices: 48.4 us -> 93.5 us  [swap(): lax.ppermute(value, axis, [(i, i ^ bit) for i in range(lax.axis_size(axis...]
    unnamed x248 -> x185, local copies, waits for them, and re-layouts: 66.1 us -> 36.7 us
    pallas_call x0 -> x7, Pallas kernels: none -> 28.5 us  [reorder(): pl.pallas_call(move_kernel, grid_spec=pltpu.PrefetchScalarGridSpec(num_sc...]
    ppermute x71 -> x43, starting transfers between devices: 71 us -> 55.2 us  [the longest x42 53.8 us: hop(): got = lax.ppermute(tie(value, self.last[forward]), 'seq', list(pairs))]
    convert_element_type x2 -> x8, other arithmetic: 0.45 us -> 13.4 us  [the longest x5 12.9 us: __call__(): part.astype(BF16)]
    ppermute x1, waiting for transfers between devices: 0.01 us -> 10.6 us  [shards(): lax.ppermute(tokens, 'seq', [(i, i + 1) for i in range(count - 1)])]
    slice x2 -> x18, local copies, waits for them, and re-layouts: 0.01 us -> 10.1 us  [the longest x4 9.38 us: shards(): grad_y = rows_of([p[rows:] for p in pairs])]
  transfers between devices with their start and end apart: 111 -> 81, of which waited for: 42 -> 30; matrix products, arithmetic and copies ran while one was open for 27% -> 44% of each run, Pallas kernels for 3% -> 8%
where the time goes in v2:
time: 712 us; the launch traced here: 703 us
  waiting for transfers between devices  230 us (32%)
  matrix products  190 us (27%)
  starting transfers between devices  85.2 us (12%)
  other arithmetic  76.1 us (11%)
  local copies, waits for them, and re-layouts  64.5 us (9%)
  Pallas kernels  53.4 us (8%)
    dot_general x55, matrix products, dot_t(): lax.dot_general(left, right, (((left_dim,), (right_dim,)), ((), ())), pre...  190 us
    ppermute x42, waiting for transfers between devices, hop(): got = lax.ppermute(tie(value, self.last[forward]), 'seq', list(pairs))  114 us
    ppermute x37, waiting for transfers between devices, swap(): lax.ppermute(value, axis, [(i, i ^ bit) for i in range(lax.axis_size(axis...  93.5 us
    ppermute x42, starting transfers between devices, hop(): got = lax.ppermute(tie(value, self.last[forward]), 'seq', list(pairs))  53.8 us
    unnamed x185, local copies, waits for them, and re-layouts  36.7 us
    pallas_call x7, Pallas kernels, reorder(): pl.pallas_call(move_kernel, grid_spec=pltpu.PrefetchScalarGridSpec(num_sc...  28.5 us
    ppermute x37, starting transfers between devices, swap(): lax.ppermute(value, axis, [(i, i ^ bit) for i in range(lax.axis_size(axis...  27.1 us
    pallas_call x2, Pallas kernels, per_chain(): pl.pallas_call(kernel, grid_spec=pltpu.PrefetchScalarGridSpec(num_scalar_...  24.9 us
  transfers between devices with their start and end apart: 81, of which 30 were waited for; matrix products, arithmetic and copies ran while one was open for 44% of the time, Pallas kernels for 8%

profile of v2, /device:TPU:0, one launch (start us, length us, event | category | flops | bytes accessed | tf_op | source)
XLA Modules:
  0.0 702.5 jit_solution(17296799302005213770)
XLA Ops:
  4.3 2.9 collective-permute-start.12
  9.4 3.0 collective-permute-start.18
  12.9 4.0 shard_map.254
  17.0 4.2 shard_map.255
  32.2 3.4 collective-permute-done.4
  37.4 2.9 collective-permute-done.5
  41.7 10.6 %collective-permute-done.18.value = bf16[256,2048]{1,0:T(8,128)(2,1)} collective-permute-done((bf16[256,2048]{1,0:T(8,128)(2,1)}, bf16[256,2048]{1,0:T(8,128)(2,1)}, u32[]{:S(2)}, u32[]{:S(2)}) %collective-permute-start.18) | collective-permute-done | bytes 1048608 | tf_op jit(solution)/shard_map/ppermute | solution.py:385
  54.7 4.1 shard_map.256
  59.3 7.8 %collective-permute-start.13 = (bf16[256,2048]{0,1:T(8,128)(2,1)}, bf16[256,2048]{0,1:T(8,128)(2,1)}, u32[]{:S(2)}, u32[]{:S(2)}) collective-permute-start(bf16[256,2048]{0,1:T(8,128)(2,1)} %collective-permute-done.12), channel_id=1, source_target_pairs={{8,0},{16,8},{24,16},{28,24},{20,28},{12,20},{4,12},{0,4},{9,1},{1... | collective-permute-start | bytes 3145736 | tf_op jit(solution)/shard_map/ppermute | solution.py:55
  67.1 7.4 %collective-permute-done.7 = bf16[16,6,64]{2,1,0:T(8,128)(2,1)S(1)} collective-permute-done((bf16[16,6,64]{2,1,0:T(8,128)(2,1)S(1)}, bf16[16,6,64]{2,1,0:T(8,128)(2,1)S(1)}, u32[]{:S(2)}, u32[]{:S(2)}) %collective-permute-start.7) | collective-permute-done | bytes 12320 | tf_op jit(solution)/shard_map/ppermute | solution.py:123
  79.1 10.7 %collective-permute-done.13 = bf16[256,2048]{0,1:T(8,128)(2,1)} collective-permute-done((bf16[256,2048]{0,1:T(8,128)(2,1)}, bf16[256,2048]{0,1:T(8,128)(2,1)}, u32[]{:S(2)}, u32[]{:S(2)}) %collective-permute-start.13) | collective-permute-done | bytes 1048608 | tf_op jit(solution)/shard_map/ppermute | solution.py:55
  89.8 6.2 collective-permute-done.9
  106.4 13.1 %collective-permute-done.14 = bf16[256,2048]{0,1:T(8,128)(2,1)S(1)} collective-permute-done((bf16[256,2048]{0,1:T(8,128)(2,1)}, bf16[256,2048]{0,1:T(8,128)(2,1)S(1)}, u32[]{:S(2)}, u32[]{:S(2)}) %collective-permute-start.14) | collective-permute-done | bytes 1048608 | tf_op jit(solution)/shard_map/ppermute | solution.py:55
  124.3 3.7 fusion.4
  130.1 3.7 fusion.8
  133.7 8.9 %collective-permute-done.15 = bf16[256,2048]{1,0:T(8,128)(2,1)S(1)} collective-permute-done((bf16[256,2048]{1,0:T(8,128)(2,1)S(1)}, bf16[256,2048]{1,0:T(8,128)(2,1)S(1)}, u32[]{:S(2)}, u32[]{:S(2)}) %collective-permute-start.15) | collective-permute-done | bytes 1048608 | tf_op jit(solution)/shard_map/ppermute | solution.py:55
  143.5 12.7 %fusion.7 = (bf16[1024,2048]{1,0:T(8,128)(2,1)S(1)}, bf16[1024,2048]{1,0:T(8,128)(2,1)S(1)}) fusion(f32[1024]{0:T(1024)S(1)} %add_rsqrt_fusion, f32[1024]{0:T(1024)S(1)} %broadcast_multiply_fusion, f32[2048]{0:T(1024)S(1)} %add.522, f32[2048]{0:T(1024)S(1)} %mul.225, bf16[256,2048]{1,0:T(8,128)(2,1)S(1)} %collective-permute-done.21, ...), kind=kLoop, calls=%fused_computation.17 | loop fusion | flops 54525952 | bytes 16809984 | tf_op jit(solution)/shard_map/convert_element_type | solution.py:397
  161.5 8.2 %add_convert_fusion.packed = bf16[1024,1536]{1,0:T(8,128)(2,1)} fusion(bf16[1024,2048]{1,0:T(8,128)(2,1)S(1)} %get-tuple-element.73, bf16[2048,2048]{0,1:T(8,128)(2,1)S(1)} %constant_dynamic-update-slice_fusion.11, f32[1536]{0:T(1024)S(1)} %pad_maximum_fusion.14), kind=kOutput, calls=%fused_computation.31 | convolution fusion | flops 6445596672 | bytes 13639680 | tf_op jit(solution)/shard_map/dot_general | solution.py:232
  169.7 5.7 add_convert_fusion.1.early
  177.4 9.9 %shard_map.257 = bf16[1024,512]{1,0:T(8,128)(2,1)} custom-call(s32[4]{0:T(128)} %copy-done.63, s32[1]{0:T(128)} %bitcast.3.start, bf16[1024,1536]{1,0:T(8,128)(2,1)} %add_convert_fusion.packed, bf16[1024,1024]{1,0:T(8,128)(2,1)} %add_convert_fusion.1.early), custom_call_target="tpu_custom_call" | custom-call | flops 1073741824 | bytes 6291456 | tf_op jit(solution)/shard_map/pallas_call | solution.py:295
  187.4 3.1 convolution_convert_fusion.4
  192.6 2.9 convolution_convert_fusion.5
  206.3 17.5 %collective-permute-done.32 = bf16[256,2048]{1,0:T(8,128)(2,1)} collective-permute-done((bf16[256,2048]{1,0:T(8,128)(2,1)}, bf16[256,2048]{1,0:T(8,128)(2,1)}, u32[]{:S(2)}, u32[]{:S(2)}) %collective-permute-start.32) | collective-permute-done | bytes 1048608 | tf_op jit(solution)/shard_map/ppermute | solution.py:55
  238.9 10.1 %collective-permute-done.33 = bf16[2048,256]{1,0:T(8,128)(2,1)S(1)} collective-permute-done((bf16[2048,256]{1,0:T(8,128)(2,1)}, bf16[2048,256]{1,0:T(8,128)(2,1)S(1)}, u32[]{:S(2)}, u32[]{:S(2)}) %collective-permute-start.33) | collective-permute-done | bytes 1048608 | tf_op jit(solution)/shard_map/ppermute | solution.py:55
  251.1 3.6 collective-permute-done.28
  261.2 11.8 %collective-permute-done.39 = bf16[2048,256]{1,0:T(8,128)(2,1)S(1)} collective-permute-done((bf16[2048,256]{1,0:T(8,128)(2,1)S(1)}, bf16[2048,256]{1,0:T(8,128)(2,1)S(1)}, u32[]{:S(2)}, u32[]{:S(2)}) %collective-permute-start.39) | collective-permute-done | bytes 1048608 | tf_op jit(solution)/shard_map/ppermute | solution.py:55
  275.4 13.1 %multiply_convert_fusion.1 = (bf16[1024,2048]{1,0:T(8,128)(2,1)}, f32[1024,2048]{1,0:T(8,128)}) fusion(f32[2048]{0:T(1024)S(1)} %convert_element_type.374, bf16[1024,2048]{1,0:T(8,128)(2,1)S(1)} %pad_maximum_fusion.2, bf16[2048,2048]{1,0:T(8,128)(2,1)S(1)} %constant_dynamic-update-slice_fusion.19), kind=kOutput, calls=%fused_computation.29 | convolution fusion | flops 8608808960 | bytes 25174016 | tf_op jit(solution)/shard_map/dot_general | solution.py:232
  288.5 3.7 convolution_convert_fusion.8
  292.1 5.1 collective-permute-done.35
  304.4 16.2 %collective-permute-done.36 = bf16[2048,256]{1,0:T(8,128)(2,1)S(1)} collective-permute-done((bf16[2048,256]{1,0:T(8,128)(2,1)S(1)}, bf16[2048,256]{1,0:T(8,128)(2,1)S(1)}, u32[]{:S(2)}, u32[]{:S(2)}) %collective-permute-start.36) | collective-permute-done | bytes 1048608 | tf_op jit(solution)/shard_map/ppermute | solution.py:55
  329.6 16.4 %convert_reduce_fusion.2 = (f32[2048]{0:T(1024)}, bf16[1024,2048]{1,0:T(8,128)(2,1)S(1)}) fusion(f32[1024,2048]{1,0:T(8,128)} %get-tuple-element.208, f32[2048]{0:T(1024)S(1)} %convert_element_type.374, bf16[1024,2048]{1,0:T(8,128)(2,1)S(1)} %pad_maximum_fusion.3, bf16[2048,2048]{1,0:T(8,128)(2,1)} %constant_dynamic-update-slice_fusion.27), kind=kOutput, calls=%fused_computation.27 | convolution fusion | flops 8631875584 | bytes 25182208 | tf_op jit(solution)/shard_map/dot_general | solution.py:232
  353.7 3.6 fusion.48
  358.3 8.4 %convolution_convert_fusion = bf16[512,2048]{1,0:T(8,128)(2,1)S(1)} fusion(bf16[2048,2048]{1,0:T(8,128)(2,1)} %copy-done.45, bf16[1024,2048]{1,0:T(8,128)(2,1)S(1)} %get-tuple-element.98), kind=kOutput, calls=%fused_computation.57 | convolution fusion | flops 4296015872 | bytes 12582912 | tf_op jit(solution)/shard_map/dot_general | solution.py:232
  367.7 8.4 %convolution_convert_fusion.1 = bf16[512,2048]{1,0:T(8,128)(2,1)S(1)} fusion(bf16[2048,2048]{1,0:T(8,128)(2,1)} %copy-done.45, bf16[1024,2048]{1,0:T(8,128)(2,1)S(1)} %get-tuple-element.98), kind=kOutput, calls=%fused_computation.58 | convolution fusion | flops 4296015872 | bytes 12582912 | tf_op jit(solution)/shard_map/dot_general | solution.py:232
  376.8 4.2 fusion.50
  388.1 8.5 %convolution_convert_fusion.2 = bf16[512,2048]{1,0:T(8,128)(2,1)S(1)} fusion(bf16[2048,2048]{1,0:T(8,128)(2,1)} %constant_dynamic-update-slice_fusion.27, bf16[1024,2048]{1,0:T(8,128)(2,1)} %get-tuple-element.96), kind=kOutput, calls=%fused_computation.59 | convolution fusion | flops 4296015872 | bytes 12582912 | tf_op jit(solution)/shard_map/dot_general | solution.py:232
  396.8 8.5 %convolution_convert_fusion.3 = bf16[512,2048]{1,0:T(8,128)(2,1)S(1)} fusion(bf16[2048,2048]{1,0:T(8,128)(2,1)} %constant_dynamic-update-slice_fusion.27, bf16[1024,2048]{1,0:T(8,128)(2,1)} %get-tuple-element.96), kind=kOutput, calls=%fused_computation.60 | convolution fusion | flops 4296015872 | bytes 12582912 | tf_op jit(solution)/shard_map/dot_general | solution.py:232
  414.0 19.5 %collective-permute-done.46 = bf16[256,2048]{1,0:T(8,128)(2,1)S(1)} collective-permute-done((bf16[256,2048]{1,0:T(8,128)(2,1)S(1)}, bf16[256,2048]{1,0:T(8,128)(2,1)S(1)}, u32[]{:S(2)}, u32[]{:S(2)}) %collective-permute-start.46) | collective-permute-done | bytes 1048608 | tf_op jit(solution)/shard_map/ppermute | solution.py:123
  433.5 3.2 convert_reduce_fusion.9
  445.1 15.3 %collective-permute-done.51 = bf16[256,2048]{1,0:T(8,128)(2,1)} collective-permute-done((bf16[256,2048]{1,0:T(8,128)(2,1)S(1)}, bf16[256,2048]{1,0:T(8,128)(2,1)}, u32[]{:S(2)}, u32[]{:S(2)}) %collective-permute-start.51) | collective-permute-done | bytes 1048608 | tf_op jit(solution)/shard_map/ppermute | solution.py:123
  465.1 4.1 shard_map.258
  469.2 4.8 fusion.54
  475.6 3.7 fusion.52
  490.4 4.9 fusion.94.grad
  495.3 14.9 %shard_map.259 = (bf16[1024,1536]{1,0:T(8,128)(2,1)}, bf16[1024,1024]{1,0:T(8,128)(2,1)}) custom-call(s32[4]{0:T(128)} %copy-done.63, s32[1]{0:T(128)} %bitcast.3.start, bf16[1024,1536]{1,0:T(8,128)(2,1)} %add_convert_fusion.packed, bf16[1024,1024]{1,0:T(8,128)(2,1)} %add_convert_fusion.1.early, bf16[1024,512]{1,0:T(8,128)(2,1)} %fusion.94.grad), custom_call_target="tpu_custom_call" | custom-call | flops 2684354560 | bytes 11534336 | tf_op jit(solution)/shard_map/pallas_call | solution.py:295
  520.7 3.7 fusion.56
  525.7 4.5 fusion.31
  531.4 4.7 fusion.34
  548.8 6.4 fusion.40
  556.6 6.4 fusion.37
  568.8 2.8 collective-permute-done.77
  577.9 13.7 %collective-permute-done.66 = bf16[256,2048]{1,0:T(8,128)(2,1)S(1)} collective-permute-done((bf16[256,2048]{1,0:T(8,128)(2,1)S(1)}, bf16[256,2048]{1,0:T(8,128)(2,1)S(1)}, u32[]{:S(2)}, u32[]{:S(2)}) %collective-permute-start.66) | collective-permute-done | bytes 1048608 | tf_op jit(solution)/shard_map/ppermute | solution.py:123
  594.3 4.1 shard_map.260
  599.7 5.6 fusion.43
  608.1 3.9 collective-permute-start.75
  614.5 12.2 %collective-permute-done.67.value = bf16[256,2048]{1,0:T(8,128)(2,1)} collective-permute-done((bf16[256,2048]{1,0:T(8,128)(2,1)}, bf16[256,2048]{1,0:T(8,128)(2,1)}, u32[]{:S(2)}, u32[]{:S(2)}) %collective-permute-start.67) | collective-permute-done | bytes 1048608 | tf_op jit(solution)/shard_map/ppermute | solution.py:462
  626.8 4.1 shard_map.261
  630.9 4.4 fusion.99
  638.1 9.4 %collective-permute-done.75 = bf16[256,2048]{1,0:T(8,128)(2,1)} collective-permute-done((bf16[256,2048]{1,0:T(8,128)(2,1)}, bf16[256,2048]{1,0:T(8,128)(2,1)}, u32[]{:S(2)}, u32[]{:S(2)}) %collective-permute-start.75) | collective-permute-done | bytes 1048608 | tf_op jit(solution)/shard_map/ppermute | solution.py:55
  647.5 3.2 fusion.76
  650.8 3.1 fusion.78
  656.4 21.1 %collective-permute-done.70 = f32[4608]{0:T(1024)S(1)} collective-permute-done((f32[4608]{0:T(1024)S(1)}, f32[4608]{0:T(1024)S(1)}, u32[]{:S(2)}, u32[]{:S(2)}) %collective-permute-start.70) | collective-permute-done | bytes 18464 | tf_op jit(solution)/shard_map/ppermute | solution.py:123
  684.1 4.5 fusion.68.value
  688.7 4.1 shard_map.262
  (501 shorter events, 230.1 us)
Async XLA Ops:
  4.3 54.4 %collective-permute-start.12 = (bf16[256,2048]{0,1:T(8,128)(2,1)S(1)}, bf16[256,2048]{0,1:T(8,128)(2,1)}, u32[]{:S(2)}, u32[]{:S(2)}) collective-permute-start(bf16[256,2048]{0,1:T(8,128)(2,1)S(1)} %get-tuple-element.183), channel_id=1, source_target_pairs={{8,0},{16,8},{24,16},{28,24},{20,28},{12,20},{4,12},{0,4},{9,1},{1... | collective-permute-start | bytes 3145736 | tf_op jit(solution)/shard_map/ppermute | solution.py:55
  7.3 52.0 %collective-permute-start.8 = (bf16[256,2048]{0,1:T(8,128)(2,1)S(1)}, bf16[256,2048]{0,1:T(8,128)(2,1)}, u32[]{:S(2)}, u32[]{:S(2)}) collective-permute-start(bf16[256,2048]{0,1:T(8,128)(2,1)S(1)} %get-tuple-element.183), channel_id=1, source_target_pairs={{0,8},{8,16},{16,24},{24,28},{28,20},{20,12},{12,4},{4,0},{1,9},{9... | collective-permute-start | bytes 3145736 | tf_op jit(solution)/shard_map/ppermute | solution.py:55
  7.4 24.6 %collective-permute-start.3 = (bf16[1,6,64]{2,1,0:T(8,128)(2,1)S(1)}, bf16[1,6,64]{2,1,0:T(8,128)(2,1)S(1)}, u32[]{:S(2)}, u32[]{:S(2)}) collective-permute-start(bf16[1,6,64]{2,1,0:T(8,128)(2,1)S(1)} %bitcast.106), channel_id=1, source_target_pairs={{0,4},{4,0},{8,12},{12,8},{16,20},{20,16},{24,28},{28,24},{1,5},{5... | collective-permute-start | bytes 2312 | tf_op jit(solution)/shard_map/ppermute | solution.py:123
  9.4 42.9 %collective-permute-start.18 = (bf16[256,2048]{1,0:T(8,128)(2,1)}, bf16[256,2048]{1,0:T(8,128)(2,1)}, u32[]{:S(2)}, u32[]{:S(2)}) collective-permute-start(bf16[256,2048]{1,0:T(8,128)(2,1)} %bitcast.value), channel_id=1, source_target_pairs={{0,4},{4,8},{8,12},{12,16},{16,20},{20,24},{24,28},{1,5},{5,9},{9,... | collective-permute-start | bytes 3145736 | tf_op jit(solution)/shard_map/ppermute | solution.py:385
  25.0 73.0 %collective-permute-start.1 = (bf16[512,2048]{1,0:T(8,128)(2,1)}, bf16[512,2048]{1,0:T(8,128)(2,1)}, u32[]{:S(2)}, u32[]{:S(2)}) collective-permute-start(bf16[512,2048]{1,0:T(8,128)(2,1)} %pad_maximum_fusion.5), channel_id=1, source_target_pairs={{0,2},{1,3},{2,0},{3,1},{4,6},{5,7},{6,4},{7,5},{8,10},{9,11},{10,... | collective-permute-start | bytes 6291464 | tf_op jit(solution)/shard_map/ppermute | solution.py:123
  41.5 59.2 %collective-permute-start = (bf16[512,2048]{1,0:T(8,128)(2,1)}, bf16[512,2048]{1,0:T(8,128)(2,1)}, u32[]{:S(2)}, u32[]{:S(2)}) collective-permute-start(bf16[512,2048]{1,0:T(8,128)(2,1)} %pad_maximum_fusion.5), channel_id=1, source_target_pairs={{0,1},{1,0},{2,3},{3,2},{4,5},{5,4},{6,7},{7,6},{8,9},{9,8},{10,11... | collective-permute-start | bytes 6291464 | tf_op jit(solution)/shard_map/ppermute | solution.py:123
  52.3 22.1 %collective-permute-start.7 = (bf16[16,6,64]{2,1,0:T(8,128)(2,1)S(1)}, bf16[16,6,64]{2,1,0:T(8,128)(2,1)S(1)}, u32[]{:S(2)}, u32[]{:S(2)}) collective-permute-start(bf16[16,6,64]{2,1,0:T(8,128)(2,1)S(1)} %get-tuple-element.189), channel_id=1, source_target_pairs={{0,2},{1,3},{2,0},{3,1},{4,6},{5,7},{6,4},{7,5},{8,10},{9,11},{10,... | collective-permute-start | bytes 36872 | tf_op jit(solution)/shard_map/ppermute | solution.py:123
  58.8 38.7 %collective-permute-start.20 = (bf16[256,2048]{1,0:T(8,128)(2,1)}, bf16[256,2048]{1,0:T(8,128)(2,1)}, u32[]{:S(2)}, u32[]{:S(2)}) collective-permute-start(bf16[256,2048]{1,0:T(8,128)(2,1)} %shard_map.256), channel_id=1, source_target_pairs={{0,2},{1,3},{2,0},{3,1},{4,6},{5,7},{6,4},{7,5},{8,10},{9,11},{10,... | collective-permute-start | bytes 3145736 | tf_op jit(solution)/shard_map/ppermute | solution.py:123
  59.3 30.5 %collective-permute-start.13 = (bf16[256,2048]{0,1:T(8,128)(2,1)}, bf16[256,2048]{0,1:T(8,128)(2,1)}, u32[]{:S(2)}, u32[]{:S(2)}) collective-permute-start(bf16[256,2048]{0,1:T(8,128)(2,1)} %collective-permute-done.12), channel_id=1, source_target_pairs={{8,0},{16,8},{24,16},{28,24},{20,28},{12,20},{4,12},{0,4},{9,1},{1... | collective-permute-start | bytes 3145736 | tf_op jit(solution)/shard_map/ppermute | solution.py:55
  74.4 21.5 %collective-permute-start.9 = (bf16[256,2048]{0,1:T(8,128)(2,1)}, bf16[256,2048]{0,1:T(8,128)(2,1)}, u32[]{:S(2)}, u32[]{:S(2)}) collective-permute-start(bf16[256,2048]{0,1:T(8,128)(2,1)} %collective-permute-done.8), channel_id=1, source_target_pairs={{0,8},{8,16},{16,24},{24,28},{28,20},{20,12},{12,4},{4,0},{1,9},{9... | collective-permute-start | bytes 3145736 | tf_op jit(solution)/shard_map/ppermute | solution.py:55
  89.8 31.8 %collective-permute-start.19 = (bf16[256,2048]{1,0:T(8,128)(2,1)}, bf16[256,2048]{1,0:T(8,128)(2,1)S(1)}, u32[]{:S(2)}, u32[]{:S(2)}) collective-permute-start(bf16[256,2048]{1,0:T(8,128)(2,1)} %shard_map.256), channel_id=1, source_target_pairs={{0,1},{1,0},{2,3},{3,2},{4,5},{5,4},{6,7},{7,6},{8,9},{9,8},{10,11... | collective-permute-start | bytes 3145736 | tf_op jit(solution)/shard_map/ppermute | solution.py:123
  96.0 23.5 %collective-permute-start.14 = (bf16[256,2048]{0,1:T(8,128)(2,1)}, bf16[256,2048]{0,1:T(8,128)(2,1)S(1)}, u32[]{:S(2)}, u32[]{:S(2)}) collective-permute-start(bf16[256,2048]{0,1:T(8,128)(2,1)} %collective-permute-done.13), channel_id=1, source_target_pairs={{8,0},{16,8},{24,16},{28,24},{20,28},{12,20},{4,12},{0,4},{9,1},{1... | collective-permute-start | bytes 3145736 | tf_op jit(solution)/shard_map/ppermute | solution.py:55
  97.4 23.1 %collective-permute-start.10 = (bf16[256,2048]{0,1:T(8,128)(2,1)}, bf16[256,2048]{0,1:T(8,128)(2,1)S(1)}, u32[]{:S(2)}, u32[]{:S(2)}) collective-permute-start(bf16[256,2048]{0,1:T(8,128)(2,1)} %collective-permute-done.9), channel_id=1, source_target_pairs={{0,8},{8,16},{16,24},{24,28},{28,20},{20,12},{12,4},{4,0},{1,9},{9... | collective-permute-start | bytes 3145736 | tf_op jit(solution)/shard_map/ppermute | solution.py:55
  98.0 23.5 %collective-permute-start.21 = (bf16[256,2048]{1,0:T(8,128)(2,1)}, bf16[256,2048]{1,0:T(8,128)(2,1)S(1)}, u32[]{:S(2)}, u32[]{:S(2)}) collective-permute-start(bf16[256,2048]{1,0:T(8,128)(2,1)} %collective-permute-done.20), channel_id=1, source_target_pairs={{0,1},{1,0},{2,3},{3,2},{4,5},{5,4},{6,7},{7,6},{8,9},{9,8},{10,11... | collective-permute-start | bytes 3145736 | tf_op jit(solution)/shard_map/ppermute | solution.py:123
  100.7 27.5 %collective-permute-start.2 = (bf16[512,2048]{1,0:T(8,128)(2,1)}, bf16[512,2048]{1,0:T(8,128)(2,1)S(1)}, u32[]{:S(2)}, u32[]{:S(2)}) collective-permute-start(bf16[512,2048]{1,0:T(8,128)(2,1)} %collective-permute-done.1), channel_id=1, source_target_pairs={{0,1},{1,0},{2,3},{3,2},{4,5},{5,4},{6,7},{7,6},{8,9},{9,8},{10,11... | collective-permute-start | bytes 6291464 | tf_op jit(solution)/shard_map/ppermute | solution.py:123
  119.5 23.2 %collective-permute-start.15 = (bf16[256,2048]{1,0:T(8,128)(2,1)S(1)}, bf16[256,2048]{1,0:T(8,128)(2,1)S(1)}, u32[]{:S(2)}, u32[]{:S(2)}) collective-permute-start(bf16[256,2048]{1,0:T(8,128)(2,1)S(1)} %copy-done.30), channel_id=1, source_target_pairs={{8,0},{16,8},{24,16},{28,24},{20,28},{12,20},{4,12},{0,4},{9,1},{1... | collective-permute-start | bytes 3145736 | tf_op jit(solution)/shard_map/ppermute | solution.py:55
  120.5 35.8 %collective-permute-start.11 = (bf16[256,2048]{0,1:T(8,128)(2,1)S(1)}, bf16[256,2048]{0,1:T(8,128)(2,1)S(1)}, u32[]{:S(2)}, u32[]{:S(2)}) collective-permute-start(bf16[256,2048]{0,1:T(8,128)(2,1)S(1)} %collective-permute-done.10), channel_id=1, source_target_pairs={{0,8},{8,16},{16,24},{24,28},{28,20},{20,12},{12,4},{4,0},{1,9},{9... | collective-permute-start | bytes 3145736 | tf_op jit(solution)/shard_map/ppermute | solution.py:55
  142.7 32.7 %collective-permute-start.17 = (bf16[256,2048]{1,0:T(8,128)(2,1)S(1)}, bf16[256,2048]{1,0:T(8,128)(2,1)}, u32[]{:S(2)}, u32[]{:S(2)}) collective-permute-start(bf16[256,2048]{1,0:T(8,128)(2,1)S(1)} %collective-permute-done.15), channel_id=1, source_target_pairs={{8,0},{16,8},{24,16},{28,24},{20,28},{12,20},{4,12},{0,4},{9,1},{1... | collective-permute-start | bytes 3145736 | tf_op jit(solution)/shard_map/ppermute | solution.py:55
  175.4 22.9 %collective-permute-start.26 = (bf16[256,2048]{1,0:T(8,128)(2,1)}, bf16[256,2048]{1,0:T(8,128)(2,1)}, u32[]{:S(2)}, u32[]{:S(2)}) collective-permute-start(bf16[256,2048]{1,0:T(8,128)(2,1)} %collective-permute-done.17), channel_id=1, source_target_pairs={{8,0},{16,8},{24,16},{28,24},{20,28},{12,20},{4,12},{0,4},{9,1},{1... | collective-permute-start | bytes 3145736 | tf_op jit(solution)/shard_map/ppermute | solution.py:55
  177.0 22.9 %collective-permute-start.25 = (bf16[256,2048]{1,0:T(8,128)(2,1)}, bf16[256,2048]{1,0:T(8,128)(2,1)}, u32[]{:S(2)}, u32[]{:S(2)}) collective-permute-start(bf16[256,2048]{1,0:T(8,128)(2,1)} %collective-permute-done.16), channel_id=1, source_target_pairs={{0,8},{8,16},{16,24},{24,28},{28,20},{20,12},{12,4},{4,0},{1,9},{9... | collective-permute-start | bytes 3145736 | tf_op jit(solution)/shard_map/ppermute | solution.py:55
  197.8 28.2 %collective-permute-start.22 = (bf16[256,2048]{1,0:T(8,128)(2,1)}, bf16[256,2048]{1,0:T(8,128)(2,1)S(1)}, u32[]{:S(2)}, u32[]{:S(2)}) collective-permute-start(bf16[256,2048]{1,0:T(8,128)(2,1)} %slice.553), channel_id=1, source_target_pairs={{0,1},{1,0},{2,3},{3,2},{4,5},{5,4},{6,7},{7,6},{8,9},{9,8},{10,11... | collective-permute-start | bytes 3145736 | tf_op jit(solution)/shard_map/ppermute | solution.py:123
  198.3 25.4 %collective-permute-start.32 = (bf16[256,2048]{1,0:T(8,128)(2,1)}, bf16[256,2048]{1,0:T(8,128)(2,1)}, u32[]{:S(2)}, u32[]{:S(2)}) collective-permute-start(bf16[256,2048]{1,0:T(8,128)(2,1)} %collective-permute-done.26), channel_id=1, source_target_pairs={{8,0},{16,8},{24,16},{28,24},{20,28},{12,20},{4,12},{0,4},{9,1},{1... | collective-permute-start | bytes 3145736 | tf_op jit(solution)/shard_map/ppermute | solution.py:55
  200.0 25.4 %collective-permute-start.30 = (bf16[256,2048]{1,0:T(8,128)(2,1)}, bf16[256,2048]{1,0:T(8,128)(2,1)}, u32[]{:S(2)}, u32[]{:S(2)}) collective-permute-start(bf16[256,2048]{1,0:T(8,128)(2,1)} %collective-permute-done.25), channel_id=1, source_target_pairs={{0,8},{8,16},{16,24},{24,28},{28,20},{20,12},{12,4},{4,0},{1,9},{9... | collective-permute-start | bytes 3145736 | tf_op jit(solution)/shard_map/ppermute | solution.py:55
  201.9 24.8 %collective-permute-start.24 = (bf16[256,2048]{1,0:T(8,128)(2,1)}, bf16[256,2048]{1,0:T(8,128)(2,1)}, u32[]{:S(2)}, u32[]{:S(2)}) collective-permute-start(bf16[256,2048]{1,0:T(8,128)(2,1)} %add_convert_fusion.8), channel_id=1, source_target_pairs={{0,2},{1,3},{2,0},{3,1},{4,6},{5,7},{6,4},{7,5},{8,10},{9,11},{10,... | collective-permute-start | bytes 3145736 | tf_op jit(solution)/shard_map/ppermute | solution.py:123
  223.7 25.3 %collective-permute-start.33 = (bf16[2048,256]{1,0:T(8,128)(2,1)}, bf16[2048,256]{1,0:T(8,128)(2,1)S(1)}, u32[]{:S(2)}, u32[]{:S(2)}) collective-permute-start(bf16[2048,256]{1,0:T(8,128)(2,1)} %param.28), channel_id=1, source_target_pairs={{8,0},{16,8},{24,16},{28,24},{20,28},{12,20},{4,12},{0,4},{9,1},{1... | collective-permute-start | bytes 3145736 | tf_op jit(solution)/shard_map/ppermute | solution.py:55
  225.4 24.7 %collective-permute-start.31 = (bf16[2048,256]{1,0:T(8,128)(2,1)}, bf16[2048,256]{1,0:T(8,128)(2,1)S(1)}, u32[]{:S(2)}, u32[]{:S(2)}) collective-permute-start(bf16[2048,256]{1,0:T(8,128)(2,1)} %param.28), channel_id=1, source_target_pairs={{0,8},{8,16},{16,24},{24,28},{28,20},{20,12},{12,4},{4,0},{1,9},{9... | collective-permute-start | bytes 3145736 | tf_op jit(solution)/shard_map/ppermute | solution.py:55
  231.0 23.7 %collective-permute-start.28 = (bf16[256,2048]{1,0:T(8,128)(2,1)S(1)}, bf16[256,2048]{1,0:T(8,128)(2,1)S(1)}, u32[]{:S(2)}, u32[]{:S(2)}) collective-permute-start(bf16[256,2048]{1,0:T(8,128)(2,1)S(1)} %add_convert_fusion.7), channel_id=1, source_target_pairs={{0,2},{1,3},{2,0},{3,1},{4,6},{5,7},{6,4},{7,5},{8,10},{9,11},{10,... | collective-permute-start | bytes 3145736 | tf_op jit(solution)/shard_map/ppermute | solution.py:123
  238.9 36.1 %collective-permute-start.27 = (bf16[256,2048]{1,0:T(8,128)(2,1)S(1)}, bf16[256,2048]{1,0:T(8,128)(2,1)S(1)}, u32[]{:S(2)}, u32[]{:S(2)}) collective-permute-start(bf16[256,2048]{1,0:T(8,128)(2,1)S(1)} %add_convert_fusion.7), channel_id=1, source_target_pairs={{0,1},{1,0},{2,3},{3,2},{4,5},{5,4},{6,7},{7,6},{8,9},{9,8},{10,11... | collective-permute-start | bytes 3145736 | tf_op jit(solution)/shard_map/ppermute | solution.py:123
  249.0 23.9 %collective-permute-start.39 = (bf16[2048,256]{1,0:T(8,128)(2,1)S(1)}, bf16[2048,256]{1,0:T(8,128)(2,1)S(1)}, u32[]{:S(2)}, u32[]{:S(2)}) collective-permute-start(bf16[2048,256]{1,0:T(8,128)(2,1)S(1)} %collective-permute-done.33), channel_id=1, source_target_pairs={{8,0},{16,8},{24,16},{28,24},{20,28},{12,20},{4,12},{0,4},{9,1},{1... | collective-permute-start | bytes 3145736 | tf_op jit(solution)/shard_map/ppermute | solution.py:55
  250.0 23.9 %collective-permute-start.34 = (bf16[2048,256]{1,0:T(8,128)(2,1)S(1)}, bf16[2048,256]{1,0:T(8,128)(2,1)S(1)}, u32[]{:S(2)}, u32[]{:S(2)}) collective-permute-start(bf16[2048,256]{1,0:T(8,128)(2,1)S(1)} %collective-permute-done.31), channel_id=1, source_target_pairs={{0,8},{8,16},{16,24},{24,28},{28,20},{20,12},{12,4},{4,0},{1,9},{9... | collective-permute-start | bytes 3145736 | tf_op jit(solution)/shard_map/ppermute | solution.py:55
  273.0 25.4 %collective-permute-start.40 = (bf16[2048,256]{1,0:T(8,128)(2,1)S(1)}, bf16[2048,256]{1,0:T(8,128)(2,1)S(1)}, u32[]{:S(2)}, u32[]{:S(2)}) collective-permute-start(bf16[2048,256]{1,0:T(8,128)(2,1)S(1)} %collective-permute-done.39), channel_id=1, source_target_pairs={{8,0},{16,8},{24,16},{28,24},{20,28},{12,20},{4,12},{0,4},{9,1},{1... | collective-permute-start | bytes 3145736 | tf_op jit(solution)/shard_map/ppermute | solution.py:55
  273.9 23.3 %collective-permute-start.35 = (bf16[2048,256]{1,0:T(8,128)(2,1)S(1)}, bf16[2048,256]{1,0:T(8,128)(2,1)S(1)}, u32[]{:S(2)}, u32[]{:S(2)}) collective-permute-start(bf16[2048,256]{1,0:T(8,128)(2,1)S(1)} %collective-permute-done.34), channel_id=1, source_target_pairs={{0,8},{8,16},{16,24},{24,28},{28,20},{20,12},{12,4},{4,0},{1,9},{9... | collective-permute-start | bytes 3145736 | tf_op jit(solution)/shard_map/ppermute | solution.py:55
  297.2 23.3 %collective-permute-start.36 = (bf16[2048,256]{1,0:T(8,128)(2,1)S(1)}, bf16[2048,256]{1,0:T(8,128)(2,1)S(1)}, u32[]{:S(2)}, u32[]{:S(2)}) collective-permute-start(bf16[2048,256]{1,0:T(8,128)(2,1)S(1)} %collective-permute-done.35), channel_id=1, source_target_pairs={{0,8},{8,16},{16,24},{24,28},{28,20},{20,12},{12,4},{4,0},{1,9},{9... | collective-permute-start | bytes 3145736 | tf_op jit(solution)/shard_map/ppermute | solution.py:55
  298.3 23.3 %collective-permute-start.41 = (bf16[2048,256]{1,0:T(8,128)(2,1)S(1)}, bf16[2048,256]{1,0:T(8,128)(2,1)S(1)}, u32[]{:S(2)}, u32[]{:S(2)}) collective-permute-start(bf16[2048,256]{1,0:T(8,128)(2,1)S(1)} %convolution_convert_fusion.8), channel_id=1, source_target_pairs={{8,0},{16,8},{24,16},{28,24},{20,28},{12,20},{4,12},{0,4},{9,1},{1... | collective-permute-start | bytes 3145736 | tf_op jit(solution)/shard_map/ppermute | solution.py:55
  320.6 27.7 %collective-permute-start.37 = (bf16[2048,256]{1,0:T(8,128)(2,1)S(1)}, bf16[2048,256]{1,0:T(8,128)(2,1)S(1)}, u32[]{:S(2)}, u32[]{:S(2)}) collective-permute-start(bf16[2048,256]{1,0:T(8,128)(2,1)S(1)} %convolution_convert_fusion.9), channel_id=1, source_target_pairs={{0,8},{8,16},{16,24},{24,28},{28,20},{20,12},{12,4},{4,0},{1,9},{9... | collective-permute-start | bytes 3145736 | tf_op jit(solution)/shard_map/ppermute | solution.py:55
  324.0 29.7 %collective-permute-start.42 = (bf16[2048,256]{1,0:T(8,128)(2,1)}, bf16[2048,256]{1,0:T(8,128)(2,1)}, u32[]{:S(2)}, u32[]{:S(2)}) collective-permute-start(bf16[2048,256]{1,0:T(8,128)(2,1)} %fusion.49), channel_id=1, source_target_pairs={{8,0},{16,8},{24,16},{28,24},{20,28},{12,20},{4,12},{0,4},{9,1},{1... | collective-permute-start | bytes 3145736 | tf_op jit(solution)/shard_map/ppermute | solution.py:55
  352.5 24.3 %collective-permute-start.38 = (bf16[2048,256]{1,0:T(8,128)(2,1)}, bf16[2048,256]{1,0:T(8,128)(2,1)}, u32[]{:S(2)}, u32[]{:S(2)}) collective-permute-start(bf16[2048,256]{1,0:T(8,128)(2,1)} %fusion.47), channel_id=1, source_target_pairs={{0,8},{8,16},{16,24},{24,28},{28,20},{20,12},{12,4},{4,0},{1,9},{9... | collective-permute-start | bytes 3145736 | tf_op jit(solution)/shard_map/ppermute | solution.py:55
  357.4 24.7 %collective-permute-start.43 = (bf16[2048,256]{1,0:T(8,128)(2,1)}, bf16[2048,256]{1,0:T(8,128)(2,1)}, u32[]{:S(2)}, u32[]{:S(2)}) collective-permute-start(bf16[2048,256]{1,0:T(8,128)(2,1)} %fusion.48), channel_id=1, source_target_pairs={{8,0},{16,8},{24,16},{28,24},{20,28},{12,20},{4,12},{0,4},{9,1},{1... | collective-permute-start | bytes 3145736 | tf_op jit(solution)/shard_map/ppermute | solution.py:55
  376.2 34.6 %collective-permute-start.47 = (bf16[256,2048]{1,0:T(8,128)(2,1)S(1)}, bf16[256,2048]{1,0:T(8,128)(2,1)S(1)}, u32[]{:S(2)}, u32[]{:S(2)}) collective-permute-start(bf16[256,2048]{1,0:T(8,128)(2,1)S(1)} %slice.575), channel_id=1, source_target_pairs={{0,1},{1,0},{2,3},{3,2},{4,5},{5,4},{6,7},{7,6},{8,9},{9,8},{10,11... | collective-permute-start | bytes 3145736 | tf_op jit(solution)/shard_map/ppermute | solution.py:123
  380.9 25.5 %collective-permute-start.53 = (bf16[2048,256]{1,0:T(8,128)(2,1)S(1)}, bf16[2048,256]{1,0:T(8,128)(2,1)S(1)}, u32[]{:S(2)}, u32[]{:S(2)}) collective-permute-start(bf16[2048,256]{1,0:T(8,128)(2,1)S(1)} %fusion.50), channel_id=1, source_target_pairs={{0,8},{8,16},{16,24},{24,28},{28,20},{20,12},{12,4},{4,0},{1,9},{9... | collective-permute-start | bytes 3145736 | tf_op jit(solution)/shard_map/ppermute | solution.py:55
  384.7 25.1 %collective-permute-start.55 = (bf16[2048,256]{1,0:T(8,128)(2,1)S(1)}, bf16[2048,256]{1,0:T(8,128)(2,1)S(1)}, u32[]{:S(2)}, u32[]{:S(2)}) collective-permute-start(bf16[2048,256]{1,0:T(8,128)(2,1)S(1)} %fusion.51), channel_id=1, source_target_pairs={{8,0},{16,8},{24,16},{28,24},{20,28},{12,20},{4,12},{0,4},{9,1},{1... | collective-permute-start | bytes 3145736 | tf_op jit(solution)/shard_map/ppermute | solution.py:55
  386.5 26.2 %collective-permute-start.49 = (bf16[256,2048]{1,0:T(8,128)(2,1)S(1)}, bf16[256,2048]{1,0:T(8,128)(2,1)S(1)}, u32[]{:S(2)}, u32[]{:S(2)}) collective-permute-start(bf16[256,2048]{1,0:T(8,128)(2,1)S(1)} %add_convert_fusion.4), channel_id=1, source_target_pairs={{0,2},{1,3},{2,0},{3,1},{4,6},{5,7},{6,4},{7,5},{8,10},{9,11},{10,... | collective-permute-start | bytes 3145736 | tf_op jit(solution)/shard_map/ppermute | solution.py:123
  406.4 27.0 %collective-permute-start.46 = (bf16[256,2048]{1,0:T(8,128)(2,1)S(1)}, bf16[256,2048]{1,0:T(8,128)(2,1)S(1)}, u32[]{:S(2)}, u32[]{:S(2)}) collective-permute-start(bf16[256,2048]{1,0:T(8,128)(2,1)S(1)} %add_convert_fusion.6), channel_id=1, source_target_pairs={{0,2},{1,3},{2,0},{3,1},{4,6},{5,7},{6,4},{7,5},{8,10},{9,11},{10,... | collective-permute-start | bytes 3145736 | tf_op jit(solution)/shard_map/ppermute | solution.py:123
  409.9 28.4 %collective-permute-start.56 = (bf16[256,2048]{1,0:T(8,128)(2,1)S(1)}, bf16[256,2048]{1,0:T(8,128)(2,1)S(1)}, u32[]{:S(2)}, u32[]{:S(2)}) collective-permute-start(bf16[256,2048]{1,0:T(8,128)(2,1)S(1)} %copy-done.74), channel_id=1, source_target_pairs={{8,0},{16,8},{24,16},{28,24},{20,28},{12,20},{4,12},{0,4},{9,1},{1... | collective-permute-start | bytes 3145736 | tf_op jit(solution)/shard_map/ppermute | solution.py:55
  410.8 31.6 %collective-permute-start.54 = (bf16[256,2048]{1,0:T(8,128)(2,1)S(1)}, bf16[256,2048]{1,0:T(8,128)(2,1)S(1)}, u32[]{:S(2)}, u32[]{:S(2)}) collective-permute-start(bf16[256,2048]{1,0:T(8,128)(2,1)S(1)} %convolution_convert_fusion.7), channel_id=1, source_target_pairs={{0,8},{8,16},{16,24},{24,28},{28,20},{20,12},{12,4},{4,0},{1,9},{9... | collective-permute-start | bytes 3145736 | tf_op jit(solution)/shard_map/ppermute | solution.py:55
  436.7 23.6 %collective-permute-start.51 = (bf16[256,2048]{1,0:T(8,128)(2,1)S(1)}, bf16[256,2048]{1,0:T(8,128)(2,1)}, u32[]{:S(2)}, u32[]{:S(2)}) collective-permute-start(bf16[256,2048]{1,0:T(8,128)(2,1)S(1)} %get-tuple-element.169), channel_id=1, source_target_pairs={{0,2},{1,3},{2,0},{3,1},{4,6},{5,7},{6,4},{7,5},{8,10},{9,11},{10,... | collective-permute-start | bytes 3145736 | tf_op jit(solution)/shard_map/ppermute | solution.py:123
  440.5 28.6 %collective-permute-start.59 = (bf16[256,2048]{1,0:T(8,128)(2,1)}, bf16[256,2048]{1,0:T(8,128)(2,1)S(1)}, u32[]{:S(2)}, u32[]{:S(2)}) collective-permute-start(bf16[256,2048]{1,0:T(8,128)(2,1)} %fusion.55), channel_id=1, source_target_pairs={{8,0},{16,8},{24,16},{28,24},{20,28},{12,20},{4,12},{0,4},{9,1},{1... | collective-permute-start | bytes 3145736 | tf_op jit(solution)/shard_map/ppermute | solution.py:55
  444.7 30.9 %collective-permute-start.57 = (bf16[256,2048]{1,0:T(8,128)(2,1)}, bf16[256,2048]{1,0:T(8,128)(2,1)}, u32[]{:S(2)}, u32[]{:S(2)}) collective-permute-start(bf16[256,2048]{1,0:T(8,128)(2,1)} %fusion.53), channel_id=1, source_target_pairs={{0,8},{8,16},{16,24},{24,28},{28,20},{20,12},{12,4},{4,0},{1,9},{9... | collective-permute-start | bytes 3145736 | tf_op jit(solution)/shard_map/ppermute | solution.py:55
  445.1 34.6 %collective-permute-start.50 = (bf16[256,2048]{1,0:T(8,128)(2,1)S(1)}, bf16[256,2048]{1,0:T(8,128)(2,1)}, u32[]{:S(2)}, u32[]{:S(2)}) collective-permute-start(bf16[256,2048]{1,0:T(8,128)(2,1)S(1)} %get-tuple-element.169), channel_id=1, source_target_pairs={{0,1},{1,0},{2,3},{3,2},{4,5},{5,4},{6,7},{7,6},{8,9},{9,8},{10,11... | collective-permute-start | bytes 3145736 | tf_op jit(solution)/shard_map/ppermute | solution.py:123
  473.9 62.1 %collective-permute-start.60 = (bf16[256,2048]{1,0:T(8,128)(2,1)}, bf16[256,2048]{1,0:T(8,128)(2,1)S(1)}, u32[]{:S(2)}, u32[]{:S(2)}) collective-permute-start(bf16[256,2048]{1,0:T(8,128)(2,1)} %fusion.54), channel_id=1, source_target_pairs={{8,0},{16,8},{24,16},{28,24},{20,28},{12,20},{4,12},{0,4},{9,1},{1... | collective-permute-start | bytes 3145736 | tf_op jit(solution)/shard_map/ppermute | solution.py:55
  479.3 40.7 %collective-permute-start.58 = (bf16[256,2048]{1,0:T(8,128)(2,1)}, bf16[256,2048]{1,0:T(8,128)(2,1)}, u32[]{:S(2)}, u32[]{:S(2)}) collective-permute-start(bf16[256,2048]{1,0:T(8,128)(2,1)} %fusion.52), channel_id=1, source_target_pairs={{0,8},{8,16},{16,24},{24,28},{28,20},{20,12},{12,4},{4,0},{1,9},{9... | collective-permute-start | bytes 3145736 | tf_op jit(solution)/shard_map/ppermute | solution.py:55
  524.3 44.2 %collective-permute-start.73 = (bf16[256,2048]{1,0:T(8,128)(2,1)}, bf16[256,2048]{1,0:T(8,128)(2,1)S(1)}, u32[]{:S(2)}, u32[]{:S(2)}) collective-permute-start(bf16[256,2048]{1,0:T(8,128)(2,1)} %fusion.56), channel_id=1, source_target_pairs={{0,8},{8,16},{16,24},{24,28},{28,20},{20,12},{12,4},{4,0},{1,9},{9... | collective-permute-start | bytes 3145736 | tf_op jit(solution)/shard_map/ppermute | solution.py:55
  546.7 24.9 %collective-permute-start.77 = (bf16[256,2048]{1,0:T(8,128)(2,1)S(1)}, bf16[256,2048]{1,0:T(8,128)(2,1)S(1)}, u32[]{:S(2)}, u32[]{:S(2)}) collective-permute-start(bf16[256,2048]{1,0:T(8,128)(2,1)S(1)} %pad_maximum_fusion.8), channel_id=1, source_target_pairs={{8,0},{16,8},{24,16},{28,24},{20,28},{12,20},{4,12},{0,4},{9,1},{1... | collective-permute-start | bytes 3145736 | tf_op jit(solution)/shard_map/ppermute | solution.py:55
  548.2 28.2 %collective-permute-start.64 = (bf16[256,2048]{1,0:T(8,128)(2,1)S(1)}, bf16[256,2048]{1,0:T(8,128)(2,1)S(1)}, u32[]{:S(2)}, u32[]{:S(2)}) collective-permute-start(bf16[256,2048]{1,0:T(8,128)(2,1)S(1)} %slice.591), channel_id=1, source_target_pairs={{0,1},{1,0},{2,3},{3,2},{4,5},{5,4},{6,7},{7,6},{8,9},{9,8},{10,11... | collective-permute-start | bytes 3145736 | tf_op jit(solution)/shard_map/ppermute | solution.py:123
  565.6 26.0 %collective-permute-start.66 = (bf16[256,2048]{1,0:T(8,128)(2,1)S(1)}, bf16[256,2048]{1,0:T(8,128)(2,1)S(1)}, u32[]{:S(2)}, u32[]{:S(2)}) collective-permute-start(bf16[256,2048]{1,0:T(8,128)(2,1)S(1)} %add_convert_fusion.2), channel_id=1, source_target_pairs={{0,2},{1,3},{2,0},{3,1},{4,6},{5,7},{6,4},{7,5},{8,10},{9,11},{10,... | collective-permute-start | bytes 3145736 | tf_op jit(solution)/shard_map/ppermute | solution.py:123
  568.5 62.3 %collective-permute-start.61 = (bf16[256,2048]{1,0:T(8,128)(2,1)}, bf16[256,2048]{1,0:T(8,128)(2,1)S(1)}, u32[]{:S(2)}, u32[]{:S(2)}) collective-permute-start(bf16[256,2048]{1,0:T(8,128)(2,1)} %slice.587), channel_id=1, source_target_pairs={{0,1},{1,0},{2,3},{3,2},{4,5},{5,4},{6,7},{7,6},{8,9},{9,8},{10,11... | collective-permute-start | bytes 3145736 | tf_op jit(solution)/shard_map/ppermute | solution.py:123
  571.6 33.8 %collective-permute-start.74 = (bf16[256,2048]{1,0:T(8,128)(2,1)}, bf16[256,2048]{1,0:T(8,128)(2,1)}, u32[]{:S(2)}, u32[]{:S(2)}) collective-permute-start(bf16[256,2048]{1,0:T(8,128)(2,1)} %pad_maximum_fusion.7), channel_id=1, source_target_pairs={{0,8},{8,16},{16,24},{24,28},{28,20},{20,12},{12,4},{4,0},{1,9},{9... | collective-permute-start | bytes 3145736 | tf_op jit(solution)/shard_map/ppermute | solution.py:55
  574.3 37.6 %collective-permute-start.78 = (bf16[256,2048]{1,0:T(8,128)(2,1)}, bf16[256,2048]{1,0:T(8,128)(2,1)}, u32[]{:S(2)}, u32[]{:S(2)}) collective-permute-start(bf16[256,2048]{1,0:T(8,128)(2,1)} %fusion.80), channel_id=1, source_target_pairs={{8,0},{16,8},{24,16},{28,24},{20,28},{12,20},{4,12},{0,4},{9,1},{1... | collective-permute-start | bytes 3145736 | tf_op jit(solution)/shard_map/ppermute | solution.py:55
  576.4 54.4 %collective-permute-start.63 = (bf16[256,2048]{1,0:T(8,128)(2,1)}, bf16[256,2048]{1,0:T(8,128)(2,1)}, u32[]{:S(2)}, u32[]{:S(2)}) collective-permute-start(bf16[256,2048]{1,0:T(8,128)(2,1)} %add_convert_fusion.3), channel_id=1, source_target_pairs={{0,2},{1,3},{2,0},{3,1},{4,6},{5,7},{6,4},{7,5},{8,10},{9,11},{10,... | collective-permute-start | bytes 3145736 | tf_op jit(solution)/shard_map/ppermute | solution.py:123
  598.3 28.4 %collective-permute-start.67 = (bf16[256,2048]{1,0:T(8,128)(2,1)}, bf16[256,2048]{1,0:T(8,128)(2,1)}, u32[]{:S(2)}, u32[]{:S(2)}) collective-permute-start(bf16[256,2048]{1,0:T(8,128)(2,1)} %shard_map.260), channel_id=1, source_target_pairs={{4,0},{8,4},{12,8},{16,12},{20,16},{24,20},{28,24},{5,1},{9,5},{13... | collective-permute-start | bytes 3145736 | tf_op jit(solution)/shard_map/ppermute | solution.py:462
  608.1 39.5 %collective-permute-start.75 = (bf16[256,2048]{1,0:T(8,128)(2,1)}, bf16[256,2048]{1,0:T(8,128)(2,1)}, u32[]{:S(2)}, u32[]{:S(2)}) collective-permute-start(bf16[256,2048]{1,0:T(8,128)(2,1)} %fusion.77), channel_id=1, source_target_pairs={{0,8},{8,16},{16,24},{24,28},{28,20},{20,12},{12,4},{4,0},{1,9},{9... | collective-permute-start | bytes 3145736 | tf_op jit(solution)/shard_map/ppermute | solution.py:55
  614.5 36.3 %collective-permute-start.79 = (bf16[256,2048]{1,0:T(8,128)(2,1)}, bf16[256,2048]{1,0:T(8,128)(2,1)}, u32[]{:S(2)}, u32[]{:S(2)}) collective-permute-start(bf16[256,2048]{1,0:T(8,128)(2,1)} %fusion.79), channel_id=1, source_target_pairs={{8,0},{16,8},{24,16},{28,24},{20,28},{12,20},{4,12},{0,4},{9,1},{1... | collective-permute-start | bytes 3145736 | tf_op jit(solution)/shard_map/ppermute | solution.py:55
  650.7 43.9 %collective-permute-start.76 = (bf16[256,2048]{1,0:T(8,128)(2,1)}, bf16[256,2048]{1,0:T(8,128)(2,1)}, u32[]{:S(2)}, u32[]{:S(2)}) collective-permute-start(bf16[256,2048]{1,0:T(8,128)(2,1)} %fusion.76), channel_id=1, source_target_pairs={{0,8},{8,16},{16,24},{24,28},{28,20},{20,12},{12,4},{4,0},{1,9},{9... | collective-permute-start | bytes 3145736 | tf_op jit(solution)/shard_map/ppermute | solution.py:55
  653.9 40.6 %collective-permute-start.80 = (bf16[256,2048]{1,0:T(8,128)(2,1)}, bf16[256,2048]{1,0:T(8,128)(2,1)}, u32[]{:S(2)}, u32[]{:S(2)}) collective-permute-start(bf16[256,2048]{1,0:T(8,128)(2,1)} %fusion.78), channel_id=1, source_target_pairs={{8,0},{16,8},{24,16},{28,24},{20,28},{12,20},{4,12},{0,4},{9,1},{1... | collective-permute-start | bytes 3145736 | tf_op jit(solution)/shard_map/ppermute | solution.py:55
  (96 other events, 1461.8 us)

commit v3 on v2

v3 whole, which is shorter than its diff:
```python
import jax
import jax.numpy as jnp
from jax import lax
from jax.experimental import pallas as pl
from jax.experimental.pallas import tpu as pltpu
from jax.sharding import PartitionSpec as P

HEAD_DIM = 128
TILE = 512
WINDOW = 256
F32 = jnp.float32
BF16 = jnp.bfloat16


def ring_order(count):
    return list(range(0, count, 2)) + list(range(count - 1, 0, -2))


def ring_place(index, count):
    return jnp.where(index % 2 == 0, index // 2, count - 1 - index // 2)


def ring_index(place, count):
    return jnp.where(place < count // 2, 2 * place, 2 * (count - 1 - place) + 1)


def slot_owners(ahead=0):
    count = lax.axis_size("seq")
    place = ring_place((lax.axis_index("seq") + ahead) % count, count)
    return ring_index((place + jnp.arange(count, dtype=jnp.int32)) % count, count)


def owner_slots():
    count = lax.axis_size("seq")
    place = ring_place(lax.axis_index("seq"), count)
    return (ring_place(jnp.arange(count, dtype=jnp.int32), count) - place) % count


def tie(value, *after):
    after = [v for v in after if v is not None]
    return lax.optimization_barrier((value, *after))[0] if after else value


class Ring:
    def __init__(self, after):
        self.count = lax.axis_size("seq")
        self.queue = {True: [], False: []}
        self.last = {True: after, False: after}
        self.before, self.wanted = [], []

    def hop(self, value, forward):
        order = ring_order(self.count)
        ahead = order[1:] + order[:1]
        pairs = zip(order, ahead) if forward else zip(ahead, order)
        value = tie(value, *self.wanted)
        self.before.append(value)
        self.last[forward] = lax.ppermute(value, "seq", list(pairs))
        return self.last[forward]

    def advance(self, times=1):
        for _ in range(times):
            self.before = []
            self.wanted += self.last.values()
            steps = [(way, *queue.pop(0)) for way, queue in self.queue.items() if queue]
            while steps:
                same = [s for s in steps if s[1] is steps[0][1]]
                moved = same[0][1]
                ways = [(w, j) for w, _, j in same]
                for (way, _, j), value in zip(same, moved.blocks(ways, self.wanted)):
                    moved.landed[way, j] = self.hop(value, way)
                steps = [s for s in steps if s not in same]
            self.wanted = []

    def now(self, *values):
        values = tie(values if len(values) > 1 else values[0], *self.before)
        return values

    def due(self, *values):
        self.wanted += values

    def add(self, moved, more_ahead):
        ahead = self.count // 2 if more_ahead else self.count - 1 - self.count // 2
        for forward, steps in ((True, ahead), (False, self.count - 1 - ahead)):
            self.queue[forward] += [(moved, j) for j in moved.slots(forward, steps)]
        return moved


class Gather:
    def __init__(self, value, axis):
        self.value, self.axis = value, axis
        self.landed, self.count = {}, lax.axis_size("seq")
        self.base = None

    def slots(self, forward, steps):
        return [self.count - 1 - t if forward else 1 + t for t in range(steps)]

    def blocks(self, steps, after):
        return [self.landed.get((w, j + (1 if w else -1)), self.value) for w, j in steps]

    def pieces(self):
        landed = self.landed
        return [self.value] + [
            landed.get((False, j), landed.get((True, j))) for j in range(1, self.count)
        ]

    def early(self, ring):
        pieces = self.pieces()
        pieces[self.count // 2] = self.value
        self.base = jnp.concatenate(pieces, axis=self.axis)
        ring.due(self.base)

    def all(self):
        if self.base is None:
            return jnp.concatenate(self.pieces(), axis=self.axis)
        j = self.count // 2
        last = self.landed[True, j]
        return lax.dynamic_update_slice_in_dim(
            self.base, last, j * last.shape[self.axis], self.axis
        )


class Scatter:
    def __init__(self, find):
        self.find, self.landed, self.count = find, {}, lax.axis_size("seq")

    def slots(self, forward, steps):
        return [steps - t if forward else self.count - steps + t for t in range(steps)]

    def blocks(self, steps, after):
        received = [self.landed.get((w, j + (1 if w else -1))) for w, j in steps]
        received = [v if v is None else tie(v, *after) for v in received]
        return join([self.find(j) for _, j in steps], received)

    def total(self, ring):
        value, at, rows = self.find(0)
        own = ring.now(value)[at * rows : (at + 1) * rows].astype(F32)
        return own + self.landed[True, 1].astype(F32) + (
            self.landed[False, self.count - 1].astype(F32)
        )


QUICK = pl.CostEstimate(flops=10**8, bytes_accessed=0, transcendentals=0)


def join(found, received):
    ways, width = len(found), found[0][0].shape[1]
    rows = found[0][2]
    steps = 2 if rows % 32 == 0 else 1
    step, got = rows // steps, [v for v in received if v is not None]

    def kernel(*refs):
        got_refs = list(refs[ways : ways + len(got)])
        for way in range(ways):
            value = refs[way][...]
            if received[way] is not None:
                value = (value.astype(F32) + got_refs.pop(0)[...].astype(F32)).astype(BF16)
            refs[len(refs) - ways + way][...] = value

    block = pl.BlockSpec((step, width), lambda i: (i, 0))
    return pl.pallas_call(
        kernel,
        grid=(steps,),
        in_specs=[
            pl.BlockSpec((step, width), lambda i, j=j: (j * steps + i, 0)) for _, j, _ in found
        ]
        + [block] * len(got),
        out_specs=[block] * ways,
        out_shape=[jax.ShapeDtypeStruct((rows, width), BF16)] * ways,
        cost_estimate=QUICK,
    )(*(v for v, _, _ in found), *got)


def matmul(lefts, right, finish, outs, nt=False, first=0, tiles=None, extra=(), keep=False):
    depth = lefts[0].shape[1]
    columns = right.shape[0 if nt else 1]
    tiles = tiles or columns // TILE
    blocks = sum(v.shape[0] for v in lefts) // WINDOW
    rows = blocks * WINDOW
    specs, shapes = [], []
    for kind in outs:
        high = {"rows": rows, "parts": WINDOW, "sums": 1}[kind]
        for _ in range(blocks if kind == "parts" else 1):
            specs.append(pl.BlockSpec((high, TILE), lambda t: (0, t)))
            kept = F32 if kind == "sums" else BF16
            shapes.append(jax.ShapeDtypeStruct((high, tiles * TILE), kept))
    if keep:
        specs.append(pl.BlockSpec((rows, depth), lambda t: (0, 0)))
        shapes.append(jax.ShapeDtypeStruct((rows, depth), BF16))

    def kernel(*refs):
        left_refs, right_ref = refs[: len(lefts)], refs[len(lefts)]
        extra_refs = refs[len(lefts) + 1 : -len(specs)]
        out_refs = refs[-len(specs) :]
        weights = right_ref[:, first : first + depth] if nt else right_ref[...]
        at = 0
        for ref in left_refs:
            for row in range(0, ref.shape[0], WINDOW):
                value = dot_t(ref[row : row + WINDOW, :], weights, 1, 1 if nt else 0)
                finish(value, at, extra_refs, out_refs)
                at += WINDOW
        if keep:

            @pl.when(pl.program_id(0) == 0)
            def _():
                at = 0
                for ref in left_refs:
                    out_refs[-1][at : at + ref.shape[0], :] = ref[...]
                    at += ref.shape[0]

    if nt:
        right_spec = pl.BlockSpec((TILE, right.shape[1]), lambda t: (t, 0))
    else:
        right_spec = pl.BlockSpec((depth, TILE), lambda t: (0, t + first))
    return pl.pallas_call(
        kernel,
        grid=(tiles,),
        in_specs=[pl.BlockSpec(v.shape, lambda t: (0, 0)) for v in lefts]
        + [right_spec]
        + [pl.BlockSpec((v.shape[0], TILE), lambda t: (0, t)) for v in extra],
        out_specs=specs,
        out_shape=shapes,
        cost_estimate=QUICK,
    )(*lefts, right, *extra)


def finish_parts(value, at, extra, outs):
    outs[at // WINDOW][...] = value.astype(BF16)


def finish_rows(value, at, extra, outs):
    outs[0][at : at + WINDOW, :] = value.astype(BF16)


def finish_bias(value, at, extra, outs):
    outs[0][at : at + WINDOW, :] = (value + extra[0][...]).astype(BF16)


def finish_gelu(value, at, extra, outs):
    active, slope = gelu_and_slope(value + extra[0][...])
    outs[0][at : at + WINDOW, :] = active.astype(BF16)
    outs[1][at : at + WINDOW, :] = slope.astype(BF16)


def finish_slope(value, at, extra, outs):
    value = (value * extra[0][at : at + WINDOW, :].astype(F32)).astype(BF16)
    outs[0][at : at + WINDOW, :] = value
    total = jnp.sum(value.astype(F32), axis=0, keepdims=True)
    outs[1][...] = total if at == 0 else outs[1][...] + total


def token_products(pairs, plan, first=0, width=None):
    width = width or pairs[0][0].shape[1]

    def kernel(*refs):
        for t, parts in enumerate(plan):

            def run(parts=parts):
                value = None
                for k in parts:
                    term = dot_t(refs[2 * k][...], refs[2 * k + 1][...], 0, 0)
                    value = term if value is None else value + term
                refs[-1][...] = value.astype(BF16)

            if all(p == plan[0] for p in plan):
                if t == 0:
                    run()
            else:
                pl.when(pl.program_id(0) == t)(run)

    specs, arrays = [], []
    for left, right, tile, start, tiles in pairs:
        specs.append(pl.BlockSpec((left.shape[0], width), lambda t: (0, first)))
        specs.append(
            pl.BlockSpec(
                (right.shape[0], TILE),
                lambda t, tile=tile, start=start, tiles=tiles: (
                    0,
                    tile + jnp.clip(t - start, 0, tiles - 1),
                ),
            )
        )
        arrays += [left, right]
    return pl.pallas_call(
        kernel,
        grid=(len(plan),),
        in_specs=specs,
        out_specs=pl.BlockSpec((width, TILE), lambda t: (0, t)),
        out_shape=jax.ShapeDtypeStruct((width, len(plan) * TILE), BF16),
        cost_estimate=QUICK,
    )(*arrays)


def norm_parts(parts, gain, shift):
    rows, width = parts[0].shape
    step = 64

    def kernel(*refs):
        for i in range(len(parts)):
            unit, _ = norm_stats(refs[i][...].astype(F32))
            refs[-1][i] = (unit * refs[-3][...] + refs[-2][...]).astype(BF16)

    vector = pl.BlockSpec((1, width), lambda i: (0, 0))
    return pl.pallas_call(
        kernel,
        grid=(rows // step,),
        in_specs=[pl.BlockSpec((step, width), lambda i: (i, 0))] * len(parts) + [vector] * 2,
        out_specs=pl.BlockSpec((len(parts), step, width), lambda i: (0, i, 0)),
        out_shape=jax.ShapeDtypeStruct((len(parts), rows, width), BF16),
        cost_estimate=QUICK,
    )(*parts, gain[None], shift[None]).reshape(len(parts) * rows, width)


def swap(value, axis, bit):
    return lax.ppermute(value, axis, [(i, i ^ bit) for i in range(lax.axis_size(axis))])


def bits_of(count):
    return [1 << k for k in range(count.bit_length() - 1)]


def doubled(parts, axis):
    for bit in bits_of(lax.axis_size(axis)):
        parts = jnp.concatenate([parts, swap(parts, axis, bit)], axis=0)
    return parts


def in_slot_order(parts):
    count, groups = lax.axis_size("seq"), lax.axis_size("batch")
    own_s, own_b = lax.axis_index("seq"), lax.axis_index("batch")
    order = (slot_owners() ^ own_s)[:, None] + count * (
        jnp.arange(groups, dtype=jnp.int32) ^ own_b
    )
    parts = jnp.take(parts, order.reshape(-1), axis=0)
    return jnp.moveaxis(parts, 0, -2).reshape(*parts.shape[1:-1], -1)


def small_totals(value, flat, after):
    count, groups = lax.axis_size("seq"), lax.axis_size("batch")
    own_s, own_b = lax.axis_index("seq"), lax.axis_index("batch")
    parts = jnp.moveaxis(value.reshape(*value.shape[:-1], count * groups, -1), -2, 0)
    order = owner_slots()[jnp.arange(count, dtype=jnp.int32) ^ own_s] * groups + (
        jnp.arange(groups, dtype=jnp.int32) ^ own_b
    )[:, None]
    parts = jnp.take(parts, order.reshape(-1), axis=0)
    for bit in reversed(bits_of(groups)):
        half = parts.shape[0] // 2
        parts = parts[:half] + swap(parts[half:], "batch", bit)
    piece = parts.shape[1:]
    parts = tie(parts.reshape(count, -1), *after)
    for bit in reversed(bits_of(count)):
        half = parts.shape[0] // 2
        sent = jnp.concatenate([parts[half:].reshape(-1), flat])
        got = swap(sent, "seq", bit)
        at = half * parts.shape[1]
        parts = parts[:half] + got[:at].reshape(half, -1)
        flat = flat + got[at:]
    return parts.reshape(piece), flat


def batch_gather(value, later=None):
    parts = {0: value}
    for bit in reversed(bits_of(lax.axis_size("batch"))):
        passed = {r: later(v) if later and r else v for r, v in parts.items()}
        parts.update({r | bit: swap(v, "batch", bit) for r, v in passed.items()})
    return [parts[r] for r in range(len(parts))]


def batch_scatter(parts, seen=None):
    parts = {r: [v] for r, v in enumerate(parts)}
    added = lambda values: sum(v.astype(F32) for v in values)
    bits = bits_of(len(parts))
    for bit in bits:
        for r in sorted((r for r in parts if r & bit), reverse=True):
            values = parts.pop(r)
            sent = values[0] if len(values) == 1 else total_of(values)
            if seen and bit == bits[-1]:
                seen(sent)
            parts[r ^ bit].append(swap(sent, "batch", bit))
    return added(parts[0])


def total_of(values):
    rows, width = values[0].shape

    def kernel(*refs):
        total = refs[0][...].astype(F32)
        for ref in refs[1:-1]:
            total = total + ref[...].astype(F32)
        refs[-1][...] = total.astype(BF16)

    block = pl.BlockSpec((rows // 2, width), lambda i: (i, 0))
    return pl.pallas_call(
        kernel,
        grid=(2,),
        in_specs=[block] * len(values),
        out_specs=block,
        out_shape=jax.ShapeDtypeStruct((rows, width), BF16),
        cost_estimate=QUICK,
    )(*values)


def move_kernel(order, value, moved):
    width = value.shape[1] // order.shape[0]
    for i in range(order.shape[0]):
        source = pl.multiple_of(order[i] * width, width)
        moved[:, i * width : (i + 1) * width] = value[:, pl.ds(source, width)]


def reorder(value, order):
    rows, columns = value.shape
    width = columns // order.shape[0]
    if width % 128:
        return jnp.take(value.reshape(rows, -1, width), order, axis=1).reshape(value.shape)
    block = pl.BlockSpec((rows // 2, columns), lambda i, *_: (i, 0))
    return pl.pallas_call(
        move_kernel,
        grid_spec=pltpu.PrefetchScalarGridSpec(
            num_scalar_prefetch=1, grid=(2,), in_specs=[block], out_specs=block
        ),
        out_shape=jax.ShapeDtypeStruct(value.shape, value.dtype),
        cost_estimate=QUICK,
    )(order, value)


def norm_stats(values):
    mean = jnp.mean(values, axis=-1, keepdims=True)
    centered = values - mean
    factor = lax.rsqrt(jnp.mean(centered * centered, axis=-1, keepdims=True) + 1e-05)
    return centered * factor, factor


def norm_back(grad, unit, factor, gain):
    scaled = grad * gain
    inner = jnp.mean(scaled * unit, axis=-1, keepdims=True)
    return factor * (scaled - jnp.mean(scaled, axis=-1, keepdims=True) - unit * inner)


def gelu_and_slope(values):
    root, cubic = (2 / jnp.pi) ** 0.5, 0.044715
    square = values * values
    bend = jnp.tanh(values * (root + root * cubic * square))
    half = 0.5 + 0.5 * bend
    slope = half + values * (0.5 - 0.5 * bend * bend) * (root + 3 * root * cubic * square)
    return values * half, slope


def dot_t(left, right, left_dim, right_dim):
    return lax.dot_general(
        left, right, (((left_dim,), (right_dim,)), ((), ())), preferred_element_type=F32
    )


def masks(start, limit):
    row = lax.broadcasted_iota(jnp.int32, (WINDOW, WINDOW), 0)
    col = lax.broadcasted_iota(jnp.int32, (WINDOW, WINDOW), 1)
    own = col <= row
    spot = jnp.where(own, start + col, start - WINDOW + col)
    return own, (spot >= 0) & ((spot < limit) | (row == col))


def weights_of(query, key, early_key, own, live):
    scores = jnp.where(own, dot_t(query, key, 1, 1), dot_t(query, early_key, 1, 1))
    scores = jnp.where(live, scores * (HEAD_DIM**-0.5), -1e30)
    expo = jnp.exp(scores - jnp.max(scores, axis=-1, keepdims=True))
    return expo / jnp.sum(expo, axis=-1, keepdims=True)


def attend_kernel(limits, start, packed, early, mix, mixed, weights, *branch):
    width = mixed.shape[1]
    own, live = masks(start[0], limits[pl.program_id(0)])
    for head, at in enumerate(range(0, width, HEAD_DIM)):
        cols = lambda k: slice(k * width + at, k * width + at + HEAD_DIM)
        probs = weights_of(packed[:, cols(0)], packed[:, cols(1)], early[:, cols(0)], own, live)
        weights[:, head * WINDOW : (head + 1) * WINDOW] = probs.astype(BF16)
        near = jnp.where(own, probs, 0.0).astype(BF16)
        far = jnp.where(own, 0.0, probs).astype(BF16)
        mixed[:, cols(0)] = (
            dot_t(near, packed[:, cols(2)], 1, 0) + dot_t(far, early[:, cols(1)], 1, 0)
        ).astype(BF16)
    out = dot_t(mixed[...], mix[...], 1, 1).astype(BF16)
    for i, part in enumerate(branch):
        @pl.when(pl.program_id(0) == i)
        def _(part=part):
            part[...] = out


def attend_back_kernel(limits, start, packed, early, weights, grad, g_packed, g_early):
    width = grad.shape[1]
    scale = HEAD_DIM**-0.5
    row = lax.broadcasted_iota(jnp.int32, (WINDOW, WINDOW), 0)
    own = lax.broadcasted_iota(jnp.int32, (WINDOW, WINDOW), 1) <= row
    for head, at in enumerate(range(0, width, HEAD_DIM)):
        cols = lambda k: slice(k * width + at, k * width + at + HEAD_DIM)
        query, key, value = (packed[:, cols(k)] for k in range(3))
        early_key, early_value = (early[:, cols(k)] for k in range(2))
        out = grad[:, cols(0)]
        probs = weights[:, head * WINDOW : (head + 1) * WINDOW].astype(F32)
        g_probs = jnp.where(own, dot_t(out, value, 1, 1), dot_t(out, early_value, 1, 1))
        delta = jnp.sum(probs * g_probs, axis=-1, keepdims=True)
        g_scores = probs * (g_probs - delta)
        near = jnp.where(own, probs, 0.0).astype(BF16)
        far = jnp.where(own, 0.0, probs).astype(BF16)
        g_near = jnp.where(own, g_scores, 0.0).astype(BF16)
        g_far = jnp.where(own, 0.0, g_scores).astype(BF16)
        g_packed[:, cols(0)] = (
            (dot_t(g_near, key, 1, 0) + dot_t(g_far, early_key, 1, 0)) * scale
        ).astype(BF16)
        g_packed[:, cols(1)] = (dot_t(g_near, query, 0, 0) * scale).astype(BF16)
        g_packed[:, cols(2)] = dot_t(near, out, 0, 0).astype(BF16)
        g_early[:, cols(0)] = (dot_t(g_far, query, 0, 0) * scale).astype(BF16)
        g_early[:, cols(1)] = dot_t(far, out, 0, 0).astype(BF16)


def per_chain(kernel, limits, start, arrays, widths, shared=(), parts=0):
    rows = arrays[0].shape[0]
    whole = lambda shape: pl.BlockSpec(shape, lambda i, *_: (0, 0))
    block = lambda w: pl.BlockSpec((WINDOW, w), lambda i, *_: (i, 0))
    part = (WINDOW, shared[0].shape[0] if shared else 0)
    return pl.pallas_call(
        kernel,
        grid_spec=pltpu.PrefetchScalarGridSpec(
            num_scalar_prefetch=2,
            grid=(rows // WINDOW,),
            in_specs=[block(a.shape[1]) for a in arrays]
            + [pl.BlockSpec((v.shape[0], TILE), lambda i, *_: (0, 3)) for v in shared],
            out_specs=[block(w) for w in widths] + [whole(part)] * parts,
        ),
        out_shape=[jax.ShapeDtypeStruct((rows, w), BF16) for w in widths]
        + [jax.ShapeDtypeStruct(part, BF16)] * parts,
        cost_estimate=QUICK,
    )(limits, start, *arrays, *shared)


def shards(
    tokens,
    lengths,
    cotangent,
    ln1_gain,
    ln1_bias,
    w_qkv,
    qv_bias,
    w_out,
    out_bias,
    ln2_gain,
    ln2_bias,
    w_fc,
    fc_bias,
    w_proj,
    proj_bias,
):
    groups = lax.axis_size("batch")
    chain = lax.axis_index("batch")
    place = lax.axis_index("seq")
    rows, width = tokens.shape[1:]
    count = lax.axis_size("seq")
    slice_width = width // count
    heads_width = w_out.shape[0]
    assert rows == WINDOW and lengths.shape[1] == 1 and tokens.shape[0] == 1
    start = (place * rows).astype(jnp.int32)
    limits = lengths[:, 0][chain ^ jnp.arange(groups, dtype=jnp.int32)]
    valid = (start + jnp.arange(rows, dtype=jnp.int32) < limits[0]).astype(F32)
    to_slots, from_slots = slot_owners(), owner_slots()
    back_order = from_slots[slot_owners(-1)]

    tokens, cotangent = tokens[0], cotangent[0]
    vectors = jnp.stack([ln1_gain, ln1_bias, out_bias, ln2_gain, ln2_bias, proj_bias])
    vectors = doubled(vectors[None], "seq")
    ring = Ring(vectors)
    vectors = in_slot_order(doubled(vectors, "batch"))
    gain_one, shift_one, mix_shift, gain_two, shift_two, down_shift = (
        vectors[i].astype(F32) for i in range(6)
    )

    qkv_width = 3 * heads_width
    assert heads_width == TILE
    mix_in = jnp.concatenate([w_qkv.reshape(slice_width, qkv_width), w_out.T], axis=1)
    mix_in, up_in, down_in = Gather(mix_in, 0), Gather(w_fc, 0), Gather(w_proj, 1)
    late = {}
    g_down, g_up = (Scatter(lambda j, n=n: (late[n], j, slice_width)) for n in ("down", "up"))

    def find_mix(j):
        for value, lo, wide in late["mix"]:
            if lo <= j * slice_width < lo + wide:
                return value, j - lo // slice_width, slice_width

    g_mix = Scatter(find_mix)
    for moved, more_ahead in (
        (mix_in, True), (up_in, False), (down_in, True), (g_down, False), (g_up, True), (g_mix, False)
    ):
        ring.add(moved, more_ahead)
    more = max(0, count // 2 - 4)

    ring.advance()
    own_tokens = reorder(ring.now(tokens), to_slots)
    next_tokens = reorder(ring.now(tokens), slot_owners(1))
    early_tokens = lax.ppermute(next_tokens, "seq", [(i, i + 1) for i in range(count - 1)])
    parts = batch_gather(tie(own_tokens, vectors))
    ring.advance()
    early_parts = batch_gather(early_tokens)
    grad_out = reorder(ring.now(cotangent), to_slots).astype(F32) * valid[:, None]
    grad_y_own = grad_out.astype(BF16)
    ring.due(grad_y_own)
    ring.advance(1 + more)
    normed = norm_parts(ring.now(*parts), gain_one, shift_one)
    ring.due(normed)
    grad_y = batch_gather(tie(grad_y_own, early_parts[0]))
    ring.advance()
    normed_early = norm_parts(ring.now(*early_parts), gain_one, shift_one)
    ring.due(normed_early)
    mix_in.early(ring)
    ring.advance()
    ring.due(*grad_y)

    mix_in = mix_in.all()
    zeros = jnp.zeros((heads_width,), F32)
    shift = jnp.concatenate([qv_bias[0].astype(F32), zeros, qv_bias[1].astype(F32)])[None]
    (packed,) = matmul(
        [ring.now(normed)], mix_in, finish_bias, ["rows"], tiles=3, extra=[shift]
    )
    (early,) = matmul(
        [ring.now(normed_early)],
        mix_in,
        finish_bias,
        ["rows"],
        first=1,
        tiles=2,
        extra=[shift[:, heads_width:]],
    )
    starts = start.reshape(1)
    ring.due(packed, early)
    ring.advance()
    mixed, weights, *branch = per_chain(
        attend_kernel,
        limits,
        starts,
        (ring.now(packed), early),
        (heads_width, heads_width // HEAD_DIM * WINDOW),
        (mix_in,),
        groups,
    )
    ring.due(*branch)
    ring.advance()
    branch = batch_scatter(ring.now(*branch), ring.due)
    ring.advance(1 + more)
    inputs = own_tokens.astype(F32)
    resid = inputs + branch + mix_shift
    unit_two, factor_two = norm_stats(resid)
    second_own = (unit_two * gain_two + shift_two).astype(BF16)
    up_in = up_in.all()
    ring.due(second_own, up_in)
    ring.advance()
    second = batch_gather(second_own, ring.now)

    active, slope, second = matmul(
        ring.now(*second),
        up_in,
        finish_gelu,
        ["rows", "rows"],
        extra=[fc_bias.astype(F32)[None]],
        keep=True,
    )
    ring.due(active)
    ring.advance(1 + more)
    straight = lambda left, right: token_products(
        [(left, right, 0, 0, right.shape[1] // TILE)], [[0]] * (right.shape[1] // TILE)
    )
    grad_y = jnp.concatenate(grad_y, axis=0)
    late["down"] = straight(grad_y, ring.now(active))
    ring.due(late["down"])
    ring.advance()
    down_in.early(ring)
    ring.advance()
    down_in = down_in.all()
    grad_pre, grad_fc_bias = matmul(
        [ring.now(grad_y)], down_in, finish_slope, ["rows", "sums"], nt=True, extra=[slope]
    )
    ring.due(grad_pre)
    ring.advance()
    parts = matmul([ring.now(grad_pre)], up_in, finish_parts, ["parts"], nt=True)
    ring.due(*parts)
    ring.advance()
    sent = []
    grad_second = batch_scatter(ring.now(*parts), sent.append)
    late["up"] = straight(tie(second, *sent), grad_pre)
    ring.due(late["up"])
    ring.advance()
    grad_second = ring.now(grad_second)
    grad_resid = grad_out + norm_back(grad_second, unit_two, factor_two, gain_two)
    grad_branch_own = grad_resid.astype(BF16)
    result = matmul([tie(active, grad_branch_own)], down_in, finish_parts, ["parts"])
    ring.due(*result)
    ring.advance(1 + more)
    grad_branch = batch_gather(grad_branch_own, ring.now)
    grad_w_proj = g_down.total(ring).T
    ring.due(grad_w_proj)

    grad_mixed, grad_branch = matmul(
        tie(grad_branch, grad_w_proj), mix_in, finish_rows, ["rows"], first=3, tiles=1, keep=True
    )
    ring.due(grad_mixed)
    ring.advance()
    g_packed, g_early = per_chain(
        attend_back_kernel,
        limits,
        starts,
        (packed, early, weights, ring.now(grad_mixed)),
        (qkv_width, 2 * heads_width),
    )
    pairs = [
        (normed, g_packed, 0, 0, 3), (normed_early, g_early, 0, 1, 2), (grad_branch, mixed, 0, 3, 1)
    ]

    def mix_piece(first, wide):
        return token_products(pairs, [[0], [0, 1], [0, 1], [2]], first, wide), first * wide, wide

    late["mix"] = [mix_piece(2, TILE)]
    ring.due(late["mix"][0][0])
    result = batch_scatter(ring.now(*result), ring.due)
    ring.advance()
    back = matmul(
        [ring.now(g_early)], mix_in, finish_parts, ["parts"], nt=True, first=heads_width
    )
    sent = []
    back = batch_scatter(back, sent.append)
    pairs[0] = (tie(normed, *sent), *pairs[0][1:])
    late["mix"].append(mix_piece(1, TILE))
    ring.due(late["mix"][1][0])
    ring.advance()
    grad_own = matmul([ring.now(g_packed)], mix_in, finish_parts, ["parts"], nt=True)
    pairs[0] = (ring.now(normed), *pairs[0][1:])
    late["mix"].append(mix_piece(3, TILE))
    ring.due(late["mix"][2][0], *grad_own)
    ring.advance()
    back = ring.now(back)
    moved = reorder(back.astype(BF16), back_order)
    grad_own = batch_scatter(tie(grad_own, moved), ring.due)
    moved = lax.ppermute(moved, "seq", [(i + 1, i) for i in range(count - 1)])
    pairs[0] = (ring.now(normed), *pairs[0][1:])
    late["mix"].append(mix_piece(0, TILE))
    ring.due(late["mix"][3][0])
    ring.advance()
    result = resid + result + down_shift
    block_out = reorder(ring.now(result).astype(BF16), from_slots)
    while any(ring.queue.values()):
        ring.advance()
    unit_one, factor_one = norm_stats(inputs)
    unit_early, _ = norm_stats(early_tokens.astype(F32))
    grad_normed = grad_own + moved.astype(F32)
    grad_tokens = grad_resid + norm_back(grad_normed, unit_one, factor_one, gain_one)

    column = lambda value: jnp.sum(value.astype(F32), axis=0)
    flat = jnp.concatenate(
        [
            grad_fc_bias[0],
            column(g_packed[:, :heads_width]),
            column(g_packed[:, 2 * heads_width :]) + column(g_early[:, heads_width:]),
        ]
    )
    ff = grad_fc_bias.shape[1]
    sums = jnp.stack(
        [
            jnp.sum(grad_own * unit_one + back * unit_early, axis=0),
            jnp.sum(grad_own + back, axis=0),
            column(grad_branch_own),
            jnp.sum(grad_second * unit_two, axis=0),
            jnp.sum(grad_second, axis=0),
            column(grad_y_own),
        ]
    )
    sums, flat = small_totals(sums, flat, ring.last.values())
    grad_mix_in = g_mix.total(ring)
    return (
        block_out[None],
        reorder(grad_tokens.astype(BF16), from_slots)[None],
        sums[0],
        sums[1],
        grad_mix_in[:, :qkv_width].reshape(slice_width, 3, heads_width),
        flat[ff:].reshape(2, heads_width),
        grad_mix_in[:, qkv_width:].T,
        sums[2],
        sums[3],
        sums[4],
        g_up.total(ring),
        flat[:ff],
        grad_w_proj,
        sums[5],
    )


def solution(mesh):
    everywhere = P(("seq", "batch"))
    rows = P("batch", "seq", None)
    return jax.shard_map(
        shards,
        mesh=mesh,
        in_specs=(
            rows,
            P(),
            rows,
            everywhere,
            everywhere,
            P("seq", None, "batch"),
            P(None, "batch"),
            P("batch", "seq"),
            everywhere,
            everywhere,
            everywhere,
            P("seq", "batch"),
            P("batch"),
            P("batch", "seq"),
            everywhere,
        ),
        out_specs=(
            rows,
            rows,
            everywhere,
            everywhere,
            P("seq", None, "batch"),
            P(None, "batch"),
            P("batch", "seq"),
            everywhere,
            everywhere,
            everywhere,
            P("seq", "batch"),
            P("batch"),
            P("batch", "seq"),
            everywhere,
        ),
        check_vma=False,
    )
```

time: 712 us -> 678 us (0.952)
  Pallas kernels: 53.4 us -> 269 us
  matrix products: 190 us -> 0 us
  waiting for transfers between devices: 230 us -> 165 us
  other arithmetic: 76.1 us -> 45 us
  local copies, waits for them, and re-layouts: 64.5 us -> 92.5 us
  starting transfers between devices: 85.2 us -> 95 us
    pallas_call x0 -> x34, Pallas kernels: none -> 226 us  [the longest x9 106 us: matmul(): pl.pallas_call(kernel, grid=(tiles,), in_specs=[pl.BlockSpec(v.shape, lam...]
    dot_general x55 -> x0, matrix products: 190 us -> none  [dot_t(): lax.dot_general(left, right, (((left_dim,), (right_dim,)), ((), ())), pre...]
    ppermute x37 -> x40, waiting for transfers between devices: 93.5 us -> 28.4 us  [swap(): lax.ppermute(value, axis, [(i, i ^ bit) for i in range(lax.axis_size(axis...]
    convert_element_type x14 -> x4, other arithmetic: 31.3 us -> 1.41 us  [the longest x1 1.11 us: shards(): moved = reorder(back.astype(BF16), back_order)]
    unnamed x185 -> x155, local copies, waits for them, and re-layouts: 36.7 us -> 66.1 us
    slice x16 -> x1, local copies, waits for them, and re-layouts: 13.5 us -> 0.6 us  [shards(): shift[:, heads_width:]]
    ppermute x44, starting transfers between devices: 58.1 us -> 70.7 us  [the longest x42 65.7 us: hop(): self.last[forward] = lax.ppermute(value, 'seq', list(pairs))]
    pallas_call x7 -> x6, Pallas kernels: 28.5 us -> 16.5 us  [reorder(): pl.pallas_call(move_kernel, grid_spec=pltpu.PrefetchScalarGridSpec(num_sc...]
  transfers between devices with their start and end apart: 81 -> 84, of which waited for: 30 -> 41; matrix products, arithmetic and copies ran while one was open for 44% -> 18% of each run, Pallas kernels for 8% -> 37%
where the time goes in v3:
time: 678 us; the launch traced here: 669 us
  Pallas kernels  269 us (40%)
  waiting for transfers between devices  165 us (24%)
  starting transfers between devices  95 us (14%)
  local copies, waits for them, and re-layouts  92.5 us (14%)
  other arithmetic  45 us (7%)
    ppermute x42, waiting for transfers between devices, hop(): self.last[forward] = lax.ppermute(value, 'seq', list(pairs))  118 us
    pallas_call x9, Pallas kernels, matmul(): pl.pallas_call(kernel, grid=(tiles,), in_specs=[pl.BlockSpec(v.shape, lam...  106 us
    unnamed x155, local copies, waits for them, and re-layouts  66.1 us
    ppermute x42, starting transfers between devices, hop(): self.last[forward] = lax.ppermute(value, 'seq', list(pairs))  65.7 us
    pallas_call x6, Pallas kernels, token_products(): pl.pallas_call(kernel, grid=(len(plan),), in_specs=specs, out_specs=pl.Bl...  60 us
    pallas_call x12, Pallas kernels, join(): pl.pallas_call(kernel, grid=(steps,), in_specs=[pl.BlockSpec((step, width...  35.4 us
    ppermute x40, waiting for transfers between devices, swap(): lax.ppermute(value, axis, [(i, i ^ bit) for i in range(lax.axis_size(axis...  28.4 us
    pallas_call x2, Pallas kernels, per_chain(): pl.pallas_call(kernel, grid_spec=pltpu.PrefetchScalarGridSpec(num_scalar_...  26.6 us
  transfers between devices with their start and end apart: 84, of which 41 were waited for; matrix products, arithmetic and copies ran while one was open for 18% of the time, Pallas kernels for 37%

profile of v3, /device:TPU:0, one launch (start us, length us, event | category | flops | bytes accessed | tf_op | source)
XLA Modules:
  0.0 668.7 jit_solution(15412394173816499502)
XLA Ops:
  1.4 3.0 collective-permute-start
  10.9 2.7 collective-permute-start.2
  19.2 2.8 shard_map.254.refs_0_
  23.5 2.7 shard_map.257
  26.2 3.4 collective-permute-start.12
  29.9 11.1 %collective-permute-done.7 = bf16[256,2048]{1,0:T(8,128)(2,1)} collective-permute-done((bf16[256,2048]{1,0:T(8,128)(2,1)}, bf16[256,2048]{1,0:T(8,128)(2,1)}, u32[]{:S(2)}, u32[]{:S(2)}) %collective-permute-start.7) | collective-permute-done | bytes 1048608 | tf_op jit(solution)/shard_map/ppermute | solution.py:57
  41.0 2.5 collective-permute-start.9
  45.3 18.2 %collective-permute-done.12.refs_0_ = bf16[256,2048]{1,0:T(8,128)(2,1)S(1)} collective-permute-done((bf16[256,2048]{1,0:T(8,128)(2,1)}, bf16[256,2048]{1,0:T(8,128)(2,1)S(1)}, u32[]{:S(2)}, u32[]{:S(2)}) %collective-permute-start.12) | collective-permute-done | bytes 1048608 | tf_op jit(solution)/shard_map/ppermute | solution.py:596
  65.1 2.8 shard_map.255
  70.9 12.0 %collective-permute-done.9 = bf16[256,2048]{1,0:T(8,128)(2,1)} collective-permute-done((bf16[256,2048]{1,0:T(8,128)(2,1)}, bf16[256,2048]{1,0:T(8,128)(2,1)}, u32[]{:S(2)}, u32[]{:S(2)}) %collective-permute-start.9) | collective-permute-done | bytes 1048608 | tf_op jit(solution)/shard_map/ppermute | solution.py:57
  92.1 6.2 shard_map.256
  100.7 5.7 collective-permute-done.16
  111.7 6.2 shard_map.258
  135.1 10.9 %shard_map.259.packed = bf16[1024,1536]{1,0:T(8,128)(2,1)} custom-call(bf16[1024,2048]{1,0:T(8,128)(2,1)} %bitcast.57, bf16[2048,2048]{1,0:T(8,128)(2,1)} %constant_dynamic-update-slice_fusion.40.refs_1_.mix.refs_4_, f32[1,1536]{1,0:T(1,128)} %copy-done.54), custom_call_target="tpu_custom_call" | custom-call | flops 100000000 | tf_op jit(solution)/shard_map/pallas_call | solution.py:214
  146.0 8.5 %shard_map.260.early = bf16[1024,1024]{1,0:T(8,128)(2,1)} custom-call(bf16[1024,2048]{1,0:T(8,128)(2,1)} %bitcast.62, bf16[2048,2048]{1,0:T(8,128)(2,1)} %constant_dynamic-update-slice_fusion.40.refs_1_.mix.refs_4_, f32[1,1024]{1,0:T(1,128)} %slice.227.refs_2_), custom_call_target="tpu_custom_call" | custom-call | flops 100000000 | tf_op jit(solution)/shard_map/pallas_call | solution.py:214
  156.8 14.9 %shard_map.261 = (bf16[1024,512]{1,0:T(8,128)(2,1)}, bf16[1024,1024]{1,0:T(8,128)(2,1)}, bf16[256,2048]{1,0:T(8,128)(2,1)}, bf16[256,2048]{1,0:T(8,128)(2,1)}, b...) custom-call(s32[4]{0:T(128)} %copy-done.59, s32[1]{0:T(128)} %bitcast.12.start, ...), custom_call_target="tpu_custom_call" | custom-call | flops 100000000 | tf_op jit(solution)/shard_map/pallas_call | solution.py:519
  171.8 4.3 collective-permute-done.25
  194.2 11.1 %collective-permute-done.32 = bf16[256,2048]{1,0:T(8,128)(2,1)} collective-permute-done((bf16[256,2048]{1,0:T(8,128)(2,1)}, bf16[256,2048]{1,0:T(8,128)(2,1)}, u32[]{:S(2)}, u32[]{:S(2)}) %collective-permute-start.32) | collective-permute-done | bytes 1048608 | tf_op jit(solution)/shard_map/ppermute | solution.py:57
  211.2 2.7 fusion.37
  225.6 5.7 collective-permute-done.35
  231.3 7.9 %collective-permute-done.31.refs_2_ = bf16[256,2048]{1,0:T(8,128)(2,1)S(1)} collective-permute-done((bf16[256,2048]{1,0:T(8,128)(2,1)S(1)}, bf16[256,2048]{1,0:T(8,128)(2,1)S(1)}, u32[]{:S(2)}, u32[]{:S(2)}) %collective-permute-start.31) | collective-permute-done | bytes 1048608 | tf_op jit(solution)/shard_map/ppermute | solution.py:314
  246.0 19.1 %shard_map.263 = (bf16[1024,2048]{1,0:T(8,128)(2,1)}, bf16[1024,2048]{1,0:T(8,128)(2,1)}, bf16[1024,2048]{1,0:T(8,128)(2,1)}) custom-call(bf16[256,2048]{1,0:T(8,128)(2,1)} %copy-done.21, bf16[256,2048]{1,0:T(8,128)(2,1)} %copy-done.52, bf16[256,2048]{1,0:T(8,128)(2,1)} %copy-done.51, bf16[256,2048]{1,0:T(8,128)(2,1)} %copy-done.53, ...), custom_call_target="tpu_custom_call" | custom-call | flops 100000000 | tf_op jit(solution)/shard_map/pallas_call | solution.py:214
  279.4 13.6 %shard_map.264.refs_0_.refs_1_ = bf16[2048,2048]{1,0:T(8,128)(2,1)} custom-call(bf16[1024,2048]{1,0:T(8,128)(2,1)} %constant_dynamic-update-slice_fusion.27.refs_0_, bf16[1024,2048]{1,0:T(8,128)(2,1)} %get-tuple-element.261.refs_1_.refs_0_), custom_call_target="tpu_custom_call" | custom-call | flops 100000000 | tf_op jit(solution)/shard_map/pallas_call | solution.py:283
  307.8 11.5 %collective-permute-done.41.refs_2_ = bf16[256,2048]{1,0:T(8,128)(2,1)S(1)} collective-permute-done((bf16[256,2048]{1,0:T(8,128)(2,1)}, bf16[256,2048]{1,0:T(8,128)(2,1)S(1)}, u32[]{:S(2)}, u32[]{:S(2)}) %collective-permute-start.41) | collective-permute-done | bytes 1048608 | tf_op jit(solution)/shard_map/ppermute | solution.py:57
  320.2 2.9 shard_map.266
  327.5 14.7 %shard_map.267 = (bf16[1024,2048]{1,0:T(8,128)(2,1)}, f32[1,2048]{1,0:T(1,128)}) custom-call(bf16[1024,2048]{1,0:T(8,128)(2,1)} %constant_dynamic-update-slice_fusion.27.refs_0_, bf16[2048,2048]{1,0:T(8,128)(2,1)} %constant_dynamic-update-slice_fusion.39.refs_1_, bf16[1024,2048]{1,0:T(8,128)(2,1)} %get-tuple-element.231.refs_2_), custom_call_target="tpu_custom_call" | custom-call | flops 100000000 | tf_op jit(solution)/shard_map/pallas_call | solution.py:214
  342.2 4.2 collective-permute-done.44.refs_3_
  347.4 3.3 shard_map.268
  352.8 13.1 %shard_map.269 = (bf16[256,2048]{1,0:T(8,128)(2,1)}, bf16[256,2048]{1,0:T(8,128)(2,1)}, bf16[256,2048]{1,0:T(8,128)(2,1)}, bf16[256,2048]{1,0:T(8,128)(2,1)}) custom-call(bf16[1024,2048]{1,0:T(8,128)(2,1)} %get-tuple-element.239.refs_0_.refs_1_, bf16[2048,2048]{1,0:T(8,128)(2,1)} %constant_dynamic-update-slice_fusion.19.refs_4_.refs_1_), custom_call_target="tpu_custom_call" | custom-call | flops 100000000 | tf_op jit(solution)/shard_map/pallas_call | solution.py:214
  365.8 7.4 %collective-permute-done.46.refs_3_ = bf16[256,2048]{1,0:T(8,128)(2,1)S(1)} collective-permute-done((bf16[256,2048]{1,0:T(8,128)(2,1)}, bf16[256,2048]{1,0:T(8,128)(2,1)S(1)}, u32[]{:S(2)}, u32[]{:S(2)}) %collective-permute-start.46) | collective-permute-done | bytes 1048608 | tf_op jit(solution)/shard_map/ppermute | solution.py:57
  374.2 3.3 shard_map.270
  383.8 13.6 %shard_map.272.refs_0_.refs_1_ = bf16[2048,2048]{1,0:T(8,128)(2,1)} custom-call(bf16[1024,2048]{1,0:T(8,128)(2,1)} %get-tuple-element.255.refs_0_, bf16[1024,2048]{1,0:T(8,128)(2,1)} %get-tuple-element.239.refs_0_.refs_1_), custom_call_target="tpu_custom_call" | custom-call | flops 100000000 | tf_op jit(solution)/shard_map/pallas_call | solution.py:283
  397.4 2.6 shard_map.273
  400.0 3.3 collective-permute-done.51
  405.6 2.9 collective-permute-done.49
  415.3 13.0 %shard_map.274 = (bf16[256,2048]{1,0:T(8,128)(2,1)}, bf16[256,2048]{1,0:T(8,128)(2,1)}, bf16[256,2048]{1,0:T(8,128)(2,1)}, bf16[256,2048]{1,0:T(8,128)(2,1)}) custom-call(bf16[1024,2048]{1,0:T(8,128)(2,1)} %get-tuple-element.261.refs_1_.refs_0_, bf16[2048,2048]{1,0:T(8,128)(2,1)} %constant_dynamic-update-slice_fusion.39.refs_1_), custom_call_target="tpu_custom_call" | custom-call | flops 100000000 | tf_op jit(solution)/shard_map/pallas_call | solution.py:214
  429.5 3.4 shard_map.275
  432.9 5.9 collective-permute-done.56.refs_2_
  440.8 3.4 add_bitcast_fusion
  444.2 7.6 %shard_map.276 = (bf16[1024,512]{1,0:T(8,128)(2,1)}, bf16[1024,2048]{1,0:T(8,128)(2,1)}) custom-call(bf16[256,2048]{1,0:T(8,128)(2,1)} %copy-done.20, bf16[256,2048]{1,0:T(8,128)(2,1)} %collective-permute-done.55.refs_1_, bf16[256,2048]{1,0:T(8,128)(2,1)} %copy-done.34, bf16[256,2048]{1,0:T(8,128)(2,1)} %collective-permute-done.57.refs_3_, ...), custom_call_target="tpu_custom_call" | custom-call | flops 100000000 | tf_op jit(solution)/shard_map/pallas_call | solution.py:214
  451.8 12.9 %collective-permute-done.58.refs_3_ = bf16[256,2048]{1,0:T(8,128)(2,1)} collective-permute-done((bf16[256,2048]{1,0:T(8,128)(2,1)}, bf16[256,2048]{1,0:T(8,128)(2,1)}, u32[]{:S(2)}, u32[]{:S(2)}) %collective-permute-start.58) | collective-permute-done | bytes 1048608 | tf_op jit(solution)/shard_map/ppermute | solution.py:57
  464.7 3.4 shard_map.277
  470.3 11.7 %shard_map.279 = (bf16[1024,1536]{1,0:T(8,128)(2,1)}, bf16[1024,1024]{1,0:T(8,128)(2,1)}) custom-call(s32[4]{0:T(128)} %copy-done.59, s32[1]{0:T(128)} %bitcast.12.start, bf16[1024,1536]{1,0:T(8,128)(2,1)} %shard_map.259.packed, bf16[1024,1024]{1,0:T(8,128)(2,1)} %shard_map.260.early, bf16[1024,1024]{1,0:T(8,128)(2,1)} %get-tuple-element.289.weights, ...), custom_call_target="tpu_custom_call" | custom-call | flops 100000000 | tf_op jit(solution)/shard_map/pallas_call | solution.py:519
  482.0 8.2 %shard_map.280.refs_0_.refs_1_ = bf16[512,2048]{1,0:T(8,128)(2,1)} custom-call(bf16[1024,2048]{1,0:T(8,128)(2,1)} %bitcast.58, bf16[1024,1536]{1,0:T(8,128)(2,1)} %get-tuple-element.308.refs_1_.refs_0_, bf16[1024,2048]{1,0:T(8,128)(2,1)} %bitcast.63, bf16[1024,1024]{1,0:T(8,128)(2,1)} %get-tuple-element.298.refs_3_.refs_0_, ...), custom_call_target="tpu_custom_call" | custom-call | flops 100000000 | tf_op jit(solution)/shard_map/pallas_call | solution.py:283
  499.2 8.7 %shard_map.283 = (bf16[256,2048]{1,0:T(8,128)(2,1)}, bf16[256,2048]{1,0:T(8,128)(2,1)}, bf16[256,2048]{1,0:T(8,128)(2,1)}, bf16[256,2048]{1,0:T(8,128)(2,1)}) custom-call(bf16[1024,1024]{1,0:T(8,128)(2,1)} %get-tuple-element.298.refs_3_.refs_0_, bf16[2048,2048]{1,0:T(8,128)(2,1)} %constant_dynamic-update-slice_fusion.40.refs_1_.mix.refs_4_), custom_call_target="tpu_custom_call" | custom-call | flops 100000000 | tf_op jit(solution)/shard_map/pallas_call | solution.py:214
  515.9 8.2 %shard_map.285.refs_0_ = bf16[512,2048]{1,0:T(8,128)(2,1)} custom-call(bf16[1024,2048]{1,0:T(8,128)(2,1)} %bitcast.59, bf16[1024,1536]{1,0:T(8,128)(2,1)} %get-tuple-element.308.refs_1_.refs_0_, bf16[1024,2048]{1,0:T(8,128)(2,1)} %bitcast.64, bf16[1024,1024]{1,0:T(8,128)(2,1)} %get-tuple-element.298.refs_3_.refs_0_, ...), custom_call_target="tpu_custom_call" | custom-call | flops 100000000 | tf_op jit(solution)/shard_map/pallas_call | solution.py:283
  524.1 9.6 %collective-permute-done.65.refs_2_ = bf16[256,2048]{1,0:T(8,128)(2,1)} collective-permute-done((bf16[256,2048]{1,0:T(8,128)(2,1)S(1)}, bf16[256,2048]{1,0:T(8,128)(2,1)}, u32[]{:S(2)}, u32[]{:S(2)}) %collective-permute-start.65) | collective-permute-done | bytes 1048608 | tf_op jit(solution)/shard_map/ppermute | solution.py:57
  535.0 3.2 shard_map.286
  542.1 10.6 %shard_map.288 = (bf16[256,2048]{1,0:T(8,128)(2,1)}, bf16[256,2048]{1,0:T(8,128)(2,1)}, bf16[256,2048]{1,0:T(8,128)(2,1)}, bf16[256,2048]{1,0:T(8,128)(2,1)}) custom-call(bf16[1024,1536]{1,0:T(8,128)(2,1)} %get-tuple-element.308.refs_1_.refs_0_, bf16[2048,2048]{1,0:T(8,128)(2,1)} %constant_dynamic-update-slice_fusion.40.refs_1_.mix.refs_4_), custom_call_target="tpu_custom_call" | custom-call | flops 100000000 | tf_op jit(solution)/shard_map/pallas_call | solution.py:214
  552.8 8.2 %shard_map.287.refs_1_ = bf16[512,2048]{1,0:T(8,128)(2,1)} custom-call(bf16[1024,2048]{1,0:T(8,128)(2,1)} %bitcast.60, bf16[1024,1536]{1,0:T(8,128)(2,1)} %get-tuple-element.308.refs_1_.refs_0_, bf16[1024,2048]{1,0:T(8,128)(2,1)} %bitcast.65, bf16[1024,1024]{1,0:T(8,128)(2,1)} %get-tuple-element.298.refs_3_.refs_0_, ...), custom_call_target="tpu_custom_call" | custom-call | flops 100000000 | tf_op jit(solution)/shard_map/pallas_call | solution.py:283
  565.6 3.4 shard_map.289
  573.6 2.8 shard_map.291
  578.9 3.0 copy.40
  589.8 3.2 add_add_fusion.value
  593.0 8.2 %shard_map.290.refs_0_ = bf16[512,2048]{1,0:T(8,128)(2,1)} custom-call(bf16[1024,2048]{1,0:T(8,128)(2,1)} %bitcast.61, bf16[1024,1536]{1,0:T(8,128)(2,1)} %get-tuple-element.308.refs_1_.refs_0_, bf16[1024,2048]{1,0:T(8,128)(2,1)} %bitcast.66, bf16[1024,1024]{1,0:T(8,128)(2,1)} %get-tuple-element.298.refs_3_.refs_0_, ...), custom_call_target="tpu_custom_call" | custom-call | flops 100000000 | tf_op jit(solution)/shard_map/pallas_call | solution.py:283
  604.9 3.3 shard_map.293
  608.2 22.1 %collective-permute-start.80 = (bf16[256,2048]{1,0:T(8,128)(2,1)}, bf16[256,2048]{1,0:T(8,128)(2,1)}, u32[]{:S(2)}, u32[]{:S(2)}) collective-permute-start(bf16[256,2048]{1,0:T(8,128)(2,1)} %get-tuple-element.330), channel_id=1, source_target_pairs={{8,0},{16,8},{24,16},{28,24},{20,28},{12,20},{4,12},{0,4},{9,1},{1... | collective-permute-start | bytes 3145736 | tf_op jit(solution)/shard_map/ppermute | solution.py:57
  630.6 2.8 shard_map.294
  633.4 3.2 convert_add_fusion.1
  636.6 4.4 add_reduce_fusion
  642.2 4.2 collective-permute-done.77
  649.3 4.1 fusion.11.value
  654.6 3.4 convert_add_fusion.2
  663.6 2.8 shard_map.295
  (431 shorter events, 217.2 us)
Async XLA Ops:
  15.5 25.5 %collective-permute-start.7 = (bf16[256,2048]{1,0:T(8,128)(2,1)}, bf16[256,2048]{1,0:T(8,128)(2,1)}, u32[]{:S(2)}, u32[]{:S(2)}) collective-permute-start(bf16[256,2048]{1,0:T(8,128)(2,1)} %get-tuple-element.176), channel_id=1, source_target_pairs={{8,0},{16,8},{24,16},{28,24},{20,28},{12,20},{4,12},{0,4},{9,1},{1... | collective-permute-start | bytes 3145736 | tf_op jit(solution)/shard_map/ppermute | solution.py:57
  17.1 23.9 %collective-permute-start.6 = (bf16[256,2048]{1,0:T(8,128)(2,1)}, bf16[256,2048]{1,0:T(8,128)(2,1)}, u32[]{:S(2)}, u32[]{:S(2)}) collective-permute-start(bf16[256,2048]{1,0:T(8,128)(2,1)} %get-tuple-element.176), channel_id=1, source_target_pairs={{0,8},{8,16},{16,24},{24,28},{28,20},{20,12},{12,4},{4,0},{1,9},{9... | collective-permute-start | bytes 3145736 | tf_op jit(solution)/shard_map/ppermute | solution.py:57
  22.0 23.0 %collective-permute-start.4 = (bf16[256,2048]{1,0:T(8,128)(2,1)}, bf16[256,2048]{1,0:T(8,128)(2,1)}, u32[]{:S(2)}, u32[]{:S(2)}) collective-permute-start(bf16[256,2048]{1,0:T(8,128)(2,1)} %shard_map.254.refs_0_), channel_id=1, source_target_pairs={{0,2},{1,3},{2,0},{3,1},{4,6},{5,7},{6,4},{7,5},{8,10},{9,11},{10,... | collective-permute-start | bytes 3145736 | tf_op jit(solution)/shard_map/ppermute | solution.py:314
  26.2 37.3 %collective-permute-start.12 = (bf16[256,2048]{1,0:T(8,128)(2,1)}, bf16[256,2048]{1,0:T(8,128)(2,1)S(1)}, u32[]{:S(2)}, u32[]{:S(2)}) collective-permute-start(bf16[256,2048]{1,0:T(8,128)(2,1)} %shard_map.257), channel_id=1, source_target_pairs={{0,4},{4,8},{8,12},{12,16},{16,20},{20,24},{24,28},{1,5},{5,9},{9,... | collective-permute-start | bytes 3145736 | tf_op jit(solution)/shard_map/ppermute | solution.py:596
  41.0 26.9 %collective-permute-start.8 = (bf16[256,2048]{1,0:T(8,128)(2,1)}, bf16[256,2048]{1,0:T(8,128)(2,1)}, u32[]{:S(2)}, u32[]{:S(2)}) collective-permute-start(bf16[256,2048]{1,0:T(8,128)(2,1)} %collective-permute-done.6), channel_id=1, source_target_pairs={{0,8},{8,16},{16,24},{24,28},{28,20},{20,12},{12,4},{4,0},{1,9},{9... | collective-permute-start | bytes 3145736 | tf_op jit(solution)/shard_map/ppermute | solution.py:57
  41.0 41.8 %collective-permute-start.9 = (bf16[256,2048]{1,0:T(8,128)(2,1)}, bf16[256,2048]{1,0:T(8,128)(2,1)}, u32[]{:S(2)}, u32[]{:S(2)}) collective-permute-start(bf16[256,2048]{1,0:T(8,128)(2,1)} %collective-permute-done.7), channel_id=1, source_target_pairs={{8,0},{16,8},{24,16},{28,24},{20,28},{12,20},{4,12},{0,4},{9,1},{1... | collective-permute-start | bytes 3145736 | tf_op jit(solution)/shard_map/ppermute | solution.py:57
  44.8 41.2 %collective-permute-start.3 = (bf16[256,2048]{1,0:T(8,128)(2,1)S(1)}, bf16[256,2048]{1,0:T(8,128)(2,1)}, u32[]{:S(2)}, u32[]{:S(2)}) collective-permute-start(bf16[256,2048]{1,0:T(8,128)(2,1)S(1)} %copy-done.6), channel_id=1, source_target_pairs={{0,1},{1,0},{2,3},{3,2},{4,5},{5,4},{6,7},{7,6},{8,9},{9,8},{10,11... | collective-permute-start | bytes 3145736 | tf_op jit(solution)/shard_map/ppermute | solution.py:314
  44.9 42.6 %collective-permute-start.5 = (bf16[256,2048]{1,0:T(8,128)(2,1)}, bf16[256,2048]{1,0:T(8,128)(2,1)}, u32[]{:S(2)}, u32[]{:S(2)}) collective-permute-start(bf16[256,2048]{1,0:T(8,128)(2,1)} %collective-permute-done.4.refs_2_), channel_id=1, source_target_pairs={{0,1},{1,0},{2,3},{3,2},{4,5},{5,4},{6,7},{7,6},{8,9},{9,8},{10,11... | collective-permute-start | bytes 3145736 | tf_op jit(solution)/shard_map/ppermute | solution.py:314
  63.5 24.1 %collective-permute-start.14 = (bf16[256,2048]{1,0:T(8,128)(2,1)S(1)}, bf16[256,2048]{1,0:T(8,128)(2,1)}, u32[]{:S(2)}, u32[]{:S(2)}) collective-permute-start(bf16[256,2048]{1,0:T(8,128)(2,1)S(1)} %collective-permute-done.12.refs_0_), channel_id=1, source_target_pairs={{0,2},{1,3},{2,0},{3,1},{4,6},{5,7},{6,4},{7,5},{8,10},{9,11},{10,... | collective-permute-start | bytes 3145736 | tf_op jit(solution)/shard_map/ppermute | solution.py:314
  82.9 23.6 %collective-permute-start.16 = (bf16[256,2048]{1,0:T(8,128)(2,1)}, bf16[256,2048]{1,0:T(8,128)(2,1)}, u32[]{:S(2)}, u32[]{:S(2)}) collective-permute-start(bf16[256,2048]{1,0:T(8,128)(2,1)} %collective-permute-done.8), channel_id=1, source_target_pairs={{0,8},{8,16},{16,24},{24,28},{28,20},{20,12},{12,4},{4,0},{1,9},{9... | collective-permute-start | bytes 3145736 | tf_op jit(solution)/shard_map/ppermute | solution.py:57
  82.9 23.6 %collective-permute-start.17 = (bf16[256,2048]{1,0:T(8,128)(2,1)}, bf16[256,2048]{1,0:T(8,128)(2,1)}, u32[]{:S(2)}, u32[]{:S(2)}) collective-permute-start(bf16[256,2048]{1,0:T(8,128)(2,1)} %collective-permute-done.9), channel_id=1, source_target_pairs={{8,0},{16,8},{24,16},{28,24},{20,28},{12,20},{4,12},{0,4},{9,1},{1... | collective-permute-start | bytes 3145736 | tf_op jit(solution)/shard_map/ppermute | solution.py:57
  86.0 25.2 %collective-permute-start.22 = (bf16[256,2048]{1,0:T(8,128)(2,1)}, bf16[256,2048]{1,0:T(8,128)(2,1)}, u32[]{:S(2)}, u32[]{:S(2)}) collective-permute-start(bf16[256,2048]{1,0:T(8,128)(2,1)} %get-tuple-element.196), channel_id=1, source_target_pairs={{0,2},{1,3},{2,0},{3,1},{4,6},{5,7},{6,4},{7,5},{8,10},{9,11},{10,... | collective-permute-start | bytes 3145736 | tf_op jit(solution)/shard_map/ppermute | solution.py:314
  87.6 23.6 %collective-permute-start.13 = (bf16[256,2048]{1,0:T(8,128)(2,1)S(1)}, bf16[256,2048]{1,0:T(8,128)(2,1)}, u32[]{:S(2)}, u32[]{:S(2)}) collective-permute-start(bf16[256,2048]{1,0:T(8,128)(2,1)S(1)} %collective-permute-done.12.refs_0_), channel_id=1, source_target_pairs={{0,1},{1,0},{2,3},{3,2},{4,5},{5,4},{6,7},{7,6},{8,9},{9,8},{10,11... | collective-permute-start | bytes 3145736 | tf_op jit(solution)/shard_map/ppermute | solution.py:314
  87.6 24.1 %collective-permute-start.15 = (bf16[256,2048]{1,0:T(8,128)(2,1)}, bf16[256,2048]{1,0:T(8,128)(2,1)}, u32[]{:S(2)}, u32[]{:S(2)}) collective-permute-start(bf16[256,2048]{1,0:T(8,128)(2,1)} %collective-permute-done.14.refs_2_), channel_id=1, source_target_pairs={{0,1},{1,0},{2,3},{3,2},{4,5},{5,4},{6,7},{7,6},{8,9},{9,8},{10,11... | collective-permute-start | bytes 3145736 | tf_op jit(solution)/shard_map/ppermute | solution.py:314
  106.4 21.7 %collective-permute-start.18 = (bf16[256,2048]{1,0:T(8,128)(2,1)}, bf16[256,2048]{1,0:T(8,128)(2,1)}, u32[]{:S(2)}, u32[]{:S(2)}) collective-permute-start(bf16[256,2048]{1,0:T(8,128)(2,1)} %collective-permute-done.16), channel_id=1, source_target_pairs={{0,8},{8,16},{16,24},{24,28},{28,20},{20,12},{12,4},{4,0},{1,9},{9... | collective-permute-start | bytes 3145736 | tf_op jit(solution)/shard_map/ppermute | solution.py:57
  111.2 43.4 %collective-permute-start.21 = (bf16[256,2048]{1,0:T(8,128)(2,1)S(1)}, bf16[256,2048]{1,0:T(8,128)(2,1)S(1)}, u32[]{:S(2)}, u32[]{:S(2)}) collective-permute-start(bf16[256,2048]{1,0:T(8,128)(2,1)S(1)} %copy-done.18), channel_id=1, source_target_pairs={{0,1},{1,0},{2,3},{3,2},{4,5},{5,4},{6,7},{7,6},{8,9},{9,8},{10,11... | collective-permute-start | bytes 3145736 | tf_op jit(solution)/shard_map/ppermute | solution.py:314
  111.2 43.3 %collective-permute-start.23 = (bf16[256,2048]{1,0:T(8,128)(2,1)}, bf16[256,2048]{1,0:T(8,128)(2,1)}, u32[]{:S(2)}, u32[]{:S(2)}) collective-permute-start(bf16[256,2048]{1,0:T(8,128)(2,1)} %collective-permute-done.22), channel_id=1, source_target_pairs={{0,1},{1,0},{2,3},{3,2},{4,5},{5,4},{6,7},{7,6},{8,9},{9,8},{10,11... | collective-permute-start | bytes 3145736 | tf_op jit(solution)/shard_map/ppermute | solution.py:314
  130.1 24.4 %collective-permute-start.20 = (bf16[256,2048]{1,0:T(8,128)(2,1)}, bf16[256,2048]{1,0:T(8,128)(2,1)}, u32[]{:S(2)}, u32[]{:S(2)}) collective-permute-start(bf16[256,2048]{1,0:T(8,128)(2,1)} %param.26), channel_id=1, source_target_pairs={{0,8},{8,16},{16,24},{24,28},{28,20},{20,12},{12,4},{4,0},{1,9},{9... | collective-permute-start | bytes 3145736 | tf_op jit(solution)/shard_map/ppermute | solution.py:57
  132.1 22.4 %collective-permute-start.24 = (bf16[256,2048]{1,0:T(8,128)(2,1)}, bf16[256,2048]{1,0:T(8,128)(2,1)}, u32[]{:S(2)}, u32[]{:S(2)}) collective-permute-start(bf16[256,2048]{1,0:T(8,128)(2,1)} %collective-permute-done.19), channel_id=1, source_target_pairs={{8,0},{16,8},{24,16},{28,24},{20,28},{12,20},{4,12},{0,4},{9,1},{1... | collective-permute-start | bytes 3145736 | tf_op jit(solution)/shard_map/ppermute | solution.py:57
  156.6 21.8 %collective-permute-start.26 = (bf16[256,2048]{1,0:T(8,128)(2,1)}, bf16[256,2048]{1,0:T(8,128)(2,1)S(1)}, u32[]{:S(2)}, u32[]{:S(2)}) collective-permute-start(bf16[256,2048]{1,0:T(8,128)(2,1)} %collective-permute-done.24), channel_id=1, source_target_pairs={{8,0},{16,8},{24,16},{28,24},{20,28},{12,20},{4,12},{0,4},{9,1},{1... | collective-permute-start | bytes 3145736 | tf_op jit(solution)/shard_map/ppermute | solution.py:57
  179.4 25.9 %collective-permute-start.32 = (bf16[256,2048]{1,0:T(8,128)(2,1)}, bf16[256,2048]{1,0:T(8,128)(2,1)}, u32[]{:S(2)}, u32[]{:S(2)}) collective-permute-start(bf16[256,2048]{1,0:T(8,128)(2,1)} %copy-done.44), channel_id=1, source_target_pairs={{0,8},{8,16},{16,24},{24,28},{28,20},{20,12},{12,4},{4,0},{1,9},{9... | collective-permute-start | bytes 3145736 | tf_op jit(solution)/shard_map/ppermute | solution.py:57
  181.2 25.6 %collective-permute-start.33 = (bf16[256,2048]{1,0:T(8,128)(2,1)}, bf16[256,2048]{1,0:T(8,128)(2,1)}, u32[]{:S(2)}, u32[]{:S(2)}) collective-permute-start(bf16[256,2048]{1,0:T(8,128)(2,1)} %copy-done.46), channel_id=1, source_target_pairs={{8,0},{16,8},{24,16},{28,24},{20,28},{12,20},{4,12},{0,4},{9,1},{1... | collective-permute-start | bytes 3145736 | tf_op jit(solution)/shard_map/ppermute | solution.py:57
  181.4 27.4 %collective-permute-start.27 = (bf16[256,2048]{1,0:T(8,128)(2,1)}, bf16[256,2048]{1,0:T(8,128)(2,1)S(1)}, u32[]{:S(2)}, u32[]{:S(2)}) collective-permute-start(bf16[256,2048]{1,0:T(8,128)(2,1)} %get-tuple-element.208), channel_id=1, source_target_pairs={{0,1},{1,0},{2,3},{3,2},{4,5},{5,4},{6,7},{7,6},{8,9},{9,8},{10,11... | collective-permute-start | bytes 3145736 | tf_op jit(solution)/shard_map/ppermute | solution.py:314
  185.7 25.5 %collective-permute-start.29 = (bf16[256,2048]{1,0:T(8,128)(2,1)}, bf16[256,2048]{1,0:T(8,128)(2,1)}, u32[]{:S(2)}, u32[]{:S(2)}) collective-permute-start(bf16[256,2048]{1,0:T(8,128)(2,1)} %shard_map.262), channel_id=1, source_target_pairs={{0,2},{1,3},{2,0},{3,1},{4,6},{5,7},{6,4},{7,5},{8,10},{9,11},{10,... | collective-permute-start | bytes 3145736 | tf_op jit(solution)/shard_map/ppermute | solution.py:314
  206.8 24.6 %collective-permute-start.35 = (bf16[2048,256]{1,0:T(8,128)(2,1)S(1)}, bf16[2048,256]{1,0:T(8,128)(2,1)}, u32[]{:S(2)}, u32[]{:S(2)}) collective-permute-start(bf16[2048,256]{1,0:T(8,128)(2,1)S(1)} %copy-done.16), channel_id=1, source_target_pairs={{8,0},{16,8},{24,16},{28,24},{20,28},{12,20},{4,12},{0,4},{9,1},{1... | collective-permute-start | bytes 3145736 | tf_op jit(solution)/shard_map/ppermute | solution.py:57
  207.1 24.3 %collective-permute-start.34 = (bf16[2048,256]{1,0:T(8,128)(2,1)S(1)}, bf16[2048,256]{1,0:T(8,128)(2,1)}, u32[]{:S(2)}, u32[]{:S(2)}) collective-permute-start(bf16[2048,256]{1,0:T(8,128)(2,1)S(1)} %copy-done.16), channel_id=1, source_target_pairs={{0,8},{8,16},{16,24},{24,28},{28,20},{20,12},{12,4},{4,0},{1,9},{9... | collective-permute-start | bytes 3145736 | tf_op jit(solution)/shard_map/ppermute | solution.py:57
  214.8 24.4 %collective-permute-start.31 = (bf16[256,2048]{1,0:T(8,128)(2,1)S(1)}, bf16[256,2048]{1,0:T(8,128)(2,1)S(1)}, u32[]{:S(2)}, u32[]{:S(2)}) collective-permute-start(bf16[256,2048]{1,0:T(8,128)(2,1)S(1)} %add_convert_fusion.refs_0_), channel_id=1, source_target_pairs={{0,2},{1,3},{2,0},{3,1},{4,6},{5,7},{6,4},{7,5},{8,10},{9,11},{10,... | collective-permute-start | bytes 3145736 | tf_op jit(solution)/shard_map/ppermute | solution.py:314
  239.2 25.9 %collective-permute-start.37 = (bf16[2048,256]{1,0:T(8,128)(2,1)}, bf16[2048,256]{1,0:T(8,128)(2,1)}, u32[]{:S(2)}, u32[]{:S(2)}) collective-permute-start(bf16[2048,256]{1,0:T(8,128)(2,1)} %collective-permute-done.34), channel_id=1, source_target_pairs={{0,8},{8,16},{16,24},{24,28},{28,20},{20,12},{12,4},{4,0},{1,9},{9... | collective-permute-start | bytes 3145736 | tf_op jit(solution)/shard_map/ppermute | solution.py:57
  241.0 25.6 %collective-permute-start.38 = (bf16[2048,256]{1,0:T(8,128)(2,1)}, bf16[2048,256]{1,0:T(8,128)(2,1)}, u32[]{:S(2)}, u32[]{:S(2)}) collective-permute-start(bf16[2048,256]{1,0:T(8,128)(2,1)} %collective-permute-done.35), channel_id=1, source_target_pairs={{8,0},{16,8},{24,16},{28,24},{20,28},{12,20},{4,12},{0,4},{9,1},{1... | collective-permute-start | bytes 3145736 | tf_op jit(solution)/shard_map/ppermute | solution.py:57
  266.6 28.5 %collective-permute-start.39 = (bf16[2048,256]{1,0:T(8,128)(2,1)}, bf16[2048,256]{1,0:T(8,128)(2,1)}, u32[]{:S(2)}, u32[]{:S(2)}) collective-permute-start(bf16[2048,256]{1,0:T(8,128)(2,1)} %collective-permute-done.37), channel_id=1, source_target_pairs={{0,8},{8,16},{16,24},{24,28},{28,20},{20,12},{12,4},{4,0},{1,9},{9... | collective-permute-start | bytes 3145736 | tf_op jit(solution)/shard_map/ppermute | solution.py:57
  268.3 26.7 %collective-permute-start.40 = (bf16[2048,256]{1,0:T(8,128)(2,1)}, bf16[2048,256]{1,0:T(8,128)(2,1)}, u32[]{:S(2)}, u32[]{:S(2)}) collective-permute-start(bf16[2048,256]{1,0:T(8,128)(2,1)} %collective-permute-done.38), channel_id=1, source_target_pairs={{8,0},{16,8},{24,16},{28,24},{20,28},{12,20},{4,12},{0,4},{9,1},{1... | collective-permute-start | bytes 3145736 | tf_op jit(solution)/shard_map/ppermute | solution.py:57
  295.0 24.2 %collective-permute-start.41 = (bf16[256,2048]{1,0:T(8,128)(2,1)}, bf16[256,2048]{1,0:T(8,128)(2,1)S(1)}, u32[]{:S(2)}, u32[]{:S(2)}) collective-permute-start(bf16[256,2048]{1,0:T(8,128)(2,1)} %shard_map.265), channel_id=1, source_target_pairs={{8,0},{16,8},{24,16},{28,24},{20,28},{12,20},{4,12},{0,4},{9,1},{1... | collective-permute-start | bytes 3145736 | tf_op jit(solution)/shard_map/ppermute | solution.py:57
  295.4 24.0 %collective-permute-start.42 = (bf16[2048,256]{1,0:T(8,128)(2,1)}, bf16[2048,256]{1,0:T(8,128)(2,1)}, u32[]{:S(2)}, u32[]{:S(2)}) collective-permute-start(bf16[2048,256]{1,0:T(8,128)(2,1)} %collective-permute-done.39), channel_id=1, source_target_pairs={{0,8},{8,16},{16,24},{24,28},{28,20},{20,12},{12,4},{4,0},{1,9},{9... | collective-permute-start | bytes 3145736 | tf_op jit(solution)/shard_map/ppermute | solution.py:57
  323.1 23.3 %collective-permute-start.44 = (bf16[256,2048]{1,0:T(8,128)(2,1)}, bf16[256,2048]{1,0:T(8,128)(2,1)S(1)}, u32[]{:S(2)}, u32[]{:S(2)}) collective-permute-start(bf16[256,2048]{1,0:T(8,128)(2,1)} %get-tuple-element.229), channel_id=1, source_target_pairs={{8,0},{16,8},{24,16},{28,24},{20,28},{12,20},{4,12},{0,4},{9,1},{1... | collective-permute-start | bytes 3145736 | tf_op jit(solution)/shard_map/ppermute | solution.py:57
  323.4 23.1 %collective-permute-start.43 = (bf16[256,2048]{1,0:T(8,128)(2,1)}, bf16[256,2048]{1,0:T(8,128)(2,1)}, u32[]{:S(2)}, u32[]{:S(2)}) collective-permute-start(bf16[256,2048]{1,0:T(8,128)(2,1)} %get-tuple-element.227), channel_id=1, source_target_pairs={{0,8},{8,16},{16,24},{24,28},{28,20},{20,12},{12,4},{4,0},{1,9},{9... | collective-permute-start | bytes 3145736 | tf_op jit(solution)/shard_map/ppermute | solution.py:57
  350.7 22.5 %collective-permute-start.46 = (bf16[256,2048]{1,0:T(8,128)(2,1)}, bf16[256,2048]{1,0:T(8,128)(2,1)S(1)}, u32[]{:S(2)}, u32[]{:S(2)}) collective-permute-start(bf16[256,2048]{1,0:T(8,128)(2,1)} %get-tuple-element.238), channel_id=1, source_target_pairs={{8,0},{16,8},{24,16},{28,24},{20,28},{12,20},{4,12},{0,4},{9,1},{1... | collective-permute-start | bytes 3145736 | tf_op jit(solution)/shard_map/ppermute | solution.py:57
  351.0 22.4 %collective-permute-start.45 = (bf16[256,2048]{1,0:T(8,128)(2,1)}, bf16[256,2048]{1,0:T(8,128)(2,1)}, u32[]{:S(2)}, u32[]{:S(2)}) collective-permute-start(bf16[256,2048]{1,0:T(8,128)(2,1)} %get-tuple-element.236), channel_id=1, source_target_pairs={{0,8},{8,16},{16,24},{24,28},{28,20},{20,12},{12,4},{4,0},{1,9},{9... | collective-permute-start | bytes 3145736 | tf_op jit(solution)/shard_map/ppermute | solution.py:57
  377.5 25.8 %collective-permute-start.51 = (bf16[256,2048]{1,0:T(8,128)(2,1)}, bf16[256,2048]{1,0:T(8,128)(2,1)S(1)}, u32[]{:S(2)}, u32[]{:S(2)}) collective-permute-start(bf16[256,2048]{1,0:T(8,128)(2,1)} %get-tuple-element.249), channel_id=1, source_target_pairs={{8,0},{16,8},{24,16},{28,24},{20,28},{12,20},{4,12},{0,4},{9,1},{1... | collective-permute-start | bytes 3145736 | tf_op jit(solution)/shard_map/ppermute | solution.py:57
  377.9 25.6 %collective-permute-start.50 = (bf16[256,2048]{1,0:T(8,128)(2,1)}, bf16[256,2048]{1,0:T(8,128)(2,1)}, u32[]{:S(2)}, u32[]{:S(2)}) collective-permute-start(bf16[256,2048]{1,0:T(8,128)(2,1)} %get-tuple-element.247), channel_id=1, source_target_pairs={{0,8},{8,16},{16,24},{24,28},{28,20},{20,12},{12,4},{4,0},{1,9},{9... | collective-permute-start | bytes 3145736 | tf_op jit(solution)/shard_map/ppermute | solution.py:57
  379.6 26.0 %collective-permute-start.47 = (bf16[256,2048]{1,0:T(8,128)(2,1)}, bf16[256,2048]{1,0:T(8,128)(2,1)}, u32[]{:S(2)}, u32[]{:S(2)}) collective-permute-start(bf16[256,2048]{1,0:T(8,128)(2,1)} %get-tuple-element.251), channel_id=1, source_target_pairs={{0,1},{1,0},{2,3},{3,2},{4,5},{5,4},{6,7},{7,6},{8,9},{9,8},{10,11... | collective-permute-start | bytes 3145736 | tf_op jit(solution)/shard_map/ppermute | solution.py:314
  382.9 25.5 %collective-permute-start.49 = (bf16[256,2048]{1,0:T(8,128)(2,1)}, bf16[256,2048]{1,0:T(8,128)(2,1)}, u32[]{:S(2)}, u32[]{:S(2)}) collective-permute-start(bf16[256,2048]{1,0:T(8,128)(2,1)} %shard_map.271), channel_id=1, source_target_pairs={{0,2},{1,3},{2,0},{3,1},{4,6},{5,7},{6,4},{7,5},{8,10},{9,11},{10,... | collective-permute-start | bytes 3145736 | tf_op jit(solution)/shard_map/ppermute | solution.py:314
  403.4 25.1 %collective-permute-start.53 = (bf16[256,2048]{1,0:T(8,128)(2,1)}, bf16[256,2048]{1,0:T(8,128)(2,1)}, u32[]{:S(2)}, u32[]{:S(2)}) collective-permute-start(bf16[256,2048]{1,0:T(8,128)(2,1)} %get-tuple-element.259), channel_id=1, source_target_pairs={{8,0},{16,8},{24,16},{28,24},{20,28},{12,20},{4,12},{0,4},{9,1},{1... | collective-permute-start | bytes 3145736 | tf_op jit(solution)/shard_map/ppermute | solution.py:57
  404.9 24.6 %collective-permute-start.52 = (bf16[256,2048]{1,0:T(8,128)(2,1)}, bf16[256,2048]{1,0:T(8,128)(2,1)}, u32[]{:S(2)}, u32[]{:S(2)}) collective-permute-start(bf16[256,2048]{1,0:T(8,128)(2,1)} %get-tuple-element.257), channel_id=1, source_target_pairs={{0,8},{8,16},{16,24},{24,28},{28,20},{20,12},{12,4},{4,0},{1,9},{9... | collective-permute-start | bytes 3145736 | tf_op jit(solution)/shard_map/ppermute | solution.py:57
  414.4 24.4 %collective-permute-start.56 = (bf16[256,2048]{1,0:T(8,128)(2,1)S(1)}, bf16[256,2048]{1,0:T(8,128)(2,1)S(1)}, u32[]{:S(2)}, u32[]{:S(2)}) collective-permute-start(bf16[256,2048]{1,0:T(8,128)(2,1)S(1)} %get-tuple-element.274.refs_0_), channel_id=1, source_target_pairs={{0,2},{1,3},{2,0},{3,1},{4,6},{5,7},{6,4},{7,5},{8,10},{9,11},{10,... | collective-permute-start | bytes 3145736 | tf_op jit(solution)/shard_map/ppermute | solution.py:314
  415.3 28.9 %collective-permute-start.55 = (bf16[256,2048]{1,0:T(8,128)(2,1)S(1)}, bf16[256,2048]{1,0:T(8,128)(2,1)}, u32[]{:S(2)}, u32[]{:S(2)}) collective-permute-start(bf16[256,2048]{1,0:T(8,128)(2,1)S(1)} %get-tuple-element.274.refs_0_), channel_id=1, source_target_pairs={{0,1},{1,0},{2,3},{3,2},{4,5},{5,4},{6,7},{7,6},{8,9},{9,8},{10,11... | collective-permute-start | bytes 3145736 | tf_op jit(solution)/shard_map/ppermute | solution.py:314
  438.8 25.9 %collective-permute-start.58 = (bf16[256,2048]{1,0:T(8,128)(2,1)}, bf16[256,2048]{1,0:T(8,128)(2,1)}, u32[]{:S(2)}, u32[]{:S(2)}) collective-permute-start(bf16[256,2048]{1,0:T(8,128)(2,1)} %get-tuple-element.271), channel_id=1, source_target_pairs={{8,0},{16,8},{24,16},{28,24},{20,28},{12,20},{4,12},{0,4},{9,1},{1... | collective-permute-start | bytes 3145736 | tf_op jit(solution)/shard_map/ppermute | solution.py:57
  439.1 25.6 %collective-permute-start.54 = (bf16[256,2048]{1,0:T(8,128)(2,1)}, bf16[256,2048]{1,0:T(8,128)(2,1)}, u32[]{:S(2)}, u32[]{:S(2)}) collective-permute-start(bf16[256,2048]{1,0:T(8,128)(2,1)} %get-tuple-element.269), channel_id=1, source_target_pairs={{0,8},{8,16},{16,24},{24,28},{28,20},{20,12},{12,4},{4,0},{1,9},{9... | collective-permute-start | bytes 3145736 | tf_op jit(solution)/shard_map/ppermute | solution.py:57
  468.1 24.2 %collective-permute-start.60 = (bf16[256,2048]{1,0:T(8,128)(2,1)}, bf16[256,2048]{1,0:T(8,128)(2,1)S(1)}, u32[]{:S(2)}, u32[]{:S(2)}) collective-permute-start(bf16[256,2048]{1,0:T(8,128)(2,1)} %get-tuple-element.288), channel_id=1, source_target_pairs={{0,1},{1,0},{2,3},{3,2},{4,5},{5,4},{6,7},{7,6},{8,9},{9,8},{10,11... | collective-permute-start | bytes 3145736 | tf_op jit(solution)/shard_map/ppermute | solution.py:314
  468.1 27.7 %collective-permute-start.63 = (bf16[256,2048]{1,0:T(8,128)(2,1)}, bf16[256,2048]{1,0:T(8,128)(2,1)S(1)}, u32[]{:S(2)}, u32[]{:S(2)}) collective-permute-start(bf16[256,2048]{1,0:T(8,128)(2,1)} %get-tuple-element.284), channel_id=1, source_target_pairs={{8,0},{16,8},{24,16},{28,24},{20,28},{12,20},{4,12},{0,4},{9,1},{1... | collective-permute-start | bytes 3145736 | tf_op jit(solution)/shard_map/ppermute | solution.py:57
  469.6 26.1 %collective-permute-start.62 = (bf16[256,2048]{1,0:T(8,128)(2,1)}, bf16[256,2048]{1,0:T(8,128)(2,1)S(1)}, u32[]{:S(2)}, u32[]{:S(2)}) collective-permute-start(bf16[256,2048]{1,0:T(8,128)(2,1)} %get-tuple-element.282), channel_id=1, source_target_pairs={{0,8},{8,16},{16,24},{24,28},{28,20},{20,12},{12,4},{4,0},{1,9},{9... | collective-permute-start | bytes 3145736 | tf_op jit(solution)/shard_map/ppermute | solution.py:57
  507.9 25.7 %collective-permute-start.65 = (bf16[256,2048]{1,0:T(8,128)(2,1)S(1)}, bf16[256,2048]{1,0:T(8,128)(2,1)}, u32[]{:S(2)}, u32[]{:S(2)}) collective-permute-start(bf16[256,2048]{1,0:T(8,128)(2,1)S(1)} %copy-done.29), channel_id=1, source_target_pairs={{8,0},{16,8},{24,16},{28,24},{20,28},{12,20},{4,12},{0,4},{9,1},{1... | collective-permute-start | bytes 3145736 | tf_op jit(solution)/shard_map/ppermute | solution.py:57
  509.5 25.4 %collective-permute-start.66 = (bf16[256,2048]{1,0:T(8,128)(2,1)}, bf16[256,2048]{1,0:T(8,128)(2,1)S(1)}, u32[]{:S(2)}, u32[]{:S(2)}) collective-permute-start(bf16[256,2048]{1,0:T(8,128)(2,1)} %shard_map.281), channel_id=1, source_target_pairs={{0,8},{8,16},{16,24},{24,28},{28,20},{20,12},{12,4},{4,0},{1,9},{9... | collective-permute-start | bytes 3145736 | tf_op jit(solution)/shard_map/ppermute | solution.py:57
  511.0 58.1 %collective-permute-start.70 = (bf16[256,2048]{1,0:T(8,128)(2,1)}, bf16[256,2048]{1,0:T(8,128)(2,1)}, u32[]{:S(2)}, u32[]{:S(2)}) collective-permute-start(bf16[256,2048]{1,0:T(8,128)(2,1)} %get-tuple-element.321), channel_id=1, source_target_pairs={{0,1},{1,0},{2,3},{3,2},{4,5},{5,4},{6,7},{7,6},{8,9},{9,8},{10,11... | collective-permute-start | bytes 3145736 | tf_op jit(solution)/shard_map/ppermute | solution.py:314
  514.4 54.6 %collective-permute-start.71 = (bf16[256,2048]{1,0:T(8,128)(2,1)}, bf16[256,2048]{1,0:T(8,128)(2,1)}, u32[]{:S(2)}, u32[]{:S(2)}) collective-permute-start(bf16[256,2048]{1,0:T(8,128)(2,1)} %shard_map.284), channel_id=1, source_target_pairs={{0,2},{1,3},{2,0},{3,1},{4,6},{5,7},{6,4},{7,5},{8,10},{9,11},{10,... | collective-permute-start | bytes 3145736 | tf_op jit(solution)/shard_map/ppermute | solution.py:314
  538.2 24.7 %collective-permute-start.68 = (bf16[256,2048]{1,0:T(8,128)(2,1)}, bf16[256,2048]{1,0:T(8,128)(2,1)S(1)}, u32[]{:S(2)}, u32[]{:S(2)}) collective-permute-start(bf16[256,2048]{1,0:T(8,128)(2,1)} %get-tuple-element.306), channel_id=1, source_target_pairs={{8,0},{16,8},{24,16},{28,24},{20,28},{12,20},{4,12},{0,4},{9,1},{1... | collective-permute-start | bytes 3145736 | tf_op jit(solution)/shard_map/ppermute | solution.py:57
  539.9 24.7 %collective-permute-start.67 = (bf16[256,2048]{1,0:T(8,128)(2,1)}, bf16[256,2048]{1,0:T(8,128)(2,1)S(1)}, u32[]{:S(2)}, u32[]{:S(2)}) collective-permute-start(bf16[256,2048]{1,0:T(8,128)(2,1)} %get-tuple-element.304), channel_id=1, source_target_pairs={{0,8},{8,16},{16,24},{24,28},{28,20},{20,12},{12,4},{4,0},{1,9},{9... | collective-permute-start | bytes 3145736 | tf_op jit(solution)/shard_map/ppermute | solution.py:57
  542.0 46.0 %collective-permute-start.59 = (bf16[256,2048]{1,0:T(8,128)(2,1)}, bf16[256,2048]{1,0:T(8,128)(2,1)}, u32[]{:S(2)}, u32[]{:S(2)}) collective-permute-start(bf16[256,2048]{1,0:T(8,128)(2,1)} %get-tuple-element.286), channel_id=1, source_target_pairs={{0,1},{1,0},{2,3},{3,2},{4,5},{5,4},{6,7},{7,6},{8,9},{9,8},{10,11... | collective-permute-start | bytes 3145736 | tf_op jit(solution)/shard_map/ppermute | solution.py:314
  562.9 25.1 %collective-permute-start.61 = (bf16[256,2048]{1,0:T(8,128)(2,1)}, bf16[256,2048]{1,0:T(8,128)(2,1)}, u32[]{:S(2)}, u32[]{:S(2)}) collective-permute-start(bf16[256,2048]{1,0:T(8,128)(2,1)} %shard_map.278), channel_id=1, source_target_pairs={{0,2},{1,3},{2,0},{3,1},{4,6},{5,7},{6,4},{7,5},{8,10},{9,11},{10,... | collective-permute-start | bytes 3145736 | tf_op jit(solution)/shard_map/ppermute | solution.py:314
  576.8 26.3 %collective-permute-start.73 = (bf16[256,2048]{1,0:T(8,128)(2,1)}, bf16[256,2048]{1,0:T(8,128)(2,1)}, u32[]{:S(2)}, u32[]{:S(2)}) collective-permute-start(bf16[256,2048]{1,0:T(8,128)(2,1)} %get-tuple-element.318), channel_id=1, source_target_pairs={{8,0},{16,8},{24,16},{28,24},{20,28},{12,20},{4,12},{0,4},{9,1},{1... | collective-permute-start | bytes 3145736 | tf_op jit(solution)/shard_map/ppermute | solution.py:57
  578.6 26.3 %collective-permute-start.69 = (bf16[256,2048]{1,0:T(8,128)(2,1)}, bf16[256,2048]{1,0:T(8,128)(2,1)}, u32[]{:S(2)}, u32[]{:S(2)}) collective-permute-start(bf16[256,2048]{1,0:T(8,128)(2,1)} %get-tuple-element.316), channel_id=1, source_target_pairs={{0,8},{8,16},{16,24},{24,28},{28,20},{20,12},{12,4},{4,0},{1,9},{9... | collective-permute-start | bytes 3145736 | tf_op jit(solution)/shard_map/ppermute | solution.py:57
  584.0 52.6 %collective-permute-start.76 = (bf16[256,2048]{1,0:T(8,128)(2,1)}, bf16[256,2048]{1,0:T(8,128)(2,1)}, u32[]{:S(2)}, u32[]{:S(2)}) collective-permute-start(bf16[256,2048]{1,0:T(8,128)(2,1)} %shard_map.291), channel_id=1, source_target_pairs={{4,0},{8,4},{12,8},{16,12},{20,16},{24,20},{28,24},{5,1},{9,5},{13... | collective-permute-start | bytes 3145736 | tf_op jit(solution)/shard_map/ppermute | solution.py:737
  588.0 48.6 %collective-permute-start.74 = (bf16[256,2048]{1,0:T(8,128)(2,1)}, bf16[256,2048]{1,0:T(8,128)(2,1)}, u32[]{:S(2)}, u32[]{:S(2)}) collective-permute-start(bf16[256,2048]{1,0:T(8,128)(2,1)} %get-tuple-element.333), channel_id=1, source_target_pairs={{0,1},{1,0},{2,3},{3,2},{4,5},{5,4},{6,7},{7,6},{8,9},{9,8},{10,11... | collective-permute-start | bytes 3145736 | tf_op jit(solution)/shard_map/ppermute | solution.py:314
  588.0 48.6 %collective-permute-start.75 = (bf16[256,2048]{1,0:T(8,128)(2,1)}, bf16[256,2048]{1,0:T(8,128)(2,1)}, u32[]{:S(2)}, u32[]{:S(2)}) collective-permute-start(bf16[256,2048]{1,0:T(8,128)(2,1)} %shard_map.292), channel_id=1, source_target_pairs={{0,2},{1,3},{2,0},{3,1},{4,6},{5,7},{6,4},{7,5},{8,10},{9,11},{10,... | collective-permute-start | bytes 3145736 | tf_op jit(solution)/shard_map/ppermute | solution.py:314
  608.2 39.6 %collective-permute-start.80 = (bf16[256,2048]{1,0:T(8,128)(2,1)}, bf16[256,2048]{1,0:T(8,128)(2,1)}, u32[]{:S(2)}, u32[]{:S(2)}) collective-permute-start(bf16[256,2048]{1,0:T(8,128)(2,1)} %get-tuple-element.330), channel_id=1, source_target_pairs={{8,0},{16,8},{24,16},{28,24},{20,28},{12,20},{4,12},{0,4},{9,1},{1... | collective-permute-start | bytes 3145736 | tf_op jit(solution)/shard_map/ppermute | solution.py:57
  (83 other events, 1395.5 us)

commit v4 on v3

--- a/solution.py
+++ b/solution.py
@@ -365,7 +365,7 @@
     return [parts[r] for r in range(len(parts))]
 
 
-def batch_scatter(parts, seen=None):
+def batch_scatter(parts, seen=None, apart=False):
     parts = {r: [v] for r, v in enumerate(parts)}
     added = lambda values: sum(v.astype(F32) for v in values)
     bits = bits_of(len(parts))
@@ -376,7 +376,7 @@
             if seen and bit == bits[-1]:
                 seen(sent)
             parts[r ^ bit].append(swap(sent, "batch", bit))
-    return added(parts[0])
+    return parts[0] if apart else added(parts[0])
 
 
 def total_of(values):
@@ -399,27 +399,34 @@
     )(*values)
 
 
-def move_kernel(order, value, moved):
-    width = value.shape[1] // order.shape[0]
+def move_kernel(order, *refs):
+    *values, moved = refs
+    width = moved.shape[1] // order.shape[0]
     for i in range(order.shape[0]):
-        source = pl.multiple_of(order[i] * width, width)
-        moved[:, i * width : (i + 1) * width] = value[:, pl.ds(source, width)]
+        source = pl.ds(pl.multiple_of(order[i] * width, width), width)
+        block = values[0][:, source]
+        if len(values) > 1:
+            block = sum(v[:, source].astype(F32) for v in values).astype(moved.dtype)
+        moved[:, i * width : (i + 1) * width] = block
 
 
 def reorder(value, order):
+    values = value if isinstance(value, (list, tuple)) else [value]
+    value = values[0]
     rows, columns = value.shape
     width = columns // order.shape[0]
     if width % 128:
+        value = value if len(values) == 1 else total_of(values)
         return jnp.take(value.reshape(rows, -1, width), order, axis=1).reshape(value.shape)
     block = pl.BlockSpec((rows // 2, columns), lambda i, *_: (i, 0))
     return pl.pallas_call(
         move_kernel,
         grid_spec=pltpu.PrefetchScalarGridSpec(
-            num_scalar_prefetch=1, grid=(2,), in_specs=[block], out_specs=block
+            num_scalar_prefetch=1, grid=(2,), in_specs=[block] * len(values), out_specs=block
         ),
         out_shape=jax.ShapeDtypeStruct(value.shape, value.dtype),
         cost_estimate=QUICK,
-    )(order, value)
+    )(order, *values)
 
 
 def norm_stats(values):
@@ -641,6 +648,8 @@
     ring.due(*branch)
     ring.advance()
     branch = batch_scatter(ring.now(*branch), ring.due)
+    grad_y = jnp.concatenate(grad_y, axis=0)
+    ring.due(grad_y)
     ring.advance(1 + more)
     inputs = own_tokens.astype(F32)
     resid = inputs + branch + mix_shift
@@ -664,7 +673,6 @@
     straight = lambda left, right: token_products(
         [(left, right, 0, 0, right.shape[1] // TILE)], [[0]] * (right.shape[1] // TILE)
     )
-    grad_y = jnp.concatenate(grad_y, axis=0)
     late["down"] = straight(grad_y, ring.now(active))
     ring.due(late["down"])
     ring.advance()
@@ -720,21 +728,21 @@
     back = matmul(
         [ring.now(g_early)], mix_in, finish_parts, ["parts"], nt=True, first=heads_width
     )
-    sent = []
-    back = batch_scatter(back, sent.append)
-    pairs[0] = (tie(normed, *sent), *pairs[0][1:])
+    pairs[0] = (tie(normed, back[0]), *pairs[0][1:])
     late["mix"].append(mix_piece(1, TILE))
     ring.due(late["mix"][1][0])
     ring.advance()
-    grad_own = matmul([ring.now(g_packed)], mix_in, finish_parts, ["parts"], nt=True)
-    pairs[0] = (ring.now(normed), *pairs[0][1:])
+    sent = []
+    back = batch_scatter(ring.now(*back), sent.append, True)
+    grad_own = matmul([tie(g_packed, *sent)], mix_in, finish_parts, ["parts"], nt=True)
+    pairs[0] = (tie(normed, grad_own[0]), *pairs[0][1:])
     late["mix"].append(mix_piece(3, TILE))
-    ring.due(late["mix"][2][0], *grad_own)
-    ring.advance()
-    back = ring.now(back)
-    moved = reorder(back.astype(BF16), back_order)
+    ring.due(late["mix"][2][0])
+    ring.advance()
+    moved = reorder(ring.now(*back), back_order)
     grad_own = batch_scatter(tie(grad_own, moved), ring.due)
     moved = lax.ppermute(moved, "seq", [(i + 1, i) for i in range(count - 1)])
+    back = sum(v.astype(F32) for v in back)
     pairs[0] = (ring.now(normed), *pairs[0][1:])
     late["mix"].append(mix_piece(0, TILE))
     ring.due(late["mix"][3][0])
@@ -767,11 +775,12 @@
             column(grad_y_own),
         ]
     )
-    sums, flat = small_totals(sums, flat, ring.last.values())
+    grad_tokens = reorder(grad_tokens.astype(BF16), from_slots)
+    sums, flat = small_totals(sums, flat, [*ring.last.values(), grad_tokens])
     grad_mix_in = g_mix.total(ring)
     return (
         block_out[None],
-        reorder(grad_tokens.astype(BF16), from_slots)[None],
+        grad_tokens[None],
         sums[0],
         sums[1],
         grad_mix_in[:, :qkv_width].reshape(slice_width, 3, heads_width),

time: 678 us -> 666 us (0.982)
  starting transfers between devices: 95 us -> 75.6 us
  waiting for transfers between devices: 165 us -> 174 us
    ppermute x42, starting transfers between devices: 65.7 us -> 45.7 us  [hop(): self.last[forward] = lax.ppermute(value, 'seq', list(pairs))]
    ppermute x1, waiting for transfers between devices: 0.01 us -> 11.1 us  [shards(): moved = lax.ppermute(moved, 'seq', [(i + 1, i) for i in range(count - 1)])]
    unnamed x155 -> x137, local copies, waits for them, and re-layouts: 66.1 us -> 66.5 us
  transfers between devices with their start and end apart: 84 -> 84, of which waited for: 41 -> 43; matrix products, arithmetic and copies ran while one was open for 18% -> 19% of each run, Pallas kernels for 37% -> 38%
where the time goes in v4:
time: 666 us; the launch traced here: 657 us
  Pallas kernels  270 us (41%)
  waiting for transfers between devices  174 us (26%)
  local copies, waits for them, and re-layouts  93 us (14%)
  starting transfers between devices  75.6 us (11%)
  other arithmetic  42 us (6%)
    ppermute x42, waiting for transfers between devices, hop(): self.last[forward] = lax.ppermute(value, 'seq', list(pairs))  112 us
    pallas_call x9, Pallas kernels, matmul(): pl.pallas_call(kernel, grid=(tiles,), in_specs=[pl.BlockSpec(v.shape, lam...  106 us
    unnamed x137, local copies, waits for them, and re-layouts  66.5 us
    pallas_call x6, Pallas kernels, token_products(): pl.pallas_call(kernel, grid=(len(plan),), in_specs=specs, out_specs=pl.Bl...  59.9 us
    ppermute x42, starting transfers between devices, hop(): self.last[forward] = lax.ppermute(value, 'seq', list(pairs))  45.7 us
    pallas_call x12, Pallas kernels, join(): pl.pallas_call(kernel, grid=(steps,), in_specs=[pl.BlockSpec((step, width...  35.4 us
    ppermute x40, waiting for transfers between devices, swap(): lax.ppermute(value, axis, [(i, i ^ bit) for i in range(lax.axis_size(axis...  32.6 us
    pallas_call x2, Pallas kernels, per_chain(): pl.pallas_call(kernel, grid_spec=pltpu.PrefetchScalarGridSpec(num_scalar_...  26.6 us
  transfers between devices with their start and end apart: 84, of which 43 were waited for; matrix products, arithmetic and copies ran while one was open for 19% of the time, Pallas kernels for 38%

profile of v4, /device:TPU:0, one launch (start us, length us, event | category | flops | bytes accessed | tf_op | source)
XLA Modules:
  0.0 656.7 jit_solution(15101208981285365337)
XLA Ops:
  1.4 3.0 collective-permute-start
  10.9 2.7 collective-permute-start.2
  19.2 2.8 shard_map.254.refs_0_
  23.5 2.7 shard_map.257
  26.2 3.4 collective-permute-start.12
  29.9 11.1 %collective-permute-done.7 = bf16[256,2048]{1,0:T(8,128)(2,1)} collective-permute-done((bf16[256,2048]{1,0:T(8,128)(2,1)}, bf16[256,2048]{1,0:T(8,128)(2,1)}, u32[]{:S(2)}, u32[]{:S(2)}) %collective-permute-start.7) | collective-permute-done | bytes 1048608 | tf_op jit(solution)/shard_map/ppermute | solution.py:57
  45.3 18.2 %collective-permute-done.12.refs_0_ = bf16[256,2048]{1,0:T(8,128)(2,1)S(1)} collective-permute-done((bf16[256,2048]{1,0:T(8,128)(2,1)}, bf16[256,2048]{1,0:T(8,128)(2,1)S(1)}, u32[]{:S(2)}, u32[]{:S(2)}) %collective-permute-start.12) | collective-permute-done | bytes 1048608 | tf_op jit(solution)/shard_map/ppermute | solution.py:603
  65.1 2.7 shard_map.255
  70.9 12.0 %collective-permute-done.9 = bf16[256,2048]{1,0:T(8,128)(2,1)} collective-permute-done((bf16[256,2048]{1,0:T(8,128)(2,1)}, bf16[256,2048]{1,0:T(8,128)(2,1)}, u32[]{:S(2)}, u32[]{:S(2)}) %collective-permute-start.9) | collective-permute-done | bytes 1048608 | tf_op jit(solution)/shard_map/ppermute | solution.py:57
  92.2 6.1 shard_map.256
  100.7 5.8 collective-permute-done.16
  111.7 6.2 shard_map.258
  135.0 10.9 %shard_map.259.packed = bf16[1024,1536]{1,0:T(8,128)(2,1)} custom-call(bf16[1024,2048]{1,0:T(8,128)(2,1)} %bitcast.57, bf16[2048,2048]{1,0:T(8,128)(2,1)} %constant_dynamic-update-slice_fusion.40.refs_1_.mix.refs_4_, f32[1,1536]{1,0:T(1,128)} %copy-done.47), custom_call_target="tpu_custom_call" | custom-call | flops 100000000 | tf_op jit(solution)/shard_map/pallas_call | solution.py:214
  145.9 8.5 %shard_map.260.early = bf16[1024,1024]{1,0:T(8,128)(2,1)} custom-call(bf16[1024,2048]{1,0:T(8,128)(2,1)} %bitcast.62, bf16[2048,2048]{1,0:T(8,128)(2,1)} %constant_dynamic-update-slice_fusion.40.refs_1_.mix.refs_4_, f32[1,1024]{1,0:T(1,128)} %slice.227.refs_2_), custom_call_target="tpu_custom_call" | custom-call | flops 100000000 | tf_op jit(solution)/shard_map/pallas_call | solution.py:214
  156.7 14.9 %shard_map.261 = (bf16[1024,512]{1,0:T(8,128)(2,1)}, bf16[1024,1024]{1,0:T(8,128)(2,1)}, bf16[256,2048]{1,0:T(8,128)(2,1)}, bf16[256,2048]{1,0:T(8,128)(2,1)}, b...) custom-call(s32[4]{0:T(128)} %copy-done.50, s32[1]{0:T(128)} %bitcast.12.start, ...), custom_call_target="tpu_custom_call" | custom-call | flops 100000000 | tf_op jit(solution)/shard_map/pallas_call | solution.py:526
  171.6 4.6 collective-permute-done.25
  200.5 7.9 %collective-permute-done.32 = bf16[256,2048]{1,0:T(8,128)(2,1)} collective-permute-done((bf16[256,2048]{1,0:T(8,128)(2,1)}, bf16[256,2048]{1,0:T(8,128)(2,1)}, u32[]{:S(2)}, u32[]{:S(2)}) %collective-permute-start.32) | collective-permute-done | bytes 1048608 | tf_op jit(solution)/shard_map/ppermute | solution.py:57
  229.6 4.8 collective-permute-done.35
  234.5 7.4 %collective-permute-done.31.refs_2_ = bf16[256,2048]{1,0:T(8,128)(2,1)S(1)} collective-permute-done((bf16[256,2048]{1,0:T(8,128)(2,1)S(1)}, bf16[256,2048]{1,0:T(8,128)(2,1)S(1)}, u32[]{:S(2)}, u32[]{:S(2)}) %collective-permute-start.31) | collective-permute-done | bytes 1048608 | tf_op jit(solution)/shard_map/ppermute | solution.py:314
  246.5 19.1 %shard_map.263 = (bf16[1024,2048]{1,0:T(8,128)(2,1)}, bf16[1024,2048]{1,0:T(8,128)(2,1)}, bf16[1024,2048]{1,0:T(8,128)(2,1)}) custom-call(bf16[256,2048]{1,0:T(8,128)(2,1)} %copy-done.22, bf16[256,2048]{1,0:T(8,128)(2,1)} %copy-done.45, bf16[256,2048]{1,0:T(8,128)(2,1)} %copy-done.44, bf16[256,2048]{1,0:T(8,128)(2,1)} %copy-done.46, ...), custom_call_target="tpu_custom_call" | custom-call | flops 100000000 | tf_op jit(solution)/shard_map/pallas_call | solution.py:214
  277.1 13.5 %shard_map.264.refs_0_.refs_1_ = bf16[2048,2048]{1,0:T(8,128)(2,1)} custom-call(bf16[1024,2048]{1,0:T(8,128)(2,1)} %constant_dynamic-update-slice_fusion.19.refs_0_, bf16[1024,2048]{1,0:T(8,128)(2,1)} %get-tuple-element.267.refs_1_.refs_0_), custom_call_target="tpu_custom_call" | custom-call | flops 100000000 | tf_op jit(solution)/shard_map/pallas_call | solution.py:283
  308.4 11.1 %collective-permute-done.41.refs_2_ = bf16[256,2048]{1,0:T(8,128)(2,1)} collective-permute-done((bf16[256,2048]{1,0:T(8,128)(2,1)}, bf16[256,2048]{1,0:T(8,128)(2,1)}, u32[]{:S(2)}, u32[]{:S(2)}) %collective-permute-start.41) | collective-permute-done | bytes 1048608 | tf_op jit(solution)/shard_map/ppermute | solution.py:57
  319.8 2.9 shard_map.266
  327.0 14.8 %shard_map.267 = (bf16[1024,2048]{1,0:T(8,128)(2,1)}, f32[1,2048]{1,0:T(1,128)}) custom-call(bf16[1024,2048]{1,0:T(8,128)(2,1)} %constant_dynamic-update-slice_fusion.19.refs_0_, bf16[2048,2048]{1,0:T(8,128)(2,1)} %constant_dynamic-update-slice_fusion.39.refs_1_, bf16[1024,2048]{1,0:T(8,128)(2,1)} %get-tuple-element.237.refs_2_), custom_call_target="tpu_custom_call" | custom-call | flops 100000000 | tf_op jit(solution)/shard_map/pallas_call | solution.py:214
  341.8 3.3 collective-permute-done.44.refs_3_
  346.0 3.3 shard_map.268
  351.4 13.1 %shard_map.269 = (bf16[256,2048]{1,0:T(8,128)(2,1)}, bf16[256,2048]{1,0:T(8,128)(2,1)}, bf16[256,2048]{1,0:T(8,128)(2,1)}, bf16[256,2048]{1,0:T(8,128)(2,1)}) custom-call(bf16[1024,2048]{1,0:T(8,128)(2,1)} %get-tuple-element.245.refs_0_.refs_1_, bf16[2048,2048]{1,0:T(8,128)(2,1)} %constant_dynamic-update-slice_fusion.23.refs_4_.refs_1_), custom_call_target="tpu_custom_call" | custom-call | flops 100000000 | tf_op jit(solution)/shard_map/pallas_call | solution.py:214
  364.4 6.5 collective-permute-done.46.refs_3_
  371.9 3.3 shard_map.270
  381.4 13.5 %shard_map.272.refs_0_.refs_1_ = bf16[2048,2048]{1,0:T(8,128)(2,1)} custom-call(bf16[1024,2048]{1,0:T(8,128)(2,1)} %get-tuple-element.261.refs_0_, bf16[1024,2048]{1,0:T(8,128)(2,1)} %get-tuple-element.245.refs_0_.refs_1_), custom_call_target="tpu_custom_call" | custom-call | flops 100000000 | tf_op jit(solution)/shard_map/pallas_call | solution.py:283
  394.9 2.6 shard_map.273
  397.5 3.4 collective-permute-done.51
  412.9 13.0 %shard_map.274 = (bf16[256,2048]{1,0:T(8,128)(2,1)}, bf16[256,2048]{1,0:T(8,128)(2,1)}, bf16[256,2048]{1,0:T(8,128)(2,1)}, bf16[256,2048]{1,0:T(8,128)(2,1)}) custom-call(bf16[1024,2048]{1,0:T(8,128)(2,1)} %get-tuple-element.267.refs_1_.refs_0_, bf16[2048,2048]{1,0:T(8,128)(2,1)} %constant_dynamic-update-slice_fusion.39.refs_1_), custom_call_target="tpu_custom_call" | custom-call | flops 100000000 | tf_op jit(solution)/shard_map/pallas_call | solution.py:214
  427.0 3.4 shard_map.275
  430.4 6.0 collective-permute-done.56.refs_2_
  438.5 3.3 add_bitcast_fusion
  441.8 7.6 %shard_map.276 = (bf16[1024,512]{1,0:T(8,128)(2,1)}, bf16[1024,2048]{1,0:T(8,128)(2,1)}) custom-call(bf16[256,2048]{1,0:T(8,128)(2,1)} %copy-done.21, bf16[256,2048]{1,0:T(8,128)(2,1)} %collective-permute-done.55.refs_1_, bf16[256,2048]{1,0:T(8,128)(2,1)} %copy-done.32, bf16[256,2048]{1,0:T(8,128)(2,1)} %collective-permute-done.57.refs_3_, ...), custom_call_target="tpu_custom_call" | custom-call | flops 100000000 | tf_op jit(solution)/shard_map/pallas_call | solution.py:214
  449.4 12.9 %collective-permute-done.58.refs_3_ = bf16[256,2048]{1,0:T(8,128)(2,1)} collective-permute-done((bf16[256,2048]{1,0:T(8,128)(2,1)}, bf16[256,2048]{1,0:T(8,128)(2,1)}, u32[]{:S(2)}, u32[]{:S(2)}) %collective-permute-start.58) | collective-permute-done | bytes 1048608 | tf_op jit(solution)/shard_map/ppermute | solution.py:57
  462.8 3.3 shard_map.277
  468.4 11.7 %shard_map.279 = (bf16[1024,1536]{1,0:T(8,128)(2,1)}, bf16[1024,1024]{1,0:T(8,128)(2,1)}) custom-call(s32[4]{0:T(128)} %copy-done.50, s32[1]{0:T(128)} %bitcast.12.start, bf16[1024,1536]{1,0:T(8,128)(2,1)} %shard_map.259.packed, bf16[1024,1024]{1,0:T(8,128)(2,1)} %shard_map.260.early, bf16[1024,1024]{1,0:T(8,128)(2,1)} %get-tuple-element.295.weights, ...), custom_call_target="tpu_custom_call" | custom-call | flops 100000000 | tf_op jit(solution)/shard_map/pallas_call | solution.py:526
  480.1 8.2 %shard_map.280.refs_0_.refs_1_ = bf16[512,2048]{1,0:T(8,128)(2,1)} custom-call(bf16[1024,2048]{1,0:T(8,128)(2,1)} %bitcast.58, bf16[1024,1536]{1,0:T(8,128)(2,1)} %get-tuple-element.317.refs_1_.refs_0_, bf16[1024,2048]{1,0:T(8,128)(2,1)} %bitcast.63, bf16[1024,1024]{1,0:T(8,128)(2,1)} %get-tuple-element.304.refs_3_.refs_0_, ...), custom_call_target="tpu_custom_call" | custom-call | flops 100000000 | tf_op jit(solution)/shard_map/pallas_call | solution.py:283
  494.8 2.5 shard_map.281
  499.4 8.7 %shard_map.283 = (bf16[256,2048]{1,0:T(8,128)(2,1)}, bf16[256,2048]{1,0:T(8,128)(2,1)}, bf16[256,2048]{1,0:T(8,128)(2,1)}, bf16[256,2048]{1,0:T(8,128)(2,1)}) custom-call(bf16[1024,1024]{1,0:T(8,128)(2,1)} %get-tuple-element.304.refs_3_.refs_0_, bf16[2048,2048]{1,0:T(8,128)(2,1)} %constant_dynamic-update-slice_fusion.40.refs_1_.mix.refs_4_), custom_call_target="tpu_custom_call" | custom-call | flops 100000000 | tf_op jit(solution)/shard_map/pallas_call | solution.py:214
  508.1 8.2 %shard_map.284.refs_0_ = bf16[512,2048]{1,0:T(8,128)(2,1)} custom-call(bf16[1024,2048]{1,0:T(8,128)(2,1)} %bitcast.59, bf16[1024,1536]{1,0:T(8,128)(2,1)} %get-tuple-element.317.refs_1_.refs_0_, bf16[1024,2048]{1,0:T(8,128)(2,1)} %bitcast.64, bf16[1024,1024]{1,0:T(8,128)(2,1)} %get-tuple-element.304.refs_3_.refs_0_, ...), custom_call_target="tpu_custom_call" | custom-call | flops 100000000 | tf_op jit(solution)/shard_map/pallas_call | solution.py:283
  516.3 6.1 collective-permute-done.64.refs_2_
  523.4 3.2 shard_map.285
  536.6 10.7 %shard_map.287 = (bf16[256,2048]{1,0:T(8,128)(2,1)}, bf16[256,2048]{1,0:T(8,128)(2,1)}, bf16[256,2048]{1,0:T(8,128)(2,1)}, bf16[256,2048]{1,0:T(8,128)(2,1)}) custom-call(bf16[1024,1536]{1,0:T(8,128)(2,1)} %get-tuple-element.317.refs_1_.refs_0_, bf16[2048,2048]{1,0:T(8,128)(2,1)} %constant_dynamic-update-slice_fusion.40.refs_1_.mix.refs_4_), custom_call_target="tpu_custom_call" | custom-call | flops 100000000 | tf_op jit(solution)/shard_map/pallas_call | solution.py:214
  547.2 8.2 %shard_map.288.refs_1_ = bf16[512,2048]{1,0:T(8,128)(2,1)} custom-call(bf16[1024,2048]{1,0:T(8,128)(2,1)} %bitcast.60, bf16[1024,1536]{1,0:T(8,128)(2,1)} %get-tuple-element.317.refs_1_.refs_0_, bf16[1024,2048]{1,0:T(8,128)(2,1)} %bitcast.65, bf16[1024,1024]{1,0:T(8,128)(2,1)} %get-tuple-element.304.refs_3_.refs_0_, ...), custom_call_target="tpu_custom_call" | custom-call | flops 100000000 | tf_op jit(solution)/shard_map/pallas_call | solution.py:283
  556.0 3.3 shard_map.289
  561.4 3.5 shard_map.291
  571.8 9.5 %collective-permute-done.61 = bf16[256,2048]{1,0:T(8,128)(2,1)} collective-permute-done((bf16[256,2048]{1,0:T(8,128)(2,1)}, bf16[256,2048]{1,0:T(8,128)(2,1)}, u32[]{:S(2)}, u32[]{:S(2)}) %collective-permute-start.61) | collective-permute-done | bytes 1048608 | tf_op jit(solution)/shard_map/ppermute | solution.py:314
  582.4 3.0 copy.40
  587.8 3.1 add_add_fusion.refs_0_
  591.0 8.2 %shard_map.290.refs_0_ = bf16[512,2048]{1,0:T(8,128)(2,1)} custom-call(bf16[1024,2048]{1,0:T(8,128)(2,1)} %bitcast.61, bf16[1024,1536]{1,0:T(8,128)(2,1)} %get-tuple-element.317.refs_1_.refs_0_, bf16[1024,2048]{1,0:T(8,128)(2,1)} %bitcast.66, bf16[1024,1024]{1,0:T(8,128)(2,1)} %get-tuple-element.304.refs_3_.refs_0_, ...), custom_call_target="tpu_custom_call" | custom-call | flops 100000000 | tf_op jit(solution)/shard_map/pallas_call | solution.py:283
  599.2 3.4 shard_map.293
  605.0 11.1 %collective-permute-done.76 = bf16[256,2048]{1,0:T(8,128)(2,1)} collective-permute-done((bf16[256,2048]{1,0:T(8,128)(2,1)}, bf16[256,2048]{1,0:T(8,128)(2,1)}, u32[]{:S(2)}, u32[]{:S(2)}) %collective-permute-start.76) | collective-permute-done | bytes 1048608 | tf_op jit(solution)/shard_map/ppermute | solution.py:744
  616.1 5.3 add_reduce_fusion
  624.2 2.6 collective-permute-done.77
  626.9 3.9 fusion.11.refs_0_
  630.8 2.9 shard_map.295
  633.8 2.9 collective-permute-done.80
  638.7 3.1 convert_add_fusion.1
  641.8 2.9 shard_map.294
  645.8 3.3 convert_add_fusion.2
  (411 shorter events, 219.5 us)
Async XLA Ops:
  15.5 25.5 %collective-permute-start.7 = (bf16[256,2048]{1,0:T(8,128)(2,1)}, bf16[256,2048]{1,0:T(8,128)(2,1)}, u32[]{:S(2)}, u32[]{:S(2)}) collective-permute-start(bf16[256,2048]{1,0:T(8,128)(2,1)} %get-tuple-element.182), channel_id=1, source_target_pairs={{8,0},{16,8},{24,16},{28,24},{20,28},{12,20},{4,12},{0,4},{9,1},{1... | collective-permute-start | bytes 3145736 | tf_op jit(solution)/shard_map/ppermute | solution.py:57
  17.1 23.9 %collective-permute-start.6 = (bf16[256,2048]{1,0:T(8,128)(2,1)}, bf16[256,2048]{1,0:T(8,128)(2,1)}, u32[]{:S(2)}, u32[]{:S(2)}) collective-permute-start(bf16[256,2048]{1,0:T(8,128)(2,1)} %get-tuple-element.182), channel_id=1, source_target_pairs={{0,8},{8,16},{16,24},{24,28},{28,20},{20,12},{12,4},{4,0},{1,9},{9... | collective-permute-start | bytes 3145736 | tf_op jit(solution)/shard_map/ppermute | solution.py:57
  21.9 23.0 %collective-permute-start.4 = (bf16[256,2048]{1,0:T(8,128)(2,1)}, bf16[256,2048]{1,0:T(8,128)(2,1)}, u32[]{:S(2)}, u32[]{:S(2)}) collective-permute-start(bf16[256,2048]{1,0:T(8,128)(2,1)} %shard_map.254.refs_0_), channel_id=1, source_target_pairs={{0,2},{1,3},{2,0},{3,1},{4,6},{5,7},{6,4},{7,5},{8,10},{9,11},{10,... | collective-permute-start | bytes 3145736 | tf_op jit(solution)/shard_map/ppermute | solution.py:314
  26.2 37.3 %collective-permute-start.12 = (bf16[256,2048]{1,0:T(8,128)(2,1)}, bf16[256,2048]{1,0:T(8,128)(2,1)S(1)}, u32[]{:S(2)}, u32[]{:S(2)}) collective-permute-start(bf16[256,2048]{1,0:T(8,128)(2,1)} %shard_map.257), channel_id=1, source_target_pairs={{0,4},{4,8},{8,12},{12,16},{16,20},{20,24},{24,28},{1,5},{5,9},{9,... | collective-permute-start | bytes 3145736 | tf_op jit(solution)/shard_map/ppermute | solution.py:603
  41.0 26.8 %collective-permute-start.8 = (bf16[256,2048]{1,0:T(8,128)(2,1)}, bf16[256,2048]{1,0:T(8,128)(2,1)}, u32[]{:S(2)}, u32[]{:S(2)}) collective-permute-start(bf16[256,2048]{1,0:T(8,128)(2,1)} %collective-permute-done.6), channel_id=1, source_target_pairs={{0,8},{8,16},{16,24},{24,28},{28,20},{20,12},{12,4},{4,0},{1,9},{9... | collective-permute-start | bytes 3145736 | tf_op jit(solution)/shard_map/ppermute | solution.py:57
  41.0 41.8 %collective-permute-start.9 = (bf16[256,2048]{1,0:T(8,128)(2,1)}, bf16[256,2048]{1,0:T(8,128)(2,1)}, u32[]{:S(2)}, u32[]{:S(2)}) collective-permute-start(bf16[256,2048]{1,0:T(8,128)(2,1)} %collective-permute-done.7), channel_id=1, source_target_pairs={{8,0},{16,8},{24,16},{28,24},{20,28},{12,20},{4,12},{0,4},{9,1},{1... | collective-permute-start | bytes 3145736 | tf_op jit(solution)/shard_map/ppermute | solution.py:57
  44.8 41.2 %collective-permute-start.3 = (bf16[256,2048]{1,0:T(8,128)(2,1)S(1)}, bf16[256,2048]{1,0:T(8,128)(2,1)}, u32[]{:S(2)}, u32[]{:S(2)}) collective-permute-start(bf16[256,2048]{1,0:T(8,128)(2,1)S(1)} %copy-done.6), channel_id=1, source_target_pairs={{0,1},{1,0},{2,3},{3,2},{4,5},{5,4},{6,7},{7,6},{8,9},{9,8},{10,11... | collective-permute-start | bytes 3145736 | tf_op jit(solution)/shard_map/ppermute | solution.py:314
  44.9 42.6 %collective-permute-start.5 = (bf16[256,2048]{1,0:T(8,128)(2,1)}, bf16[256,2048]{1,0:T(8,128)(2,1)}, u32[]{:S(2)}, u32[]{:S(2)}) collective-permute-start(bf16[256,2048]{1,0:T(8,128)(2,1)} %collective-permute-done.4.refs_2_), channel_id=1, source_target_pairs={{0,1},{1,0},{2,3},{3,2},{4,5},{5,4},{6,7},{7,6},{8,9},{9,8},{10,11... | collective-permute-start | bytes 3145736 | tf_op jit(solution)/shard_map/ppermute | solution.py:314
  63.5 24.1 %collective-permute-start.14 = (bf16[256,2048]{1,0:T(8,128)(2,1)S(1)}, bf16[256,2048]{1,0:T(8,128)(2,1)}, u32[]{:S(2)}, u32[]{:S(2)}) collective-permute-start(bf16[256,2048]{1,0:T(8,128)(2,1)S(1)} %collective-permute-done.12.refs_0_), channel_id=1, source_target_pairs={{0,2},{1,3},{2,0},{3,1},{4,6},{5,7},{6,4},{7,5},{8,10},{9,11},{10,... | collective-permute-start | bytes 3145736 | tf_op jit(solution)/shard_map/ppermute | solution.py:314
  82.9 23.5 %collective-permute-start.16 = (bf16[256,2048]{1,0:T(8,128)(2,1)}, bf16[256,2048]{1,0:T(8,128)(2,1)}, u32[]{:S(2)}, u32[]{:S(2)}) collective-permute-start(bf16[256,2048]{1,0:T(8,128)(2,1)} %collective-permute-done.8), channel_id=1, source_target_pairs={{0,8},{8,16},{16,24},{24,28},{28,20},{20,12},{12,4},{4,0},{1,9},{9... | collective-permute-start | bytes 3145736 | tf_op jit(solution)/shard_map/ppermute | solution.py:57
  82.9 23.5 %collective-permute-start.17 = (bf16[256,2048]{1,0:T(8,128)(2,1)}, bf16[256,2048]{1,0:T(8,128)(2,1)}, u32[]{:S(2)}, u32[]{:S(2)}) collective-permute-start(bf16[256,2048]{1,0:T(8,128)(2,1)} %collective-permute-done.9), channel_id=1, source_target_pairs={{8,0},{16,8},{24,16},{28,24},{20,28},{12,20},{4,12},{0,4},{9,1},{1... | collective-permute-start | bytes 3145736 | tf_op jit(solution)/shard_map/ppermute | solution.py:57
  86.0 25.3 %collective-permute-start.22 = (bf16[256,2048]{1,0:T(8,128)(2,1)}, bf16[256,2048]{1,0:T(8,128)(2,1)}, u32[]{:S(2)}, u32[]{:S(2)}) collective-permute-start(bf16[256,2048]{1,0:T(8,128)(2,1)} %get-tuple-element.202), channel_id=1, source_target_pairs={{0,2},{1,3},{2,0},{3,1},{4,6},{5,7},{6,4},{7,5},{8,10},{9,11},{10,... | collective-permute-start | bytes 3145736 | tf_op jit(solution)/shard_map/ppermute | solution.py:314
  87.6 23.7 %collective-permute-start.13 = (bf16[256,2048]{1,0:T(8,128)(2,1)S(1)}, bf16[256,2048]{1,0:T(8,128)(2,1)}, u32[]{:S(2)}, u32[]{:S(2)}) collective-permute-start(bf16[256,2048]{1,0:T(8,128)(2,1)S(1)} %collective-permute-done.12.refs_0_), channel_id=1, source_target_pairs={{0,1},{1,0},{2,3},{3,2},{4,5},{5,4},{6,7},{7,6},{8,9},{9,8},{10,11... | collective-permute-start | bytes 3145736 | tf_op jit(solution)/shard_map/ppermute | solution.py:314
  87.6 24.2 %collective-permute-start.15 = (bf16[256,2048]{1,0:T(8,128)(2,1)}, bf16[256,2048]{1,0:T(8,128)(2,1)}, u32[]{:S(2)}, u32[]{:S(2)}) collective-permute-start(bf16[256,2048]{1,0:T(8,128)(2,1)} %collective-permute-done.14.refs_2_), channel_id=1, source_target_pairs={{0,1},{1,0},{2,3},{3,2},{4,5},{5,4},{6,7},{7,6},{8,9},{9,8},{10,11... | collective-permute-start | bytes 3145736 | tf_op jit(solution)/shard_map/ppermute | solution.py:314
  106.4 21.7 %collective-permute-start.18 = (bf16[256,2048]{1,0:T(8,128)(2,1)}, bf16[256,2048]{1,0:T(8,128)(2,1)}, u32[]{:S(2)}, u32[]{:S(2)}) collective-permute-start(bf16[256,2048]{1,0:T(8,128)(2,1)} %collective-permute-done.16), channel_id=1, source_target_pairs={{0,8},{8,16},{16,24},{24,28},{28,20},{20,12},{12,4},{4,0},{1,9},{9... | collective-permute-start | bytes 3145736 | tf_op jit(solution)/shard_map/ppermute | solution.py:57
  111.2 43.2 %collective-permute-start.21 = (bf16[256,2048]{1,0:T(8,128)(2,1)S(1)}, bf16[256,2048]{1,0:T(8,128)(2,1)S(1)}, u32[]{:S(2)}, u32[]{:S(2)}) collective-permute-start(bf16[256,2048]{1,0:T(8,128)(2,1)S(1)} %copy-done.19), channel_id=1, source_target_pairs={{0,1},{1,0},{2,3},{3,2},{4,5},{5,4},{6,7},{7,6},{8,9},{9,8},{10,11... | collective-permute-start | bytes 3145736 | tf_op jit(solution)/shard_map/ppermute | solution.py:314
  111.2 43.2 %collective-permute-start.23 = (bf16[256,2048]{1,0:T(8,128)(2,1)}, bf16[256,2048]{1,0:T(8,128)(2,1)}, u32[]{:S(2)}, u32[]{:S(2)}) collective-permute-start(bf16[256,2048]{1,0:T(8,128)(2,1)} %collective-permute-done.22), channel_id=1, source_target_pairs={{0,1},{1,0},{2,3},{3,2},{4,5},{5,4},{6,7},{7,6},{8,9},{9,8},{10,11... | collective-permute-start | bytes 3145736 | tf_op jit(solution)/shard_map/ppermute | solution.py:314
  130.0 24.4 %collective-permute-start.20 = (bf16[256,2048]{1,0:T(8,128)(2,1)}, bf16[256,2048]{1,0:T(8,128)(2,1)}, u32[]{:S(2)}, u32[]{:S(2)}) collective-permute-start(bf16[256,2048]{1,0:T(8,128)(2,1)} %param.26), channel_id=1, source_target_pairs={{0,8},{8,16},{16,24},{24,28},{28,20},{20,12},{12,4},{4,0},{1,9},{9... | collective-permute-start | bytes 3145736 | tf_op jit(solution)/shard_map/ppermute | solution.py:57
  132.0 22.4 %collective-permute-start.24 = (bf16[256,2048]{1,0:T(8,128)(2,1)}, bf16[256,2048]{1,0:T(8,128)(2,1)}, u32[]{:S(2)}, u32[]{:S(2)}) collective-permute-start(bf16[256,2048]{1,0:T(8,128)(2,1)} %collective-permute-done.19), channel_id=1, source_target_pairs={{8,0},{16,8},{24,16},{28,24},{20,28},{12,20},{4,12},{0,4},{9,1},{1... | collective-permute-start | bytes 3145736 | tf_op jit(solution)/shard_map/ppermute | solution.py:57
  154.4 21.8 %collective-permute-start.25 = (bf16[256,2048]{1,0:T(8,128)(2,1)}, bf16[256,2048]{1,0:T(8,128)(2,1)}, u32[]{:S(2)}, u32[]{:S(2)}) collective-permute-start(bf16[256,2048]{1,0:T(8,128)(2,1)} %collective-permute-done.20), channel_id=1, source_target_pairs={{0,8},{8,16},{16,24},{24,28},{28,20},{20,12},{12,4},{4,0},{1,9},{9... | collective-permute-start | bytes 3145736 | tf_op jit(solution)/shard_map/ppermute | solution.py:57
  156.5 22.2 %collective-permute-start.26 = (bf16[256,2048]{1,0:T(8,128)(2,1)}, bf16[256,2048]{1,0:T(8,128)(2,1)}, u32[]{:S(2)}, u32[]{:S(2)}) collective-permute-start(bf16[256,2048]{1,0:T(8,128)(2,1)} %collective-permute-done.24), channel_id=1, source_target_pairs={{8,0},{16,8},{24,16},{28,24},{20,28},{12,20},{4,12},{0,4},{9,1},{1... | collective-permute-start | bytes 3145736 | tf_op jit(solution)/shard_map/ppermute | solution.py:57
  182.5 25.9 %collective-permute-start.32 = (bf16[256,2048]{1,0:T(8,128)(2,1)}, bf16[256,2048]{1,0:T(8,128)(2,1)}, u32[]{:S(2)}, u32[]{:S(2)}) collective-permute-start(bf16[256,2048]{1,0:T(8,128)(2,1)} %collective-permute-done.25), channel_id=1, source_target_pairs={{0,8},{8,16},{16,24},{24,28},{28,20},{20,12},{12,4},{4,0},{1,9},{9... | collective-permute-start | bytes 3145736 | tf_op jit(solution)/shard_map/ppermute | solution.py:57
  184.3 25.6 %collective-permute-start.33 = (bf16[256,2048]{1,0:T(8,128)(2,1)}, bf16[256,2048]{1,0:T(8,128)(2,1)}, u32[]{:S(2)}, u32[]{:S(2)}) collective-permute-start(bf16[256,2048]{1,0:T(8,128)(2,1)} %collective-permute-done.26), channel_id=1, source_target_pairs={{8,0},{16,8},{24,16},{28,24},{20,28},{12,20},{4,12},{0,4},{9,1},{1... | collective-permute-start | bytes 3145736 | tf_op jit(solution)/shard_map/ppermute | solution.py:57
  184.6 27.4 %collective-permute-start.27 = (bf16[256,2048]{1,0:T(8,128)(2,1)}, bf16[256,2048]{1,0:T(8,128)(2,1)S(1)}, u32[]{:S(2)}, u32[]{:S(2)}) collective-permute-start(bf16[256,2048]{1,0:T(8,128)(2,1)} %get-tuple-element.214), channel_id=1, source_target_pairs={{0,1},{1,0},{2,3},{3,2},{4,5},{5,4},{6,7},{7,6},{8,9},{9,8},{10,11... | collective-permute-start | bytes 3145736 | tf_op jit(solution)/shard_map/ppermute | solution.py:314
  188.0 25.8 %collective-permute-start.29 = (bf16[256,2048]{1,0:T(8,128)(2,1)}, bf16[256,2048]{1,0:T(8,128)(2,1)S(1)}, u32[]{:S(2)}, u32[]{:S(2)}) collective-permute-start(bf16[256,2048]{1,0:T(8,128)(2,1)} %shard_map.262), channel_id=1, source_target_pairs={{0,2},{1,3},{2,0},{3,1},{4,6},{5,7},{6,4},{7,5},{8,10},{9,11},{10,... | collective-permute-start | bytes 3145736 | tf_op jit(solution)/shard_map/ppermute | solution.py:314
  209.9 24.6 %collective-permute-start.35 = (bf16[2048,256]{1,0:T(8,128)(2,1)S(1)}, bf16[2048,256]{1,0:T(8,128)(2,1)}, u32[]{:S(2)}, u32[]{:S(2)}) collective-permute-start(bf16[2048,256]{1,0:T(8,128)(2,1)S(1)} %copy-done.17), channel_id=1, source_target_pairs={{8,0},{16,8},{24,16},{28,24},{20,28},{12,20},{4,12},{0,4},{9,1},{1... | collective-permute-start | bytes 3145736 | tf_op jit(solution)/shard_map/ppermute | solution.py:57
  210.2 24.3 %collective-permute-start.34 = (bf16[2048,256]{1,0:T(8,128)(2,1)S(1)}, bf16[2048,256]{1,0:T(8,128)(2,1)}, u32[]{:S(2)}, u32[]{:S(2)}) collective-permute-start(bf16[2048,256]{1,0:T(8,128)(2,1)S(1)} %copy-done.17), channel_id=1, source_target_pairs={{0,8},{8,16},{16,24},{24,28},{28,20},{20,12},{12,4},{4,0},{1,9},{9... | collective-permute-start | bytes 3145736 | tf_op jit(solution)/shard_map/ppermute | solution.py:57
  217.0 24.9 %collective-permute-start.31 = (bf16[256,2048]{1,0:T(8,128)(2,1)S(1)}, bf16[256,2048]{1,0:T(8,128)(2,1)S(1)}, u32[]{:S(2)}, u32[]{:S(2)}) collective-permute-start(bf16[256,2048]{1,0:T(8,128)(2,1)S(1)} %add_convert_fusion.refs_0_), channel_id=1, source_target_pairs={{0,2},{1,3},{2,0},{3,1},{4,6},{5,7},{6,4},{7,5},{8,10},{9,11},{10,... | collective-permute-start | bytes 3145736 | tf_op jit(solution)/shard_map/ppermute | solution.py:314
  241.8 25.9 %collective-permute-start.37 = (bf16[2048,256]{1,0:T(8,128)(2,1)}, bf16[2048,256]{1,0:T(8,128)(2,1)}, u32[]{:S(2)}, u32[]{:S(2)}) collective-permute-start(bf16[2048,256]{1,0:T(8,128)(2,1)} %collective-permute-done.34), channel_id=1, source_target_pairs={{0,8},{8,16},{16,24},{24,28},{28,20},{20,12},{12,4},{4,0},{1,9},{9... | collective-permute-start | bytes 3145736 | tf_op jit(solution)/shard_map/ppermute | solution.py:57
  243.6 25.7 %collective-permute-start.38 = (bf16[2048,256]{1,0:T(8,128)(2,1)}, bf16[2048,256]{1,0:T(8,128)(2,1)}, u32[]{:S(2)}, u32[]{:S(2)}) collective-permute-start(bf16[2048,256]{1,0:T(8,128)(2,1)} %collective-permute-done.35), channel_id=1, source_target_pairs={{8,0},{16,8},{24,16},{28,24},{20,28},{12,20},{4,12},{0,4},{9,1},{1... | collective-permute-start | bytes 3145736 | tf_op jit(solution)/shard_map/ppermute | solution.py:57
  269.3 24.9 %collective-permute-start.39 = (bf16[2048,256]{1,0:T(8,128)(2,1)}, bf16[2048,256]{1,0:T(8,128)(2,1)}, u32[]{:S(2)}, u32[]{:S(2)}) collective-permute-start(bf16[2048,256]{1,0:T(8,128)(2,1)} %collective-permute-done.37), channel_id=1, source_target_pairs={{0,8},{8,16},{16,24},{24,28},{28,20},{20,12},{12,4},{4,0},{1,9},{9... | collective-permute-start | bytes 3145736 | tf_op jit(solution)/shard_map/ppermute | solution.py:57
  271.0 24.5 %collective-permute-start.40 = (bf16[2048,256]{1,0:T(8,128)(2,1)}, bf16[2048,256]{1,0:T(8,128)(2,1)}, u32[]{:S(2)}, u32[]{:S(2)}) collective-permute-start(bf16[2048,256]{1,0:T(8,128)(2,1)} %collective-permute-done.38), channel_id=1, source_target_pairs={{8,0},{16,8},{24,16},{28,24},{20,28},{12,20},{4,12},{0,4},{9,1},{1... | collective-permute-start | bytes 3145736 | tf_op jit(solution)/shard_map/ppermute | solution.py:57
  295.5 24.0 %collective-permute-start.41 = (bf16[256,2048]{1,0:T(8,128)(2,1)}, bf16[256,2048]{1,0:T(8,128)(2,1)}, u32[]{:S(2)}, u32[]{:S(2)}) collective-permute-start(bf16[256,2048]{1,0:T(8,128)(2,1)} %shard_map.265), channel_id=1, source_target_pairs={{8,0},{16,8},{24,16},{28,24},{20,28},{12,20},{4,12},{0,4},{9,1},{1... | collective-permute-start | bytes 3145736 | tf_op jit(solution)/shard_map/ppermute | solution.py:57
  296.4 23.4 %collective-permute-start.42 = (bf16[2048,256]{1,0:T(8,128)(2,1)}, bf16[2048,256]{1,0:T(8,128)(2,1)}, u32[]{:S(2)}, u32[]{:S(2)}) collective-permute-start(bf16[2048,256]{1,0:T(8,128)(2,1)} %collective-permute-done.39), channel_id=1, source_target_pairs={{0,8},{8,16},{16,24},{24,28},{28,20},{20,12},{12,4},{4,0},{1,9},{9... | collective-permute-start | bytes 3145736 | tf_op jit(solution)/shard_map/ppermute | solution.py:57
  322.7 22.4 %collective-permute-start.44 = (bf16[256,2048]{1,0:T(8,128)(2,1)}, bf16[256,2048]{1,0:T(8,128)(2,1)S(1)}, u32[]{:S(2)}, u32[]{:S(2)}) collective-permute-start(bf16[256,2048]{1,0:T(8,128)(2,1)} %get-tuple-element.235), channel_id=1, source_target_pairs={{8,0},{16,8},{24,16},{28,24},{20,28},{12,20},{4,12},{0,4},{9,1},{1... | collective-permute-start | bytes 3145736 | tf_op jit(solution)/shard_map/ppermute | solution.py:57
  323.0 22.4 %collective-permute-start.43 = (bf16[256,2048]{1,0:T(8,128)(2,1)}, bf16[256,2048]{1,0:T(8,128)(2,1)}, u32[]{:S(2)}, u32[]{:S(2)}) collective-permute-start(bf16[256,2048]{1,0:T(8,128)(2,1)} %get-tuple-element.233), channel_id=1, source_target_pairs={{0,8},{8,16},{16,24},{24,28},{28,20},{20,12},{12,4},{4,0},{1,9},{9... | collective-permute-start | bytes 3145736 | tf_op jit(solution)/shard_map/ppermute | solution.py:57
  375.2 25.8 %collective-permute-start.51 = (bf16[256,2048]{1,0:T(8,128)(2,1)}, bf16[256,2048]{1,0:T(8,128)(2,1)S(1)}, u32[]{:S(2)}, u32[]{:S(2)}) collective-permute-start(bf16[256,2048]{1,0:T(8,128)(2,1)} %get-tuple-element.255), channel_id=1, source_target_pairs={{8,0},{16,8},{24,16},{28,24},{20,28},{12,20},{4,12},{0,4},{9,1},{1... | collective-permute-start | bytes 3145736 | tf_op jit(solution)/shard_map/ppermute | solution.py:57
  376.0 25.6 %collective-permute-start.50 = (bf16[256,2048]{1,0:T(8,128)(2,1)}, bf16[256,2048]{1,0:T(8,128)(2,1)}, u32[]{:S(2)}, u32[]{:S(2)}) collective-permute-start(bf16[256,2048]{1,0:T(8,128)(2,1)} %get-tuple-element.253), channel_id=1, source_target_pairs={{0,8},{8,16},{16,24},{24,28},{28,20},{20,12},{12,4},{4,0},{1,9},{9... | collective-permute-start | bytes 3145736 | tf_op jit(solution)/shard_map/ppermute | solution.py:57
  377.2 26.5 %collective-permute-start.47 = (bf16[256,2048]{1,0:T(8,128)(2,1)}, bf16[256,2048]{1,0:T(8,128)(2,1)}, u32[]{:S(2)}, u32[]{:S(2)}) collective-permute-start(bf16[256,2048]{1,0:T(8,128)(2,1)} %get-tuple-element.257), channel_id=1, source_target_pairs={{0,1},{1,0},{2,3},{3,2},{4,5},{5,4},{6,7},{7,6},{8,9},{9,8},{10,11... | collective-permute-start | bytes 3145736 | tf_op jit(solution)/shard_map/ppermute | solution.py:314
  380.6 25.5 %collective-permute-start.49 = (bf16[256,2048]{1,0:T(8,128)(2,1)}, bf16[256,2048]{1,0:T(8,128)(2,1)}, u32[]{:S(2)}, u32[]{:S(2)}) collective-permute-start(bf16[256,2048]{1,0:T(8,128)(2,1)} %shard_map.271), channel_id=1, source_target_pairs={{0,2},{1,3},{2,0},{3,1},{4,6},{5,7},{6,4},{7,5},{8,10},{9,11},{10,... | collective-permute-start | bytes 3145736 | tf_op jit(solution)/shard_map/ppermute | solution.py:314
  401.5 24.7 %collective-permute-start.53 = (bf16[256,2048]{1,0:T(8,128)(2,1)}, bf16[256,2048]{1,0:T(8,128)(2,1)}, u32[]{:S(2)}, u32[]{:S(2)}) collective-permute-start(bf16[256,2048]{1,0:T(8,128)(2,1)} %get-tuple-element.265), channel_id=1, source_target_pairs={{8,0},{16,8},{24,16},{28,24},{20,28},{12,20},{4,12},{0,4},{9,1},{1... | collective-permute-start | bytes 3145736 | tf_op jit(solution)/shard_map/ppermute | solution.py:57
  402.4 24.6 %collective-permute-start.52 = (bf16[256,2048]{1,0:T(8,128)(2,1)}, bf16[256,2048]{1,0:T(8,128)(2,1)}, u32[]{:S(2)}, u32[]{:S(2)}) collective-permute-start(bf16[256,2048]{1,0:T(8,128)(2,1)} %get-tuple-element.263), channel_id=1, source_target_pairs={{0,8},{8,16},{16,24},{24,28},{28,20},{20,12},{12,4},{4,0},{1,9},{9... | collective-permute-start | bytes 3145736 | tf_op jit(solution)/shard_map/ppermute | solution.py:57
  412.0 24.4 %collective-permute-start.56 = (bf16[256,2048]{1,0:T(8,128)(2,1)S(1)}, bf16[256,2048]{1,0:T(8,128)(2,1)S(1)}, u32[]{:S(2)}, u32[]{:S(2)}) collective-permute-start(bf16[256,2048]{1,0:T(8,128)(2,1)S(1)} %get-tuple-element.280.refs_0_), channel_id=1, source_target_pairs={{0,2},{1,3},{2,0},{3,1},{4,6},{5,7},{6,4},{7,5},{8,10},{9,11},{10,... | collective-permute-start | bytes 3145736 | tf_op jit(solution)/shard_map/ppermute | solution.py:314
  412.9 28.9 %collective-permute-start.55 = (bf16[256,2048]{1,0:T(8,128)(2,1)S(1)}, bf16[256,2048]{1,0:T(8,128)(2,1)}, u32[]{:S(2)}, u32[]{:S(2)}) collective-permute-start(bf16[256,2048]{1,0:T(8,128)(2,1)S(1)} %get-tuple-element.280.refs_0_), channel_id=1, source_target_pairs={{0,1},{1,0},{2,3},{3,2},{4,5},{5,4},{6,7},{7,6},{8,9},{9,8},{10,11... | collective-permute-start | bytes 3145736 | tf_op jit(solution)/shard_map/ppermute | solution.py:314
  436.4 25.9 %collective-permute-start.58 = (bf16[256,2048]{1,0:T(8,128)(2,1)}, bf16[256,2048]{1,0:T(8,128)(2,1)}, u32[]{:S(2)}, u32[]{:S(2)}) collective-permute-start(bf16[256,2048]{1,0:T(8,128)(2,1)} %get-tuple-element.277), channel_id=1, source_target_pairs={{8,0},{16,8},{24,16},{28,24},{20,28},{12,20},{4,12},{0,4},{9,1},{1... | collective-permute-start | bytes 3145736 | tf_op jit(solution)/shard_map/ppermute | solution.py:57
  437.2 25.6 %collective-permute-start.54 = (bf16[256,2048]{1,0:T(8,128)(2,1)}, bf16[256,2048]{1,0:T(8,128)(2,1)}, u32[]{:S(2)}, u32[]{:S(2)}) collective-permute-start(bf16[256,2048]{1,0:T(8,128)(2,1)} %get-tuple-element.275), channel_id=1, source_target_pairs={{0,8},{8,16},{16,24},{24,28},{28,20},{20,12},{12,4},{4,0},{1,9},{9... | collective-permute-start | bytes 3145736 | tf_op jit(solution)/shard_map/ppermute | solution.py:57
  466.1 24.2 %collective-permute-start.60 = (bf16[256,2048]{1,0:T(8,128)(2,1)}, bf16[256,2048]{1,0:T(8,128)(2,1)S(1)}, u32[]{:S(2)}, u32[]{:S(2)}) collective-permute-start(bf16[256,2048]{1,0:T(8,128)(2,1)} %get-tuple-element.294), channel_id=1, source_target_pairs={{0,1},{1,0},{2,3},{3,2},{4,5},{5,4},{6,7},{7,6},{8,9},{9,8},{10,11... | collective-permute-start | bytes 3145736 | tf_op jit(solution)/shard_map/ppermute | solution.py:314
  466.1 27.7 %collective-permute-start.63 = (bf16[256,2048]{1,0:T(8,128)(2,1)}, bf16[256,2048]{1,0:T(8,128)(2,1)S(1)}, u32[]{:S(2)}, u32[]{:S(2)}) collective-permute-start(bf16[256,2048]{1,0:T(8,128)(2,1)} %get-tuple-element.290), channel_id=1, source_target_pairs={{8,0},{16,8},{24,16},{28,24},{20,28},{12,20},{4,12},{0,4},{9,1},{1... | collective-permute-start | bytes 3145736 | tf_op jit(solution)/shard_map/ppermute | solution.py:57
  467.0 26.8 %collective-permute-start.62 = (bf16[256,2048]{1,0:T(8,128)(2,1)}, bf16[256,2048]{1,0:T(8,128)(2,1)S(1)}, u32[]{:S(2)}, u32[]{:S(2)}) collective-permute-start(bf16[256,2048]{1,0:T(8,128)(2,1)} %get-tuple-element.288), channel_id=1, source_target_pairs={{0,8},{8,16},{16,24},{24,28},{28,20},{20,12},{12,4},{4,0},{1,9},{9... | collective-permute-start | bytes 3145736 | tf_op jit(solution)/shard_map/ppermute | solution.py:57
  497.3 25.0 %collective-permute-start.64 = (bf16[256,2048]{1,0:T(8,128)(2,1)S(1)}, bf16[256,2048]{1,0:T(8,128)(2,1)S(1)}, u32[]{:S(2)}, u32[]{:S(2)}) collective-permute-start(bf16[256,2048]{1,0:T(8,128)(2,1)S(1)} %copy-done.35), channel_id=1, source_target_pairs={{8,0},{16,8},{24,16},{28,24},{20,28},{12,20},{4,12},{0,4},{9,1},{1... | collective-permute-start | bytes 3145736 | tf_op jit(solution)/shard_map/ppermute | solution.py:57
  498.2 24.9 %collective-permute-start.65 = (bf16[256,2048]{1,0:T(8,128)(2,1)}, bf16[256,2048]{1,0:T(8,128)(2,1)S(1)}, u32[]{:S(2)}, u32[]{:S(2)}) collective-permute-start(bf16[256,2048]{1,0:T(8,128)(2,1)} %shard_map.281), channel_id=1, source_target_pairs={{0,8},{8,16},{16,24},{24,28},{28,20},{20,12},{12,4},{4,0},{1,9},{9... | collective-permute-start | bytes 3145736 | tf_op jit(solution)/shard_map/ppermute | solution.py:57
  526.8 28.7 %collective-permute-start.68 = (bf16[256,2048]{1,0:T(8,128)(2,1)}, bf16[256,2048]{1,0:T(8,128)(2,1)}, u32[]{:S(2)}, u32[]{:S(2)}) collective-permute-start(bf16[256,2048]{1,0:T(8,128)(2,1)} %get-tuple-element.314), channel_id=1, source_target_pairs={{8,0},{16,8},{24,16},{28,24},{20,28},{12,20},{4,12},{0,4},{9,1},{1... | collective-permute-start | bytes 3145736 | tf_op jit(solution)/shard_map/ppermute | solution.py:57
  528.1 28.0 %collective-permute-start.67 = (bf16[256,2048]{1,0:T(8,128)(2,1)}, bf16[256,2048]{1,0:T(8,128)(2,1)}, u32[]{:S(2)}, u32[]{:S(2)}) collective-permute-start(bf16[256,2048]{1,0:T(8,128)(2,1)} %get-tuple-element.312), channel_id=1, source_target_pairs={{0,8},{8,16},{16,24},{24,28},{28,20},{20,12},{12,4},{4,0},{1,9},{9... | collective-permute-start | bytes 3145736 | tf_op jit(solution)/shard_map/ppermute | solution.py:57
  529.1 30.3 %collective-permute-start.70 = (bf16[256,2048]{1,0:T(8,128)(2,1)}, bf16[256,2048]{1,0:T(8,128)(2,1)S(1)}, u32[]{:S(2)}, u32[]{:S(2)}) collective-permute-start(bf16[256,2048]{1,0:T(8,128)(2,1)} %get-tuple-element.331), channel_id=1, source_target_pairs={{0,1},{1,0},{2,3},{3,2},{4,5},{5,4},{6,7},{7,6},{8,9},{9,8},{10,11... | collective-permute-start | bytes 3145736 | tf_op jit(solution)/shard_map/ppermute | solution.py:314
  533.0 26.4 %collective-permute-start.71 = (bf16[256,2048]{1,0:T(8,128)(2,1)}, bf16[256,2048]{1,0:T(8,128)(2,1)S(1)}, u32[]{:S(2)}, u32[]{:S(2)}) collective-permute-start(bf16[256,2048]{1,0:T(8,128)(2,1)} %shard_map.286), channel_id=1, source_target_pairs={{0,2},{1,3},{2,0},{3,1},{4,6},{5,7},{6,4},{7,5},{8,10},{9,11},{10,... | collective-permute-start | bytes 3145736 | tf_op jit(solution)/shard_map/ppermute | solution.py:314
  536.5 35.3 %collective-permute-start.59 = (bf16[256,2048]{1,0:T(8,128)(2,1)}, bf16[256,2048]{1,0:T(8,128)(2,1)}, u32[]{:S(2)}, u32[]{:S(2)}) collective-permute-start(bf16[256,2048]{1,0:T(8,128)(2,1)} %get-tuple-element.292), channel_id=1, source_target_pairs={{0,1},{1,0},{2,3},{3,2},{4,5},{5,4},{6,7},{7,6},{8,9},{9,8},{10,11... | collective-permute-start | bytes 3145736 | tf_op jit(solution)/shard_map/ppermute | solution.py:314
  555.5 25.9 %collective-permute-start.61 = (bf16[256,2048]{1,0:T(8,128)(2,1)}, bf16[256,2048]{1,0:T(8,128)(2,1)}, u32[]{:S(2)}, u32[]{:S(2)}) collective-permute-start(bf16[256,2048]{1,0:T(8,128)(2,1)} %shard_map.278), channel_id=1, source_target_pairs={{0,2},{1,3},{2,0},{3,1},{4,6},{5,7},{6,4},{7,5},{8,10},{9,11},{10,... | collective-permute-start | bytes 3145736 | tf_op jit(solution)/shard_map/ppermute | solution.py:314
  566.0 33.2 %collective-permute-start.73 = (bf16[256,2048]{1,0:T(8,128)(2,1)}, bf16[256,2048]{1,0:T(8,128)(2,1)}, u32[]{:S(2)}, u32[]{:S(2)}) collective-permute-start(bf16[256,2048]{1,0:T(8,128)(2,1)} %get-tuple-element.325), channel_id=1, source_target_pairs={{8,0},{16,8},{24,16},{28,24},{20,28},{12,20},{4,12},{0,4},{9,1},{1... | collective-permute-start | bytes 3145736 | tf_op jit(solution)/shard_map/ppermute | solution.py:57
  567.3 32.0 %collective-permute-start.69 = (bf16[256,2048]{1,0:T(8,128)(2,1)}, bf16[256,2048]{1,0:T(8,128)(2,1)}, u32[]{:S(2)}, u32[]{:S(2)}) collective-permute-start(bf16[256,2048]{1,0:T(8,128)(2,1)} %get-tuple-element.323), channel_id=1, source_target_pairs={{0,8},{8,16},{16,24},{24,28},{28,20},{20,12},{12,4},{4,0},{1,9},{9... | collective-permute-start | bytes 3145736 | tf_op jit(solution)/shard_map/ppermute | solution.py:57
  568.1 48.0 %collective-permute-start.76 = (bf16[256,2048]{1,0:T(8,128)(2,1)}, bf16[256,2048]{1,0:T(8,128)(2,1)}, u32[]{:S(2)}, u32[]{:S(2)}) collective-permute-start(bf16[256,2048]{1,0:T(8,128)(2,1)} %shard_map.291), channel_id=1, source_target_pairs={{4,0},{8,4},{12,8},{16,12},{20,16},{24,20},{28,24},{5,1},{9,5},{13... | collective-permute-start | bytes 3145736 | tf_op jit(solution)/shard_map/ppermute | solution.py:744
  571.8 33.2 %collective-permute-start.74 = (bf16[256,2048]{1,0:T(8,128)(2,1)}, bf16[256,2048]{1,0:T(8,128)(2,1)}, u32[]{:S(2)}, u32[]{:S(2)}) collective-permute-start(bf16[256,2048]{1,0:T(8,128)(2,1)} %get-tuple-element.345), channel_id=1, source_target_pairs={{0,1},{1,0},{2,3},{3,2},{4,5},{5,4},{6,7},{7,6},{8,9},{9,8},{10,11... | collective-permute-start | bytes 3145736 | tf_op jit(solution)/shard_map/ppermute | solution.py:314
  581.3 34.8 %collective-permute-start.75 = (bf16[256,2048]{1,0:T(8,128)(2,1)}, bf16[256,2048]{1,0:T(8,128)(2,1)}, u32[]{:S(2)}, u32[]{:S(2)}) collective-permute-start(bf16[256,2048]{1,0:T(8,128)(2,1)} %shard_map.292), channel_id=1, source_target_pairs={{0,2},{1,3},{2,0},{3,1},{4,6},{5,7},{6,4},{7,5},{8,10},{9,11},{10,... | collective-permute-start | bytes 3145736 | tf_op jit(solution)/shard_map/ppermute | solution.py:314
  602.7 34.0 %collective-permute-start.80 = (bf16[256,2048]{1,0:T(8,128)(2,1)}, bf16[256,2048]{1,0:T(8,128)(2,1)}, u32[]{:S(2)}, u32[]{:S(2)}) collective-permute-start(bf16[256,2048]{1,0:T(8,128)(2,1)} %get-tuple-element.342), channel_id=1, source_target_pairs={{8,0},{16,8},{24,16},{28,24},{20,28},{12,20},{4,12},{0,4},{9,1},{1... | collective-permute-start | bytes 3145736 | tf_op jit(solution)/shard_map/ppermute | solution.py:57
  604.2 33.5 %collective-permute-start.79 = (bf16[256,2048]{1,0:T(8,128)(2,1)}, bf16[256,2048]{1,0:T(8,128)(2,1)}, u32[]{:S(2)}, u32[]{:S(2)}) collective-permute-start(bf16[256,2048]{1,0:T(8,128)(2,1)} %get-tuple-element.340), channel_id=1, source_target_pairs={{0,8},{8,16},{16,24},{24,28},{28,20},{20,12},{12,4},{4,0},{1,9},{9... | collective-permute-start | bytes 3145736 | tf_op jit(solution)/shard_map/ppermute | solution.py:57
  (74 other events, 791.3 us)

commit v5 on v4

--- a/solution.py
+++ b/solution.py
@@ -737,17 +737,17 @@
     grad_own = matmul([tie(g_packed, *sent)], mix_in, finish_parts, ["parts"], nt=True)
     pairs[0] = (tie(normed, grad_own[0]), *pairs[0][1:])
     late["mix"].append(mix_piece(3, TILE))
-    ring.due(late["mix"][2][0])
+    result = resid + result + down_shift
+    ring.due(late["mix"][2][0], result)
     ring.advance()
     moved = reorder(ring.now(*back), back_order)
-    grad_own = batch_scatter(tie(grad_own, moved), ring.due)
+    grad_own = batch_scatter(ring.now(*grad_own), ring.due)
     moved = lax.ppermute(moved, "seq", [(i + 1, i) for i in range(count - 1)])
     back = sum(v.astype(F32) for v in back)
     pairs[0] = (ring.now(normed), *pairs[0][1:])
     late["mix"].append(mix_piece(0, TILE))
     ring.due(late["mix"][3][0])
     ring.advance()
-    result = resid + result + down_shift
     block_out = reorder(ring.now(result).astype(BF16), from_slots)
     while any(ring.queue.values()):
         ring.advance()
@@ -776,7 +776,9 @@
         ]
     )
     grad_tokens = reorder(grad_tokens.astype(BF16), from_slots)
-    sums, flat = small_totals(sums, flat, [*ring.last.values(), grad_tokens])
+    grad_w_fc = g_up.total(ring)
+    after = [*ring.last.values(), grad_tokens, block_out, grad_w_fc]
+    sums, flat = small_totals(sums, flat, after)
     grad_mix_in = g_mix.total(ring)
     return (
         block_out[None],
@@ -789,7 +791,7 @@
         sums[2],
         sums[3],
         sums[4],
-        g_up.total(ring),
+        grad_w_fc,
         flat[:ff],
         grad_w_proj,
         sums[5],

time: 666 us -> 662 us (level)
  waiting for transfers between devices: 174 us -> 165 us
  starting transfers between devices: 75.6 us -> 82.8 us
    ppermute x40, waiting for transfers between devices: 32.6 us -> 25 us  [swap(): lax.ppermute(value, axis, [(i, i ^ bit) for i in range(lax.axis_size(axis...]
    ppermute x40, starting transfers between devices: 25.2 us -> 32.1 us  [swap(): lax.ppermute(value, axis, [(i, i ^ bit) for i in range(lax.axis_size(axis...]
    unnamed x137 -> x125, local copies, waits for them, and re-layouts: 66.5 us -> 63.1 us
  transfers between devices with their start and end apart: 84 -> 84, of which waited for: 43 -> 44; matrix products, arithmetic and copies ran while one was open for 19% -> 19% of each run, Pallas kernels for 38% -> 39%
where the time goes in v5:
time: 662 us; the launch traced here: 652 us
  Pallas kernels  271 us (41%)
  waiting for transfers between devices  165 us (25%)
  local copies, waits for them, and re-layouts  89.5 us (14%)
  starting transfers between devices  82.8 us (13%)
  other arithmetic  41.7 us (6%)
    ppermute x42, waiting for transfers between devices, hop(): self.last[forward] = lax.ppermute(value, 'seq', list(pairs))  111 us
    pallas_call x9, Pallas kernels, matmul(): pl.pallas_call(kernel, grid=(tiles,), in_specs=[pl.BlockSpec(v.shape, lam...  106 us
    unnamed x125, local copies, waits for them, and re-layouts  63.1 us
    pallas_call x6, Pallas kernels, token_products(): pl.pallas_call(kernel, grid=(len(plan),), in_specs=specs, out_specs=pl.Bl...  60.1 us
    ppermute x42, starting transfers between devices, hop(): self.last[forward] = lax.ppermute(value, 'seq', list(pairs))  45.8 us
    pallas_call x12, Pallas kernels, join(): pl.pallas_call(kernel, grid=(steps,), in_specs=[pl.BlockSpec((step, width...  35.6 us
    ppermute x40, starting transfers between devices, swap(): lax.ppermute(value, axis, [(i, i ^ bit) for i in range(lax.axis_size(axis...  32.1 us
    pallas_call x2, Pallas kernels, per_chain(): pl.pallas_call(kernel, grid_spec=pltpu.PrefetchScalarGridSpec(num_scalar_...  26.6 us
  transfers between devices with their start and end apart: 84, of which 44 were waited for; matrix products, arithmetic and copies ran while one was open for 19% of the time, Pallas kernels for 39%

profile of v5, /device:TPU:0, one launch (start us, length us, event | category | flops | bytes accessed | tf_op | source)
XLA Modules:
  0.0 651.9 jit_solution(2195045617407414555)
XLA Ops:
  1.4 3.0 collective-permute-start
  10.9 2.7 collective-permute-start.2
  19.2 2.8 shard_map.254.refs_0_
  23.5 2.7 shard_map.257
  26.2 3.4 collective-permute-start.12
  29.9 11.1 %collective-permute-done.7 = bf16[256,2048]{1,0:T(8,128)(2,1)} collective-permute-done((bf16[256,2048]{1,0:T(8,128)(2,1)}, bf16[256,2048]{1,0:T(8,128)(2,1)}, u32[]{:S(2)}, u32[]{:S(2)}) %collective-permute-start.7) | collective-permute-done | bytes 1048608 | tf_op jit(solution)/shard_map/ppermute | solution.py:57
  45.3 18.2 %collective-permute-done.12.refs_0_ = bf16[256,2048]{1,0:T(8,128)(2,1)S(1)} collective-permute-done((bf16[256,2048]{1,0:T(8,128)(2,1)}, bf16[256,2048]{1,0:T(8,128)(2,1)S(1)}, u32[]{:S(2)}, u32[]{:S(2)}) %collective-permute-start.12) | collective-permute-done | bytes 1048608 | tf_op jit(solution)/shard_map/ppermute | solution.py:603
  65.1 2.8 shard_map.255
  71.0 11.9 %collective-permute-done.9 = bf16[256,2048]{1,0:T(8,128)(2,1)} collective-permute-done((bf16[256,2048]{1,0:T(8,128)(2,1)}, bf16[256,2048]{1,0:T(8,128)(2,1)}, u32[]{:S(2)}, u32[]{:S(2)}) %collective-permute-start.9) | collective-permute-done | bytes 1048608 | tf_op jit(solution)/shard_map/ppermute | solution.py:57
  92.2 6.1 shard_map.256
  100.7 5.7 collective-permute-done.16
  106.4 2.6 collective-permute-start.18
  111.8 6.2 shard_map.258
  134.9 10.9 %shard_map.259.packed = bf16[1024,1536]{1,0:T(8,128)(2,1)} custom-call(bf16[1024,2048]{1,0:T(8,128)(2,1)} %bitcast.57, bf16[2048,2048]{1,0:T(8,128)(2,1)} %constant_dynamic-update-slice_fusion.40.refs_1_.mix.refs_4_, f32[1,1536]{1,0:T(1,128)} %copy-done.38), custom_call_target="tpu_custom_call" | custom-call | flops 100000000 | tf_op jit(solution)/shard_map/pallas_call | solution.py:214
  145.8 8.5 %shard_map.260.early = bf16[1024,1024]{1,0:T(8,128)(2,1)} custom-call(bf16[1024,2048]{1,0:T(8,128)(2,1)} %bitcast.62, bf16[2048,2048]{1,0:T(8,128)(2,1)} %constant_dynamic-update-slice_fusion.40.refs_1_.mix.refs_4_, f32[1,1024]{1,0:T(1,128)} %slice.227.refs_2_), custom_call_target="tpu_custom_call" | custom-call | flops 100000000 | tf_op jit(solution)/shard_map/pallas_call | solution.py:214
  156.7 14.9 %shard_map.261 = (bf16[1024,512]{1,0:T(8,128)(2,1)}, bf16[1024,1024]{1,0:T(8,128)(2,1)}, bf16[256,2048]{1,0:T(8,128)(2,1)}, bf16[256,2048]{1,0:T(8,128)(2,1)}, b...) custom-call(s32[4]{0:T(128)} %copy-done.43, s32[1]{0:T(128)} %bitcast.12.start, ...), custom_call_target="tpu_custom_call" | custom-call | flops 100000000 | tf_op jit(solution)/shard_map/pallas_call | solution.py:526
  171.7 4.8 collective-permute-done.25
  200.4 8.2 %collective-permute-done.32 = bf16[256,2048]{1,0:T(8,128)(2,1)} collective-permute-done((bf16[256,2048]{1,0:T(8,128)(2,1)}, bf16[256,2048]{1,0:T(8,128)(2,1)}, u32[]{:S(2)}, u32[]{:S(2)}) %collective-permute-start.32) | collective-permute-done | bytes 1048608 | tf_op jit(solution)/shard_map/ppermute | solution.py:57
  229.5 5.1 collective-permute-done.35
  234.6 7.4 %collective-permute-done.31.refs_2_ = bf16[256,2048]{1,0:T(8,128)(2,1)S(1)} collective-permute-done((bf16[256,2048]{1,0:T(8,128)(2,1)S(1)}, bf16[256,2048]{1,0:T(8,128)(2,1)S(1)}, u32[]{:S(2)}, u32[]{:S(2)}) %collective-permute-start.31) | collective-permute-done | bytes 1048608 | tf_op jit(solution)/shard_map/ppermute | solution.py:314
  246.8 19.1 %shard_map.263 = (bf16[1024,2048]{1,0:T(8,128)(2,1)}, bf16[1024,2048]{1,0:T(8,128)(2,1)}, bf16[1024,2048]{1,0:T(8,128)(2,1)}) custom-call(bf16[256,2048]{1,0:T(8,128)(2,1)} %copy-done.22, bf16[256,2048]{1,0:T(8,128)(2,1)} %copy-done.36, bf16[256,2048]{1,0:T(8,128)(2,1)} %copy-done.35, bf16[256,2048]{1,0:T(8,128)(2,1)} %copy-done.37, ...), custom_call_target="tpu_custom_call" | custom-call | flops 100000000 | tf_op jit(solution)/shard_map/pallas_call | solution.py:214
  277.3 13.5 %shard_map.264.refs_0_.refs_1_ = bf16[2048,2048]{1,0:T(8,128)(2,1)} custom-call(bf16[1024,2048]{1,0:T(8,128)(2,1)} %constant_dynamic-update-slice_fusion.19.refs_0_, bf16[1024,2048]{1,0:T(8,128)(2,1)} %get-tuple-element.267.refs_1_.refs_0_), custom_call_target="tpu_custom_call" | custom-call | flops 100000000 | tf_op jit(solution)/shard_map/pallas_call | solution.py:283
  308.7 11.1 %collective-permute-done.41.refs_2_ = bf16[256,2048]{1,0:T(8,128)(2,1)} collective-permute-done((bf16[256,2048]{1,0:T(8,128)(2,1)}, bf16[256,2048]{1,0:T(8,128)(2,1)}, u32[]{:S(2)}, u32[]{:S(2)}) %collective-permute-start.41) | collective-permute-done | bytes 1048608 | tf_op jit(solution)/shard_map/ppermute | solution.py:57
  320.0 2.9 shard_map.266
  327.2 14.8 %shard_map.267 = (bf16[1024,2048]{1,0:T(8,128)(2,1)}, f32[1,2048]{1,0:T(1,128)}) custom-call(bf16[1024,2048]{1,0:T(8,128)(2,1)} %constant_dynamic-update-slice_fusion.19.refs_0_, bf16[2048,2048]{1,0:T(8,128)(2,1)} %constant_dynamic-update-slice_fusion.39.refs_1_, bf16[1024,2048]{1,0:T(8,128)(2,1)} %get-tuple-element.237.refs_2_), custom_call_target="tpu_custom_call" | custom-call | flops 100000000 | tf_op jit(solution)/shard_map/pallas_call | solution.py:214
  342.0 3.3 collective-permute-done.44.refs_3_
  346.2 3.3 shard_map.268
  351.6 13.1 %shard_map.269 = (bf16[256,2048]{1,0:T(8,128)(2,1)}, bf16[256,2048]{1,0:T(8,128)(2,1)}, bf16[256,2048]{1,0:T(8,128)(2,1)}, bf16[256,2048]{1,0:T(8,128)(2,1)}) custom-call(bf16[1024,2048]{1,0:T(8,128)(2,1)} %get-tuple-element.245.refs_0_.refs_1_, bf16[2048,2048]{1,0:T(8,128)(2,1)} %constant_dynamic-update-slice_fusion.23.refs_4_.refs_1_), custom_call_target="tpu_custom_call" | custom-call | flops 100000000 | tf_op jit(solution)/shard_map/pallas_call | solution.py:214
  364.7 6.5 collective-permute-done.46.refs_3_
  372.1 3.3 shard_map.270
  381.3 13.5 %shard_map.272.refs_0_.refs_1_ = bf16[2048,2048]{1,0:T(8,128)(2,1)} custom-call(bf16[1024,2048]{1,0:T(8,128)(2,1)} %get-tuple-element.261.refs_0_, bf16[1024,2048]{1,0:T(8,128)(2,1)} %get-tuple-element.245.refs_0_.refs_1_), custom_call_target="tpu_custom_call" | custom-call | flops 100000000 | tf_op jit(solution)/shard_map/pallas_call | solution.py:283
  394.8 2.6 shard_map.273
  397.4 3.7 collective-permute-done.51
  412.8 13.0 %shard_map.274 = (bf16[256,2048]{1,0:T(8,128)(2,1)}, bf16[256,2048]{1,0:T(8,128)(2,1)}, bf16[256,2048]{1,0:T(8,128)(2,1)}, bf16[256,2048]{1,0:T(8,128)(2,1)}) custom-call(bf16[1024,2048]{1,0:T(8,128)(2,1)} %get-tuple-element.267.refs_1_.refs_0_, bf16[2048,2048]{1,0:T(8,128)(2,1)} %constant_dynamic-update-slice_fusion.39.refs_1_), custom_call_target="tpu_custom_call" | custom-call | flops 100000000 | tf_op jit(solution)/shard_map/pallas_call | solution.py:214
  427.0 3.3 shard_map.275
  430.3 6.5 collective-permute-done.56.refs_2_
  438.8 3.7 add_bitcast_fusion
  442.5 7.7 %shard_map.276 = (bf16[1024,512]{1,0:T(8,128)(2,1)}, bf16[1024,2048]{1,0:T(8,128)(2,1)}) custom-call(bf16[256,2048]{1,0:T(8,128)(2,1)} %copy-done.21, bf16[256,2048]{1,0:T(8,128)(2,1)} %collective-permute-done.55.refs_1_, bf16[256,2048]{1,0:T(8,128)(2,1)} %collective-permute-done.56.refs_2_, bf16[256,2048]{1,0:T(8,128)(2,1)} %collective-permute-done.57.refs_3_, ...), custom_call_target="tpu_custom_call" | custom-call | flops 100000000 | tf_op jit(solution)/shard_map/pallas_call | solution.py:214
  450.2 12.5 %collective-permute-done.58.refs_3_ = bf16[256,2048]{1,0:T(8,128)(2,1)} collective-permute-done((bf16[256,2048]{1,0:T(8,128)(2,1)}, bf16[256,2048]{1,0:T(8,128)(2,1)}, u32[]{:S(2)}, u32[]{:S(2)}) %collective-permute-start.58) | collective-permute-done | bytes 1048608 | tf_op jit(solution)/shard_map/ppermute | solution.py:57
  463.2 3.3 shard_map.277
  468.7 11.7 %shard_map.279 = (bf16[1024,1536]{1,0:T(8,128)(2,1)}, bf16[1024,1024]{1,0:T(8,128)(2,1)}) custom-call(s32[4]{0:T(128)} %copy-done.43, s32[1]{0:T(128)} %bitcast.12.start, bf16[1024,1536]{1,0:T(8,128)(2,1)} %shard_map.259.packed, bf16[1024,1024]{1,0:T(8,128)(2,1)} %shard_map.260.early, bf16[1024,1024]{1,0:T(8,128)(2,1)} %get-tuple-element.295.weights, ...), custom_call_target="tpu_custom_call" | custom-call | flops 100000000 | tf_op jit(solution)/shard_map/pallas_call | solution.py:526
  480.4 8.3 %shard_map.280.refs_0_.refs_1_ = bf16[512,2048]{1,0:T(8,128)(2,1)} custom-call(bf16[1024,2048]{1,0:T(8,128)(2,1)} %bitcast.58, bf16[1024,1536]{1,0:T(8,128)(2,1)} %get-tuple-element.317.refs_1_.refs_0_, bf16[1024,2048]{1,0:T(8,128)(2,1)} %bitcast.63, bf16[1024,1024]{1,0:T(8,128)(2,1)} %get-tuple-element.304.refs_3_.refs_0_, ...), custom_call_target="tpu_custom_call" | custom-call | flops 100000000 | tf_op jit(solution)/shard_map/pallas_call | solution.py:283
  493.3 2.8 shard_map.281
  500.0 8.6 %shard_map.283 = (bf16[256,2048]{1,0:T(8,128)(2,1)}, bf16[256,2048]{1,0:T(8,128)(2,1)}, bf16[256,2048]{1,0:T(8,128)(2,1)}, bf16[256,2048]{1,0:T(8,128)(2,1)}) custom-call(bf16[1024,1024]{1,0:T(8,128)(2,1)} %get-tuple-element.304.refs_3_.refs_0_, bf16[2048,2048]{1,0:T(8,128)(2,1)} %constant_dynamic-update-slice_fusion.40.refs_1_.mix.refs_4_), custom_call_target="tpu_custom_call" | custom-call | flops 100000000 | tf_op jit(solution)/shard_map/pallas_call | solution.py:214
  508.6 8.3 %shard_map.284.refs_0_ = bf16[512,2048]{1,0:T(8,128)(2,1)} custom-call(bf16[1024,2048]{1,0:T(8,128)(2,1)} %bitcast.59, bf16[1024,1536]{1,0:T(8,128)(2,1)} %get-tuple-element.317.refs_1_.refs_0_, bf16[1024,2048]{1,0:T(8,128)(2,1)} %bitcast.64, bf16[1024,1024]{1,0:T(8,128)(2,1)} %get-tuple-element.304.refs_3_.refs_0_, ...), custom_call_target="tpu_custom_call" | custom-call | flops 100000000 | tf_op jit(solution)/shard_map/pallas_call | solution.py:283
  516.9 4.5 collective-permute-done.64.refs_2_
  521.5 3.2 shard_map.285
  528.2 3.6 add_add_fusion.refs_0_
  535.9 10.6 %shard_map.287 = (bf16[256,2048]{1,0:T(8,128)(2,1)}, bf16[256,2048]{1,0:T(8,128)(2,1)}, bf16[256,2048]{1,0:T(8,128)(2,1)}, bf16[256,2048]{1,0:T(8,128)(2,1)}) custom-call(bf16[1024,1536]{1,0:T(8,128)(2,1)} %get-tuple-element.317.refs_1_.refs_0_, bf16[2048,2048]{1,0:T(8,128)(2,1)} %constant_dynamic-update-slice_fusion.40.refs_1_.mix.refs_4_), custom_call_target="tpu_custom_call" | custom-call | flops 100000000 | tf_op jit(solution)/shard_map/pallas_call | solution.py:214
  546.5 8.2 %shard_map.288.refs_1_ = bf16[512,2048]{1,0:T(8,128)(2,1)} custom-call(bf16[1024,2048]{1,0:T(8,128)(2,1)} %bitcast.60, bf16[1024,1536]{1,0:T(8,128)(2,1)} %get-tuple-element.317.refs_1_.refs_0_, bf16[1024,2048]{1,0:T(8,128)(2,1)} %bitcast.65, bf16[1024,1024]{1,0:T(8,128)(2,1)} %get-tuple-element.304.refs_3_.refs_0_, ...), custom_call_target="tpu_custom_call" | custom-call | flops 100000000 | tf_op jit(solution)/shard_map/pallas_call | solution.py:283
  554.8 3.5 shard_map.289
  564.3 3.5 shard_map.294
  574.2 8.3 %shard_map.290.refs_0_ = bf16[512,2048]{1,0:T(8,128)(2,1)} custom-call(bf16[1024,2048]{1,0:T(8,128)(2,1)} %bitcast.61, bf16[1024,1536]{1,0:T(8,128)(2,1)} %get-tuple-element.317.refs_1_.refs_0_, bf16[1024,2048]{1,0:T(8,128)(2,1)} %bitcast.66, bf16[1024,1024]{1,0:T(8,128)(2,1)} %get-tuple-element.304.refs_3_.refs_0_, ...), custom_call_target="tpu_custom_call" | custom-call | flops 100000000 | tf_op jit(solution)/shard_map/pallas_call | solution.py:283
  582.5 3.5 collective-permute-done.71.refs_3_
  587.6 3.3 shard_map.292
  593.2 2.8 shard_map.293
  596.0 3.2 convert_add_fusion.2
  599.2 10.8 %collective-permute-done.76 = bf16[256,2048]{1,0:T(8,128)(2,1)} collective-permute-done((bf16[256,2048]{1,0:T(8,128)(2,1)}, bf16[256,2048]{1,0:T(8,128)(2,1)}, u32[]{:S(2)}, u32[]{:S(2)}) %collective-permute-start.76) | collective-permute-done | bytes 1048608 | tf_op jit(solution)/shard_map/ppermute | solution.py:745
  610.1 4.2 add_reduce_fusion
  615.3 9.8 %collective-permute-start.77 = (f32[16,6,64]{2,1,0:T(8,128)S(1)}, f32[16,6,64]{2,1,0:T(8,128)S(1)}, u32[]{:S(2)}, u32[]{:S(2)}) collective-permute-start(f32[16,6,64]{2,1,0:T(8,128)S(1)} %slice.233), channel_id=1, source_target_pairs={{0,2},{1,3},{2,0},{3,1},{4,6},{5,7},{6,4},{7,5},{8,10},{9,11},{10,... | collective-permute-start | bytes 73736 | tf_op jit(solution)/shard_map/ppermute | solution.py:314
  627.5 3.3 fusion.11.refs_0_
  630.8 2.9 shard_map.295
  633.9 3.0 copy.40
  638.7 3.4 convert_add_fusion.1
  (399 shorter events, 215.1 us)
Async XLA Ops:
  15.5 25.5 %collective-permute-start.7 = (bf16[256,2048]{1,0:T(8,128)(2,1)}, bf16[256,2048]{1,0:T(8,128)(2,1)}, u32[]{:S(2)}, u32[]{:S(2)}) collective-permute-start(bf16[256,2048]{1,0:T(8,128)(2,1)} %get-tuple-element.182), channel_id=1, source_target_pairs={{8,0},{16,8},{24,16},{28,24},{20,28},{12,20},{4,12},{0,4},{9,1},{1... | collective-permute-start | bytes 3145736 | tf_op jit(solution)/shard_map/ppermute | solution.py:57
  17.1 23.9 %collective-permute-start.6 = (bf16[256,2048]{1,0:T(8,128)(2,1)}, bf16[256,2048]{1,0:T(8,128)(2,1)}, u32[]{:S(2)}, u32[]{:S(2)}) collective-permute-start(bf16[256,2048]{1,0:T(8,128)(2,1)} %get-tuple-element.182), channel_id=1, source_target_pairs={{0,8},{8,16},{16,24},{24,28},{28,20},{20,12},{12,4},{4,0},{1,9},{9... | collective-permute-start | bytes 3145736 | tf_op jit(solution)/shard_map/ppermute | solution.py:57
  21.9 23.0 %collective-permute-start.4 = (bf16[256,2048]{1,0:T(8,128)(2,1)}, bf16[256,2048]{1,0:T(8,128)(2,1)}, u32[]{:S(2)}, u32[]{:S(2)}) collective-permute-start(bf16[256,2048]{1,0:T(8,128)(2,1)} %shard_map.254.refs_0_), channel_id=1, source_target_pairs={{0,2},{1,3},{2,0},{3,1},{4,6},{5,7},{6,4},{7,5},{8,10},{9,11},{10,... | collective-permute-start | bytes 3145736 | tf_op jit(solution)/shard_map/ppermute | solution.py:314
  26.2 37.3 %collective-permute-start.12 = (bf16[256,2048]{1,0:T(8,128)(2,1)}, bf16[256,2048]{1,0:T(8,128)(2,1)S(1)}, u32[]{:S(2)}, u32[]{:S(2)}) collective-permute-start(bf16[256,2048]{1,0:T(8,128)(2,1)} %shard_map.257), channel_id=1, source_target_pairs={{0,4},{4,8},{8,12},{12,16},{16,20},{20,24},{24,28},{1,5},{5,9},{9,... | collective-permute-start | bytes 3145736 | tf_op jit(solution)/shard_map/ppermute | solution.py:603
  41.0 26.9 %collective-permute-start.8 = (bf16[256,2048]{1,0:T(8,128)(2,1)}, bf16[256,2048]{1,0:T(8,128)(2,1)}, u32[]{:S(2)}, u32[]{:S(2)}) collective-permute-start(bf16[256,2048]{1,0:T(8,128)(2,1)} %collective-permute-done.6), channel_id=1, source_target_pairs={{0,8},{8,16},{16,24},{24,28},{28,20},{20,12},{12,4},{4,0},{1,9},{9... | collective-permute-start | bytes 3145736 | tf_op jit(solution)/shard_map/ppermute | solution.py:57
  41.0 41.8 %collective-permute-start.9 = (bf16[256,2048]{1,0:T(8,128)(2,1)}, bf16[256,2048]{1,0:T(8,128)(2,1)}, u32[]{:S(2)}, u32[]{:S(2)}) collective-permute-start(bf16[256,2048]{1,0:T(8,128)(2,1)} %collective-permute-done.7), channel_id=1, source_target_pairs={{8,0},{16,8},{24,16},{28,24},{20,28},{12,20},{4,12},{0,4},{9,1},{1... | collective-permute-start | bytes 3145736 | tf_op jit(solution)/shard_map/ppermute | solution.py:57
  44.8 41.2 %collective-permute-start.3 = (bf16[256,2048]{1,0:T(8,128)(2,1)S(1)}, bf16[256,2048]{1,0:T(8,128)(2,1)}, u32[]{:S(2)}, u32[]{:S(2)}) collective-permute-start(bf16[256,2048]{1,0:T(8,128)(2,1)S(1)} %copy-done.4), channel_id=1, source_target_pairs={{0,1},{1,0},{2,3},{3,2},{4,5},{5,4},{6,7},{7,6},{8,9},{9,8},{10,11... | collective-permute-start | bytes 3145736 | tf_op jit(solution)/shard_map/ppermute | solution.py:314
  44.9 42.6 %collective-permute-start.5 = (bf16[256,2048]{1,0:T(8,128)(2,1)}, bf16[256,2048]{1,0:T(8,128)(2,1)}, u32[]{:S(2)}, u32[]{:S(2)}) collective-permute-start(bf16[256,2048]{1,0:T(8,128)(2,1)} %collective-permute-done.4.refs_2_), channel_id=1, source_target_pairs={{0,1},{1,0},{2,3},{3,2},{4,5},{5,4},{6,7},{7,6},{8,9},{9,8},{10,11... | collective-permute-start | bytes 3145736 | tf_op jit(solution)/shard_map/ppermute | solution.py:314
  63.5 24.1 %collective-permute-start.14 = (bf16[256,2048]{1,0:T(8,128)(2,1)S(1)}, bf16[256,2048]{1,0:T(8,128)(2,1)}, u32[]{:S(2)}, u32[]{:S(2)}) collective-permute-start(bf16[256,2048]{1,0:T(8,128)(2,1)S(1)} %collective-permute-done.12.refs_0_), channel_id=1, source_target_pairs={{0,2},{1,3},{2,0},{3,1},{4,6},{5,7},{6,4},{7,5},{8,10},{9,11},{10,... | collective-permute-start | bytes 3145736 | tf_op jit(solution)/shard_map/ppermute | solution.py:314
  82.9 23.5 %collective-permute-start.16 = (bf16[256,2048]{1,0:T(8,128)(2,1)}, bf16[256,2048]{1,0:T(8,128)(2,1)}, u32[]{:S(2)}, u32[]{:S(2)}) collective-permute-start(bf16[256,2048]{1,0:T(8,128)(2,1)} %collective-permute-done.8), channel_id=1, source_target_pairs={{0,8},{8,16},{16,24},{24,28},{28,20},{20,12},{12,4},{4,0},{1,9},{9... | collective-permute-start | bytes 3145736 | tf_op jit(solution)/shard_map/ppermute | solution.py:57
  82.9 23.5 %collective-permute-start.17 = (bf16[256,2048]{1,0:T(8,128)(2,1)}, bf16[256,2048]{1,0:T(8,128)(2,1)}, u32[]{:S(2)}, u32[]{:S(2)}) collective-permute-start(bf16[256,2048]{1,0:T(8,128)(2,1)} %collective-permute-done.9), channel_id=1, source_target_pairs={{8,0},{16,8},{24,16},{28,24},{20,28},{12,20},{4,12},{0,4},{9,1},{1... | collective-permute-start | bytes 3145736 | tf_op jit(solution)/shard_map/ppermute | solution.py:57
  86.0 25.3 %collective-permute-start.22 = (bf16[256,2048]{1,0:T(8,128)(2,1)}, bf16[256,2048]{1,0:T(8,128)(2,1)}, u32[]{:S(2)}, u32[]{:S(2)}) collective-permute-start(bf16[256,2048]{1,0:T(8,128)(2,1)} %get-tuple-element.202), channel_id=1, source_target_pairs={{0,2},{1,3},{2,0},{3,1},{4,6},{5,7},{6,4},{7,5},{8,10},{9,11},{10,... | collective-permute-start | bytes 3145736 | tf_op jit(solution)/shard_map/ppermute | solution.py:314
  87.6 23.7 %collective-permute-start.13 = (bf16[256,2048]{1,0:T(8,128)(2,1)S(1)}, bf16[256,2048]{1,0:T(8,128)(2,1)}, u32[]{:S(2)}, u32[]{:S(2)}) collective-permute-start(bf16[256,2048]{1,0:T(8,128)(2,1)S(1)} %collective-permute-done.12.refs_0_), channel_id=1, source_target_pairs={{0,1},{1,0},{2,3},{3,2},{4,5},{5,4},{6,7},{7,6},{8,9},{9,8},{10,11... | collective-permute-start | bytes 3145736 | tf_op jit(solution)/shard_map/ppermute | solution.py:314
  87.6 24.2 %collective-permute-start.15 = (bf16[256,2048]{1,0:T(8,128)(2,1)}, bf16[256,2048]{1,0:T(8,128)(2,1)}, u32[]{:S(2)}, u32[]{:S(2)}) collective-permute-start(bf16[256,2048]{1,0:T(8,128)(2,1)} %collective-permute-done.14.refs_2_), channel_id=1, source_target_pairs={{0,1},{1,0},{2,3},{3,2},{4,5},{5,4},{6,7},{7,6},{8,9},{9,8},{10,11... | collective-permute-start | bytes 3145736 | tf_op jit(solution)/shard_map/ppermute | solution.py:314
  106.4 21.7 %collective-permute-start.18 = (bf16[256,2048]{1,0:T(8,128)(2,1)}, bf16[256,2048]{1,0:T(8,128)(2,1)}, u32[]{:S(2)}, u32[]{:S(2)}) collective-permute-start(bf16[256,2048]{1,0:T(8,128)(2,1)} %collective-permute-done.16), channel_id=1, source_target_pairs={{0,8},{8,16},{16,24},{24,28},{28,20},{20,12},{12,4},{4,0},{1,9},{9... | collective-permute-start | bytes 3145736 | tf_op jit(solution)/shard_map/ppermute | solution.py:57
  111.3 43.0 %collective-permute-start.21 = (bf16[256,2048]{1,0:T(8,128)(2,1)S(1)}, bf16[256,2048]{1,0:T(8,128)(2,1)S(1)}, u32[]{:S(2)}, u32[]{:S(2)}) collective-permute-start(bf16[256,2048]{1,0:T(8,128)(2,1)S(1)} %copy-done.19), channel_id=1, source_target_pairs={{0,1},{1,0},{2,3},{3,2},{4,5},{5,4},{6,7},{7,6},{8,9},{9,8},{10,11... | collective-permute-start | bytes 3145736 | tf_op jit(solution)/shard_map/ppermute | solution.py:314
  111.3 43.0 %collective-permute-start.23 = (bf16[256,2048]{1,0:T(8,128)(2,1)}, bf16[256,2048]{1,0:T(8,128)(2,1)}, u32[]{:S(2)}, u32[]{:S(2)}) collective-permute-start(bf16[256,2048]{1,0:T(8,128)(2,1)} %collective-permute-done.22), channel_id=1, source_target_pairs={{0,1},{1,0},{2,3},{3,2},{4,5},{5,4},{6,7},{7,6},{8,9},{9,8},{10,11... | collective-permute-start | bytes 3145736 | tf_op jit(solution)/shard_map/ppermute | solution.py:314
  129.9 24.4 %collective-permute-start.20 = (bf16[256,2048]{1,0:T(8,128)(2,1)}, bf16[256,2048]{1,0:T(8,128)(2,1)}, u32[]{:S(2)}, u32[]{:S(2)}) collective-permute-start(bf16[256,2048]{1,0:T(8,128)(2,1)} %param.26), channel_id=1, source_target_pairs={{0,8},{8,16},{16,24},{24,28},{28,20},{20,12},{12,4},{4,0},{1,9},{9... | collective-permute-start | bytes 3145736 | tf_op jit(solution)/shard_map/ppermute | solution.py:57
  131.9 22.5 %collective-permute-start.24 = (bf16[256,2048]{1,0:T(8,128)(2,1)}, bf16[256,2048]{1,0:T(8,128)(2,1)}, u32[]{:S(2)}, u32[]{:S(2)}) collective-permute-start(bf16[256,2048]{1,0:T(8,128)(2,1)} %collective-permute-done.19), channel_id=1, source_target_pairs={{8,0},{16,8},{24,16},{28,24},{20,28},{12,20},{4,12},{0,4},{9,1},{1... | collective-permute-start | bytes 3145736 | tf_op jit(solution)/shard_map/ppermute | solution.py:57
  154.5 22.0 %collective-permute-start.25 = (bf16[256,2048]{1,0:T(8,128)(2,1)}, bf16[256,2048]{1,0:T(8,128)(2,1)}, u32[]{:S(2)}, u32[]{:S(2)}) collective-permute-start(bf16[256,2048]{1,0:T(8,128)(2,1)} %collective-permute-done.20), channel_id=1, source_target_pairs={{0,8},{8,16},{16,24},{24,28},{28,20},{20,12},{12,4},{4,0},{1,9},{9... | collective-permute-start | bytes 3145736 | tf_op jit(solution)/shard_map/ppermute | solution.py:57
  156.5 22.4 %collective-permute-start.26 = (bf16[256,2048]{1,0:T(8,128)(2,1)}, bf16[256,2048]{1,0:T(8,128)(2,1)}, u32[]{:S(2)}, u32[]{:S(2)}) collective-permute-start(bf16[256,2048]{1,0:T(8,128)(2,1)} %collective-permute-done.24), channel_id=1, source_target_pairs={{8,0},{16,8},{24,16},{28,24},{20,28},{12,20},{4,12},{0,4},{9,1},{1... | collective-permute-start | bytes 3145736 | tf_op jit(solution)/shard_map/ppermute | solution.py:57
  182.7 25.9 %collective-permute-start.32 = (bf16[256,2048]{1,0:T(8,128)(2,1)}, bf16[256,2048]{1,0:T(8,128)(2,1)}, u32[]{:S(2)}, u32[]{:S(2)}) collective-permute-start(bf16[256,2048]{1,0:T(8,128)(2,1)} %collective-permute-done.25), channel_id=1, source_target_pairs={{0,8},{8,16},{16,24},{24,28},{28,20},{20,12},{12,4},{4,0},{1,9},{9... | collective-permute-start | bytes 3145736 | tf_op jit(solution)/shard_map/ppermute | solution.py:57
  184.4 25.6 %collective-permute-start.33 = (bf16[256,2048]{1,0:T(8,128)(2,1)}, bf16[256,2048]{1,0:T(8,128)(2,1)}, u32[]{:S(2)}, u32[]{:S(2)}) collective-permute-start(bf16[256,2048]{1,0:T(8,128)(2,1)} %collective-permute-done.26), channel_id=1, source_target_pairs={{8,0},{16,8},{24,16},{28,24},{20,28},{12,20},{4,12},{0,4},{9,1},{1... | collective-permute-start | bytes 3145736 | tf_op jit(solution)/shard_map/ppermute | solution.py:57
  184.7 27.4 %collective-permute-start.27 = (bf16[256,2048]{1,0:T(8,128)(2,1)}, bf16[256,2048]{1,0:T(8,128)(2,1)S(1)}, u32[]{:S(2)}, u32[]{:S(2)}) collective-permute-start(bf16[256,2048]{1,0:T(8,128)(2,1)} %get-tuple-element.214), channel_id=1, source_target_pairs={{0,1},{1,0},{2,3},{3,2},{4,5},{5,4},{6,7},{7,6},{8,9},{9,8},{10,11... | collective-permute-start | bytes 3145736 | tf_op jit(solution)/shard_map/ppermute | solution.py:314
  188.2 25.8 %collective-permute-start.29 = (bf16[256,2048]{1,0:T(8,128)(2,1)}, bf16[256,2048]{1,0:T(8,128)(2,1)S(1)}, u32[]{:S(2)}, u32[]{:S(2)}) collective-permute-start(bf16[256,2048]{1,0:T(8,128)(2,1)} %shard_map.262), channel_id=1, source_target_pairs={{0,2},{1,3},{2,0},{3,1},{4,6},{5,7},{6,4},{7,5},{8,10},{9,11},{10,... | collective-permute-start | bytes 3145736 | tf_op jit(solution)/shard_map/ppermute | solution.py:314
  210.0 24.6 %collective-permute-start.35 = (bf16[2048,256]{1,0:T(8,128)(2,1)S(1)}, bf16[2048,256]{1,0:T(8,128)(2,1)}, u32[]{:S(2)}, u32[]{:S(2)}) collective-permute-start(bf16[2048,256]{1,0:T(8,128)(2,1)S(1)} %copy-done.17), channel_id=1, source_target_pairs={{8,0},{16,8},{24,16},{28,24},{20,28},{12,20},{4,12},{0,4},{9,1},{1... | collective-permute-start | bytes 3145736 | tf_op jit(solution)/shard_map/ppermute | solution.py:57
  210.3 24.3 %collective-permute-start.34 = (bf16[2048,256]{1,0:T(8,128)(2,1)S(1)}, bf16[2048,256]{1,0:T(8,128)(2,1)}, u32[]{:S(2)}, u32[]{:S(2)}) collective-permute-start(bf16[2048,256]{1,0:T(8,128)(2,1)S(1)} %copy-done.17), channel_id=1, source_target_pairs={{0,8},{8,16},{16,24},{24,28},{28,20},{20,12},{12,4},{4,0},{1,9},{9... | collective-permute-start | bytes 3145736 | tf_op jit(solution)/shard_map/ppermute | solution.py:57
  217.2 24.9 %collective-permute-start.31 = (bf16[256,2048]{1,0:T(8,128)(2,1)S(1)}, bf16[256,2048]{1,0:T(8,128)(2,1)S(1)}, u32[]{:S(2)}, u32[]{:S(2)}) collective-permute-start(bf16[256,2048]{1,0:T(8,128)(2,1)S(1)} %add_convert_fusion.refs_0_), channel_id=1, source_target_pairs={{0,2},{1,3},{2,0},{3,1},{4,6},{5,7},{6,4},{7,5},{8,10},{9,11},{10,... | collective-permute-start | bytes 3145736 | tf_op jit(solution)/shard_map/ppermute | solution.py:314
  242.0 25.9 %collective-permute-start.37 = (bf16[2048,256]{1,0:T(8,128)(2,1)}, bf16[2048,256]{1,0:T(8,128)(2,1)}, u32[]{:S(2)}, u32[]{:S(2)}) collective-permute-start(bf16[2048,256]{1,0:T(8,128)(2,1)} %collective-permute-done.34), channel_id=1, source_target_pairs={{0,8},{8,16},{16,24},{24,28},{28,20},{20,12},{12,4},{4,0},{1,9},{9... | collective-permute-start | bytes 3145736 | tf_op jit(solution)/shard_map/ppermute | solution.py:57
  243.8 25.7 %collective-permute-start.38 = (bf16[2048,256]{1,0:T(8,128)(2,1)}, bf16[2048,256]{1,0:T(8,128)(2,1)}, u32[]{:S(2)}, u32[]{:S(2)}) collective-permute-start(bf16[2048,256]{1,0:T(8,128)(2,1)} %collective-permute-done.35), channel_id=1, source_target_pairs={{8,0},{16,8},{24,16},{28,24},{20,28},{12,20},{4,12},{0,4},{9,1},{1... | collective-permute-start | bytes 3145736 | tf_op jit(solution)/shard_map/ppermute | solution.py:57
  269.5 24.9 %collective-permute-start.39 = (bf16[2048,256]{1,0:T(8,128)(2,1)}, bf16[2048,256]{1,0:T(8,128)(2,1)}, u32[]{:S(2)}, u32[]{:S(2)}) collective-permute-start(bf16[2048,256]{1,0:T(8,128)(2,1)} %collective-permute-done.37), channel_id=1, source_target_pairs={{0,8},{8,16},{16,24},{24,28},{28,20},{20,12},{12,4},{4,0},{1,9},{9... | collective-permute-start | bytes 3145736 | tf_op jit(solution)/shard_map/ppermute | solution.py:57
  271.2 24.5 %collective-permute-start.40 = (bf16[2048,256]{1,0:T(8,128)(2,1)}, bf16[2048,256]{1,0:T(8,128)(2,1)}, u32[]{:S(2)}, u32[]{:S(2)}) collective-permute-start(bf16[2048,256]{1,0:T(8,128)(2,1)} %collective-permute-done.38), channel_id=1, source_target_pairs={{8,0},{16,8},{24,16},{28,24},{20,28},{12,20},{4,12},{0,4},{9,1},{1... | collective-permute-start | bytes 3145736 | tf_op jit(solution)/shard_map/ppermute | solution.py:57
  295.8 24.0 %collective-permute-start.41 = (bf16[256,2048]{1,0:T(8,128)(2,1)}, bf16[256,2048]{1,0:T(8,128)(2,1)}, u32[]{:S(2)}, u32[]{:S(2)}) collective-permute-start(bf16[256,2048]{1,0:T(8,128)(2,1)} %shard_map.265), channel_id=1, source_target_pairs={{8,0},{16,8},{24,16},{28,24},{20,28},{12,20},{4,12},{0,4},{9,1},{1... | collective-permute-start | bytes 3145736 | tf_op jit(solution)/shard_map/ppermute | solution.py:57
  296.6 23.4 %collective-permute-start.42 = (bf16[2048,256]{1,0:T(8,128)(2,1)}, bf16[2048,256]{1,0:T(8,128)(2,1)}, u32[]{:S(2)}, u32[]{:S(2)}) collective-permute-start(bf16[2048,256]{1,0:T(8,128)(2,1)} %collective-permute-done.39), channel_id=1, source_target_pairs={{0,8},{8,16},{16,24},{24,28},{28,20},{20,12},{12,4},{4,0},{1,9},{9... | collective-permute-start | bytes 3145736 | tf_op jit(solution)/shard_map/ppermute | solution.py:57
  322.9 22.4 %collective-permute-start.44 = (bf16[256,2048]{1,0:T(8,128)(2,1)}, bf16[256,2048]{1,0:T(8,128)(2,1)S(1)}, u32[]{:S(2)}, u32[]{:S(2)}) collective-permute-start(bf16[256,2048]{1,0:T(8,128)(2,1)} %get-tuple-element.235), channel_id=1, source_target_pairs={{8,0},{16,8},{24,16},{28,24},{20,28},{12,20},{4,12},{0,4},{9,1},{1... | collective-permute-start | bytes 3145736 | tf_op jit(solution)/shard_map/ppermute | solution.py:57
  323.2 22.4 %collective-permute-start.43 = (bf16[256,2048]{1,0:T(8,128)(2,1)}, bf16[256,2048]{1,0:T(8,128)(2,1)}, u32[]{:S(2)}, u32[]{:S(2)}) collective-permute-start(bf16[256,2048]{1,0:T(8,128)(2,1)} %get-tuple-element.233), channel_id=1, source_target_pairs={{0,8},{8,16},{16,24},{24,28},{28,20},{20,12},{12,4},{4,0},{1,9},{9... | collective-permute-start | bytes 3145736 | tf_op jit(solution)/shard_map/ppermute | solution.py:57
  375.4 25.8 %collective-permute-start.51 = (bf16[256,2048]{1,0:T(8,128)(2,1)}, bf16[256,2048]{1,0:T(8,128)(2,1)S(1)}, u32[]{:S(2)}, u32[]{:S(2)}) collective-permute-start(bf16[256,2048]{1,0:T(8,128)(2,1)} %get-tuple-element.255), channel_id=1, source_target_pairs={{8,0},{16,8},{24,16},{28,24},{20,28},{12,20},{4,12},{0,4},{9,1},{1... | collective-permute-start | bytes 3145736 | tf_op jit(solution)/shard_map/ppermute | solution.py:57
  376.2 25.6 %collective-permute-start.50 = (bf16[256,2048]{1,0:T(8,128)(2,1)}, bf16[256,2048]{1,0:T(8,128)(2,1)}, u32[]{:S(2)}, u32[]{:S(2)}) collective-permute-start(bf16[256,2048]{1,0:T(8,128)(2,1)} %get-tuple-element.253), channel_id=1, source_target_pairs={{0,8},{8,16},{16,24},{24,28},{28,20},{20,12},{12,4},{4,0},{1,9},{9... | collective-permute-start | bytes 3145736 | tf_op jit(solution)/shard_map/ppermute | solution.py:57
  377.5 26.5 %collective-permute-start.47 = (bf16[256,2048]{1,0:T(8,128)(2,1)}, bf16[256,2048]{1,0:T(8,128)(2,1)}, u32[]{:S(2)}, u32[]{:S(2)}) collective-permute-start(bf16[256,2048]{1,0:T(8,128)(2,1)} %get-tuple-element.257), channel_id=1, source_target_pairs={{0,1},{1,0},{2,3},{3,2},{4,5},{5,4},{6,7},{7,6},{8,9},{9,8},{10,11... | collective-permute-start | bytes 3145736 | tf_op jit(solution)/shard_map/ppermute | solution.py:314
  380.8 25.5 %collective-permute-start.49 = (bf16[256,2048]{1,0:T(8,128)(2,1)}, bf16[256,2048]{1,0:T(8,128)(2,1)}, u32[]{:S(2)}, u32[]{:S(2)}) collective-permute-start(bf16[256,2048]{1,0:T(8,128)(2,1)} %shard_map.271), channel_id=1, source_target_pairs={{0,2},{1,3},{2,0},{3,1},{4,6},{5,7},{6,4},{7,5},{8,10},{9,11},{10,... | collective-permute-start | bytes 3145736 | tf_op jit(solution)/shard_map/ppermute | solution.py:314
  401.8 24.7 %collective-permute-start.53 = (bf16[256,2048]{1,0:T(8,128)(2,1)}, bf16[256,2048]{1,0:T(8,128)(2,1)}, u32[]{:S(2)}, u32[]{:S(2)}) collective-permute-start(bf16[256,2048]{1,0:T(8,128)(2,1)} %get-tuple-element.265), channel_id=1, source_target_pairs={{8,0},{16,8},{24,16},{28,24},{20,28},{12,20},{4,12},{0,4},{9,1},{1... | collective-permute-start | bytes 3145736 | tf_op jit(solution)/shard_map/ppermute | solution.py:57
  402.4 24.6 %collective-permute-start.52 = (bf16[256,2048]{1,0:T(8,128)(2,1)}, bf16[256,2048]{1,0:T(8,128)(2,1)}, u32[]{:S(2)}, u32[]{:S(2)}) collective-permute-start(bf16[256,2048]{1,0:T(8,128)(2,1)} %get-tuple-element.263), channel_id=1, source_target_pairs={{0,8},{8,16},{16,24},{24,28},{28,20},{20,12},{12,4},{4,0},{1,9},{9... | collective-permute-start | bytes 3145736 | tf_op jit(solution)/shard_map/ppermute | solution.py:57
  412.3 24.5 %collective-permute-start.56 = (bf16[256,2048]{1,0:T(8,128)(2,1)S(1)}, bf16[256,2048]{1,0:T(8,128)(2,1)}, u32[]{:S(2)}, u32[]{:S(2)}) collective-permute-start(bf16[256,2048]{1,0:T(8,128)(2,1)S(1)} %get-tuple-element.280.refs_0_), channel_id=1, source_target_pairs={{0,2},{1,3},{2,0},{3,1},{4,6},{5,7},{6,4},{7,5},{8,10},{9,11},{10,... | collective-permute-start | bytes 3145736 | tf_op jit(solution)/shard_map/ppermute | solution.py:314
  412.8 29.7 %collective-permute-start.55 = (bf16[256,2048]{1,0:T(8,128)(2,1)S(1)}, bf16[256,2048]{1,0:T(8,128)(2,1)}, u32[]{:S(2)}, u32[]{:S(2)}) collective-permute-start(bf16[256,2048]{1,0:T(8,128)(2,1)S(1)} %get-tuple-element.280.refs_0_), channel_id=1, source_target_pairs={{0,1},{1,0},{2,3},{3,2},{4,5},{5,4},{6,7},{7,6},{8,9},{9,8},{10,11... | collective-permute-start | bytes 3145736 | tf_op jit(solution)/shard_map/ppermute | solution.py:314
  436.8 25.9 %collective-permute-start.58 = (bf16[256,2048]{1,0:T(8,128)(2,1)}, bf16[256,2048]{1,0:T(8,128)(2,1)}, u32[]{:S(2)}, u32[]{:S(2)}) collective-permute-start(bf16[256,2048]{1,0:T(8,128)(2,1)} %get-tuple-element.277), channel_id=1, source_target_pairs={{8,0},{16,8},{24,16},{28,24},{20,28},{12,20},{4,12},{0,4},{9,1},{1... | collective-permute-start | bytes 3145736 | tf_op jit(solution)/shard_map/ppermute | solution.py:57
  437.6 25.6 %collective-permute-start.54 = (bf16[256,2048]{1,0:T(8,128)(2,1)}, bf16[256,2048]{1,0:T(8,128)(2,1)}, u32[]{:S(2)}, u32[]{:S(2)}) collective-permute-start(bf16[256,2048]{1,0:T(8,128)(2,1)} %get-tuple-element.275), channel_id=1, source_target_pairs={{0,8},{8,16},{16,24},{24,28},{28,20},{20,12},{12,4},{4,0},{1,9},{9... | collective-permute-start | bytes 3145736 | tf_op jit(solution)/shard_map/ppermute | solution.py:57
  466.5 24.3 %collective-permute-start.60 = (bf16[256,2048]{1,0:T(8,128)(2,1)}, bf16[256,2048]{1,0:T(8,128)(2,1)}, u32[]{:S(2)}, u32[]{:S(2)}) collective-permute-start(bf16[256,2048]{1,0:T(8,128)(2,1)} %get-tuple-element.294), channel_id=1, source_target_pairs={{0,1},{1,0},{2,3},{3,2},{4,5},{5,4},{6,7},{7,6},{8,9},{9,8},{10,11... | collective-permute-start | bytes 3145736 | tf_op jit(solution)/shard_map/ppermute | solution.py:314
  466.5 26.8 %collective-permute-start.63 = (bf16[256,2048]{1,0:T(8,128)(2,1)}, bf16[256,2048]{1,0:T(8,128)(2,1)S(1)}, u32[]{:S(2)}, u32[]{:S(2)}) collective-permute-start(bf16[256,2048]{1,0:T(8,128)(2,1)} %get-tuple-element.290), channel_id=1, source_target_pairs={{8,0},{16,8},{24,16},{28,24},{20,28},{12,20},{4,12},{0,4},{9,1},{1... | collective-permute-start | bytes 3145736 | tf_op jit(solution)/shard_map/ppermute | solution.py:57
  467.1 26.1 %collective-permute-start.62 = (bf16[256,2048]{1,0:T(8,128)(2,1)}, bf16[256,2048]{1,0:T(8,128)(2,1)}, u32[]{:S(2)}, u32[]{:S(2)}) collective-permute-start(bf16[256,2048]{1,0:T(8,128)(2,1)} %get-tuple-element.288), channel_id=1, source_target_pairs={{0,8},{8,16},{16,24},{24,28},{28,20},{20,12},{12,4},{4,0},{1,9},{9... | collective-permute-start | bytes 3145736 | tf_op jit(solution)/shard_map/ppermute | solution.py:57
  496.1 25.3 %collective-permute-start.64 = (bf16[256,2048]{1,0:T(8,128)(2,1)}, bf16[256,2048]{1,0:T(8,128)(2,1)}, u32[]{:S(2)}, u32[]{:S(2)}) collective-permute-start(bf16[256,2048]{1,0:T(8,128)(2,1)} %shard_map.282), channel_id=1, source_target_pairs={{8,0},{16,8},{24,16},{28,24},{20,28},{12,20},{4,12},{0,4},{9,1},{1... | collective-permute-start | bytes 3145736 | tf_op jit(solution)/shard_map/ppermute | solution.py:57
  496.9 24.6 %collective-permute-start.65 = (bf16[256,2048]{1,0:T(8,128)(2,1)}, bf16[256,2048]{1,0:T(8,128)(2,1)S(1)}, u32[]{:S(2)}, u32[]{:S(2)}) collective-permute-start(bf16[256,2048]{1,0:T(8,128)(2,1)} %shard_map.281), channel_id=1, source_target_pairs={{0,8},{8,16},{16,24},{24,28},{28,20},{20,12},{12,4},{4,0},{1,9},{9... | collective-permute-start | bytes 3145736 | tf_op jit(solution)/shard_map/ppermute | solution.py:57
  498.2 29.6 %collective-permute-start.59 = (bf16[256,2048]{1,0:T(8,128)(2,1)}, bf16[256,2048]{1,0:T(8,128)(2,1)}, u32[]{:S(2)}, u32[]{:S(2)}) collective-permute-start(bf16[256,2048]{1,0:T(8,128)(2,1)} %get-tuple-element.292), channel_id=1, source_target_pairs={{0,1},{1,0},{2,3},{3,2},{4,5},{5,4},{6,7},{7,6},{8,9},{9,8},{10,11... | collective-permute-start | bytes 3145736 | tf_op jit(solution)/shard_map/ppermute | solution.py:314
  498.2 30.0 %collective-permute-start.61 = (bf16[256,2048]{1,0:T(8,128)(2,1)}, bf16[256,2048]{1,0:T(8,128)(2,1)}, u32[]{:S(2)}, u32[]{:S(2)}) collective-permute-start(bf16[256,2048]{1,0:T(8,128)(2,1)} %shard_map.278), channel_id=1, source_target_pairs={{0,2},{1,3},{2,0},{3,1},{4,6},{5,7},{6,4},{7,5},{8,10},{9,11},{10,... | collective-permute-start | bytes 3145736 | tf_op jit(solution)/shard_map/ppermute | solution.py:314
  524.8 30.0 %collective-permute-start.68 = (bf16[256,2048]{1,0:T(8,128)(2,1)}, bf16[256,2048]{1,0:T(8,128)(2,1)}, u32[]{:S(2)}, u32[]{:S(2)}) collective-permute-start(bf16[256,2048]{1,0:T(8,128)(2,1)} %get-tuple-element.314), channel_id=1, source_target_pairs={{8,0},{16,8},{24,16},{28,24},{20,28},{12,20},{4,12},{0,4},{9,1},{1... | collective-permute-start | bytes 3145736 | tf_op jit(solution)/shard_map/ppermute | solution.py:57
  526.5 28.3 %collective-permute-start.67 = (bf16[256,2048]{1,0:T(8,128)(2,1)}, bf16[256,2048]{1,0:T(8,128)(2,1)}, u32[]{:S(2)}, u32[]{:S(2)}) collective-permute-start(bf16[256,2048]{1,0:T(8,128)(2,1)} %get-tuple-element.312), channel_id=1, source_target_pairs={{0,8},{8,16},{16,24},{24,28},{28,20},{20,12},{12,4},{4,0},{1,9},{9... | collective-permute-start | bytes 3145736 | tf_op jit(solution)/shard_map/ppermute | solution.py:57
  527.7 34.6 %collective-permute-start.74 = (bf16[256,2048]{1,0:T(8,128)(2,1)}, bf16[256,2048]{1,0:T(8,128)(2,1)S(1)}, u32[]{:S(2)}, u32[]{:S(2)}) collective-permute-start(bf16[256,2048]{1,0:T(8,128)(2,1)} %get-tuple-element.342), channel_id=1, source_target_pairs={{0,1},{1,0},{2,3},{3,2},{4,5},{5,4},{6,7},{7,6},{8,9},{9,8},{10,11... | collective-permute-start | bytes 3145736 | tf_op jit(solution)/shard_map/ppermute | solution.py:314
  534.3 28.1 %collective-permute-start.75 = (bf16[256,2048]{1,0:T(8,128)(2,1)}, bf16[256,2048]{1,0:T(8,128)(2,1)S(1)}, u32[]{:S(2)}, u32[]{:S(2)}) collective-permute-start(bf16[256,2048]{1,0:T(8,128)(2,1)} %shard_map.286), channel_id=1, source_target_pairs={{0,2},{1,3},{2,0},{3,1},{4,6},{5,7},{6,4},{7,5},{8,10},{9,11},{10,... | collective-permute-start | bytes 3145736 | tf_op jit(solution)/shard_map/ppermute | solution.py:314
  559.7 26.3 %collective-permute-start.71 = (bf16[256,2048]{1,0:T(8,128)(2,1)}, bf16[256,2048]{1,0:T(8,128)(2,1)}, u32[]{:S(2)}, u32[]{:S(2)}) collective-permute-start(bf16[256,2048]{1,0:T(8,128)(2,1)} %get-tuple-element.325), channel_id=1, source_target_pairs={{8,0},{16,8},{24,16},{28,24},{20,28},{12,20},{4,12},{0,4},{9,1},{1... | collective-permute-start | bytes 3145736 | tf_op jit(solution)/shard_map/ppermute | solution.py:57
  561.2 26.3 %collective-permute-start.69 = (bf16[256,2048]{1,0:T(8,128)(2,1)}, bf16[256,2048]{1,0:T(8,128)(2,1)}, u32[]{:S(2)}, u32[]{:S(2)}) collective-permute-start(bf16[256,2048]{1,0:T(8,128)(2,1)} %get-tuple-element.323), channel_id=1, source_target_pairs={{0,8},{8,16},{16,24},{24,28},{28,20},{20,12},{12,4},{4,0},{1,9},{9... | collective-permute-start | bytes 3145736 | tf_op jit(solution)/shard_map/ppermute | solution.py:57
  562.3 36.9 %collective-permute-start.72 = (bf16[256,2048]{1,0:T(8,128)(2,1)}, bf16[256,2048]{1,0:T(8,128)(2,1)}, u32[]{:S(2)}, u32[]{:S(2)}) collective-permute-start(bf16[256,2048]{1,0:T(8,128)(2,1)} %get-tuple-element.340), channel_id=1, source_target_pairs={{0,1},{1,0},{2,3},{3,2},{4,5},{5,4},{6,7},{7,6},{8,9},{9,8},{10,11... | collective-permute-start | bytes 3145736 | tf_op jit(solution)/shard_map/ppermute | solution.py:314
  567.8 42.2 %collective-permute-start.76 = (bf16[256,2048]{1,0:T(8,128)(2,1)}, bf16[256,2048]{1,0:T(8,128)(2,1)}, u32[]{:S(2)}, u32[]{:S(2)}) collective-permute-start(bf16[256,2048]{1,0:T(8,128)(2,1)} %shard_map.294), channel_id=1, source_target_pairs={{4,0},{8,4},{12,8},{16,12},{20,16},{24,20},{28,24},{5,1},{9,5},{13... | collective-permute-start | bytes 3145736 | tf_op jit(solution)/shard_map/ppermute | solution.py:745
  571.8 38.2 %collective-permute-start.73 = (bf16[256,2048]{1,0:T(8,128)(2,1)}, bf16[256,2048]{1,0:T(8,128)(2,1)}, u32[]{:S(2)}, u32[]{:S(2)}) collective-permute-start(bf16[256,2048]{1,0:T(8,128)(2,1)} %shard_map.291), channel_id=1, source_target_pairs={{0,2},{1,3},{2,0},{3,1},{4,6},{5,7},{6,4},{7,5},{8,10},{9,11},{10,... | collective-permute-start | bytes 3145736 | tf_op jit(solution)/shard_map/ppermute | solution.py:314
  590.9 42.9 %collective-permute-start.80 = (bf16[256,2048]{1,0:T(8,128)(2,1)}, bf16[256,2048]{1,0:T(8,128)(2,1)}, u32[]{:S(2)}, u32[]{:S(2)}) collective-permute-start(bf16[256,2048]{1,0:T(8,128)(2,1)} %get-tuple-element.337), channel_id=1, source_target_pairs={{8,0},{16,8},{24,16},{28,24},{20,28},{12,20},{4,12},{0,4},{9,1},{1... | collective-permute-start | bytes 3145736 | tf_op jit(solution)/shard_map/ppermute | solution.py:57
  591.3 42.4 %collective-permute-start.79 = (bf16[256,2048]{1,0:T(8,128)(2,1)}, bf16[256,2048]{1,0:T(8,128)(2,1)}, u32[]{:S(2)}, u32[]{:S(2)}) collective-permute-start(bf16[256,2048]{1,0:T(8,128)(2,1)} %get-tuple-element.335), channel_id=1, source_target_pairs={{0,8},{8,16},{16,24},{24,28},{28,20},{20,12},{12,4},{4,0},{1,9},{9... | collective-permute-start | bytes 3145736 | tf_op jit(solution)/shard_map/ppermute | solution.py:57
  (68 other events, 667.9 us)

commit v6 on v5

--- a/solution.py
+++ b/solution.py
@@ -131,6 +131,10 @@
         received = [v if v is None else tie(v, *after) for v in received]
         return join([self.find(j) for _, j in steps], received)
 
+    def ends(self, ring):
+        value, at, rows = self.find(0)
+        return ring.now(value), at, rows, self.landed[True, 1], self.landed[False, self.count - 1]
+
     def total(self, ring):
         value, at, rows = self.find(0)
         own = ring.now(value)[at * rows : (at + 1) * rows].astype(F32)
@@ -140,6 +144,51 @@
 
 
 QUICK = pl.CostEstimate(flops=10**8, bytes_accessed=0, transcendentals=0)
+
+
+def flipped_total(value, at, rows, *received):
+    def kernel(own, ahead, behind, out):
+        total = own[...].astype(F32) + ahead[...].astype(F32) + behind[...].astype(F32)
+        out[...] = total.T
+
+    block = pl.BlockSpec((rows, TILE), lambda t: (0, t))
+    return pl.pallas_call(
+        kernel,
+        grid=(value.shape[1] // TILE,),
+        in_specs=[pl.BlockSpec((rows, TILE), lambda t: (at, t)), block, block],
+        out_specs=pl.BlockSpec((TILE, rows), lambda t: (t, 0)),
+        out_shape=jax.ShapeDtypeStruct((value.shape[1], rows), F32),
+        cost_estimate=QUICK,
+    )(value, *received)
+
+
+def mixed_total(value, at, rows, *received):
+    def kernel(own, ahead, behind, straight, flipped):
+        total = own[...].astype(F32) + ahead[...].astype(F32) + behind[...].astype(F32)
+
+        @pl.when(pl.program_id(0) < 3)
+        def _():
+            straight[0] = total
+
+        @pl.when(pl.program_id(0) == 3)
+        def _():
+            flipped[...] = total.T
+
+    block = pl.BlockSpec((rows, TILE), lambda t: (0, t))
+    return pl.pallas_call(
+        kernel,
+        grid=(4,),
+        in_specs=[pl.BlockSpec((rows, TILE), lambda t: (at, t)), block, block],
+        out_specs=[
+            pl.BlockSpec((1, rows, TILE), lambda t: (jnp.minimum(t, 2), 0, 0)),
+            pl.BlockSpec((TILE, rows), lambda t: (0, 0)),
+        ],
+        out_shape=[
+            jax.ShapeDtypeStruct((3, rows, TILE), F32),
+            jax.ShapeDtypeStruct((TILE, rows), F32),
+        ],
+        cost_estimate=QUICK,
+    )(value, *received)
 
 
 def join(found, received):
@@ -252,7 +301,11 @@
     width = width or pairs[0][0].shape[1]
 
     def kernel(*refs):
-        for t, parts in enumerate(plan):
+        at = 0
+        while at < len(plan):
+            parts, end = plan[at], at + 1
+            while end < len(plan) and plan[end] == parts:
+                end += 1
 
             def run(parts=parts):
                 value = None
@@ -261,11 +314,12 @@
                     value = term if value is None else value + term
                 refs[-1][...] = value.astype(BF16)
 
-            if all(p == plan[0] for p in plan):
-                if t == 0:
-                    run()
+            if end - at == len(plan):
+                run()
             else:
-                pl.when(pl.program_id(0) == t)(run)
+                tile = pl.program_id(0)
+                pl.when((tile >= at) & (tile < end))(run)
+            at = end
 
     specs, arrays = [], []
     for left, right, tile, start, tiles in pairs:
@@ -334,7 +388,7 @@
     return jnp.moveaxis(parts, 0, -2).reshape(*parts.shape[1:-1], -1)
 
 
-def small_totals(value, flat, after):
+def small_totals(value, flat, after, beside):
     count, groups = lax.axis_size("seq"), lax.axis_size("batch")
     own_s, own_b = lax.axis_index("seq"), lax.axis_index("batch")
     parts = jnp.moveaxis(value.reshape(*value.shape[:-1], count * groups, -1), -2, 0)
@@ -350,6 +404,8 @@
     for bit in reversed(bits_of(count)):
         half = parts.shape[0] // 2
         sent = jnp.concatenate([parts[half:].reshape(-1), flat])
+        if bit == 1:
+            sent = tie(sent, *beside)
         got = swap(sent, "seq", bit)
         at = half * parts.shape[1]
         parts = parts[:half] + got[:at].reshape(half, -1)
@@ -699,7 +755,7 @@
     ring.due(*result)
     ring.advance(1 + more)
     grad_branch = batch_gather(grad_branch_own, ring.now)
-    grad_w_proj = g_down.total(ring).T
+    grad_w_proj = flipped_total(*g_down.ends(ring))
     ring.due(grad_w_proj)
 
     grad_mixed, grad_branch = matmul(
@@ -730,15 +786,15 @@
     )
     pairs[0] = (tie(normed, back[0]), *pairs[0][1:])
     late["mix"].append(mix_piece(1, TILE))
-    ring.due(late["mix"][1][0])
+    result = resid + result + down_shift
+    ring.due(late["mix"][1][0], result)
     ring.advance()
     sent = []
     back = batch_scatter(ring.now(*back), sent.append, True)
     grad_own = matmul([tie(g_packed, *sent)], mix_in, finish_parts, ["parts"], nt=True)
     pairs[0] = (tie(normed, grad_own[0]), *pairs[0][1:])
     late["mix"].append(mix_piece(3, TILE))
-    result = resid + result + down_shift
-    ring.due(late["mix"][2][0], result)
+    ring.due(late["mix"][2][0])
     ring.advance()
     moved = reorder(ring.now(*back), back_order)
     grad_own = batch_scatter(ring.now(*grad_own), ring.due)
@@ -778,16 +834,16 @@
     grad_tokens = reorder(grad_tokens.astype(BF16), from_slots)
     grad_w_fc = g_up.total(ring)
     after = [*ring.last.values(), grad_tokens, block_out, grad_w_fc]
-    sums, flat = small_totals(sums, flat, after)
-    grad_mix_in = g_mix.total(ring)
+    grad_w_qkv, grad_w_out = mixed_total(*g_mix.ends(ring))
+    sums, flat = small_totals(sums, flat, after, [grad_w_qkv, grad_w_out])
     return (
         block_out[None],
         grad_tokens[None],
         sums[0],
         sums[1],
-        grad_mix_in[:, :qkv_width].reshape(slice_width, 3, heads_width),
+        grad_w_qkv.transpose(1, 0, 2),
         flat[ff:].reshape(2, heads_width),
-        grad_mix_in[:, qkv_width:].T,
+        grad_w_out,
         sums[2],
         sums[3],
         sums[4],

time: 662 us -> 661 us (level)
  starting transfers between devices: 82.8 us -> 92.2 us
  Pallas kernels: 271 us -> 279 us
  other arithmetic: 41.7 us -> 34.2 us
  local copies, waits for them, and re-layouts: 89.5 us -> 82.5 us
    ppermute x42, starting transfers between devices: 45.8 us -> 65 us  [hop(): self.last[forward] = lax.ppermute(value, 'seq', list(pairs))]
    ppermute x1, waiting for transfers between devices: 10.8 us -> 0.01 us  [shards(): moved = lax.ppermute(moved, 'seq', [(i + 1, i) for i in range(count - 1)])]
    ppermute x40, starting transfers between devices: 32.1 us -> 22 us  [swap(): lax.ppermute(value, axis, [(i, i ^ bit) for i in range(lax.axis_size(axis...]
    pallas_call x0 -> x2, Pallas kernels: none -> 8.85 us  [the longest x1 4.58 us: mixed_total(): pl.pallas_call(kernel, grid=(4,), in_specs=[pl.BlockSpec((rows, TILE), la...]
    ppermute x40, waiting for transfers between devices: 25 us -> 33.5 us  [swap(): lax.ppermute(value, axis, [(i, i ^ bit) for i in range(lax.axis_size(axis...]
    unnamed x125 -> x118, local copies, waits for them, and re-layouts: 63.1 us -> 58.6 us
  transfers between devices with their start and end apart: 84 -> 84, of which waited for: 44 -> 45; matrix products, arithmetic and copies ran while one was open for 19% -> 16% of each run, Pallas kernels for 39% -> 40%
where the time goes in v6:
time: 661 us; the launch traced here: 651 us
  Pallas kernels  279 us (42%)
  waiting for transfers between devices  161 us (24%)
  starting transfers between devices  92.2 us (14%)
  local copies, waits for them, and re-layouts  82.5 us (12%)
  other arithmetic  34.2 us (5%)
    ppermute x42, waiting for transfers between devices, hop(): self.last[forward] = lax.ppermute(value, 'seq', list(pairs))  109 us
    pallas_call x9, Pallas kernels, matmul(): pl.pallas_call(kernel, grid=(tiles,), in_specs=[pl.BlockSpec(v.shape, lam...  106 us
    ppermute x42, starting transfers between devices, hop(): self.last[forward] = lax.ppermute(value, 'seq', list(pairs))  65 us
    pallas_call x6, Pallas kernels, token_products(): pl.pallas_call(kernel, grid=(len(plan),), in_specs=specs, out_specs=pl.Bl...  60.1 us
    unnamed x118, local copies, waits for them, and re-layouts  58.6 us
    pallas_call x12, Pallas kernels, join(): pl.pallas_call(kernel, grid=(steps,), in_specs=[pl.BlockSpec((step, width...  35.7 us
    ppermute x40, waiting for transfers between devices, swap(): lax.ppermute(value, axis, [(i, i ^ bit) for i in range(lax.axis_size(axis...  33.5 us
    pallas_call x2, Pallas kernels, per_chain(): pl.pallas_call(kernel, grid_spec=pltpu.PrefetchScalarGridSpec(num_scalar_...  26.6 us
  transfers between devices with their start and end apart: 84, of which 45 were waited for; matrix products, arithmetic and copies ran while one was open for 16% of the time, Pallas kernels for 40%

profile of v6, /device:TPU:0, one launch (start us, length us, event | category | flops | bytes accessed | tf_op | source)
XLA Modules:
  0.0 650.8 jit_solution(9199238523056822483)
XLA Ops:
  1.4 3.0 collective-permute-start
  10.9 2.7 collective-permute-start.2
  19.2 2.8 shard_map.254.refs_0_
  23.5 2.7 shard_map.257
  26.2 3.4 collective-permute-start.12
  29.9 11.1 %collective-permute-done.7 = bf16[256,2048]{1,0:T(8,128)(2,1)} collective-permute-done((bf16[256,2048]{1,0:T(8,128)(2,1)}, bf16[256,2048]{1,0:T(8,128)(2,1)}, u32[]{:S(2)}, u32[]{:S(2)}) %collective-permute-start.7) | collective-permute-done | bytes 1048608 | tf_op jit(solution)/shard_map/ppermute | solution.py:57
  41.0 2.5 collective-permute-start.9
  45.3 18.2 %collective-permute-done.12.refs_0_ = bf16[256,2048]{1,0:T(8,128)(2,1)S(1)} collective-permute-done((bf16[256,2048]{1,0:T(8,128)(2,1)}, bf16[256,2048]{1,0:T(8,128)(2,1)S(1)}, u32[]{:S(2)}, u32[]{:S(2)}) %collective-permute-start.12) | collective-permute-done | bytes 1048608 | tf_op jit(solution)/shard_map/ppermute | solution.py:659
  65.1 2.8 shard_map.255
  68.4 2.6 convert_reduce_fusion.5
  71.0 11.9 %collective-permute-done.9 = bf16[256,2048]{1,0:T(8,128)(2,1)} collective-permute-done((bf16[256,2048]{1,0:T(8,128)(2,1)}, bf16[256,2048]{1,0:T(8,128)(2,1)}, u32[]{:S(2)}, u32[]{:S(2)}) %collective-permute-start.9) | collective-permute-done | bytes 1048608 | tf_op jit(solution)/shard_map/ppermute | solution.py:57
  92.2 6.1 shard_map.256
  100.7 5.7 collective-permute-done.16
  106.4 2.5 collective-permute-start.18
  111.8 6.1 shard_map.258
  134.9 10.9 %shard_map.259.packed = bf16[1024,1536]{1,0:T(8,128)(2,1)} custom-call(bf16[1024,2048]{1,0:T(8,128)(2,1)} %bitcast.53, bf16[2048,2048]{1,0:T(8,128)(2,1)} %constant_dynamic-update-slice_fusion.40.refs_1_.mix.refs_4_, f32[1,1536]{1,0:T(1,128)} %copy-done.37), custom_call_target="tpu_custom_call" | custom-call | flops 100000000 | tf_op jit(solution)/shard_map/pallas_call | solution.py:263
  145.8 8.5 %shard_map.260.early = bf16[1024,1024]{1,0:T(8,128)(2,1)} custom-call(bf16[1024,2048]{1,0:T(8,128)(2,1)} %bitcast.58, bf16[2048,2048]{1,0:T(8,128)(2,1)} %constant_dynamic-update-slice_fusion.40.refs_1_.mix.refs_4_, f32[1,1024]{1,0:T(1,128)} %slice.211.refs_2_), custom_call_target="tpu_custom_call" | custom-call | flops 100000000 | tf_op jit(solution)/shard_map/pallas_call | solution.py:263
  156.7 14.9 %shard_map.261 = (bf16[1024,512]{1,0:T(8,128)(2,1)}, bf16[1024,1024]{1,0:T(8,128)(2,1)}, bf16[256,2048]{1,0:T(8,128)(2,1)}, bf16[256,2048]{1,0:T(8,128)(2,1)}, b...) custom-call(s32[4]{0:T(128)} %copy-done.42, s32[1]{0:T(128)} %bitcast.12.start, ...), custom_call_target="tpu_custom_call" | custom-call | flops 100000000 | tf_op jit(solution)/shard_map/pallas_call | solution.py:582
  171.7 4.9 collective-permute-done.25
  200.4 8.2 %collective-permute-done.32 = bf16[256,2048]{1,0:T(8,128)(2,1)} collective-permute-done((bf16[256,2048]{1,0:T(8,128)(2,1)}, bf16[256,2048]{1,0:T(8,128)(2,1)}, u32[]{:S(2)}, u32[]{:S(2)}) %collective-permute-start.32) | collective-permute-done | bytes 1048608 | tf_op jit(solution)/shard_map/ppermute | solution.py:57
  229.5 5.2 collective-permute-done.35
  234.7 7.4 %collective-permute-done.31.refs_2_ = bf16[256,2048]{1,0:T(8,128)(2,1)S(1)} collective-permute-done((bf16[256,2048]{1,0:T(8,128)(2,1)S(1)}, bf16[256,2048]{1,0:T(8,128)(2,1)S(1)}, u32[]{:S(2)}, u32[]{:S(2)}) %collective-permute-start.31) | collective-permute-done | bytes 1048608 | tf_op jit(solution)/shard_map/ppermute | solution.py:368
  246.7 19.1 %shard_map.263 = (bf16[1024,2048]{1,0:T(8,128)(2,1)}, bf16[1024,2048]{1,0:T(8,128)(2,1)}, bf16[1024,2048]{1,0:T(8,128)(2,1)}) custom-call(bf16[256,2048]{1,0:T(8,128)(2,1)} %copy-done.21, bf16[256,2048]{1,0:T(8,128)(2,1)} %copy-done.35, bf16[256,2048]{1,0:T(8,128)(2,1)} %copy-done.34, bf16[256,2048]{1,0:T(8,128)(2,1)} %copy-done.36, ...), custom_call_target="tpu_custom_call" | custom-call | flops 100000000 | tf_op jit(solution)/shard_map/pallas_call | solution.py:263
  277.3 13.5 %shard_map.264.refs_0_.refs_1_.own = bf16[2048,2048]{1,0:T(8,128)(2,1)} custom-call(bf16[1024,2048]{1,0:T(8,128)(2,1)} %constant_dynamic-update-slice_fusion.19.refs_0_, bf16[1024,2048]{1,0:T(8,128)(2,1)} %get-tuple-element.270.refs_1_.refs_0_), custom_call_target="tpu_custom_call" | custom-call | flops 100000000 | tf_op jit(solution)/shard_map/pallas_call | solution.py:337
  308.7 11.1 %collective-permute-done.41.refs_2_ = bf16[256,2048]{1,0:T(8,128)(2,1)} collective-permute-done((bf16[256,2048]{1,0:T(8,128)(2,1)}, bf16[256,2048]{1,0:T(8,128)(2,1)}, u32[]{:S(2)}, u32[]{:S(2)}) %collective-permute-start.41) | collective-permute-done | bytes 1048608 | tf_op jit(solution)/shard_map/ppermute | solution.py:57
  320.0 2.9 shard_map.266
  327.2 14.7 %shard_map.267 = (bf16[1024,2048]{1,0:T(8,128)(2,1)}, f32[1,2048]{1,0:T(1,128)}) custom-call(bf16[1024,2048]{1,0:T(8,128)(2,1)} %constant_dynamic-update-slice_fusion.19.refs_0_, bf16[2048,2048]{1,0:T(8,128)(2,1)} %constant_dynamic-update-slice_fusion.39.refs_1_, bf16[1024,2048]{1,0:T(8,128)(2,1)} %get-tuple-element.240.refs_2_), custom_call_target="tpu_custom_call" | custom-call | flops 100000000 | tf_op jit(solution)/shard_map/pallas_call | solution.py:263
  341.9 3.4 collective-permute-done.44.refs_3_
  346.2 3.3 shard_map.268
  351.6 13.1 %shard_map.269 = (bf16[256,2048]{1,0:T(8,128)(2,1)}, bf16[256,2048]{1,0:T(8,128)(2,1)}, bf16[256,2048]{1,0:T(8,128)(2,1)}, bf16[256,2048]{1,0:T(8,128)(2,1)}) custom-call(bf16[1024,2048]{1,0:T(8,128)(2,1)} %get-tuple-element.248.refs_0_.refs_1_, bf16[2048,2048]{1,0:T(8,128)(2,1)} %constant_dynamic-update-slice_fusion.23.refs_4_.refs_1_), custom_call_target="tpu_custom_call" | custom-call | flops 100000000 | tf_op jit(solution)/shard_map/pallas_call | solution.py:263
  364.7 6.5 collective-permute-done.46.refs_3_
  372.2 3.3 shard_map.270
  381.4 13.6 %shard_map.272.refs_0_.refs_1_ = bf16[2048,2048]{1,0:T(8,128)(2,1)} custom-call(bf16[1024,2048]{1,0:T(8,128)(2,1)} %get-tuple-element.264.refs_0_, bf16[1024,2048]{1,0:T(8,128)(2,1)} %get-tuple-element.248.refs_0_.refs_1_), custom_call_target="tpu_custom_call" | custom-call | flops 100000000 | tf_op jit(solution)/shard_map/pallas_call | solution.py:337
  395.0 2.6 shard_map.273
  397.6 3.7 collective-permute-done.51.behind
  412.9 13.0 %shard_map.274 = (bf16[256,2048]{1,0:T(8,128)(2,1)}, bf16[256,2048]{1,0:T(8,128)(2,1)}, bf16[256,2048]{1,0:T(8,128)(2,1)}, bf16[256,2048]{1,0:T(8,128)(2,1)}) custom-call(bf16[1024,2048]{1,0:T(8,128)(2,1)} %get-tuple-element.270.refs_1_.refs_0_, bf16[2048,2048]{1,0:T(8,128)(2,1)} %constant_dynamic-update-slice_fusion.39.refs_1_), custom_call_target="tpu_custom_call" | custom-call | flops 100000000 | tf_op jit(solution)/shard_map/pallas_call | solution.py:263
  427.1 3.3 shard_map.275
  430.4 6.5 %collective-permute-done.56.refs_2_ = bf16[256,2048]{1,0:T(8,128)(2,1)} collective-permute-done((bf16[256,2048]{1,0:T(8,128)(2,1)S(1)}, bf16[256,2048]{1,0:T(8,128)(2,1)}, u32[]{:S(2)}, u32[]{:S(2)}) %collective-permute-start.56) | collective-permute-done | bytes 1048608 | tf_op jit(solution)/shard_map/ppermute | solution.py:368
  438.9 4.3 shard_map.276
  443.2 7.7 %shard_map.277 = (bf16[1024,512]{1,0:T(8,128)(2,1)}, bf16[1024,2048]{1,0:T(8,128)(2,1)}) custom-call(bf16[256,2048]{1,0:T(8,128)(2,1)} %copy-done.20, bf16[256,2048]{1,0:T(8,128)(2,1)} %collective-permute-done.55.refs_1_, bf16[256,2048]{1,0:T(8,128)(2,1)} %collective-permute-done.56.refs_2_, bf16[256,2048]{1,0:T(8,128)(2,1)} %collective-permute-done.57.refs_3_, ...), custom_call_target="tpu_custom_call" | custom-call | flops 100000000 | tf_op jit(solution)/shard_map/pallas_call | solution.py:263
  450.9 11.9 %collective-permute-done.58.refs_3_ = bf16[256,2048]{1,0:T(8,128)(2,1)} collective-permute-done((bf16[256,2048]{1,0:T(8,128)(2,1)}, bf16[256,2048]{1,0:T(8,128)(2,1)}, u32[]{:S(2)}, u32[]{:S(2)}) %collective-permute-start.58) | collective-permute-done | bytes 1048608 | tf_op jit(solution)/shard_map/ppermute | solution.py:57
  463.3 3.3 shard_map.278
  472.7 11.7 %shard_map.280 = (bf16[1024,1536]{1,0:T(8,128)(2,1)}, bf16[1024,1024]{1,0:T(8,128)(2,1)}) custom-call(s32[4]{0:T(128)} %copy-done.42, s32[1]{0:T(128)} %bitcast.12.start, bf16[1024,1536]{1,0:T(8,128)(2,1)} %shard_map.259.packed, bf16[1024,1024]{1,0:T(8,128)(2,1)} %shard_map.260.early, bf16[1024,1024]{1,0:T(8,128)(2,1)} %get-tuple-element.298.weights, ...), custom_call_target="tpu_custom_call" | custom-call | flops 100000000 | tf_op jit(solution)/shard_map/pallas_call | solution.py:582
  484.4 8.2 %shard_map.281.refs_0_.refs_1_ = bf16[512,2048]{1,0:T(8,128)(2,1)} custom-call(bf16[1024,2048]{1,0:T(8,128)(2,1)} %bitcast.54, bf16[1024,1536]{1,0:T(8,128)(2,1)} %get-tuple-element.320.refs_1_.refs_0_, bf16[1024,2048]{1,0:T(8,128)(2,1)} %bitcast.59, bf16[1024,1024]{1,0:T(8,128)(2,1)} %get-tuple-element.307.refs_3_.refs_0_, ...), custom_call_target="tpu_custom_call" | custom-call | flops 100000000 | tf_op jit(solution)/shard_map/pallas_call | solution.py:337
  494.7 2.8 shard_map.282
  499.8 8.6 %shard_map.284 = (bf16[256,2048]{1,0:T(8,128)(2,1)}, bf16[256,2048]{1,0:T(8,128)(2,1)}, bf16[256,2048]{1,0:T(8,128)(2,1)}, bf16[256,2048]{1,0:T(8,128)(2,1)}) custom-call(bf16[1024,1024]{1,0:T(8,128)(2,1)} %get-tuple-element.307.refs_3_.refs_0_, bf16[2048,2048]{1,0:T(8,128)(2,1)} %constant_dynamic-update-slice_fusion.40.refs_1_.mix.refs_4_), custom_call_target="tpu_custom_call" | custom-call | flops 100000000 | tf_op jit(solution)/shard_map/pallas_call | solution.py:263
  508.5 8.2 %shard_map.285.refs_0_ = bf16[512,2048]{1,0:T(8,128)(2,1)} custom-call(bf16[1024,2048]{1,0:T(8,128)(2,1)} %bitcast.55, bf16[1024,1536]{1,0:T(8,128)(2,1)} %get-tuple-element.320.refs_1_.refs_0_, bf16[1024,2048]{1,0:T(8,128)(2,1)} %bitcast.60, bf16[1024,1024]{1,0:T(8,128)(2,1)} %get-tuple-element.307.refs_3_.refs_0_, ...), custom_call_target="tpu_custom_call" | custom-call | flops 100000000 | tf_op jit(solution)/shard_map/pallas_call | solution.py:337
  516.7 3.5 add_add_fusion.refs_0_
  524.0 3.2 shard_map.286
  536.1 10.6 %shard_map.288 = (bf16[256,2048]{1,0:T(8,128)(2,1)}, bf16[256,2048]{1,0:T(8,128)(2,1)}, bf16[256,2048]{1,0:T(8,128)(2,1)}, bf16[256,2048]{1,0:T(8,128)(2,1)}) custom-call(bf16[1024,1536]{1,0:T(8,128)(2,1)} %get-tuple-element.320.refs_1_.refs_0_, bf16[2048,2048]{1,0:T(8,128)(2,1)} %constant_dynamic-update-slice_fusion.40.refs_1_.mix.refs_4_), custom_call_target="tpu_custom_call" | custom-call | flops 100000000 | tf_op jit(solution)/shard_map/pallas_call | solution.py:263
  546.7 8.2 %shard_map.289.refs_1_ = bf16[512,2048]{1,0:T(8,128)(2,1)} custom-call(bf16[1024,2048]{1,0:T(8,128)(2,1)} %bitcast.56, bf16[1024,1536]{1,0:T(8,128)(2,1)} %get-tuple-element.320.refs_1_.refs_0_, bf16[1024,2048]{1,0:T(8,128)(2,1)} %bitcast.61, bf16[1024,1024]{1,0:T(8,128)(2,1)} %get-tuple-element.307.refs_3_.refs_0_, ...), custom_call_target="tpu_custom_call" | custom-call | flops 100000000 | tf_op jit(solution)/shard_map/pallas_call | solution.py:337
  555.0 3.4 shard_map.290
  564.4 3.5 shard_map.295
  575.8 8.3 %shard_map.291.refs_0_.own = bf16[512,2048]{1,0:T(8,128)(2,1)} custom-call(bf16[1024,2048]{1,0:T(8,128)(2,1)} %bitcast.57, bf16[1024,1536]{1,0:T(8,128)(2,1)} %get-tuple-element.320.refs_1_.refs_0_, bf16[1024,2048]{1,0:T(8,128)(2,1)} %bitcast.62, bf16[1024,1024]{1,0:T(8,128)(2,1)} %get-tuple-element.307.refs_3_.refs_0_, ...), custom_call_target="tpu_custom_call" | custom-call | flops 100000000 | tf_op jit(solution)/shard_map/pallas_call | solution.py:337
  587.8 3.3 shard_map.293
  591.2 21.8 %collective-permute-start.80 = (bf16[256,2048]{1,0:T(8,128)(2,1)}, bf16[256,2048]{1,0:T(8,128)(2,1)}, u32[]{:S(2)}, u32[]{:S(2)}) collective-permute-start(bf16[256,2048]{1,0:T(8,128)(2,1)} %get-tuple-element.340), channel_id=1, source_target_pairs={{8,0},{16,8},{24,16},{28,24},{20,28},{12,20},{4,12},{0,4},{9,1},{1... | collective-permute-start | bytes 3145736 | tf_op jit(solution)/shard_map/ppermute | solution.py:57
  613.0 2.8 shard_map.294
  615.8 3.2 convert_add_fusion.1
  619.0 4.2 add_reduce_fusion
  624.4 4.2 collective-permute-done.77
  628.7 3.3 fusion.11.refs_0_
  632.1 2.9 shard_map.296
  635.2 4.7 collective-permute-done.81
  640.0 4.6 shard_map.297
  (388 shorter events, 208.6 us)
Async XLA Ops:
  15.5 25.5 %collective-permute-start.7 = (bf16[256,2048]{1,0:T(8,128)(2,1)}, bf16[256,2048]{1,0:T(8,128)(2,1)}, u32[]{:S(2)}, u32[]{:S(2)}) collective-permute-start(bf16[256,2048]{1,0:T(8,128)(2,1)} %get-tuple-element.185), channel_id=1, source_target_pairs={{8,0},{16,8},{24,16},{28,24},{20,28},{12,20},{4,12},{0,4},{9,1},{1... | collective-permute-start | bytes 3145736 | tf_op jit(solution)/shard_map/ppermute | solution.py:57
  17.1 23.9 %collective-permute-start.6 = (bf16[256,2048]{1,0:T(8,128)(2,1)}, bf16[256,2048]{1,0:T(8,128)(2,1)}, u32[]{:S(2)}, u32[]{:S(2)}) collective-permute-start(bf16[256,2048]{1,0:T(8,128)(2,1)} %get-tuple-element.185), channel_id=1, source_target_pairs={{0,8},{8,16},{16,24},{24,28},{28,20},{20,12},{12,4},{4,0},{1,9},{9... | collective-permute-start | bytes 3145736 | tf_op jit(solution)/shard_map/ppermute | solution.py:57
  21.9 23.0 %collective-permute-start.4 = (bf16[256,2048]{1,0:T(8,128)(2,1)}, bf16[256,2048]{1,0:T(8,128)(2,1)}, u32[]{:S(2)}, u32[]{:S(2)}) collective-permute-start(bf16[256,2048]{1,0:T(8,128)(2,1)} %shard_map.254.refs_0_), channel_id=1, source_target_pairs={{0,2},{1,3},{2,0},{3,1},{4,6},{5,7},{6,4},{7,5},{8,10},{9,11},{10,... | collective-permute-start | bytes 3145736 | tf_op jit(solution)/shard_map/ppermute | solution.py:368
  26.2 37.3 %collective-permute-start.12 = (bf16[256,2048]{1,0:T(8,128)(2,1)}, bf16[256,2048]{1,0:T(8,128)(2,1)S(1)}, u32[]{:S(2)}, u32[]{:S(2)}) collective-permute-start(bf16[256,2048]{1,0:T(8,128)(2,1)} %shard_map.257), channel_id=1, source_target_pairs={{0,4},{4,8},{8,12},{12,16},{16,20},{20,24},{24,28},{1,5},{5,9},{9,... | collective-permute-start | bytes 3145736 | tf_op jit(solution)/shard_map/ppermute | solution.py:659
  41.0 26.9 %collective-permute-start.8 = (bf16[256,2048]{1,0:T(8,128)(2,1)}, bf16[256,2048]{1,0:T(8,128)(2,1)}, u32[]{:S(2)}, u32[]{:S(2)}) collective-permute-start(bf16[256,2048]{1,0:T(8,128)(2,1)} %collective-permute-done.6), channel_id=1, source_target_pairs={{0,8},{8,16},{16,24},{24,28},{28,20},{20,12},{12,4},{4,0},{1,9},{9... | collective-permute-start | bytes 3145736 | tf_op jit(solution)/shard_map/ppermute | solution.py:57
  41.0 41.8 %collective-permute-start.9 = (bf16[256,2048]{1,0:T(8,128)(2,1)}, bf16[256,2048]{1,0:T(8,128)(2,1)}, u32[]{:S(2)}, u32[]{:S(2)}) collective-permute-start(bf16[256,2048]{1,0:T(8,128)(2,1)} %collective-permute-done.7), channel_id=1, source_target_pairs={{8,0},{16,8},{24,16},{28,24},{20,28},{12,20},{4,12},{0,4},{9,1},{1... | collective-permute-start | bytes 3145736 | tf_op jit(solution)/shard_map/ppermute | solution.py:57
  44.8 41.2 %collective-permute-start.3 = (bf16[256,2048]{1,0:T(8,128)(2,1)S(1)}, bf16[256,2048]{1,0:T(8,128)(2,1)}, u32[]{:S(2)}, u32[]{:S(2)}) collective-permute-start(bf16[256,2048]{1,0:T(8,128)(2,1)S(1)} %copy-done.4), channel_id=1, source_target_pairs={{0,1},{1,0},{2,3},{3,2},{4,5},{5,4},{6,7},{7,6},{8,9},{9,8},{10,11... | collective-permute-start | bytes 3145736 | tf_op jit(solution)/shard_map/ppermute | solution.py:368
  44.9 42.6 %collective-permute-start.5 = (bf16[256,2048]{1,0:T(8,128)(2,1)}, bf16[256,2048]{1,0:T(8,128)(2,1)}, u32[]{:S(2)}, u32[]{:S(2)}) collective-permute-start(bf16[256,2048]{1,0:T(8,128)(2,1)} %collective-permute-done.4.refs_2_), channel_id=1, source_target_pairs={{0,1},{1,0},{2,3},{3,2},{4,5},{5,4},{6,7},{7,6},{8,9},{9,8},{10,11... | collective-permute-start | bytes 3145736 | tf_op jit(solution)/shard_map/ppermute | solution.py:368
  63.5 24.1 %collective-permute-start.14 = (bf16[256,2048]{1,0:T(8,128)(2,1)S(1)}, bf16[256,2048]{1,0:T(8,128)(2,1)}, u32[]{:S(2)}, u32[]{:S(2)}) collective-permute-start(bf16[256,2048]{1,0:T(8,128)(2,1)S(1)} %collective-permute-done.12.refs_0_), channel_id=1, source_target_pairs={{0,2},{1,3},{2,0},{3,1},{4,6},{5,7},{6,4},{7,5},{8,10},{9,11},{10,... | collective-permute-start | bytes 3145736 | tf_op jit(solution)/shard_map/ppermute | solution.py:368
  82.9 23.6 %collective-permute-start.16 = (bf16[256,2048]{1,0:T(8,128)(2,1)}, bf16[256,2048]{1,0:T(8,128)(2,1)}, u32[]{:S(2)}, u32[]{:S(2)}) collective-permute-start(bf16[256,2048]{1,0:T(8,128)(2,1)} %collective-permute-done.8), channel_id=1, source_target_pairs={{0,8},{8,16},{16,24},{24,28},{28,20},{20,12},{12,4},{4,0},{1,9},{9... | collective-permute-start | bytes 3145736 | tf_op jit(solution)/shard_map/ppermute | solution.py:57
  82.9 23.6 %collective-permute-start.17 = (bf16[256,2048]{1,0:T(8,128)(2,1)}, bf16[256,2048]{1,0:T(8,128)(2,1)}, u32[]{:S(2)}, u32[]{:S(2)}) collective-permute-start(bf16[256,2048]{1,0:T(8,128)(2,1)} %collective-permute-done.9), channel_id=1, source_target_pairs={{8,0},{16,8},{24,16},{28,24},{20,28},{12,20},{4,12},{0,4},{9,1},{1... | collective-permute-start | bytes 3145736 | tf_op jit(solution)/shard_map/ppermute | solution.py:57
  86.0 25.4 %collective-permute-start.22 = (bf16[256,2048]{1,0:T(8,128)(2,1)}, bf16[256,2048]{1,0:T(8,128)(2,1)}, u32[]{:S(2)}, u32[]{:S(2)}) collective-permute-start(bf16[256,2048]{1,0:T(8,128)(2,1)} %get-tuple-element.205), channel_id=1, source_target_pairs={{0,2},{1,3},{2,0},{3,1},{4,6},{5,7},{6,4},{7,5},{8,10},{9,11},{10,... | collective-permute-start | bytes 3145736 | tf_op jit(solution)/shard_map/ppermute | solution.py:368
  87.6 23.8 %collective-permute-start.13 = (bf16[256,2048]{1,0:T(8,128)(2,1)S(1)}, bf16[256,2048]{1,0:T(8,128)(2,1)}, u32[]{:S(2)}, u32[]{:S(2)}) collective-permute-start(bf16[256,2048]{1,0:T(8,128)(2,1)S(1)} %collective-permute-done.12.refs_0_), channel_id=1, source_target_pairs={{0,1},{1,0},{2,3},{3,2},{4,5},{5,4},{6,7},{7,6},{8,9},{9,8},{10,11... | collective-permute-start | bytes 3145736 | tf_op jit(solution)/shard_map/ppermute | solution.py:368
  87.6 24.3 %collective-permute-start.15 = (bf16[256,2048]{1,0:T(8,128)(2,1)}, bf16[256,2048]{1,0:T(8,128)(2,1)}, u32[]{:S(2)}, u32[]{:S(2)}) collective-permute-start(bf16[256,2048]{1,0:T(8,128)(2,1)} %collective-permute-done.14.refs_2_), channel_id=1, source_target_pairs={{0,1},{1,0},{2,3},{3,2},{4,5},{5,4},{6,7},{7,6},{8,9},{9,8},{10,11... | collective-permute-start | bytes 3145736 | tf_op jit(solution)/shard_map/ppermute | solution.py:368
  106.4 21.7 %collective-permute-start.18 = (bf16[256,2048]{1,0:T(8,128)(2,1)}, bf16[256,2048]{1,0:T(8,128)(2,1)}, u32[]{:S(2)}, u32[]{:S(2)}) collective-permute-start(bf16[256,2048]{1,0:T(8,128)(2,1)} %collective-permute-done.16), channel_id=1, source_target_pairs={{0,8},{8,16},{16,24},{24,28},{28,20},{20,12},{12,4},{4,0},{1,9},{9... | collective-permute-start | bytes 3145736 | tf_op jit(solution)/shard_map/ppermute | solution.py:57
  111.3 43.0 %collective-permute-start.21 = (bf16[256,2048]{1,0:T(8,128)(2,1)S(1)}, bf16[256,2048]{1,0:T(8,128)(2,1)S(1)}, u32[]{:S(2)}, u32[]{:S(2)}) collective-permute-start(bf16[256,2048]{1,0:T(8,128)(2,1)S(1)} %copy-done.18), channel_id=1, source_target_pairs={{0,1},{1,0},{2,3},{3,2},{4,5},{5,4},{6,7},{7,6},{8,9},{9,8},{10,11... | collective-permute-start | bytes 3145736 | tf_op jit(solution)/shard_map/ppermute | solution.py:368
  111.3 43.0 %collective-permute-start.23 = (bf16[256,2048]{1,0:T(8,128)(2,1)}, bf16[256,2048]{1,0:T(8,128)(2,1)}, u32[]{:S(2)}, u32[]{:S(2)}) collective-permute-start(bf16[256,2048]{1,0:T(8,128)(2,1)} %collective-permute-done.22), channel_id=1, source_target_pairs={{0,1},{1,0},{2,3},{3,2},{4,5},{5,4},{6,7},{7,6},{8,9},{9,8},{10,11... | collective-permute-start | bytes 3145736 | tf_op jit(solution)/shard_map/ppermute | solution.py:368
  129.9 24.4 %collective-permute-start.20 = (bf16[256,2048]{1,0:T(8,128)(2,1)}, bf16[256,2048]{1,0:T(8,128)(2,1)}, u32[]{:S(2)}, u32[]{:S(2)}) collective-permute-start(bf16[256,2048]{1,0:T(8,128)(2,1)} %param.26), channel_id=1, source_target_pairs={{0,8},{8,16},{16,24},{24,28},{28,20},{20,12},{12,4},{4,0},{1,9},{9... | collective-permute-start | bytes 3145736 | tf_op jit(solution)/shard_map/ppermute | solution.py:57
  131.9 22.6 %collective-permute-start.24 = (bf16[256,2048]{1,0:T(8,128)(2,1)}, bf16[256,2048]{1,0:T(8,128)(2,1)}, u32[]{:S(2)}, u32[]{:S(2)}) collective-permute-start(bf16[256,2048]{1,0:T(8,128)(2,1)} %collective-permute-done.19), channel_id=1, source_target_pairs={{8,0},{16,8},{24,16},{28,24},{20,28},{12,20},{4,12},{0,4},{9,1},{1... | collective-permute-start | bytes 3145736 | tf_op jit(solution)/shard_map/ppermute | solution.py:57
  154.5 22.1 %collective-permute-start.25 = (bf16[256,2048]{1,0:T(8,128)(2,1)}, bf16[256,2048]{1,0:T(8,128)(2,1)}, u32[]{:S(2)}, u32[]{:S(2)}) collective-permute-start(bf16[256,2048]{1,0:T(8,128)(2,1)} %collective-permute-done.20), channel_id=1, source_target_pairs={{0,8},{8,16},{16,24},{24,28},{28,20},{20,12},{12,4},{4,0},{1,9},{9... | collective-permute-start | bytes 3145736 | tf_op jit(solution)/shard_map/ppermute | solution.py:57
  156.5 22.4 %collective-permute-start.26 = (bf16[256,2048]{1,0:T(8,128)(2,1)}, bf16[256,2048]{1,0:T(8,128)(2,1)}, u32[]{:S(2)}, u32[]{:S(2)}) collective-permute-start(bf16[256,2048]{1,0:T(8,128)(2,1)} %collective-permute-done.24), channel_id=1, source_target_pairs={{8,0},{16,8},{24,16},{28,24},{20,28},{12,20},{4,12},{0,4},{9,1},{1... | collective-permute-start | bytes 3145736 | tf_op jit(solution)/shard_map/ppermute | solution.py:57
  182.7 25.9 %collective-permute-start.32 = (bf16[256,2048]{1,0:T(8,128)(2,1)}, bf16[256,2048]{1,0:T(8,128)(2,1)}, u32[]{:S(2)}, u32[]{:S(2)}) collective-permute-start(bf16[256,2048]{1,0:T(8,128)(2,1)} %collective-permute-done.25), channel_id=1, source_target_pairs={{0,8},{8,16},{16,24},{24,28},{28,20},{20,12},{12,4},{4,0},{1,9},{9... | collective-permute-start | bytes 3145736 | tf_op jit(solution)/shard_map/ppermute | solution.py:57
  184.5 25.6 %collective-permute-start.33 = (bf16[256,2048]{1,0:T(8,128)(2,1)}, bf16[256,2048]{1,0:T(8,128)(2,1)}, u32[]{:S(2)}, u32[]{:S(2)}) collective-permute-start(bf16[256,2048]{1,0:T(8,128)(2,1)} %collective-permute-done.26), channel_id=1, source_target_pairs={{8,0},{16,8},{24,16},{28,24},{20,28},{12,20},{4,12},{0,4},{9,1},{1... | collective-permute-start | bytes 3145736 | tf_op jit(solution)/shard_map/ppermute | solution.py:57
  184.7 27.4 %collective-permute-start.27 = (bf16[256,2048]{1,0:T(8,128)(2,1)}, bf16[256,2048]{1,0:T(8,128)(2,1)S(1)}, u32[]{:S(2)}, u32[]{:S(2)}) collective-permute-start(bf16[256,2048]{1,0:T(8,128)(2,1)} %get-tuple-element.217), channel_id=1, source_target_pairs={{0,1},{1,0},{2,3},{3,2},{4,5},{5,4},{6,7},{7,6},{8,9},{9,8},{10,11... | collective-permute-start | bytes 3145736 | tf_op jit(solution)/shard_map/ppermute | solution.py:368
  188.2 25.8 %collective-permute-start.29 = (bf16[256,2048]{1,0:T(8,128)(2,1)}, bf16[256,2048]{1,0:T(8,128)(2,1)S(1)}, u32[]{:S(2)}, u32[]{:S(2)}) collective-permute-start(bf16[256,2048]{1,0:T(8,128)(2,1)} %shard_map.262), channel_id=1, source_target_pairs={{0,2},{1,3},{2,0},{3,1},{4,6},{5,7},{6,4},{7,5},{8,10},{9,11},{10,... | collective-permute-start | bytes 3145736 | tf_op jit(solution)/shard_map/ppermute | solution.py:368
  210.1 24.6 %collective-permute-start.35 = (bf16[2048,256]{1,0:T(8,128)(2,1)S(1)}, bf16[2048,256]{1,0:T(8,128)(2,1)}, u32[]{:S(2)}, u32[]{:S(2)}) collective-permute-start(bf16[2048,256]{1,0:T(8,128)(2,1)S(1)} %copy-done.16), channel_id=1, source_target_pairs={{8,0},{16,8},{24,16},{28,24},{20,28},{12,20},{4,12},{0,4},{9,1},{1... | collective-permute-start | bytes 3145736 | tf_op jit(solution)/shard_map/ppermute | solution.py:57
  210.4 24.3 %collective-permute-start.34 = (bf16[2048,256]{1,0:T(8,128)(2,1)S(1)}, bf16[2048,256]{1,0:T(8,128)(2,1)}, u32[]{:S(2)}, u32[]{:S(2)}) collective-permute-start(bf16[2048,256]{1,0:T(8,128)(2,1)S(1)} %copy-done.16), channel_id=1, source_target_pairs={{0,8},{8,16},{16,24},{24,28},{28,20},{20,12},{12,4},{4,0},{1,9},{9... | collective-permute-start | bytes 3145736 | tf_op jit(solution)/shard_map/ppermute | solution.py:57
  217.2 24.9 %collective-permute-start.31 = (bf16[256,2048]{1,0:T(8,128)(2,1)S(1)}, bf16[256,2048]{1,0:T(8,128)(2,1)S(1)}, u32[]{:S(2)}, u32[]{:S(2)}) collective-permute-start(bf16[256,2048]{1,0:T(8,128)(2,1)S(1)} %add_convert_fusion.refs_0_), channel_id=1, source_target_pairs={{0,2},{1,3},{2,0},{3,1},{4,6},{5,7},{6,4},{7,5},{8,10},{9,11},{10,... | collective-permute-start | bytes 3145736 | tf_op jit(solution)/shard_map/ppermute | solution.py:368
  242.1 25.9 %collective-permute-start.37 = (bf16[2048,256]{1,0:T(8,128)(2,1)}, bf16[2048,256]{1,0:T(8,128)(2,1)}, u32[]{:S(2)}, u32[]{:S(2)}) collective-permute-start(bf16[2048,256]{1,0:T(8,128)(2,1)} %collective-permute-done.34), channel_id=1, source_target_pairs={{0,8},{8,16},{16,24},{24,28},{28,20},{20,12},{12,4},{4,0},{1,9},{9... | collective-permute-start | bytes 3145736 | tf_op jit(solution)/shard_map/ppermute | solution.py:57
  243.8 25.7 %collective-permute-start.38 = (bf16[2048,256]{1,0:T(8,128)(2,1)}, bf16[2048,256]{1,0:T(8,128)(2,1)}, u32[]{:S(2)}, u32[]{:S(2)}) collective-permute-start(bf16[2048,256]{1,0:T(8,128)(2,1)} %collective-permute-done.35), channel_id=1, source_target_pairs={{8,0},{16,8},{24,16},{28,24},{20,28},{12,20},{4,12},{0,4},{9,1},{1... | collective-permute-start | bytes 3145736 | tf_op jit(solution)/shard_map/ppermute | solution.py:57
  269.5 24.9 %collective-permute-start.39 = (bf16[2048,256]{1,0:T(8,128)(2,1)}, bf16[2048,256]{1,0:T(8,128)(2,1)}, u32[]{:S(2)}, u32[]{:S(2)}) collective-permute-start(bf16[2048,256]{1,0:T(8,128)(2,1)} %collective-permute-done.37), channel_id=1, source_target_pairs={{0,8},{8,16},{16,24},{24,28},{28,20},{20,12},{12,4},{4,0},{1,9},{9... | collective-permute-start | bytes 3145736 | tf_op jit(solution)/shard_map/ppermute | solution.py:57
  271.3 24.5 %collective-permute-start.40 = (bf16[2048,256]{1,0:T(8,128)(2,1)}, bf16[2048,256]{1,0:T(8,128)(2,1)}, u32[]{:S(2)}, u32[]{:S(2)}) collective-permute-start(bf16[2048,256]{1,0:T(8,128)(2,1)} %collective-permute-done.38), channel_id=1, source_target_pairs={{8,0},{16,8},{24,16},{28,24},{20,28},{12,20},{4,12},{0,4},{9,1},{1... | collective-permute-start | bytes 3145736 | tf_op jit(solution)/shard_map/ppermute | solution.py:57
  295.8 24.0 %collective-permute-start.41 = (bf16[256,2048]{1,0:T(8,128)(2,1)}, bf16[256,2048]{1,0:T(8,128)(2,1)}, u32[]{:S(2)}, u32[]{:S(2)}) collective-permute-start(bf16[256,2048]{1,0:T(8,128)(2,1)} %shard_map.265), channel_id=1, source_target_pairs={{8,0},{16,8},{24,16},{28,24},{20,28},{12,20},{4,12},{0,4},{9,1},{1... | collective-permute-start | bytes 3145736 | tf_op jit(solution)/shard_map/ppermute | solution.py:57
  296.6 23.4 %collective-permute-start.42 = (bf16[2048,256]{1,0:T(8,128)(2,1)}, bf16[2048,256]{1,0:T(8,128)(2,1)}, u32[]{:S(2)}, u32[]{:S(2)}) collective-permute-start(bf16[2048,256]{1,0:T(8,128)(2,1)} %collective-permute-done.39), channel_id=1, source_target_pairs={{0,8},{8,16},{16,24},{24,28},{28,20},{20,12},{12,4},{4,0},{1,9},{9... | collective-permute-start | bytes 3145736 | tf_op jit(solution)/shard_map/ppermute | solution.py:57
  322.9 22.4 %collective-permute-start.44 = (bf16[256,2048]{1,0:T(8,128)(2,1)}, bf16[256,2048]{1,0:T(8,128)(2,1)S(1)}, u32[]{:S(2)}, u32[]{:S(2)}) collective-permute-start(bf16[256,2048]{1,0:T(8,128)(2,1)} %get-tuple-element.238), channel_id=1, source_target_pairs={{8,0},{16,8},{24,16},{28,24},{20,28},{12,20},{4,12},{0,4},{9,1},{1... | collective-permute-start | bytes 3145736 | tf_op jit(solution)/shard_map/ppermute | solution.py:57
  323.3 22.4 %collective-permute-start.43 = (bf16[256,2048]{1,0:T(8,128)(2,1)}, bf16[256,2048]{1,0:T(8,128)(2,1)}, u32[]{:S(2)}, u32[]{:S(2)}) collective-permute-start(bf16[256,2048]{1,0:T(8,128)(2,1)} %get-tuple-element.236), channel_id=1, source_target_pairs={{0,8},{8,16},{16,24},{24,28},{28,20},{20,12},{12,4},{4,0},{1,9},{9... | collective-permute-start | bytes 3145736 | tf_op jit(solution)/shard_map/ppermute | solution.py:57
  350.2 21.6 %collective-permute-start.45 = (bf16[256,2048]{1,0:T(8,128)(2,1)}, bf16[256,2048]{1,0:T(8,128)(2,1)}, u32[]{:S(2)}, u32[]{:S(2)}) collective-permute-start(bf16[256,2048]{1,0:T(8,128)(2,1)} %get-tuple-element.245), channel_id=1, source_target_pairs={{0,8},{8,16},{16,24},{24,28},{28,20},{20,12},{12,4},{4,0},{1,9},{9... | collective-permute-start | bytes 3145736 | tf_op jit(solution)/shard_map/ppermute | solution.py:57
  375.5 25.8 %collective-permute-start.51 = (bf16[256,2048]{1,0:T(8,128)(2,1)}, bf16[256,2048]{1,0:T(8,128)(2,1)S(1)}, u32[]{:S(2)}, u32[]{:S(2)}) collective-permute-start(bf16[256,2048]{1,0:T(8,128)(2,1)} %get-tuple-element.258), channel_id=1, source_target_pairs={{8,0},{16,8},{24,16},{28,24},{20,28},{12,20},{4,12},{0,4},{9,1},{1... | collective-permute-start | bytes 3145736 | tf_op jit(solution)/shard_map/ppermute | solution.py:57
  376.3 25.6 %collective-permute-start.50 = (bf16[256,2048]{1,0:T(8,128)(2,1)}, bf16[256,2048]{1,0:T(8,128)(2,1)}, u32[]{:S(2)}, u32[]{:S(2)}) collective-permute-start(bf16[256,2048]{1,0:T(8,128)(2,1)} %get-tuple-element.256), channel_id=1, source_target_pairs={{0,8},{8,16},{16,24},{24,28},{28,20},{20,12},{12,4},{4,0},{1,9},{9... | collective-permute-start | bytes 3145736 | tf_op jit(solution)/shard_map/ppermute | solution.py:57
  377.6 26.5 %collective-permute-start.47 = (bf16[256,2048]{1,0:T(8,128)(2,1)}, bf16[256,2048]{1,0:T(8,128)(2,1)}, u32[]{:S(2)}, u32[]{:S(2)}) collective-permute-start(bf16[256,2048]{1,0:T(8,128)(2,1)} %get-tuple-element.260), channel_id=1, source_target_pairs={{0,1},{1,0},{2,3},{3,2},{4,5},{5,4},{6,7},{7,6},{8,9},{9,8},{10,11... | collective-permute-start | bytes 3145736 | tf_op jit(solution)/shard_map/ppermute | solution.py:368
  380.9 25.5 %collective-permute-start.49 = (bf16[256,2048]{1,0:T(8,128)(2,1)}, bf16[256,2048]{1,0:T(8,128)(2,1)}, u32[]{:S(2)}, u32[]{:S(2)}) collective-permute-start(bf16[256,2048]{1,0:T(8,128)(2,1)} %shard_map.271), channel_id=1, source_target_pairs={{0,2},{1,3},{2,0},{3,1},{4,6},{5,7},{6,4},{7,5},{8,10},{9,11},{10,... | collective-permute-start | bytes 3145736 | tf_op jit(solution)/shard_map/ppermute | solution.py:368
  401.9 24.7 %collective-permute-start.53 = (bf16[256,2048]{1,0:T(8,128)(2,1)}, bf16[256,2048]{1,0:T(8,128)(2,1)}, u32[]{:S(2)}, u32[]{:S(2)}) collective-permute-start(bf16[256,2048]{1,0:T(8,128)(2,1)} %get-tuple-element.268), channel_id=1, source_target_pairs={{8,0},{16,8},{24,16},{28,24},{20,28},{12,20},{4,12},{0,4},{9,1},{1... | collective-permute-start | bytes 3145736 | tf_op jit(solution)/shard_map/ppermute | solution.py:57
  402.4 24.7 %collective-permute-start.52 = (bf16[256,2048]{1,0:T(8,128)(2,1)}, bf16[256,2048]{1,0:T(8,128)(2,1)}, u32[]{:S(2)}, u32[]{:S(2)}) collective-permute-start(bf16[256,2048]{1,0:T(8,128)(2,1)} %get-tuple-element.266), channel_id=1, source_target_pairs={{0,8},{8,16},{16,24},{24,28},{28,20},{20,12},{12,4},{4,0},{1,9},{9... | collective-permute-start | bytes 3145736 | tf_op jit(solution)/shard_map/ppermute | solution.py:57
  412.4 24.5 %collective-permute-start.56 = (bf16[256,2048]{1,0:T(8,128)(2,1)S(1)}, bf16[256,2048]{1,0:T(8,128)(2,1)}, u32[]{:S(2)}, u32[]{:S(2)}) collective-permute-start(bf16[256,2048]{1,0:T(8,128)(2,1)S(1)} %get-tuple-element.283.refs_0_), channel_id=1, source_target_pairs={{0,2},{1,3},{2,0},{3,1},{4,6},{5,7},{6,4},{7,5},{8,10},{9,11},{10,... | collective-permute-start | bytes 3145736 | tf_op jit(solution)/shard_map/ppermute | solution.py:368
  412.9 30.3 %collective-permute-start.55 = (bf16[256,2048]{1,0:T(8,128)(2,1)S(1)}, bf16[256,2048]{1,0:T(8,128)(2,1)}, u32[]{:S(2)}, u32[]{:S(2)}) collective-permute-start(bf16[256,2048]{1,0:T(8,128)(2,1)S(1)} %get-tuple-element.283.refs_0_), channel_id=1, source_target_pairs={{0,1},{1,0},{2,3},{3,2},{4,5},{5,4},{6,7},{7,6},{8,9},{9,8},{10,11... | collective-permute-start | bytes 3145736 | tf_op jit(solution)/shard_map/ppermute | solution.py:368
  436.9 25.9 %collective-permute-start.58 = (bf16[256,2048]{1,0:T(8,128)(2,1)}, bf16[256,2048]{1,0:T(8,128)(2,1)}, u32[]{:S(2)}, u32[]{:S(2)}) collective-permute-start(bf16[256,2048]{1,0:T(8,128)(2,1)} %get-tuple-element.280), channel_id=1, source_target_pairs={{8,0},{16,8},{24,16},{28,24},{20,28},{12,20},{4,12},{0,4},{9,1},{1... | collective-permute-start | bytes 3145736 | tf_op jit(solution)/shard_map/ppermute | solution.py:57
  437.7 25.6 %collective-permute-start.54 = (bf16[256,2048]{1,0:T(8,128)(2,1)}, bf16[256,2048]{1,0:T(8,128)(2,1)}, u32[]{:S(2)}, u32[]{:S(2)}) collective-permute-start(bf16[256,2048]{1,0:T(8,128)(2,1)} %get-tuple-element.278), channel_id=1, source_target_pairs={{0,8},{8,16},{16,24},{24,28},{28,20},{20,12},{12,4},{4,0},{1,9},{9... | collective-permute-start | bytes 3145736 | tf_op jit(solution)/shard_map/ppermute | solution.py:57
  466.6 28.1 %collective-permute-start.63 = (bf16[256,2048]{1,0:T(8,128)(2,1)}, bf16[256,2048]{1,0:T(8,128)(2,1)S(1)}, u32[]{:S(2)}, u32[]{:S(2)}) collective-permute-start(bf16[256,2048]{1,0:T(8,128)(2,1)} %get-tuple-element.293), channel_id=1, source_target_pairs={{8,0},{16,8},{24,16},{28,24},{20,28},{12,20},{4,12},{0,4},{9,1},{1... | collective-permute-start | bytes 3145736 | tf_op jit(solution)/shard_map/ppermute | solution.py:57
  467.2 27.5 %collective-permute-start.62 = (bf16[256,2048]{1,0:T(8,128)(2,1)}, bf16[256,2048]{1,0:T(8,128)(2,1)}, u32[]{:S(2)}, u32[]{:S(2)}) collective-permute-start(bf16[256,2048]{1,0:T(8,128)(2,1)} %get-tuple-element.291), channel_id=1, source_target_pairs={{0,8},{8,16},{16,24},{24,28},{28,20},{20,12},{12,4},{4,0},{1,9},{9... | collective-permute-start | bytes 3145736 | tf_op jit(solution)/shard_map/ppermute | solution.py:57
  468.7 48.0 %collective-permute-start.59 = (bf16[256,2048]{1,0:T(8,128)(2,1)}, bf16[256,2048]{1,0:T(8,128)(2,1)}, u32[]{:S(2)}, u32[]{:S(2)}) collective-permute-start(bf16[256,2048]{1,0:T(8,128)(2,1)} %get-tuple-element.295), channel_id=1, source_target_pairs={{0,1},{1,0},{2,3},{3,2},{4,5},{5,4},{6,7},{7,6},{8,9},{9,8},{10,11... | collective-permute-start | bytes 3145736 | tf_op jit(solution)/shard_map/ppermute | solution.py:368
  472.1 44.7 %collective-permute-start.61 = (bf16[256,2048]{1,0:T(8,128)(2,1)}, bf16[256,2048]{1,0:T(8,128)(2,1)}, u32[]{:S(2)}, u32[]{:S(2)}) collective-permute-start(bf16[256,2048]{1,0:T(8,128)(2,1)} %shard_map.279), channel_id=1, source_target_pairs={{0,2},{1,3},{2,0},{3,1},{4,6},{5,7},{6,4},{7,5},{8,10},{9,11},{10,... | collective-permute-start | bytes 3145736 | tf_op jit(solution)/shard_map/ppermute | solution.py:368
  497.5 25.3 %collective-permute-start.64 = (bf16[256,2048]{1,0:T(8,128)(2,1)}, bf16[256,2048]{1,0:T(8,128)(2,1)}, u32[]{:S(2)}, u32[]{:S(2)}) collective-permute-start(bf16[256,2048]{1,0:T(8,128)(2,1)} %shard_map.283), channel_id=1, source_target_pairs={{8,0},{16,8},{24,16},{28,24},{20,28},{12,20},{4,12},{0,4},{9,1},{1... | collective-permute-start | bytes 3145736 | tf_op jit(solution)/shard_map/ppermute | solution.py:57
  499.0 25.0 %collective-permute-start.65 = (bf16[256,2048]{1,0:T(8,128)(2,1)}, bf16[256,2048]{1,0:T(8,128)(2,1)S(1)}, u32[]{:S(2)}, u32[]{:S(2)}) collective-permute-start(bf16[256,2048]{1,0:T(8,128)(2,1)} %shard_map.282), channel_id=1, source_target_pairs={{0,8},{8,16},{16,24},{24,28},{28,20},{20,12},{12,4},{4,0},{1,9},{9... | collective-permute-start | bytes 3145736 | tf_op jit(solution)/shard_map/ppermute | solution.py:57
  527.3 27.7 %collective-permute-start.68 = (bf16[256,2048]{1,0:T(8,128)(2,1)}, bf16[256,2048]{1,0:T(8,128)(2,1)}, u32[]{:S(2)}, u32[]{:S(2)}) collective-permute-start(bf16[256,2048]{1,0:T(8,128)(2,1)} %get-tuple-element.317), channel_id=1, source_target_pairs={{8,0},{16,8},{24,16},{28,24},{20,28},{12,20},{4,12},{0,4},{9,1},{1... | collective-permute-start | bytes 3145736 | tf_op jit(solution)/shard_map/ppermute | solution.py:57
  528.8 26.1 %collective-permute-start.67 = (bf16[256,2048]{1,0:T(8,128)(2,1)}, bf16[256,2048]{1,0:T(8,128)(2,1)}, u32[]{:S(2)}, u32[]{:S(2)}) collective-permute-start(bf16[256,2048]{1,0:T(8,128)(2,1)} %get-tuple-element.315), channel_id=1, source_target_pairs={{0,8},{8,16},{16,24},{24,28},{28,20},{20,12},{12,4},{4,0},{1,9},{9... | collective-permute-start | bytes 3145736 | tf_op jit(solution)/shard_map/ppermute | solution.py:57
  530.3 32.2 %collective-permute-start.74 = (bf16[256,2048]{1,0:T(8,128)(2,1)}, bf16[256,2048]{1,0:T(8,128)(2,1)S(1)}, u32[]{:S(2)}, u32[]{:S(2)}) collective-permute-start(bf16[256,2048]{1,0:T(8,128)(2,1)} %get-tuple-element.345), channel_id=1, source_target_pairs={{0,1},{1,0},{2,3},{3,2},{4,5},{5,4},{6,7},{7,6},{8,9},{9,8},{10,11... | collective-permute-start | bytes 3145736 | tf_op jit(solution)/shard_map/ppermute | solution.py:368
  535.6 26.9 %collective-permute-start.75 = (bf16[256,2048]{1,0:T(8,128)(2,1)}, bf16[256,2048]{1,0:T(8,128)(2,1)S(1)}, u32[]{:S(2)}, u32[]{:S(2)}) collective-permute-start(bf16[256,2048]{1,0:T(8,128)(2,1)} %shard_map.287), channel_id=1, source_target_pairs={{0,2},{1,3},{2,0},{3,1},{4,6},{5,7},{6,4},{7,5},{8,10},{9,11},{10,... | collective-permute-start | bytes 3145736 | tf_op jit(solution)/shard_map/ppermute | solution.py:368
  559.9 26.3 %collective-permute-start.71 = (bf16[256,2048]{1,0:T(8,128)(2,1)}, bf16[256,2048]{1,0:T(8,128)(2,1)}, u32[]{:S(2)}, u32[]{:S(2)}) collective-permute-start(bf16[256,2048]{1,0:T(8,128)(2,1)} %get-tuple-element.328), channel_id=1, source_target_pairs={{8,0},{16,8},{24,16},{28,24},{20,28},{12,20},{4,12},{0,4},{9,1},{1... | collective-permute-start | bytes 3145736 | tf_op jit(solution)/shard_map/ppermute | solution.py:57
  561.5 26.3 %collective-permute-start.69 = (bf16[256,2048]{1,0:T(8,128)(2,1)}, bf16[256,2048]{1,0:T(8,128)(2,1)}, u32[]{:S(2)}, u32[]{:S(2)}) collective-permute-start(bf16[256,2048]{1,0:T(8,128)(2,1)} %get-tuple-element.326), channel_id=1, source_target_pairs={{0,8},{8,16},{16,24},{24,28},{28,20},{20,12},{12,4},{4,0},{1,9},{9... | collective-permute-start | bytes 3145736 | tf_op jit(solution)/shard_map/ppermute | solution.py:57
  562.5 56.5 %collective-permute-start.72 = (bf16[256,2048]{1,0:T(8,128)(2,1)}, bf16[256,2048]{1,0:T(8,128)(2,1)}, u32[]{:S(2)}, u32[]{:S(2)}) collective-permute-start(bf16[256,2048]{1,0:T(8,128)(2,1)} %get-tuple-element.343), channel_id=1, source_target_pairs={{0,1},{1,0},{2,3},{3,2},{4,5},{5,4},{6,7},{7,6},{8,9},{9,8},{10,11... | collective-permute-start | bytes 3145736 | tf_op jit(solution)/shard_map/ppermute | solution.py:368
  567.9 51.0 %collective-permute-start.76 = (bf16[256,2048]{1,0:T(8,128)(2,1)}, bf16[256,2048]{1,0:T(8,128)(2,1)}, u32[]{:S(2)}, u32[]{:S(2)}) collective-permute-start(bf16[256,2048]{1,0:T(8,128)(2,1)} %shard_map.295), channel_id=1, source_target_pairs={{4,0},{8,4},{12,8},{16,12},{20,16},{24,20},{28,24},{5,1},{9,5},{13... | collective-permute-start | bytes 3145736 | tf_op jit(solution)/shard_map/ppermute | solution.py:801
  572.2 46.8 %collective-permute-start.73 = (bf16[256,2048]{1,0:T(8,128)(2,1)}, bf16[256,2048]{1,0:T(8,128)(2,1)}, u32[]{:S(2)}, u32[]{:S(2)}) collective-permute-start(bf16[256,2048]{1,0:T(8,128)(2,1)} %shard_map.292), channel_id=1, source_target_pairs={{0,2},{1,3},{2,0},{3,1},{4,6},{5,7},{6,4},{7,5},{8,10},{9,11},{10,... | collective-permute-start | bytes 3145736 | tf_op jit(solution)/shard_map/ppermute | solution.py:368
  591.2 43.9 %collective-permute-start.80 = (bf16[256,2048]{1,0:T(8,128)(2,1)}, bf16[256,2048]{1,0:T(8,128)(2,1)}, u32[]{:S(2)}, u32[]{:S(2)}) collective-permute-start(bf16[256,2048]{1,0:T(8,128)(2,1)} %get-tuple-element.340), channel_id=1, source_target_pairs={{8,0},{16,8},{24,16},{28,24},{20,28},{12,20},{4,12},{0,4},{9,1},{1... | collective-permute-start | bytes 3145736 | tf_op jit(solution)/shard_map/ppermute | solution.py:57
  613.0 22.1 %collective-permute-start.79 = (bf16[256,2048]{1,0:T(8,128)(2,1)}, bf16[256,2048]{1,0:T(8,128)(2,1)}, u32[]{:S(2)}, u32[]{:S(2)}) collective-permute-start(bf16[256,2048]{1,0:T(8,128)(2,1)} %get-tuple-element.338), channel_id=1, source_target_pairs={{0,8},{8,16},{16,24},{24,28},{28,20},{20,12},{12,4},{4,0},{1,9},{9... | collective-permute-start | bytes 3145736 | tf_op jit(solution)/shard_map/ppermute | solution.py:57
  (65 other events, 578.4 us)

commit v7 on v6

--- a/solution.py
+++ b/solution.py
@@ -344,9 +344,32 @@
     )(*arrays)
 
 
+def norm_back_parts(parts, unit, factor, gain, straight):
+    rows, width = unit.shape
+    step = 128
+
+    def kernel(*refs):
+        grad = sum(ref[...].astype(F32) for ref in refs[: len(parts)])
+        unit, factor, gain, straight, total, rounded = refs[len(parts) :]
+        value = straight[...] + norm_back(grad, unit[...], factor[...], gain[...])
+        total[...] = value
+        rounded[...] = value.astype(BF16)
+
+    block = lambda w: pl.BlockSpec((step, w), lambda i: (i, 0))
+    return pl.pallas_call(
+        kernel,
+        grid=(rows // step,),
+        in_specs=[block(width)] * (len(parts) + 1)
+        + [block(1), pl.BlockSpec((1, width), lambda i: (0, 0)), block(width)],
+        out_specs=[block(width)] * 2,
+        out_shape=[jax.ShapeDtypeStruct((rows, width), kind) for kind in (F32, BF16)],
+        cost_estimate=QUICK,
+    )(*parts, unit, factor, gain[None], straight)
+
+
 def norm_parts(parts, gain, shift):
     rows, width = parts[0].shape
-    step = 64
+    step = 128
 
     def kernel(*refs):
         for i in range(len(parts)):
@@ -744,13 +767,14 @@
     ring.due(*parts)
     ring.advance()
     sent = []
-    grad_second = batch_scatter(ring.now(*parts), sent.append)
+    grad_second = batch_scatter(ring.now(*parts), sent.append, True)
     late["up"] = straight(tie(second, *sent), grad_pre)
     ring.due(late["up"])
     ring.advance()
-    grad_second = ring.now(grad_second)
-    grad_resid = grad_out + norm_back(grad_second, unit_two, factor_two, gain_two)
-    grad_branch_own = grad_resid.astype(BF16)
+    grad_resid, grad_branch_own = norm_back_parts(
+        ring.now(*grad_second), unit_two, factor_two, gain_two, grad_out
+    )
+    grad_second = sum(v.astype(F32) for v in grad_second)
     result = matmul([tie(active, grad_branch_own)], down_in, finish_parts, ["parts"])
     ring.due(*result)
     ring.advance(1 + more)

time: 661 us -> 660 us (level)
  starting transfers between devices: 92.2 us -> 72.8 us
  waiting for transfers between devices: 161 us -> 175 us
    ppermute x42, starting transfers between devices: 65 us -> 46.3 us  [hop(): self.last[forward] = lax.ppermute(value, 'seq', list(pairs))]
    ppermute x1, waiting for transfers between devices: 0.01 us -> 11.1 us  [shards(): moved = lax.ppermute(moved, 'seq', [(i + 1, i) for i in range(count - 1)])]
    unnamed x118 -> x112, local copies, waits for them, and re-layouts: 58.6 us -> 57.6 us
  transfers between devices with their start and end apart: 84 -> 84, of which waited for: 45 -> 48; matrix products, arithmetic and copies ran while one was open for 16% -> 16% of each run, Pallas kernels for 40% -> 41%
where the time goes in v7:
time: 660 us; the launch traced here: 650 us
  Pallas kernels  284 us (43%)
  waiting for transfers between devices  175 us (27%)
  local copies, waits for them, and re-layouts  81.8 us (12%)
  starting transfers between devices  72.8 us (11%)
  other arithmetic  34.3 us (5%)
    ppermute x42, waiting for transfers between devices, hop(): self.last[forward] = lax.ppermute(value, 'seq', list(pairs))  113 us
    pallas_call x9, Pallas kernels, matmul(): pl.pallas_call(kernel, grid=(tiles,), in_specs=[pl.BlockSpec(v.shape, lam...  106 us
    pallas_call x6, Pallas kernels, token_products(): pl.pallas_call(kernel, grid=(len(plan),), in_specs=specs, out_specs=pl.Bl...  60.2 us
    unnamed x112, local copies, waits for them, and re-layouts  57.6 us
    ppermute x42, starting transfers between devices, hop(): self.last[forward] = lax.ppermute(value, 'seq', list(pairs))  46.3 us
    pallas_call x12, Pallas kernels, join(): pl.pallas_call(kernel, grid=(steps,), in_specs=[pl.BlockSpec((step, width...  35.6 us
    ppermute x40, waiting for transfers between devices, swap(): lax.ppermute(value, axis, [(i, i ^ bit) for i in range(lax.axis_size(axis...  32.2 us
    pallas_call x2, Pallas kernels, per_chain(): pl.pallas_call(kernel, grid_spec=pltpu.PrefetchScalarGridSpec(num_scalar_...  26.6 us
  transfers between devices with their start and end apart: 84, of which 48 were waited for; matrix products, arithmetic and copies ran while one was open for 16% of the time, Pallas kernels for 41%

profile of v7, /device:TPU:0, one launch (start us, length us, event | category | flops | bytes accessed | tf_op | source)
XLA Modules:
  0.0 649.7 jit_solution(14532007514780823861)
XLA Ops:
  1.4 3.0 collective-permute-start
  18.7 2.8 shard_map.254.refs_0_
  22.9 2.7 shard_map.257
  25.7 3.4 collective-permute-start.12
  29.4 11.6 %collective-permute-done.7 = bf16[256,2048]{1,0:T(8,128)(2,1)} collective-permute-done((bf16[256,2048]{1,0:T(8,128)(2,1)}, bf16[256,2048]{1,0:T(8,128)(2,1)}, u32[]{:S(2)}, u32[]{:S(2)}) %collective-permute-start.7) | collective-permute-done | bytes 1048608 | tf_op jit(solution)/shard_map/ppermute | solution.py:57
  45.3 18.2 %collective-permute-done.12.refs_0_ = bf16[256,2048]{1,0:T(8,128)(2,1)S(1)} collective-permute-done((bf16[256,2048]{1,0:T(8,128)(2,1)}, bf16[256,2048]{1,0:T(8,128)(2,1)S(1)}, u32[]{:S(2)}, u32[]{:S(2)}) %collective-permute-start.12) | collective-permute-done | bytes 1048608 | tf_op jit(solution)/shard_map/ppermute | solution.py:682
  65.1 2.8 shard_map.255
  68.4 3.3 convert_reduce_fusion.5
  71.7 11.2 %collective-permute-done.9 = bf16[256,2048]{1,0:T(8,128)(2,1)} collective-permute-done((bf16[256,2048]{1,0:T(8,128)(2,1)}, bf16[256,2048]{1,0:T(8,128)(2,1)}, u32[]{:S(2)}, u32[]{:S(2)}) %collective-permute-start.9) | collective-permute-done | bytes 1048608 | tf_op jit(solution)/shard_map/ppermute | solution.py:57
  92.2 5.9 shard_map.256
  100.5 5.9 collective-permute-done.16
  106.4 3.5 collective-permute-start.18
  112.8 5.9 shard_map.258
  135.1 10.9 %shard_map.259.packed = bf16[1024,1536]{1,0:T(8,128)(2,1)} custom-call(bf16[1024,2048]{1,0:T(8,128)(2,1)} %bitcast.55, bf16[2048,2048]{1,0:T(8,128)(2,1)} %constant_dynamic-update-slice_fusion.40.refs_1_.mix.refs_4_, f32[1,1536]{1,0:T(1,128)} %copy-done.37), custom_call_target="tpu_custom_call" | custom-call | flops 100000000 | tf_op jit(solution)/shard_map/pallas_call | solution.py:263
  146.0 8.5 %shard_map.260.early = bf16[1024,1024]{1,0:T(8,128)(2,1)} custom-call(bf16[1024,2048]{1,0:T(8,128)(2,1)} %bitcast.60, bf16[2048,2048]{1,0:T(8,128)(2,1)} %constant_dynamic-update-slice_fusion.40.refs_1_.mix.refs_4_, f32[1,1024]{1,0:T(1,128)} %slice.211.refs_2_), custom_call_target="tpu_custom_call" | custom-call | flops 100000000 | tf_op jit(solution)/shard_map/pallas_call | solution.py:263
  158.1 14.9 %shard_map.261 = (bf16[1024,512]{1,0:T(8,128)(2,1)}, bf16[1024,1024]{1,0:T(8,128)(2,1)}, bf16[256,2048]{1,0:T(8,128)(2,1)}, bf16[256,2048]{1,0:T(8,128)(2,1)}, b...) custom-call(s32[4]{0:T(128)} %copy-done.40, s32[1]{0:T(128)} %bitcast.12.start, ...), custom_call_target="tpu_custom_call" | custom-call | flops 100000000 | tf_op jit(solution)/shard_map/pallas_call | solution.py:605
  173.1 5.1 collective-permute-done.25
  201.3 8.8 %collective-permute-done.32 = bf16[256,2048]{1,0:T(8,128)(2,1)} collective-permute-done((bf16[256,2048]{1,0:T(8,128)(2,1)}, bf16[256,2048]{1,0:T(8,128)(2,1)}, u32[]{:S(2)}, u32[]{:S(2)}) %collective-permute-start.32) | collective-permute-done | bytes 1048608 | tf_op jit(solution)/shard_map/ppermute | solution.py:57
  230.9 5.2 collective-permute-done.35
  236.1 8.7 %collective-permute-done.31.refs_2_ = bf16[256,2048]{1,0:T(8,128)(2,1)S(1)} collective-permute-done((bf16[256,2048]{1,0:T(8,128)(2,1)S(1)}, bf16[256,2048]{1,0:T(8,128)(2,1)S(1)}, u32[]{:S(2)}, u32[]{:S(2)}) %collective-permute-start.31) | collective-permute-done | bytes 1048608 | tf_op jit(solution)/shard_map/ppermute | solution.py:391
  249.5 19.1 %shard_map.263 = (bf16[1024,2048]{1,0:T(8,128)(2,1)}, bf16[1024,2048]{1,0:T(8,128)(2,1)}, bf16[1024,2048]{1,0:T(8,128)(2,1)}) custom-call(bf16[256,2048]{1,0:T(8,128)(2,1)} %copy-done.17, bf16[256,2048]{1,0:T(8,128)(2,1)} %copy-done.35, bf16[256,2048]{1,0:T(8,128)(2,1)} %copy-done.34, bf16[256,2048]{1,0:T(8,128)(2,1)} %copy-done.36, ...), custom_call_target="tpu_custom_call" | custom-call | flops 100000000 | tf_op jit(solution)/shard_map/pallas_call | solution.py:263
  280.4 13.5 %shard_map.264.refs_0_.refs_1_.own = bf16[2048,2048]{1,0:T(8,128)(2,1)} custom-call(bf16[1024,2048]{1,0:T(8,128)(2,1)} %constant_dynamic-update-slice_fusion.19.refs_0_, bf16[1024,2048]{1,0:T(8,128)(2,1)} %get-tuple-element.277.refs_1_.refs_0_), custom_call_target="tpu_custom_call" | custom-call | flops 100000000 | tf_op jit(solution)/shard_map/pallas_call | solution.py:337
  311.3 11.1 %collective-permute-done.41.refs_2_ = bf16[256,2048]{1,0:T(8,128)(2,1)} collective-permute-done((bf16[256,2048]{1,0:T(8,128)(2,1)}, bf16[256,2048]{1,0:T(8,128)(2,1)}, u32[]{:S(2)}, u32[]{:S(2)}) %collective-permute-start.41) | collective-permute-done | bytes 1048608 | tf_op jit(solution)/shard_map/ppermute | solution.py:57
  322.7 2.9 shard_map.266
  329.9 14.8 %shard_map.267 = (bf16[1024,2048]{1,0:T(8,128)(2,1)}, f32[1,2048]{1,0:T(1,128)}) custom-call(bf16[1024,2048]{1,0:T(8,128)(2,1)} %constant_dynamic-update-slice_fusion.19.refs_0_, bf16[2048,2048]{1,0:T(8,128)(2,1)} %constant_dynamic-update-slice_fusion.39.refs_1_, bf16[1024,2048]{1,0:T(8,128)(2,1)} %get-tuple-element.244.refs_2_), custom_call_target="tpu_custom_call" | custom-call | flops 100000000 | tf_op jit(solution)/shard_map/pallas_call | solution.py:263
  344.7 3.3 collective-permute-done.44.refs_3_
  348.9 3.3 shard_map.268
  354.2 13.1 %shard_map.269 = (bf16[256,2048]{1,0:T(8,128)(2,1)}, bf16[256,2048]{1,0:T(8,128)(2,1)}, bf16[256,2048]{1,0:T(8,128)(2,1)}, bf16[256,2048]{1,0:T(8,128)(2,1)}) custom-call(bf16[1024,2048]{1,0:T(8,128)(2,1)} %get-tuple-element.252.refs_0_.refs_1_, bf16[2048,2048]{1,0:T(8,128)(2,1)} %constant_dynamic-update-slice_fusion.23.refs_4_.refs_1_), custom_call_target="tpu_custom_call" | custom-call | flops 100000000 | tf_op jit(solution)/shard_map/pallas_call | solution.py:263
  367.3 6.5 collective-permute-done.46.refs_3_
  374.8 3.3 shard_map.270
  384.1 13.5 %shard_map.272.refs_0_.refs_1_ = bf16[2048,2048]{1,0:T(8,128)(2,1)} custom-call(bf16[1024,2048]{1,0:T(8,128)(2,1)} %get-tuple-element.268.refs_0_, bf16[1024,2048]{1,0:T(8,128)(2,1)} %get-tuple-element.252.refs_0_.refs_1_), custom_call_target="tpu_custom_call" | custom-call | flops 100000000 | tf_op jit(solution)/shard_map/pallas_call | solution.py:337
  400.3 3.7 collective-permute-done.51.behind
  409.1 5.2 shard_map.274
  414.8 13.0 %shard_map.275 = (bf16[256,2048]{1,0:T(8,128)(2,1)}, bf16[256,2048]{1,0:T(8,128)(2,1)}, bf16[256,2048]{1,0:T(8,128)(2,1)}, bf16[256,2048]{1,0:T(8,128)(2,1)}) custom-call(bf16[1024,2048]{1,0:T(8,128)(2,1)} %get-tuple-element.277.refs_1_.refs_0_, bf16[2048,2048]{1,0:T(8,128)(2,1)} %constant_dynamic-update-slice_fusion.39.refs_1_), custom_call_target="tpu_custom_call" | custom-call | flops 100000000 | tf_op jit(solution)/shard_map/pallas_call | solution.py:263
  429.7 3.3 shard_map.276
  433.1 5.7 collective-permute-done.56.refs_2_
  440.8 4.3 shard_map.277
  445.1 7.7 %shard_map.278 = (bf16[1024,512]{1,0:T(8,128)(2,1)}, bf16[1024,2048]{1,0:T(8,128)(2,1)}) custom-call(bf16[256,2048]{1,0:T(8,128)(2,1)} %get-tuple-element.290.refs_0_, bf16[256,2048]{1,0:T(8,128)(2,1)} %collective-permute-done.55.refs_1_, bf16[256,2048]{1,0:T(8,128)(2,1)} %copy-done.25, bf16[256,2048]{1,0:T(8,128)(2,1)} %collective-permute-done.57.refs_3_, ...), custom_call_target="tpu_custom_call" | custom-call | flops 100000000 | tf_op jit(solution)/shard_map/pallas_call | solution.py:263
  452.8 11.9 %collective-permute-done.58.refs_3_ = bf16[256,2048]{1,0:T(8,128)(2,1)} collective-permute-done((bf16[256,2048]{1,0:T(8,128)(2,1)}, bf16[256,2048]{1,0:T(8,128)(2,1)}, u32[]{:S(2)}, u32[]{:S(2)}) %collective-permute-start.58) | collective-permute-done | bytes 1048608 | tf_op jit(solution)/shard_map/ppermute | solution.py:57
  465.2 3.3 shard_map.279
  474.4 11.7 %shard_map.281 = (bf16[1024,1536]{1,0:T(8,128)(2,1)}, bf16[1024,1024]{1,0:T(8,128)(2,1)}) custom-call(s32[4]{0:T(128)} %copy-done.40, s32[1]{0:T(128)} %bitcast.12.start, bf16[1024,1536]{1,0:T(8,128)(2,1)} %shard_map.259.packed, bf16[1024,1024]{1,0:T(8,128)(2,1)} %shard_map.260.early, bf16[1024,1024]{1,0:T(8,128)(2,1)} %get-tuple-element.305.weights, ...), custom_call_target="tpu_custom_call" | custom-call | flops 100000000 | tf_op jit(solution)/shard_map/pallas_call | solution.py:605
  486.1 8.2 %shard_map.282.refs_0_.refs_1_ = bf16[512,2048]{1,0:T(8,128)(2,1)} custom-call(bf16[1024,2048]{1,0:T(8,128)(2,1)} %bitcast.56, bf16[1024,1536]{1,0:T(8,128)(2,1)} %get-tuple-element.327.refs_1_.refs_0_, bf16[1024,2048]{1,0:T(8,128)(2,1)} %bitcast.61, bf16[1024,1024]{1,0:T(8,128)(2,1)} %get-tuple-element.314.refs_3_.refs_0_, ...), custom_call_target="tpu_custom_call" | custom-call | flops 100000000 | tf_op jit(solution)/shard_map/pallas_call | solution.py:337
  496.5 2.8 shard_map.283
  502.2 8.6 %shard_map.285 = (bf16[256,2048]{1,0:T(8,128)(2,1)}, bf16[256,2048]{1,0:T(8,128)(2,1)}, bf16[256,2048]{1,0:T(8,128)(2,1)}, bf16[256,2048]{1,0:T(8,128)(2,1)}) custom-call(bf16[1024,1024]{1,0:T(8,128)(2,1)} %get-tuple-element.314.refs_3_.refs_0_, bf16[2048,2048]{1,0:T(8,128)(2,1)} %constant_dynamic-update-slice_fusion.40.refs_1_.mix.refs_4_), custom_call_target="tpu_custom_call" | custom-call | flops 100000000 | tf_op jit(solution)/shard_map/pallas_call | solution.py:263
  510.9 8.3 %shard_map.286.refs_0_ = bf16[512,2048]{1,0:T(8,128)(2,1)} custom-call(bf16[1024,2048]{1,0:T(8,128)(2,1)} %bitcast.57, bf16[1024,1536]{1,0:T(8,128)(2,1)} %get-tuple-element.327.refs_1_.refs_0_, bf16[1024,2048]{1,0:T(8,128)(2,1)} %bitcast.62, bf16[1024,1024]{1,0:T(8,128)(2,1)} %get-tuple-element.314.refs_3_.refs_0_, ...), custom_call_target="tpu_custom_call" | custom-call | flops 100000000 | tf_op jit(solution)/shard_map/pallas_call | solution.py:337
  519.2 3.5 add_add_fusion.refs_0_
  525.2 3.2 shard_map.287
  538.2 10.6 %shard_map.289 = (bf16[256,2048]{1,0:T(8,128)(2,1)}, bf16[256,2048]{1,0:T(8,128)(2,1)}, bf16[256,2048]{1,0:T(8,128)(2,1)}, bf16[256,2048]{1,0:T(8,128)(2,1)}) custom-call(bf16[1024,1536]{1,0:T(8,128)(2,1)} %get-tuple-element.327.refs_1_.refs_0_, bf16[2048,2048]{1,0:T(8,128)(2,1)} %constant_dynamic-update-slice_fusion.40.refs_1_.mix.refs_4_), custom_call_target="tpu_custom_call" | custom-call | flops 100000000 | tf_op jit(solution)/shard_map/pallas_call | solution.py:263
  548.8 8.2 %shard_map.290.refs_1_ = bf16[512,2048]{1,0:T(8,128)(2,1)} custom-call(bf16[1024,2048]{1,0:T(8,128)(2,1)} %bitcast.58, bf16[1024,1536]{1,0:T(8,128)(2,1)} %get-tuple-element.327.refs_1_.refs_0_, bf16[1024,2048]{1,0:T(8,128)(2,1)} %bitcast.63, bf16[1024,1024]{1,0:T(8,128)(2,1)} %get-tuple-element.314.refs_3_.refs_0_, ...), custom_call_target="tpu_custom_call" | custom-call | flops 100000000 | tf_op jit(solution)/shard_map/pallas_call | solution.py:337
  558.0 3.4 shard_map.291
  566.7 3.5 shard_map.296
  578.5 8.3 %shard_map.292.refs_0_.own = bf16[512,2048]{1,0:T(8,128)(2,1)} custom-call(bf16[1024,2048]{1,0:T(8,128)(2,1)} %bitcast.59, bf16[1024,1536]{1,0:T(8,128)(2,1)} %get-tuple-element.327.refs_1_.refs_0_, bf16[1024,2048]{1,0:T(8,128)(2,1)} %bitcast.64, bf16[1024,1024]{1,0:T(8,128)(2,1)} %get-tuple-element.314.refs_3_.refs_0_, ...), custom_call_target="tpu_custom_call" | custom-call | flops 100000000 | tf_op jit(solution)/shard_map/pallas_call | solution.py:337
  589.6 3.3 shard_map.294
  595.0 2.8 shard_map.295
  597.8 3.2 convert_add_fusion.1
  601.0 11.1 %collective-permute-done.76 = bf16[256,2048]{1,0:T(8,128)(2,1)} collective-permute-done((bf16[256,2048]{1,0:T(8,128)(2,1)}, bf16[256,2048]{1,0:T(8,128)(2,1)}, u32[]{:S(2)}, u32[]{:S(2)}) %collective-permute-start.76) | collective-permute-done | bytes 1048608 | tf_op jit(solution)/shard_map/ppermute | solution.py:825
  612.1 4.6 add_reduce_fusion
  618.2 3.8 collective-permute-done.77
  622.1 3.3 fusion.11.refs_0_
  625.5 2.9 shard_map.297
  628.4 4.4 collective-permute-done.80.behind
  634.9 3.7 collective-permute-done.81
  639.0 4.6 shard_map.298
  643.9 3.5 collective-permute-done.83
  (382 shorter events, 211.5 us)
Async XLA Ops:
  15.5 25.5 %collective-permute-start.7 = (bf16[256,2048]{1,0:T(8,128)(2,1)}, bf16[256,2048]{1,0:T(8,128)(2,1)}, u32[]{:S(2)}, u32[]{:S(2)}) collective-permute-start(bf16[256,2048]{1,0:T(8,128)(2,1)} %get-tuple-element.189), channel_id=1, source_target_pairs={{8,0},{16,8},{24,16},{28,24},{20,28},{12,20},{4,12},{0,4},{9,1},{1... | collective-permute-start | bytes 3145736 | tf_op jit(solution)/shard_map/ppermute | solution.py:57
  17.1 23.9 %collective-permute-start.6 = (bf16[256,2048]{1,0:T(8,128)(2,1)}, bf16[256,2048]{1,0:T(8,128)(2,1)}, u32[]{:S(2)}, u32[]{:S(2)}) collective-permute-start(bf16[256,2048]{1,0:T(8,128)(2,1)} %get-tuple-element.189), channel_id=1, source_target_pairs={{0,8},{8,16},{16,24},{24,28},{28,20},{20,12},{12,4},{4,0},{1,9},{9... | collective-permute-start | bytes 3145736 | tf_op jit(solution)/shard_map/ppermute | solution.py:57
  21.4 23.5 %collective-permute-start.4 = (bf16[256,2048]{1,0:T(8,128)(2,1)}, bf16[256,2048]{1,0:T(8,128)(2,1)}, u32[]{:S(2)}, u32[]{:S(2)}) collective-permute-start(bf16[256,2048]{1,0:T(8,128)(2,1)} %shard_map.254.refs_0_), channel_id=1, source_target_pairs={{0,2},{1,3},{2,0},{3,1},{4,6},{5,7},{6,4},{7,5},{8,10},{9,11},{10,... | collective-permute-start | bytes 3145736 | tf_op jit(solution)/shard_map/ppermute | solution.py:391
  25.7 37.8 %collective-permute-start.12 = (bf16[256,2048]{1,0:T(8,128)(2,1)}, bf16[256,2048]{1,0:T(8,128)(2,1)S(1)}, u32[]{:S(2)}, u32[]{:S(2)}) collective-permute-start(bf16[256,2048]{1,0:T(8,128)(2,1)} %shard_map.257), channel_id=1, source_target_pairs={{0,4},{4,8},{8,12},{12,16},{16,20},{20,24},{24,28},{1,5},{5,9},{9,... | collective-permute-start | bytes 3145736 | tf_op jit(solution)/shard_map/ppermute | solution.py:682
  41.0 26.8 %collective-permute-start.8 = (bf16[256,2048]{1,0:T(8,128)(2,1)}, bf16[256,2048]{1,0:T(8,128)(2,1)}, u32[]{:S(2)}, u32[]{:S(2)}) collective-permute-start(bf16[256,2048]{1,0:T(8,128)(2,1)} %collective-permute-done.6), channel_id=1, source_target_pairs={{0,8},{8,16},{16,24},{24,28},{28,20},{20,12},{12,4},{4,0},{1,9},{9... | collective-permute-start | bytes 3145736 | tf_op jit(solution)/shard_map/ppermute | solution.py:57
  41.0 41.8 %collective-permute-start.9 = (bf16[256,2048]{1,0:T(8,128)(2,1)}, bf16[256,2048]{1,0:T(8,128)(2,1)}, u32[]{:S(2)}, u32[]{:S(2)}) collective-permute-start(bf16[256,2048]{1,0:T(8,128)(2,1)} %collective-permute-done.7), channel_id=1, source_target_pairs={{8,0},{16,8},{24,16},{28,24},{20,28},{12,20},{4,12},{0,4},{9,1},{1... | collective-permute-start | bytes 3145736 | tf_op jit(solution)/shard_map/ppermute | solution.py:57
  44.8 41.2 %collective-permute-start.3 = (bf16[256,2048]{1,0:T(8,128)(2,1)S(1)}, bf16[256,2048]{1,0:T(8,128)(2,1)}, u32[]{:S(2)}, u32[]{:S(2)}) collective-permute-start(bf16[256,2048]{1,0:T(8,128)(2,1)S(1)} %copy-done.4), channel_id=1, source_target_pairs={{0,1},{1,0},{2,3},{3,2},{4,5},{5,4},{6,7},{7,6},{8,9},{9,8},{10,11... | collective-permute-start | bytes 3145736 | tf_op jit(solution)/shard_map/ppermute | solution.py:391
  44.9 42.6 %collective-permute-start.5 = (bf16[256,2048]{1,0:T(8,128)(2,1)}, bf16[256,2048]{1,0:T(8,128)(2,1)}, u32[]{:S(2)}, u32[]{:S(2)}) collective-permute-start(bf16[256,2048]{1,0:T(8,128)(2,1)} %collective-permute-done.4.refs_2_), channel_id=1, source_target_pairs={{0,1},{1,0},{2,3},{3,2},{4,5},{5,4},{6,7},{7,6},{8,9},{9,8},{10,11... | collective-permute-start | bytes 3145736 | tf_op jit(solution)/shard_map/ppermute | solution.py:391
  63.5 24.1 %collective-permute-start.14 = (bf16[256,2048]{1,0:T(8,128)(2,1)S(1)}, bf16[256,2048]{1,0:T(8,128)(2,1)}, u32[]{:S(2)}, u32[]{:S(2)}) collective-permute-start(bf16[256,2048]{1,0:T(8,128)(2,1)S(1)} %collective-permute-done.12.refs_0_), channel_id=1, source_target_pairs={{0,2},{1,3},{2,0},{3,1},{4,6},{5,7},{6,4},{7,5},{8,10},{9,11},{10,... | collective-permute-start | bytes 3145736 | tf_op jit(solution)/shard_map/ppermute | solution.py:391
  82.9 23.5 %collective-permute-start.16 = (bf16[256,2048]{1,0:T(8,128)(2,1)}, bf16[256,2048]{1,0:T(8,128)(2,1)}, u32[]{:S(2)}, u32[]{:S(2)}) collective-permute-start(bf16[256,2048]{1,0:T(8,128)(2,1)} %collective-permute-done.8), channel_id=1, source_target_pairs={{0,8},{8,16},{16,24},{24,28},{28,20},{20,12},{12,4},{4,0},{1,9},{9... | collective-permute-start | bytes 3145736 | tf_op jit(solution)/shard_map/ppermute | solution.py:57
  82.9 23.5 %collective-permute-start.17 = (bf16[256,2048]{1,0:T(8,128)(2,1)}, bf16[256,2048]{1,0:T(8,128)(2,1)}, u32[]{:S(2)}, u32[]{:S(2)}) collective-permute-start(bf16[256,2048]{1,0:T(8,128)(2,1)} %collective-permute-done.9), channel_id=1, source_target_pairs={{8,0},{16,8},{24,16},{28,24},{20,28},{12,20},{4,12},{0,4},{9,1},{1... | collective-permute-start | bytes 3145736 | tf_op jit(solution)/shard_map/ppermute | solution.py:57
  86.0 26.3 %collective-permute-start.22 = (bf16[256,2048]{1,0:T(8,128)(2,1)}, bf16[256,2048]{1,0:T(8,128)(2,1)}, u32[]{:S(2)}, u32[]{:S(2)}) collective-permute-start(bf16[256,2048]{1,0:T(8,128)(2,1)} %get-tuple-element.209), channel_id=1, source_target_pairs={{0,2},{1,3},{2,0},{3,1},{4,6},{5,7},{6,4},{7,5},{8,10},{9,11},{10,... | collective-permute-start | bytes 3145736 | tf_op jit(solution)/shard_map/ppermute | solution.py:391
  87.6 24.7 %collective-permute-start.13 = (bf16[256,2048]{1,0:T(8,128)(2,1)S(1)}, bf16[256,2048]{1,0:T(8,128)(2,1)}, u32[]{:S(2)}, u32[]{:S(2)}) collective-permute-start(bf16[256,2048]{1,0:T(8,128)(2,1)S(1)} %collective-permute-done.12.refs_0_), channel_id=1, source_target_pairs={{0,1},{1,0},{2,3},{3,2},{4,5},{5,4},{6,7},{7,6},{8,9},{9,8},{10,11... | collective-permute-start | bytes 3145736 | tf_op jit(solution)/shard_map/ppermute | solution.py:391
  87.6 25.2 %collective-permute-start.15 = (bf16[256,2048]{1,0:T(8,128)(2,1)}, bf16[256,2048]{1,0:T(8,128)(2,1)}, u32[]{:S(2)}, u32[]{:S(2)}) collective-permute-start(bf16[256,2048]{1,0:T(8,128)(2,1)} %collective-permute-done.14.refs_2_), channel_id=1, source_target_pairs={{0,1},{1,0},{2,3},{3,2},{4,5},{5,4},{6,7},{7,6},{8,9},{9,8},{10,11... | collective-permute-start | bytes 3145736 | tf_op jit(solution)/shard_map/ppermute | solution.py:391
  106.4 21.7 %collective-permute-start.18 = (bf16[256,2048]{1,0:T(8,128)(2,1)}, bf16[256,2048]{1,0:T(8,128)(2,1)}, u32[]{:S(2)}, u32[]{:S(2)}) collective-permute-start(bf16[256,2048]{1,0:T(8,128)(2,1)} %collective-permute-done.16), channel_id=1, source_target_pairs={{0,8},{8,16},{16,24},{24,28},{28,20},{20,12},{12,4},{4,0},{1,9},{9... | collective-permute-start | bytes 3145736 | tf_op jit(solution)/shard_map/ppermute | solution.py:57
  112.3 42.2 %collective-permute-start.21 = (bf16[256,2048]{1,0:T(8,128)(2,1)S(1)}, bf16[256,2048]{1,0:T(8,128)(2,1)S(1)}, u32[]{:S(2)}, u32[]{:S(2)}) collective-permute-start(bf16[256,2048]{1,0:T(8,128)(2,1)S(1)} %copy-done.12), channel_id=1, source_target_pairs={{0,1},{1,0},{2,3},{3,2},{4,5},{5,4},{6,7},{7,6},{8,9},{9,8},{10,11... | collective-permute-start | bytes 3145736 | tf_op jit(solution)/shard_map/ppermute | solution.py:391
  112.3 42.2 %collective-permute-start.23 = (bf16[256,2048]{1,0:T(8,128)(2,1)}, bf16[256,2048]{1,0:T(8,128)(2,1)}, u32[]{:S(2)}, u32[]{:S(2)}) collective-permute-start(bf16[256,2048]{1,0:T(8,128)(2,1)} %collective-permute-done.22), channel_id=1, source_target_pairs={{0,1},{1,0},{2,3},{3,2},{4,5},{5,4},{6,7},{7,6},{8,9},{9,8},{10,11... | collective-permute-start | bytes 3145736 | tf_op jit(solution)/shard_map/ppermute | solution.py:391
  130.0 24.6 %collective-permute-start.20 = (bf16[256,2048]{1,0:T(8,128)(2,1)}, bf16[256,2048]{1,0:T(8,128)(2,1)S(1)}, u32[]{:S(2)}, u32[]{:S(2)}) collective-permute-start(bf16[256,2048]{1,0:T(8,128)(2,1)} %param.26), channel_id=1, source_target_pairs={{0,8},{8,16},{16,24},{24,28},{28,20},{20,12},{12,4},{4,0},{1,9},{9... | collective-permute-start | bytes 3145736 | tf_op jit(solution)/shard_map/ppermute | solution.py:57
  132.1 23.8 %collective-permute-start.24 = (bf16[256,2048]{1,0:T(8,128)(2,1)}, bf16[256,2048]{1,0:T(8,128)(2,1)}, u32[]{:S(2)}, u32[]{:S(2)}) collective-permute-start(bf16[256,2048]{1,0:T(8,128)(2,1)} %collective-permute-done.19), channel_id=1, source_target_pairs={{8,0},{16,8},{24,16},{28,24},{20,28},{12,20},{4,12},{0,4},{9,1},{1... | collective-permute-start | bytes 3145736 | tf_op jit(solution)/shard_map/ppermute | solution.py:57
  155.9 22.2 %collective-permute-start.25 = (bf16[256,2048]{1,0:T(8,128)(2,1)S(1)}, bf16[256,2048]{1,0:T(8,128)(2,1)}, u32[]{:S(2)}, u32[]{:S(2)}) collective-permute-start(bf16[256,2048]{1,0:T(8,128)(2,1)S(1)} %collective-permute-done.20), channel_id=1, source_target_pairs={{0,8},{8,16},{16,24},{24,28},{28,20},{20,12},{12,4},{4,0},{1,9},{9... | collective-permute-start | bytes 3145736 | tf_op jit(solution)/shard_map/ppermute | solution.py:57
  157.9 22.4 %collective-permute-start.26 = (bf16[256,2048]{1,0:T(8,128)(2,1)}, bf16[256,2048]{1,0:T(8,128)(2,1)}, u32[]{:S(2)}, u32[]{:S(2)}) collective-permute-start(bf16[256,2048]{1,0:T(8,128)(2,1)} %collective-permute-done.24), channel_id=1, source_target_pairs={{8,0},{16,8},{24,16},{28,24},{20,28},{12,20},{4,12},{0,4},{9,1},{1... | collective-permute-start | bytes 3145736 | tf_op jit(solution)/shard_map/ppermute | solution.py:57
  184.2 25.9 %collective-permute-start.32 = (bf16[256,2048]{1,0:T(8,128)(2,1)}, bf16[256,2048]{1,0:T(8,128)(2,1)}, u32[]{:S(2)}, u32[]{:S(2)}) collective-permute-start(bf16[256,2048]{1,0:T(8,128)(2,1)} %collective-permute-done.25), channel_id=1, source_target_pairs={{0,8},{8,16},{16,24},{24,28},{28,20},{20,12},{12,4},{4,0},{1,9},{9... | collective-permute-start | bytes 3145736 | tf_op jit(solution)/shard_map/ppermute | solution.py:57
  185.9 25.6 %collective-permute-start.33 = (bf16[256,2048]{1,0:T(8,128)(2,1)}, bf16[256,2048]{1,0:T(8,128)(2,1)}, u32[]{:S(2)}, u32[]{:S(2)}) collective-permute-start(bf16[256,2048]{1,0:T(8,128)(2,1)} %collective-permute-done.26), channel_id=1, source_target_pairs={{8,0},{16,8},{24,16},{28,24},{20,28},{12,20},{4,12},{0,4},{9,1},{1... | collective-permute-start | bytes 3145736 | tf_op jit(solution)/shard_map/ppermute | solution.py:57
  186.2 27.4 %collective-permute-start.27 = (bf16[256,2048]{1,0:T(8,128)(2,1)}, bf16[256,2048]{1,0:T(8,128)(2,1)S(1)}, u32[]{:S(2)}, u32[]{:S(2)}) collective-permute-start(bf16[256,2048]{1,0:T(8,128)(2,1)} %get-tuple-element.221), channel_id=1, source_target_pairs={{0,1},{1,0},{2,3},{3,2},{4,5},{5,4},{6,7},{7,6},{8,9},{9,8},{10,11... | collective-permute-start | bytes 3145736 | tf_op jit(solution)/shard_map/ppermute | solution.py:391
  189.6 25.8 %collective-permute-start.29 = (bf16[256,2048]{1,0:T(8,128)(2,1)}, bf16[256,2048]{1,0:T(8,128)(2,1)S(1)}, u32[]{:S(2)}, u32[]{:S(2)}) collective-permute-start(bf16[256,2048]{1,0:T(8,128)(2,1)} %shard_map.262), channel_id=1, source_target_pairs={{0,2},{1,3},{2,0},{3,1},{4,6},{5,7},{6,4},{7,5},{8,10},{9,11},{10,... | collective-permute-start | bytes 3145736 | tf_op jit(solution)/shard_map/ppermute | solution.py:391
  211.5 24.6 %collective-permute-start.35 = (bf16[2048,256]{1,0:T(8,128)(2,1)S(1)}, bf16[2048,256]{1,0:T(8,128)(2,1)}, u32[]{:S(2)}, u32[]{:S(2)}) collective-permute-start(bf16[2048,256]{1,0:T(8,128)(2,1)S(1)} %copy-done.14), channel_id=1, source_target_pairs={{8,0},{16,8},{24,16},{28,24},{20,28},{12,20},{4,12},{0,4},{9,1},{1... | collective-permute-start | bytes 3145736 | tf_op jit(solution)/shard_map/ppermute | solution.py:57
  211.8 24.3 %collective-permute-start.34 = (bf16[2048,256]{1,0:T(8,128)(2,1)S(1)}, bf16[2048,256]{1,0:T(8,128)(2,1)}, u32[]{:S(2)}, u32[]{:S(2)}) collective-permute-start(bf16[2048,256]{1,0:T(8,128)(2,1)S(1)} %copy-done.14), channel_id=1, source_target_pairs={{0,8},{8,16},{16,24},{24,28},{28,20},{20,12},{12,4},{4,0},{1,9},{9... | collective-permute-start | bytes 3145736 | tf_op jit(solution)/shard_map/ppermute | solution.py:57
  220.0 24.8 %collective-permute-start.31 = (bf16[256,2048]{1,0:T(8,128)(2,1)S(1)}, bf16[256,2048]{1,0:T(8,128)(2,1)S(1)}, u32[]{:S(2)}, u32[]{:S(2)}) collective-permute-start(bf16[256,2048]{1,0:T(8,128)(2,1)S(1)} %get-tuple-element.228.refs_0_), channel_id=1, source_target_pairs={{0,2},{1,3},{2,0},{3,1},{4,6},{5,7},{6,4},{7,5},{8,10},{9,11},{10,... | collective-permute-start | bytes 3145736 | tf_op jit(solution)/shard_map/ppermute | solution.py:391
  244.8 25.9 %collective-permute-start.37 = (bf16[2048,256]{1,0:T(8,128)(2,1)}, bf16[2048,256]{1,0:T(8,128)(2,1)}, u32[]{:S(2)}, u32[]{:S(2)}) collective-permute-start(bf16[2048,256]{1,0:T(8,128)(2,1)} %collective-permute-done.34), channel_id=1, source_target_pairs={{0,8},{8,16},{16,24},{24,28},{28,20},{20,12},{12,4},{4,0},{1,9},{9... | collective-permute-start | bytes 3145736 | tf_op jit(solution)/shard_map/ppermute | solution.py:57
  246.5 25.7 %collective-permute-start.38 = (bf16[2048,256]{1,0:T(8,128)(2,1)}, bf16[2048,256]{1,0:T(8,128)(2,1)}, u32[]{:S(2)}, u32[]{:S(2)}) collective-permute-start(bf16[2048,256]{1,0:T(8,128)(2,1)} %collective-permute-done.35), channel_id=1, source_target_pairs={{8,0},{16,8},{24,16},{28,24},{20,28},{12,20},{4,12},{0,4},{9,1},{1... | collective-permute-start | bytes 3145736 | tf_op jit(solution)/shard_map/ppermute | solution.py:57
  272.2 24.9 %collective-permute-start.39 = (bf16[2048,256]{1,0:T(8,128)(2,1)}, bf16[2048,256]{1,0:T(8,128)(2,1)}, u32[]{:S(2)}, u32[]{:S(2)}) collective-permute-start(bf16[2048,256]{1,0:T(8,128)(2,1)} %collective-permute-done.37), channel_id=1, source_target_pairs={{0,8},{8,16},{16,24},{24,28},{28,20},{20,12},{12,4},{4,0},{1,9},{9... | collective-permute-start | bytes 3145736 | tf_op jit(solution)/shard_map/ppermute | solution.py:57
  274.0 24.9 %collective-permute-start.40 = (bf16[2048,256]{1,0:T(8,128)(2,1)}, bf16[2048,256]{1,0:T(8,128)(2,1)}, u32[]{:S(2)}, u32[]{:S(2)}) collective-permute-start(bf16[2048,256]{1,0:T(8,128)(2,1)} %collective-permute-done.38), channel_id=1, source_target_pairs={{8,0},{16,8},{24,16},{28,24},{20,28},{12,20},{4,12},{0,4},{9,1},{1... | collective-permute-start | bytes 3145736 | tf_op jit(solution)/shard_map/ppermute | solution.py:57
  298.8 23.6 %collective-permute-start.41 = (bf16[256,2048]{1,0:T(8,128)(2,1)}, bf16[256,2048]{1,0:T(8,128)(2,1)}, u32[]{:S(2)}, u32[]{:S(2)}) collective-permute-start(bf16[256,2048]{1,0:T(8,128)(2,1)} %shard_map.265), channel_id=1, source_target_pairs={{8,0},{16,8},{24,16},{28,24},{20,28},{12,20},{4,12},{0,4},{9,1},{1... | collective-permute-start | bytes 3145736 | tf_op jit(solution)/shard_map/ppermute | solution.py:57
  299.2 23.4 %collective-permute-start.42 = (bf16[2048,256]{1,0:T(8,128)(2,1)}, bf16[2048,256]{1,0:T(8,128)(2,1)}, u32[]{:S(2)}, u32[]{:S(2)}) collective-permute-start(bf16[2048,256]{1,0:T(8,128)(2,1)} %collective-permute-done.39), channel_id=1, source_target_pairs={{0,8},{8,16},{16,24},{24,28},{28,20},{20,12},{12,4},{4,0},{1,9},{9... | collective-permute-start | bytes 3145736 | tf_op jit(solution)/shard_map/ppermute | solution.py:57
  325.5 22.4 %collective-permute-start.44 = (bf16[256,2048]{1,0:T(8,128)(2,1)}, bf16[256,2048]{1,0:T(8,128)(2,1)S(1)}, u32[]{:S(2)}, u32[]{:S(2)}) collective-permute-start(bf16[256,2048]{1,0:T(8,128)(2,1)} %get-tuple-element.242), channel_id=1, source_target_pairs={{8,0},{16,8},{24,16},{28,24},{20,28},{12,20},{4,12},{0,4},{9,1},{1... | collective-permute-start | bytes 3145736 | tf_op jit(solution)/shard_map/ppermute | solution.py:57
  325.9 22.4 %collective-permute-start.43 = (bf16[256,2048]{1,0:T(8,128)(2,1)}, bf16[256,2048]{1,0:T(8,128)(2,1)}, u32[]{:S(2)}, u32[]{:S(2)}) collective-permute-start(bf16[256,2048]{1,0:T(8,128)(2,1)} %get-tuple-element.240), channel_id=1, source_target_pairs={{0,8},{8,16},{16,24},{24,28},{28,20},{20,12},{12,4},{4,0},{1,9},{9... | collective-permute-start | bytes 3145736 | tf_op jit(solution)/shard_map/ppermute | solution.py:57
  352.8 21.6 %collective-permute-start.45 = (bf16[256,2048]{1,0:T(8,128)(2,1)}, bf16[256,2048]{1,0:T(8,128)(2,1)}, u32[]{:S(2)}, u32[]{:S(2)}) collective-permute-start(bf16[256,2048]{1,0:T(8,128)(2,1)} %get-tuple-element.249), channel_id=1, source_target_pairs={{0,8},{8,16},{16,24},{24,28},{28,20},{20,12},{12,4},{4,0},{1,9},{9... | collective-permute-start | bytes 3145736 | tf_op jit(solution)/shard_map/ppermute | solution.py:57
  378.1 25.9 %collective-permute-start.51 = (bf16[256,2048]{1,0:T(8,128)(2,1)}, bf16[256,2048]{1,0:T(8,128)(2,1)}, u32[]{:S(2)}, u32[]{:S(2)}) collective-permute-start(bf16[256,2048]{1,0:T(8,128)(2,1)} %get-tuple-element.262), channel_id=1, source_target_pairs={{8,0},{16,8},{24,16},{28,24},{20,28},{12,20},{4,12},{0,4},{9,1},{1... | collective-permute-start | bytes 3145736 | tf_op jit(solution)/shard_map/ppermute | solution.py:57
  378.9 25.6 %collective-permute-start.50 = (bf16[256,2048]{1,0:T(8,128)(2,1)}, bf16[256,2048]{1,0:T(8,128)(2,1)}, u32[]{:S(2)}, u32[]{:S(2)}) collective-permute-start(bf16[256,2048]{1,0:T(8,128)(2,1)} %get-tuple-element.260), channel_id=1, source_target_pairs={{0,8},{8,16},{16,24},{24,28},{28,20},{20,12},{12,4},{4,0},{1,9},{9... | collective-permute-start | bytes 3145736 | tf_op jit(solution)/shard_map/ppermute | solution.py:57
  380.1 28.0 %collective-permute-start.47 = (bf16[256,2048]{1,0:T(8,128)(2,1)}, bf16[256,2048]{1,0:T(8,128)(2,1)S(1)}, u32[]{:S(2)}, u32[]{:S(2)}) collective-permute-start(bf16[256,2048]{1,0:T(8,128)(2,1)} %get-tuple-element.264), channel_id=1, source_target_pairs={{0,1},{1,0},{2,3},{3,2},{4,5},{5,4},{6,7},{7,6},{8,9},{9,8},{10,11... | collective-permute-start | bytes 3145736 | tf_op jit(solution)/shard_map/ppermute | solution.py:391
  383.5 25.5 %collective-permute-start.49 = (bf16[256,2048]{1,0:T(8,128)(2,1)}, bf16[256,2048]{1,0:T(8,128)(2,1)}, u32[]{:S(2)}, u32[]{:S(2)}) collective-permute-start(bf16[256,2048]{1,0:T(8,128)(2,1)} %shard_map.271), channel_id=1, source_target_pairs={{0,2},{1,3},{2,0},{3,1},{4,6},{5,7},{6,4},{7,5},{8,10},{9,11},{10,... | collective-permute-start | bytes 3145736 | tf_op jit(solution)/shard_map/ppermute | solution.py:391
  404.4 24.7 %collective-permute-start.53 = (bf16[256,2048]{1,0:T(8,128)(2,1)}, bf16[256,2048]{1,0:T(8,128)(2,1)}, u32[]{:S(2)}, u32[]{:S(2)}) collective-permute-start(bf16[256,2048]{1,0:T(8,128)(2,1)} %get-tuple-element.272), channel_id=1, source_target_pairs={{8,0},{16,8},{24,16},{28,24},{20,28},{12,20},{4,12},{0,4},{9,1},{1... | collective-permute-start | bytes 3145736 | tf_op jit(solution)/shard_map/ppermute | solution.py:57
  405.1 24.6 %collective-permute-start.52 = (bf16[256,2048]{1,0:T(8,128)(2,1)}, bf16[256,2048]{1,0:T(8,128)(2,1)}, u32[]{:S(2)}, u32[]{:S(2)}) collective-permute-start(bf16[256,2048]{1,0:T(8,128)(2,1)} %get-tuple-element.270), channel_id=1, source_target_pairs={{0,8},{8,16},{16,24},{24,28},{28,20},{20,12},{12,4},{4,0},{1,9},{9... | collective-permute-start | bytes 3145736 | tf_op jit(solution)/shard_map/ppermute | solution.py:57
  414.3 24.5 %collective-permute-start.56 = (bf16[256,2048]{1,0:T(8,128)(2,1)}, bf16[256,2048]{1,0:T(8,128)(2,1)S(1)}, u32[]{:S(2)}, u32[]{:S(2)}) collective-permute-start(bf16[256,2048]{1,0:T(8,128)(2,1)} %get-tuple-element.290.refs_0_), channel_id=1, source_target_pairs={{0,2},{1,3},{2,0},{3,1},{4,6},{5,7},{6,4},{7,5},{8,10},{9,11},{10,... | collective-permute-start | bytes 3145736 | tf_op jit(solution)/shard_map/ppermute | solution.py:391
  414.8 30.3 %collective-permute-start.55 = (bf16[256,2048]{1,0:T(8,128)(2,1)}, bf16[256,2048]{1,0:T(8,128)(2,1)}, u32[]{:S(2)}, u32[]{:S(2)}) collective-permute-start(bf16[256,2048]{1,0:T(8,128)(2,1)} %get-tuple-element.290.refs_0_), channel_id=1, source_target_pairs={{0,1},{1,0},{2,3},{3,2},{4,5},{5,4},{6,7},{7,6},{8,9},{9,8},{10,11... | collective-permute-start | bytes 3145736 | tf_op jit(solution)/shard_map/ppermute | solution.py:391
  438.8 25.9 %collective-permute-start.58 = (bf16[256,2048]{1,0:T(8,128)(2,1)}, bf16[256,2048]{1,0:T(8,128)(2,1)}, u32[]{:S(2)}, u32[]{:S(2)}) collective-permute-start(bf16[256,2048]{1,0:T(8,128)(2,1)} %get-tuple-element.287), channel_id=1, source_target_pairs={{8,0},{16,8},{24,16},{28,24},{20,28},{12,20},{4,12},{0,4},{9,1},{1... | collective-permute-start | bytes 3145736 | tf_op jit(solution)/shard_map/ppermute | solution.py:57
  439.6 25.6 %collective-permute-start.54 = (bf16[256,2048]{1,0:T(8,128)(2,1)}, bf16[256,2048]{1,0:T(8,128)(2,1)}, u32[]{:S(2)}, u32[]{:S(2)}) collective-permute-start(bf16[256,2048]{1,0:T(8,128)(2,1)} %get-tuple-element.285), channel_id=1, source_target_pairs={{0,8},{8,16},{16,24},{24,28},{28,20},{20,12},{12,4},{4,0},{1,9},{9... | collective-permute-start | bytes 3145736 | tf_op jit(solution)/shard_map/ppermute | solution.py:57
  468.5 27.9 %collective-permute-start.63 = (bf16[256,2048]{1,0:T(8,128)(2,1)}, bf16[256,2048]{1,0:T(8,128)(2,1)S(1)}, u32[]{:S(2)}, u32[]{:S(2)}) collective-permute-start(bf16[256,2048]{1,0:T(8,128)(2,1)} %get-tuple-element.300), channel_id=1, source_target_pairs={{8,0},{16,8},{24,16},{28,24},{20,28},{12,20},{4,12},{0,4},{9,1},{1... | collective-permute-start | bytes 3145736 | tf_op jit(solution)/shard_map/ppermute | solution.py:57
  469.2 27.2 %collective-permute-start.62 = (bf16[256,2048]{1,0:T(8,128)(2,1)}, bf16[256,2048]{1,0:T(8,128)(2,1)}, u32[]{:S(2)}, u32[]{:S(2)}) collective-permute-start(bf16[256,2048]{1,0:T(8,128)(2,1)} %get-tuple-element.298), channel_id=1, source_target_pairs={{0,8},{8,16},{16,24},{24,28},{28,20},{20,12},{12,4},{4,0},{1,9},{9... | collective-permute-start | bytes 3145736 | tf_op jit(solution)/shard_map/ppermute | solution.py:57
  470.6 48.7 %collective-permute-start.59 = (bf16[256,2048]{1,0:T(8,128)(2,1)}, bf16[256,2048]{1,0:T(8,128)(2,1)}, u32[]{:S(2)}, u32[]{:S(2)}) collective-permute-start(bf16[256,2048]{1,0:T(8,128)(2,1)} %get-tuple-element.302), channel_id=1, source_target_pairs={{0,1},{1,0},{2,3},{3,2},{4,5},{5,4},{6,7},{7,6},{8,9},{9,8},{10,11... | collective-permute-start | bytes 3145736 | tf_op jit(solution)/shard_map/ppermute | solution.py:391
  473.9 45.3 %collective-permute-start.61 = (bf16[256,2048]{1,0:T(8,128)(2,1)}, bf16[256,2048]{1,0:T(8,128)(2,1)}, u32[]{:S(2)}, u32[]{:S(2)}) collective-permute-start(bf16[256,2048]{1,0:T(8,128)(2,1)} %shard_map.280), channel_id=1, source_target_pairs={{0,2},{1,3},{2,0},{3,1},{4,6},{5,7},{6,4},{7,5},{8,10},{9,11},{10,... | collective-permute-start | bytes 3145736 | tf_op jit(solution)/shard_map/ppermute | solution.py:391
  499.3 25.2 %collective-permute-start.64 = (bf16[256,2048]{1,0:T(8,128)(2,1)}, bf16[256,2048]{1,0:T(8,128)(2,1)}, u32[]{:S(2)}, u32[]{:S(2)}) collective-permute-start(bf16[256,2048]{1,0:T(8,128)(2,1)} %shard_map.284), channel_id=1, source_target_pairs={{8,0},{16,8},{24,16},{28,24},{20,28},{12,20},{4,12},{0,4},{9,1},{1... | collective-permute-start | bytes 3145736 | tf_op jit(solution)/shard_map/ppermute | solution.py:57
  500.1 25.1 %collective-permute-start.65 = (bf16[256,2048]{1,0:T(8,128)(2,1)}, bf16[256,2048]{1,0:T(8,128)(2,1)S(1)}, u32[]{:S(2)}, u32[]{:S(2)}) collective-permute-start(bf16[256,2048]{1,0:T(8,128)(2,1)} %shard_map.283), channel_id=1, source_target_pairs={{0,8},{8,16},{16,24},{24,28},{28,20},{20,12},{12,4},{4,0},{1,9},{9... | collective-permute-start | bytes 3145736 | tf_op jit(solution)/shard_map/ppermute | solution.py:57
  528.4 28.6 %collective-permute-start.68 = (bf16[256,2048]{1,0:T(8,128)(2,1)}, bf16[256,2048]{1,0:T(8,128)(2,1)S(1)}, u32[]{:S(2)}, u32[]{:S(2)}) collective-permute-start(bf16[256,2048]{1,0:T(8,128)(2,1)} %get-tuple-element.324), channel_id=1, source_target_pairs={{8,0},{16,8},{24,16},{28,24},{20,28},{12,20},{4,12},{0,4},{9,1},{1... | collective-permute-start | bytes 3145736 | tf_op jit(solution)/shard_map/ppermute | solution.py:57
  529.6 28.4 %collective-permute-start.67 = (bf16[256,2048]{1,0:T(8,128)(2,1)}, bf16[256,2048]{1,0:T(8,128)(2,1)}, u32[]{:S(2)}, u32[]{:S(2)}) collective-permute-start(bf16[256,2048]{1,0:T(8,128)(2,1)} %get-tuple-element.322), channel_id=1, source_target_pairs={{0,8},{8,16},{16,24},{24,28},{28,20},{20,12},{12,4},{4,0},{1,9},{9... | collective-permute-start | bytes 3145736 | tf_op jit(solution)/shard_map/ppermute | solution.py:57
  532.2 34.4 %collective-permute-start.74 = (bf16[256,2048]{1,0:T(8,128)(2,1)}, bf16[256,2048]{1,0:T(8,128)(2,1)}, u32[]{:S(2)}, u32[]{:S(2)}) collective-permute-start(bf16[256,2048]{1,0:T(8,128)(2,1)} %get-tuple-element.353), channel_id=1, source_target_pairs={{0,1},{1,0},{2,3},{3,2},{4,5},{5,4},{6,7},{7,6},{8,9},{9,8},{10,11... | collective-permute-start | bytes 3145736 | tf_op jit(solution)/shard_map/ppermute | solution.py:391
  536.7 29.9 %collective-permute-start.75 = (bf16[256,2048]{1,0:T(8,128)(2,1)}, bf16[256,2048]{1,0:T(8,128)(2,1)}, u32[]{:S(2)}, u32[]{:S(2)}) collective-permute-start(bf16[256,2048]{1,0:T(8,128)(2,1)} %shard_map.288), channel_id=1, source_target_pairs={{0,2},{1,3},{2,0},{3,1},{4,6},{5,7},{6,4},{7,5},{8,10},{9,11},{10,... | collective-permute-start | bytes 3145736 | tf_op jit(solution)/shard_map/ppermute | solution.py:391
  561.9 26.3 %collective-permute-start.71 = (bf16[256,2048]{1,0:T(8,128)(2,1)}, bf16[256,2048]{1,0:T(8,128)(2,1)}, u32[]{:S(2)}, u32[]{:S(2)}) collective-permute-start(bf16[256,2048]{1,0:T(8,128)(2,1)} %get-tuple-element.335), channel_id=1, source_target_pairs={{8,0},{16,8},{24,16},{28,24},{20,28},{12,20},{4,12},{0,4},{9,1},{1... | collective-permute-start | bytes 3145736 | tf_op jit(solution)/shard_map/ppermute | solution.py:57
  563.3 26.3 %collective-permute-start.69 = (bf16[256,2048]{1,0:T(8,128)(2,1)}, bf16[256,2048]{1,0:T(8,128)(2,1)}, u32[]{:S(2)}, u32[]{:S(2)}) collective-permute-start(bf16[256,2048]{1,0:T(8,128)(2,1)} %get-tuple-element.333), channel_id=1, source_target_pairs={{0,8},{8,16},{16,24},{24,28},{28,20},{20,12},{12,4},{4,0},{1,9},{9... | collective-permute-start | bytes 3145736 | tf_op jit(solution)/shard_map/ppermute | solution.py:57
  566.6 34.4 %collective-permute-start.72 = (bf16[256,2048]{1,0:T(8,128)(2,1)}, bf16[256,2048]{1,0:T(8,128)(2,1)}, u32[]{:S(2)}, u32[]{:S(2)}) collective-permute-start(bf16[256,2048]{1,0:T(8,128)(2,1)} %get-tuple-element.351), channel_id=1, source_target_pairs={{0,1},{1,0},{2,3},{3,2},{4,5},{5,4},{6,7},{7,6},{8,9},{9,8},{10,11... | collective-permute-start | bytes 3145736 | tf_op jit(solution)/shard_map/ppermute | solution.py:391
  570.2 41.9 %collective-permute-start.76 = (bf16[256,2048]{1,0:T(8,128)(2,1)}, bf16[256,2048]{1,0:T(8,128)(2,1)}, u32[]{:S(2)}, u32[]{:S(2)}) collective-permute-start(bf16[256,2048]{1,0:T(8,128)(2,1)} %shard_map.296), channel_id=1, source_target_pairs={{4,0},{8,4},{12,8},{16,12},{20,16},{24,20},{28,24},{5,1},{9,5},{13... | collective-permute-start | bytes 3145736 | tf_op jit(solution)/shard_map/ppermute | solution.py:825
  574.4 37.6 %collective-permute-start.73 = (bf16[256,2048]{1,0:T(8,128)(2,1)}, bf16[256,2048]{1,0:T(8,128)(2,1)}, u32[]{:S(2)}, u32[]{:S(2)}) collective-permute-start(bf16[256,2048]{1,0:T(8,128)(2,1)} %shard_map.293), channel_id=1, source_target_pairs={{0,2},{1,3},{2,0},{3,1},{4,6},{5,7},{6,4},{7,5},{8,10},{9,11},{10,... | collective-permute-start | bytes 3145736 | tf_op jit(solution)/shard_map/ppermute | solution.py:391
  592.9 40.0 %collective-permute-start.80 = (bf16[256,2048]{1,0:T(8,128)(2,1)}, bf16[256,2048]{1,0:T(8,128)(2,1)}, u32[]{:S(2)}, u32[]{:S(2)}) collective-permute-start(bf16[256,2048]{1,0:T(8,128)(2,1)} %get-tuple-element.347), channel_id=1, source_target_pairs={{8,0},{16,8},{24,16},{28,24},{20,28},{12,20},{4,12},{0,4},{9,1},{1... | collective-permute-start | bytes 3145736 | tf_op jit(solution)/shard_map/ppermute | solution.py:57
  593.8 40.1 %collective-permute-start.79 = (bf16[256,2048]{1,0:T(8,128)(2,1)}, bf16[256,2048]{1,0:T(8,128)(2,1)}, u32[]{:S(2)}, u32[]{:S(2)}) collective-permute-start(bf16[256,2048]{1,0:T(8,128)(2,1)} %get-tuple-element.345), channel_id=1, source_target_pairs={{0,8},{8,16},{16,24},{24,28},{28,20},{20,12},{12,4},{4,0},{1,9},{9... | collective-permute-start | bytes 3145736 | tf_op jit(solution)/shard_map/ppermute | solution.py:57
  (62 other events, 589.9 us)
